TPU v7x, 32 devices: a whole 2x2x4 slice. The times are simulated.
32 devices in a mesh: rows: 8 (over z, x), text: 4 (over y, core).
Axes of the slice: x: 2, y: 2, z: 4, core: 2. Of those that a mesh axis runs over, the one named last changes fastest.
Arguments:
- frames: bfloat16 [8, 1024, 1024], P('rows', 'text'), may hold values from -6 to 6
- text_states: bfloat16 [8, 384, 1024], P('rows', 'text'), may hold values from -6 to 6
- frame_segments: int32 [8, 1024], P('rows'), may hold values from 0 to 3, never falling along the last dimension, each value on 1 to 832 neighbouring positions
- text_lengths: int32 [8, 4], P('rows'), may hold values from 1 to 312, 384 in all within a row
- self_in: bfloat16 [1024, 3072], P('rows', 'text'), may hold values from -0.1875 to 0.1875
- self_out: bfloat16 [1024, 1024], P('rows', 'text'), may hold values from -0.375 to 0.375
- cross_query: bfloat16 [1024, 1024], P('rows', 'text'), may hold values from -0.1875 to 0.1875
- cross_kv: bfloat16 [1024, 2048], P('rows', 'text'), may hold values from -0.1875 to 0.1875
- cross_out: bfloat16 [1024, 1024], P('rows', 'text'), may hold values from -0.375 to 0.375
- ffn_in: bfloat16 [1024, 4096], P('rows', 'text'), may hold values from -0.1875 to 0.1875
- ffn_out: bfloat16 [4096, 1024], P('rows', 'text'), may hold values from -0.09375 to 0.09375
- norm_gains: bfloat16 [3, 1024], P(None, 'text'), may hold values from 0.099609375 to 1.8984375
- norm_biases: bfloat16 [3, 1024], P(None, 'text'), may hold values from -1.796875 to 1.796875
- out_grad: bfloat16 [8, 1024, 1024], P('rows', 'text'), may hold values from -6 to 6
Outputs:
- output: bfloat16 [8, 1024, 1024], P('rows', 'text')
- frame_grad: float32 [8, 1024, 1024], P('rows', 'text')
- text_grad: float32 [8, 384, 1024], P('rows', 'text')
- grad_self_in: float32 [1024, 3072], P('rows', 'text')
- grad_self_out: float32 [1024, 1024], P('rows', 'text')
- grad_cross_query: float32 [1024, 1024], P('rows', 'text')
- grad_cross_kv: float32 [1024, 2048], P('rows', 'text')
- grad_cross_out: float32 [1024, 1024], P('rows', 'text')
- grad_ffn_in: float32 [1024, 4096], P('rows', 'text')
- grad_ffn_out: float32 [4096, 1024], P('rows', 'text')
- grad_norm_gains: float32 [3, 1024], P(None, 'text')
- grad_norm_biases: float32 [3, 1024], P(None, 'text')
Inputs may be any that keep to these rules, and one draw needn't show every extreme that they name: `frame_segments`: within a row the clip numbers never fall; each of the 4 clips has 1 to 832 frames, one exactly 832. `text_lengths`: each row's 4 lengths sum to 384; the largest is exactly 312.
All inputs are finite; a program needn't handle non-finite values.
Results may differ from a plain program's by a relative error of at most 0.024.
Values may be sent and summed in bfloat16 or wider, within the bound.
No kernel may reach another device: no remote copies, remote signals or barrier semaphores. Data moves between devices by JAX's collectives and lax.ppermute only.
A program may use at most 256 MiB of HBM per device.

v0:
```python
from functools import partial

import jax
import jax.numpy as jnp
from jax import lax
from jax.sharding import PartitionSpec as P

HEADS = 16


def layer_norm(values, scaling, offset):
    average = jnp.mean(values, axis=-1, keepdims=True)
    centred = values - average
    spread = jnp.mean(centred * centred, axis=-1, keepdims=True)
    return centred * lax.rsqrt(spread + 1e-05) * scaling + offset


def product(pattern, left, right):
    return jnp.einsum(pattern, left, right, preferred_element_type=jnp.float32)


def text_segment_ids(lengths, text_count):
    bounds = jnp.cumsum(lengths, axis=-1)[:, :-1]
    places = jnp.arange(text_count, dtype=jnp.int32)
    return jnp.sum((places[None, :, None] >= bounds[:, None, :]).astype(jnp.int32), axis=-1)


def split_heads(values, heads):
    return values.reshape(values.shape[0], values.shape[1], heads, values.shape[2] // heads)


def guarded(fold_piece, last_query):
    if last_query is None:
        return fold_piece

    def fold_guarded(state_now, key_block, block_start):
        return lax.cond(
            block_start <= last_query,
            lambda carried: fold_piece(carried, key_block, block_start),
            lambda carried: carried,
            state_now,
        )

    return fold_guarded


def forward_fold(query_heads, mask_for, heads, last_query):
    scaling = query_heads.shape[3] ** (-0.5)
    group_size = min(4, heads)

    def fold_piece(state_now, key_block, block_start):
        running_max, totals, weighted = state_now
        row_count, frame_count = (weighted.shape[0], weighted.shape[1])
        weighted_heads = weighted.reshape(row_count, frame_count, heads, -1)
        count_keys = key_block.shape[1]
        half_width = key_block.shape[2] // 2
        key_heads = split_heads(key_block[:, :, :half_width], heads)
        value_heads = split_heads(key_block[:, :, half_width:], heads)
        allowed = mask_for(block_start, count_keys)[:, None]
        max_parts, total_parts, weighted_parts = ([], [], [])
        for first_head in range(0, heads, group_size):
            chosen = slice(first_head, first_head + group_size)
            scores = (
                product("rqhe,rkhe->rhqk", query_heads[:, :, chosen], key_heads[:, :, chosen])
                * scaling
            )
            scores = jnp.where(allowed, scores, -1e30)
            previous = running_max[:, chosen]
            largest = jnp.maximum(previous, jnp.max(scores, axis=-1))
            weights = jnp.where(allowed, jnp.exp(scores - largest[..., None]), 0.0)
            factor = jnp.exp(previous - largest)
            total_parts.append(jnp.sum(weights, axis=-1))
            addition = product(
                "rhqk,rkhe->rqhe", weights.astype(jnp.bfloat16), value_heads[:, :, chosen]
            )
            weighted_parts.append(
                weighted_heads[:, :, chosen] * jnp.swapaxes(factor, 1, 2)[..., None] + addition
            )
            max_parts.append(largest)
        new_weighted = jnp.concatenate(weighted_parts, 2).reshape(row_count, frame_count, -1)
        return (jnp.concatenate(max_parts, 1), jnp.concatenate(total_parts, 1), new_weighted)

    return guarded(fold_piece, last_query)


def finish(state_now, heads):
    running_max, totals, weighted = state_now
    row_count, frame_count = (weighted.shape[0], weighted.shape[1])
    weighted_heads = weighted.reshape(row_count, frame_count, heads, -1)
    output_heads = weighted_heads / jnp.swapaxes(totals, 1, 2)[..., None]
    return (output_heads.reshape(row_count, frame_count, -1), running_max + jnp.log(totals))


def backward_fold(query_heads, grad_heads, delta, log_mass, mask_for, heads, last_query):
    scaling = query_heads.shape[3] ** (-0.5)
    group_size = min(4, heads)

    def fold_back(state_now, key_block, block_start):
        grad_query, grad_pairs = state_now
        row_count, frame_count = (grad_query.shape[0], grad_query.shape[1])
        count_keys = key_block.shape[1]
        half_width = key_block.shape[2] // 2
        key_heads = split_heads(key_block[:, :, :half_width], heads)
        value_heads = split_heads(key_block[:, :, half_width:], heads)
        allowed = mask_for(block_start, count_keys)[:, None]
        query_parts, key_parts, value_parts = ([], [], [])
        for first_head in range(0, heads, group_size):
            chosen = slice(first_head, first_head + group_size)
            scores = (
                product("rqhe,rkhe->rhqk", query_heads[:, :, chosen], key_heads[:, :, chosen])
                * scaling
            )
            probs = jnp.where(allowed, jnp.exp(scores - log_mass[:, chosen][..., None]), 0.0)
            value_parts.append(
                product("rhqk,rqhe->rkhe", probs.astype(jnp.bfloat16), grad_heads[:, :, chosen])
            )
            grad_prob = product(
                "rqhe,rkhe->rhqk", grad_heads[:, :, chosen], value_heads[:, :, chosen]
            )
            grad_score = (probs * (grad_prob - delta[:, chosen][..., None])).astype(jnp.bfloat16)
            query_parts.append(
                product("rhqk,rkhe->rqhe", grad_score, key_heads[:, :, chosen]) * scaling
            )
            key_parts.append(
                product("rhqk,rqhe->rkhe", grad_score, query_heads[:, :, chosen]) * scaling
            )
        grad_query = grad_query + jnp.concatenate(query_parts, 2).reshape(
            row_count, frame_count, -1
        )
        key_grads = jnp.concatenate(key_parts, 2).reshape(row_count, count_keys, -1)
        value_grads = jnp.concatenate(value_parts, 2).reshape(row_count, count_keys, -1)
        block_grads = jnp.concatenate([key_grads, value_grads], axis=2)
        current = grad_pairs
        grad_pairs = lax.dynamic_update_slice_in_dim(
            grad_pairs, current + block_grads, block_start, 1
        )
        return (grad_query, grad_pairs)

    return guarded(fold_back, last_query)


def head_delta(grad_low, output_wide, heads):
    joined = split_heads(grad_low.astype(jnp.float32) * output_wide, heads)
    return jnp.swapaxes(jnp.sum(joined, axis=-1), 1, 2)


def local(
    frames,
    text_states,
    frame_segments,
    text_lengths,
    self_in,
    self_out,
    cross_query,
    cross_kv,
    cross_out,
    ffn_in,
    ffn_out,
    norm_gains,
    norm_biases,
    out_grad,
):
    columns = (
        lax.all_gather(self_in, "text", axis=1, tiled=True),
        lax.all_gather(self_out, "text", axis=1, tiled=True),
        lax.all_gather(cross_query, "text", axis=1, tiled=True),
        lax.all_gather(cross_kv, "text", axis=1, tiled=True),
        lax.all_gather(cross_out, "text", axis=1, tiled=True),
        lax.all_gather(ffn_in, "text", axis=1, tiled=True),
        lax.all_gather(ffn_out, "text", axis=1, tiled=True),
        lax.all_gather(norm_gains, "text", axis=1, tiled=True),
        lax.all_gather(norm_biases, "text", axis=1, tiled=True),
    )
    gathered = (
        lax.all_gather(columns[0], "rows", axis=0, tiled=True),
        lax.all_gather(columns[1], "rows", axis=0, tiled=True),
        lax.all_gather(columns[2], "rows", axis=0, tiled=True),
        lax.all_gather(columns[3], "rows", axis=0, tiled=True),
        lax.all_gather(columns[4], "rows", axis=0, tiled=True),
        lax.all_gather(columns[5], "rows", axis=0, tiled=True),
        lax.all_gather(columns[6], "rows", axis=0, tiled=True),
    )
    (
        full_self_in,
        full_self_out,
        full_cross_query,
        full_cross_kv,
        full_cross_out,
        full_ffn_in,
        full_ffn_out,
    ) = gathered
    full_gains, full_biases = (columns[7], columns[8])
    row_count, frame_count, model_width = frames.shape
    heads = HEADS
    text_here = text_states.shape[1]
    member_count = lax.axis_size("text")
    first_frame = lax.axis_index("text") * frame_count
    last_query = first_frame + frame_count - 1
    query_place = first_frame + jnp.arange(frame_count, dtype=jnp.int32)
    query_segments = lax.dynamic_slice_in_dim(frame_segments, first_frame, frame_count, 1)
    all_text_segments = text_segment_ids(text_lengths, text_here * member_count)

    def self_mask(block_start, count_keys):
        key_place = jnp.arange(count_keys, dtype=jnp.int32)
        causal = key_place[None, None, :] <= query_place[None, :, None]
        return causal & (query_segments[:, :, None] == frame_segments[:, None, :])

    def cross_mask(block_start, count_keys):
        return query_segments[:, :, None] == all_text_segments[:, None, :]

    gains = full_gains.astype(jnp.float32)
    biases = full_biases.astype(jnp.float32)
    frames_wide = frames.astype(jnp.float32)
    start_state = (
        jnp.full((row_count, heads, frame_count), -1e30, jnp.float32),
        jnp.zeros((row_count, heads, frame_count), jnp.float32),
        jnp.zeros((row_count, frame_count, model_width), jnp.float32),
    )
    normed_one, pull_one = jax.vjp(layer_norm, frames_wide, gains[0], biases[0])
    normed_one_low = normed_one.astype(jnp.bfloat16)
    mixed = product("rfd,de->rfe", normed_one_low, full_self_in).astype(jnp.bfloat16)
    query_self = split_heads(mixed[:, :, :model_width], heads)
    pairs_self = mixed[:, :, model_width:]
    state_self = forward_fold(query_self, self_mask, heads, last_query)(
        start_state, lax.all_gather(pairs_self, "text", axis=1, tiled=True), jnp.int32(0)
    )
    self_wide, self_log = finish(state_self, heads)
    self_low = self_wide.astype(jnp.bfloat16)
    hidden = frames_wide + product("rfe,ed->rfd", self_low, full_self_out)
    normed_two, pull_two = jax.vjp(layer_norm, hidden, gains[1], biases[1])
    normed_two_low = normed_two.astype(jnp.bfloat16)
    query_cross_low = product("rfd,de->rfe", normed_two_low, full_cross_query).astype(jnp.bfloat16)
    query_cross = split_heads(query_cross_low, heads)
    text_pairs = product("rtd,de->rte", text_states, full_cross_kv).astype(jnp.bfloat16)
    state_cross = forward_fold(query_cross, cross_mask, heads, None)(
        start_state, lax.all_gather(text_pairs, "text", axis=1, tiled=True), jnp.int32(0)
    )
    cross_wide, cross_log = finish(state_cross, heads)
    cross_low = cross_wide.astype(jnp.bfloat16)
    hidden_two = hidden + product("rfe,ed->rfd", cross_low, full_cross_out)
    normed_three, pull_three = jax.vjp(layer_norm, hidden_two, gains[2], biases[2])
    normed_three_low = normed_three.astype(jnp.bfloat16)
    up_proj = product("rfd,dh->rfh", normed_three_low, full_ffn_in)
    activ, pull_gelu = jax.vjp(partial(jax.nn.gelu, approximate=False), up_proj)
    activ_low = activ.astype(jnp.bfloat16)
    output = (hidden_two + product("rfh,hd->rfd", activ_low, full_ffn_out)).astype(jnp.bfloat16)
    grad_ffn_out = product("rfh,rfd->hd", activ_low, out_grad)
    grad_activ = product("rfd,hd->rfh", out_grad, full_ffn_out)
    grad_up = pull_gelu(grad_activ)[0].astype(jnp.bfloat16)
    grad_ffn_in = product("rfd,rfh->dh", normed_three_low, grad_up)
    grad_normed_three = product("rfh,dh->rfd", grad_up, full_ffn_in)
    hidden_part, gain_three, bias_three = pull_three(grad_normed_three)
    grad_hidden_two = out_grad.astype(jnp.float32) + hidden_part
    grad_branch_two = grad_hidden_two.astype(jnp.bfloat16)
    grad_cross_out = product("rfe,rfd->ed", cross_low, grad_branch_two)
    grad_cross_att = product("rfd,ed->rfe", grad_branch_two, full_cross_out).astype(jnp.bfloat16)
    delta_cross = head_delta(grad_cross_att, cross_wide, heads)
    back_start = (
        jnp.zeros((row_count, frame_count, model_width), jnp.float32),
        jnp.zeros((row_count, text_here * member_count, 2 * model_width), jnp.float32),
    )
    grad_query_cross, grad_text_all = backward_fold(
        query_cross,
        split_heads(grad_cross_att, heads),
        delta_cross,
        cross_log,
        cross_mask,
        heads,
        None,
    )(back_start, lax.all_gather(text_pairs, "text", axis=1, tiled=True), jnp.int32(0))
    grad_text_pairs = lax.psum_scatter(
        grad_text_all.astype(jnp.bfloat16), "text", scatter_dimension=1, tiled=True
    )
    grad_cross_kv = product("rtd,rte->de", text_states, grad_text_pairs)
    text_grad = product("rte,de->rtd", grad_text_pairs, full_cross_kv)
    grad_cross_low = grad_query_cross.astype(jnp.bfloat16)
    grad_cross_query = product("rfd,rfe->de", normed_two_low, grad_cross_low)
    grad_normed_two = product("rfe,de->rfd", grad_cross_low, full_cross_query)
    hidden_part_two, gain_two, bias_two = pull_two(grad_normed_two)
    grad_hidden = grad_hidden_two + hidden_part_two
    grad_branch = grad_hidden.astype(jnp.bfloat16)
    grad_self_out = product("rfe,rfd->ed", self_low, grad_branch)
    grad_self_att = product("rfd,ed->rfe", grad_branch, full_self_out).astype(jnp.bfloat16)
    delta_self = head_delta(grad_self_att, self_wide, heads)
    self_start = (
        jnp.zeros((row_count, frame_count, model_width), jnp.float32),
        jnp.zeros((row_count, frame_count * member_count, 2 * model_width), jnp.float32),
    )
    grad_query_self, grad_pairs_all = backward_fold(
        query_self,
        split_heads(grad_self_att, heads),
        delta_self,
        self_log,
        self_mask,
        heads,
        last_query,
    )(self_start, lax.all_gather(pairs_self, "text", axis=1, tiled=True), jnp.int32(0))
    grad_pairs_self = lax.psum_scatter(
        grad_pairs_all.astype(jnp.bfloat16), "text", scatter_dimension=1, tiled=True
    )
    grad_mixed = jnp.concatenate([grad_query_self.astype(jnp.bfloat16), grad_pairs_self], axis=2)
    grad_self_in = product("rfd,rfe->de", normed_one_low, grad_mixed)
    grad_normed_one = product("rfe,de->rfd", grad_mixed, full_self_in)
    frame_part, gain_one, bias_one = pull_one(grad_normed_one)
    frame_grad = grad_hidden + frame_part
    grad_gains = jnp.stack([gain_one, gain_two, gain_three])
    grad_biases = jnp.stack([bias_one, bias_two, bias_three])
    parted = (
        lax.psum_scatter(
            grad_self_in.astype(jnp.bfloat16), "text", scatter_dimension=1, tiled=True
        ).astype(jnp.float32),
        lax.psum_scatter(
            grad_self_out.astype(jnp.bfloat16), "text", scatter_dimension=1, tiled=True
        ).astype(jnp.float32),
        lax.psum_scatter(
            grad_cross_query.astype(jnp.bfloat16), "text", scatter_dimension=1, tiled=True
        ).astype(jnp.float32),
        lax.psum_scatter(
            grad_cross_kv.astype(jnp.bfloat16), "text", scatter_dimension=1, tiled=True
        ).astype(jnp.float32),
        lax.psum_scatter(
            grad_cross_out.astype(jnp.bfloat16), "text", scatter_dimension=1, tiled=True
        ).astype(jnp.float32),
        lax.psum_scatter(
            grad_ffn_in.astype(jnp.bfloat16), "text", scatter_dimension=1, tiled=True
        ).astype(jnp.float32),
        lax.psum_scatter(
            grad_ffn_out.astype(jnp.bfloat16), "text", scatter_dimension=1, tiled=True
        ).astype(jnp.float32),
        lax.psum_scatter(
            grad_gains.astype(jnp.bfloat16), "text", scatter_dimension=1, tiled=True
        ).astype(jnp.float32),
        lax.psum_scatter(
            grad_biases.astype(jnp.bfloat16), "text", scatter_dimension=1, tiled=True
        ).astype(jnp.float32),
    )
    matrices = (
        lax.psum_scatter(parted[0], "rows", scatter_dimension=0, tiled=True),
        lax.psum_scatter(parted[1], "rows", scatter_dimension=0, tiled=True),
        lax.psum_scatter(parted[2], "rows", scatter_dimension=0, tiled=True),
        lax.psum_scatter(parted[3], "rows", scatter_dimension=0, tiled=True),
        lax.psum_scatter(parted[4], "rows", scatter_dimension=0, tiled=True),
        lax.psum_scatter(parted[5], "rows", scatter_dimension=0, tiled=True),
        lax.psum_scatter(parted[6], "rows", scatter_dimension=0, tiled=True),
    )
    norms_summed = lax.psum((parted[7], parted[8]), "rows")
    summed = (
        matrices[0],
        matrices[1],
        matrices[2],
        matrices[3],
        matrices[4],
        matrices[5],
        matrices[6],
        norms_summed[0],
        norms_summed[1],
    )
    return (
        output,
        frame_grad,
        text_grad,
        summed[0],
        summed[1],
        summed[2],
        summed[3],
        summed[4],
        summed[5],
        summed[6],
        summed[7],
        summed[8],
    )


def solution(mesh):
    in_specs = (
        P("rows", "text", None),
        P("rows", "text", None),
        P("rows", None),
        P("rows", None),
        P("rows", "text"),
        P("rows", "text"),
        P("rows", "text"),
        P("rows", "text"),
        P("rows", "text"),
        P("rows", "text"),
        P("rows", "text"),
        P(None, "text"),
        P(None, "text"),
        P("rows", "text", None),
    )
    out_specs = (
        P("rows", "text", None),
        P("rows", "text", None),
        P("rows", "text", None),
        P("rows", "text"),
        P("rows", "text"),
        P("rows", "text"),
        P("rows", "text"),
        P("rows", "text"),
        P("rows", "text"),
        P("rows", "text"),
        P(None, "text"),
        P(None, "text"),
    )
    return jax.shard_map(local, mesh=mesh, in_specs=in_specs, out_specs=out_specs, check_vma=False)
```

profile of v0, /device:TPU:0, one launch (start us, length us, event | category | flops | bytes accessed | tf_op | source)
XLA Modules:
  0.0 1787.1 jit_solution(6095312239457940174)
XLA Ops:
  7.3 10.4 all_gather.65
  17.7 9.5 all_gather.58
  28.6 63.0 %all-gather.21.cloned.1.call-done = bf16[1024,2048]{1,0:T(8,128)(2,1)} async-done(((bf16[128,2048]{1,0:T(8,128)(2,1)}), bf16[1024,2048]{1,0:T(8,128)(2,1)}) %all-gather.21.cloned.1.call-update) | async-done | bytes 4194320 | tf_op jit(solution)/shard_map/all_gather | solution.py:178
  91.5 3.7 convolution_convert_fusion.4
  95.4 5.2 all_gather.57
  100.5 5.1 all_gather.56
  106.2 84.8 %all-gather.13.cloned.1.call-done = bf16[1024,3072]{1,0:T(8,128)(2,1)} async-done(((bf16[128,3072]{1,0:T(8,128)(2,1)}), bf16[1024,3072]{1,0:T(8,128)(2,1)}) %all-gather.13.cloned.1.call-update) | async-done | bytes 6291472 | tf_op jit(solution)/shard_map/all_gather | solution.py:175
  191.0 4.7 fusion.152
  197.0 7.7 all_gather.61
  204.8 6.3 all_gather.63
  211.2 6.3 all_gather.68
  218.2 9.0 all-gather.29.cloned.1.call-done
  227.9 21.0 %all-gather.33.cloned.1.call-done = bf16[384,2048]{1,0:T(8,128)(2,1)} async-done(((bf16[96,2048]{1,0:T(8,128)(2,1)}), bf16[384,2048]{1,0:T(8,128)(2,1)}) %all-gather.33.cloned.1.call-update) | async-done | bytes 1572880 | tf_op jit(solution)/shard_map/all_gather | solution.py:236
  254.3 31.2 %all-gather.15.cloned.1.call-done = bf16[1,1024,2048]{2,1,0:T(8,128)(2,1)} async-done(((bf16[1,256,2048]{2,1,0:T(8,128)(2,1)}), bf16[1,1024,2048]{2,1,0:T(8,128)(2,1)}) %all-gather.15.cloned.1.call-update) | async-done | bytes 4194320 | tf_op jit(solution)/shard_map/all_gather | solution.py:225
  285.4 27.3 %conditional.2 = (f32[1,16,256]{2,1,0:T(8,128)S(1)}, f32[1,16,256]{2,1,0:T(8,128)S(1)}, f32[1,256,1024]{1,2,0:T(8,128)}, f32[1,16,256]{2,1,0:T(8,128)S(1)}, f32[256,1024]{1,0:T(8,128)S(1)}) conditional(s32[]{:T(128)} %convert_element_type.312, () %tuple.30, (s32[256]{0:T(256)S(1)}, s32[1,256]{1,0:T(1,128)S(1)}, s32[1,1024]{1,0:T(1,128)S(1)}, ...), branch_computations={%region_2.3_spmd, %region_3.12_spmd} | conditional | flops 1130135552 | bytes 87808040 | solution.py:37
  285.7 6.4 copy.84
  297.3 3.6 fusion.5
  300.9 4.0 fusion.7
  315.3 21.6 %all-gather.17.cloned.1.call-done = bf16[1024,1024]{1,0:T(8,128)(2,1)} async-done(((bf16[128,1024]{1,0:T(8,128)(2,1)}), bf16[1024,1024]{1,0:T(8,128)(2,1)}) %all-gather.17.cloned.1.call-update) | async-done | bytes 2097168 | tf_op jit(solution)/shard_map/all_gather | solution.py:176
  339.8 47.0 %all-gather.19.cloned.1.call-done = bf16[1024,1024]{1,0:T(8,128)(2,1)} async-done(((bf16[128,1024]{1,0:T(8,128)(2,1)}), bf16[1024,1024]{1,0:T(8,128)(2,1)}) %all-gather.19.cloned.1.call-update) | async-done | bytes 2097168 | tf_op jit(solution)/shard_map/all_gather | solution.py:177
  386.8 3.2 convolution_convert_fusion.10
  412.1 24.8 %all-gather.23.cloned.1.call-done = bf16[1024,1024]{1,0:T(8,128)(2,1)} async-done(((bf16[128,1024]{1,0:T(8,128)(2,1)}), bf16[1024,1024]{1,0:T(8,128)(2,1)}) %all-gather.23.cloned.1.call-update) | async-done | bytes 2097168 | tf_op jit(solution)/shard_map/all_gather | solution.py:179
  439.9 122.4 %all-gather.27.cloned.1.call-done = bf16[1024,4096]{1,0:T(8,128)(2,1)} async-done(((bf16[128,4096]{1,0:T(8,128)(2,1)}), bf16[1024,4096]{1,0:T(8,128)(2,1)}) %all-gather.27.cloned.1.call-update) | async-done | bytes 8388624 | tf_op jit(solution)/shard_map/all_gather | solution.py:180
  562.3 15.9 multiply_convert_fusion.4
  578.3 109.3 %all-gather.31.cloned.1.call-done = bf16[4096,1024]{1,0:T(8,128)(2,1)} async-done(((bf16[512,1024]{1,0:T(8,128)(2,1)}), bf16[4096,1024]{1,0:T(8,128)(2,1)}) %all-gather.31.cloned.1.call-update) | async-done | bytes 8388624 | tf_op jit(solution)/shard_map/all_gather | solution.py:181
  687.6 9.6 add_convert_fusion
  697.2 3.1 fusion.199
  722.6 8.4 copy.98
  731.0 4.0 copy.108
  755.5 44.2 %conditional.3 = (bf16[1,1024,2048]{1,2,0:T(8,128)(2,1)}, bf16[1,256,1024]{1,2,0:T(8,128)(2,1)}) conditional(s32[]{:T(128)} %convert_element_type.312, () %tuple.32, (s32[256]{0:T(256)S(1)}, s32[1,256]{1,0:T(1,128)S(1)}, s32[1,1024]{1,0:T(1,128)S(1)}, bf16[1,256,16,64]{1,3,2,0:T(8,128)(2,1)S(1)}, bf16[1,1024,2048]{2,1,0:T(8,128)(2,1)}, ...), branch_computations={%region_32.33_spmd, %region_33.34_spmd} | conditional | flops 2745176064 | bytes 171874480 | solution.py:37
  755.5 6.4 copy.95
  761.9 4.0 fusion.293
  773.1 3.5 fusion.102
  804.6 3.4 convert_bitcast_fusion
  808.1 3.5 convolution_convert_fusion.7
  811.7 3.3 convolution_convert_fusion.6
  815.1 3.3 convolution_convert_fusion.5
  818.4 7.4 convolution_convert_fusion.1
  826.9 7.3 convolution_convert_fusion
  834.2 8.5 reduce-scatter.25.cloned.1.call-done
  842.7 6.1 convolution_convert_fusion.2
  851.6 6.5 fusion.198
  860.7 28.9 %reduce-scatter.39.cloned.1.call-done = bf16[1024,512]{0,1:T(8,128)(2,1)} async-done(((bf16[1024,2048]{0,1:T(8,128)(2,1)}), bf16[1024,512]{0,1:T(8,128)(2,1)}) %reduce-scatter.39.cloned.1.call-update) | async-done | bytes 1048592 | tf_op jit(solution)/shard_map/reduce_scatter | solution.py:318
  889.6 2.8 convert_element_type.359
  892.5 31.1 %reduce-scatter.31.cloned.1.call-done = bf16[1024,256]{1,0:T(8,128)(2,1)} async-done(((bf16[1024,1024]{1,0:T(8,128)(2,1)}), bf16[1024,256]{1,0:T(8,128)(2,1)}) %reduce-scatter.31.cloned.1.call-update) | async-done | bytes 524304 | tf_op jit(solution)/shard_map/reduce_scatter | solution.py:312
  925.7 31.7 %reduce-scatter.35.cloned.1.call-done = bf16[1024,256]{1,0:T(8,128)(2,1)} async-done(((bf16[1024,1024]{1,0:T(8,128)(2,1)}), bf16[1024,256]{1,0:T(8,128)(2,1)}) %reduce-scatter.35.cloned.1.call-update) | async-done | bytes 524304 | tf_op jit(solution)/shard_map/reduce_scatter | solution.py:315
  959.6 31.8 %reduce-scatter.43.cloned.1.call-done = bf16[1024,256]{1,0:T(8,128)(2,1)} async-done(((bf16[1024,1024]{1,0:T(8,128)(2,1)}), bf16[1024,256]{1,0:T(8,128)(2,1)}) %reduce-scatter.43.cloned.1.call-update) | async-done | bytes 524304 | tf_op jit(solution)/shard_map/reduce_scatter | solution.py:321
  993.7 72.0 %reduce-scatter.47.cloned.1.call-done = bf16[1024,1024]{1,0:T(8,128)(2,1)} async-done(((bf16[1024,4096]{1,0:T(8,128)(2,1)}), bf16[1024,1024]{1,0:T(8,128)(2,1)}) %reduce-scatter.47.cloned.1.call-update) | async-done | bytes 2097168 | tf_op jit(solution)/shard_map/reduce_scatter | solution.py:324
  1065.7 4.1 convert_element_type.365
  1069.8 70.4 %reduce-scatter.51.cloned.1.call-done = bf16[4096,256]{1,0:T(8,128)(2,1)} async-done(((bf16[4096,1024]{1,0:T(8,128)(2,1)}), bf16[4096,256]{1,0:T(8,128)(2,1)}) %reduce-scatter.51.cloned.1.call-update) | async-done | bytes 2097168 | tf_op jit(solution)/shard_map/reduce_scatter | solution.py:327
  1140.2 3.9 convert_element_type.367
  1144.4 56.6 %reduce-scatter.27.cloned.1.call-done = bf16[1024,768]{1,0:T(8,128)(2,1)} async-done(((bf16[1024,3072]{1,0:T(8,128)(2,1)}), bf16[1024,768]{1,0:T(8,128)(2,1)}) %reduce-scatter.27.cloned.1.call-update) | async-done | bytes 1572880 | tf_op jit(solution)/shard_map/reduce_scatter | solution.py:309
  1201.0 3.3 convert_element_type.352
  1204.3 7.3 fusion.159
  1215.1 9.1 reduce-scatter.57.cloned.1.call-done
  1225.1 21.6 %reduce-scatter.59.cloned.1.call-done = bf16[256,3]{1,0:T(8,128)(2,1)} async-done(((bf16[1024,3]{1,0:T(8,128)(2,1)}), bf16[256,3]{1,0:T(8,128)(2,1)}) %reduce-scatter.59.cloned.1.call-update) | async-done | bytes 1552
  1247.6 22.4 %all-reduce = (f32[3,256]{1,0:T(4,128)}, f32[3,256]{1,0:T(4,128)}) all-reduce(bf16[3,256]{1,0:T(4,128)(2,1)S(1)} %copy.101, bf16[3,256]{1,0:T(4,128)(2,1)S(1)} %copy.103), channel_id=1, replica_groups=mesh['rows'=8,'text'=4] {'rows'}, use_global_device_ids=true, to_apply=%region_56.57 | all-reduce | flops 1536 | bytes 9216 | tf_op jit(solution)/shard_map/psum | solution.py:346
  1270.1 48.7 %reduce-scatter.41.cloned.1.call-done = f32[128,512]{0,1:T(8,128)} async-done(((f32[1024,512]{0,1:T(8,128)}), f32[128,512]{0,1:T(8,128)}) %reduce-scatter.41.cloned.1.call-update) | async-done | bytes 262160 | tf_op jit(solution)/shard_map/reduce_scatter | solution.py:341
  1320.6 64.9 %reduce-scatter.33.cloned.1.call-done = f32[128,256]{1,0:T(8,128)} async-done(((f32[1024,256]{1,0:T(8,128)}), f32[128,256]{1,0:T(8,128)}) %reduce-scatter.33.cloned.1.call-update) | async-done | bytes 131088 | tf_op jit(solution)/shard_map/reduce_scatter | solution.py:339
  1385.5 66.5 %reduce-scatter.37.cloned.1.call-done = f32[128,256]{1,0:T(8,128)} async-done(((f32[1024,256]{1,0:T(8,128)}), f32[128,256]{1,0:T(8,128)}) %reduce-scatter.37.cloned.1.call-update) | async-done | bytes 131088 | tf_op jit(solution)/shard_map/reduce_scatter | solution.py:340
  1452.0 66.7 %reduce-scatter.45.cloned.1.call-done = f32[128,256]{1,0:T(8,128)} async-done(((f32[1024,256]{1,0:T(8,128)}), f32[128,256]{1,0:T(8,128)}) %reduce-scatter.45.cloned.1.call-update) | async-done | bytes 131088 | tf_op jit(solution)/shard_map/reduce_scatter | solution.py:342
  1518.6 91.0 %reduce-scatter.49.cloned.1.call-done = f32[128,1024]{1,0:T(8,128)} async-done(((f32[1024,1024]{1,0:T(8,128)}), f32[128,1024]{1,0:T(8,128)}) %reduce-scatter.49.cloned.1.call-update) | async-done | bytes 524304 | tf_op jit(solution)/shard_map/reduce_scatter | solution.py:343
  1609.6 92.3 %reduce-scatter.53.cloned.1.call-done = f32[512,256]{1,0:T(8,128)} async-done(((f32[4096,256]{1,0:T(8,128)}), f32[512,256]{1,0:T(8,128)}) %reduce-scatter.53.cloned.1.call-update) | async-done | bytes 524304 | tf_op jit(solution)/shard_map/reduce_scatter | solution.py:344
  1701.9 78.4 %reduce-scatter.29.cloned.1.call-done = f32[128,768]{1,0:T(8,128)} async-done(((f32[1024,768]{1,0:T(8,128)}), f32[128,768]{1,0:T(8,128)}) %reduce-scatter.29.cloned.1.call-update) | async-done | bytes 393232 | tf_op jit(solution)/shard_map/reduce_scatter | solution.py:338
  (375 shorter events, 151.4 us)
Async XLA Ops:
  7.2 84.4 %copy-start = (bf16[1,96,1024]{2,1,0:T(8,128)(2,1)S(1)}, bf16[1,96,1024]{2,1,0:T(8,128)(2,1)}, u32[]{:S(2)}) copy-start(bf16[1,96,1024]{2,1,0:T(8,128)(2,1)} %param.19) | copy-start | bytes 589828
  7.2 88.2 %copy-start.72 = (bf16[3,256]{1,0:T(4,128)(2,1)S(1)}, bf16[3,256]{1,0:T(4,128)(2,1)}, u32[]{:S(2)}) copy-start(bf16[3,256]{1,0:T(4,128)(2,1)} %param.30) | copy-start | bytes 4612
  7.2 93.3 %copy-start.73 = (bf16[3,256]{1,0:T(4,128)(2,1)S(1)}, bf16[3,256]{1,0:T(4,128)(2,1)}, u32[]{:S(2)}) copy-start(bf16[3,256]{1,0:T(4,128)(2,1)} %param.29) | copy-start | bytes 4612
  7.2 98.5 %copy-start.1 = (bf16[1,256,1024]{2,1,0:T(8,128)(2,1)S(1)}, bf16[1,256,1024]{2,1,0:T(8,128)(2,1)}, u32[]{:S(2)}) copy-start(bf16[1,256,1024]{2,1,0:T(8,128)(2,1)} %param.18) | copy-start | bytes 1572868
  7.2 84.3 %all-gather.21.cloned.1.call-start = ((), (), s32[]{:S(2)}) async-start(), calls=%async_computation.22 | async-start | bytes 4718592 | tf_op jit(solution)/shard_map/all_gather | solution.py:178
  17.7 173.4 %all-gather.13.cloned.1.call-start = ((), (), s32[]{:S(2)}) async-start(), calls=%async_computation.18 | async-start | bytes 7077888 | tf_op jit(solution)/shard_map/all_gather | solution.py:175
  27.2 190.4 %all-gather.25.cloned.1.call-start = ((), (), s32[]{:S(2)}) async-start(), calls=%async_computation.24 | async-start | bytes 1310720 | tf_op jit(solution)/shard_map/all_gather | solution.py:169
  28.0 199.3 %all-gather.29.cloned.1.call-start = ((), (), s32[]{:S(2)}) async-start(), calls=%async_computation.26 | async-start | bytes 1310720 | tf_op jit(solution)/shard_map/all_gather | solution.py:170
  28.5 220.4 %all-gather.33.cloned.1.call-start = ((), (), s32[]{:S(2)}) async-start(), calls=%async_computation.43 | async-start | bytes 1966080 | tf_op jit(solution)/shard_map/all_gather | solution.py:236
  95.3 190.1 %all-gather.15.cloned.1.call-start = ((), (), s32[]{:S(2)}) async-start(), calls=%async_computation.19 | async-start | bytes 5242880 | tf_op jit(solution)/shard_map/all_gather | solution.py:225
  105.8 90.0 %copy-start.54 = (f32[256]{0:T(256)}, f32[256]{0:T(256)S(1)}, u32[]{:S(2)}) copy-start(f32[256]{0:T(256)S(1)} %broadcast_multiply_fusion.2) | copy-start | bytes 3076
  106.1 84.9 %copy-start.63 = (f32[256]{0:T(256)}, f32[256]{0:T(256)S(1)}, u32[]{:S(2)}) copy-start(f32[256]{0:T(256)S(1)} %fusion.197) | copy-start | bytes 3076
  106.1 89.7 %copy-start.52 = (f32[256]{0:T(256)}, f32[256]{0:T(256)S(1)}, u32[]{:S(2)}) copy-start(f32[256]{0:T(256)S(1)} %fusion.260) | copy-start | bytes 3076
  106.2 89.6 %copy-start.47 = (f32[1,1024]{1,0:T(1,128)}, f32[1,1024]{1,0:T(1,128)S(1)}, u32[]{:S(2)}) copy-start(f32[1,1024]{1,0:T(1,128)S(1)} %get-tuple-element.258) | copy-start | bytes 12292
  106.2 89.6 %copy-start.45 = (f32[1,1024]{1,0:T(1,128)}, f32[1,1024]{1,0:T(1,128)S(1)}, u32[]{:S(2)}) copy-start(f32[1,1024]{1,0:T(1,128)S(1)} %get-tuple-element.255) | copy-start | bytes 12292
  191.0 6.0 copy-start.49
  191.0 13.8 copy-start.50
  195.8 53.1 %copy-start.36 = (bf16[1,256,3072]{2,1,0:T(8,128)(2,1)}, bf16[1,256,3072]{2,1,0:T(8,128)(2,1)S(1)}, u32[]{:S(2)}) copy-start(bf16[1,256,3072]{2,1,0:T(8,128)(2,1)S(1)} %fusion.152) | copy-start | bytes 4718596
  195.8 15.4 copy-start.51
  195.8 31.7 %copy-start.77 = (s32[1,4]{1,0:T(1,128)S(1)}, s32[1,4]{1,0:T(1,128)}, u32[]{:S(2)}) copy-start(s32[1,4]{1,0:T(1,128)} %param.21) | copy-start | bytes 52
  195.9 31.8 %copy-start.56 = (s32[1,1024]{1,0:T(1,128)S(1)}, s32[1,1024]{1,0:T(1,128)}, u32[]{:S(2)}) copy-start(s32[1,1024]{1,0:T(1,128)} %param.20) | copy-start | bytes 12292
  196.9 139.9 %all-gather.17.cloned.1.call-start = ((), (), s32[]{:S(2)}) async-start(), calls=%async_computation.20 | async-start | bytes 2359296 | tf_op jit(solution)/shard_map/all_gather | solution.py:176
  204.7 182.1 %all-gather.19.cloned.1.call-start = ((), (), s32[]{:S(2)}) async-start(), calls=%async_computation.21 | async-start | bytes 2359296 | tf_op jit(solution)/shard_map/all_gather | solution.py:177
  211.2 225.7 %all-gather.23.cloned.1.call-start = ((), (), s32[]{:S(2)}) async-start(), calls=%async_computation.23 | async-start | bytes 2359296 | tf_op jit(solution)/shard_map/all_gather | solution.py:179
  217.6 344.7 %all-gather.27.cloned.1.call-start = ((), (), s32[]{:S(2)}) async-start(), calls=%async_computation.25 | async-start | bytes 9437184 | tf_op jit(solution)/shard_map/all_gather | solution.py:180
  218.2 469.4 %all-gather.31.cloned.1.call-start = ((), (), s32[]{:S(2)}) async-start(), calls=%async_computation.27 | async-start | bytes 9437184 | tf_op jit(solution)/shard_map/all_gather | solution.py:181
  227.3 572.5 %reduce-scatter.55.cloned.1.call-start = ((), (), s32[]{:S(2)}) async-start(), calls=%async_computation.44 | async-start | bytes 1966080
  227.7 57.7 %copy-start.67 = (s32[256]{0:T(256)}, s32[256]{0:T(256)S(1)}, u32[]{:S(2)}) copy-start(s32[256]{0:T(256)S(1)} %iota_add_fusion) | copy-start | bytes 3076
  248.9 5.1 slice-start
  252.9 143.6 %copy-start.17 = (bf16[1,384,1024]{1,2,0:T(8,128)(2,1)}, bf16[1,384,1024]{1,2,0:T(8,128)(2,1)S(1)}, u32[]{:S(2)}) copy-start(bf16[1,384,1024]{1,2,0:T(8,128)(2,1)S(1)} %copy.86) | copy-start | bytes 2359300
  339.5 54.0 %copy-start.57 = (f32[256]{0:T(256)}, f32[256]{0:T(256)S(1)}, u32[]{:S(2)}) copy-start(f32[256]{0:T(256)S(1)} %broadcast_multiply_fusion.1) | copy-start | bytes 3076
  339.7 55.2 %copy-start.65 = (f32[256]{0:T(256)}, f32[256]{0:T(256)S(1)}, u32[]{:S(2)}) copy-start(f32[256]{0:T(256)S(1)} %multiply_reduce_fusion.1) | copy-start | bytes 3076
  339.8 55.2 %copy-start.59 = (f32[256]{0:T(256)}, f32[256]{0:T(256)S(1)}, u32[]{:S(2)}) copy-start(f32[256]{0:T(256)S(1)} %fusion.261) | copy-start | bytes 3076
  393.4 9.1 copy-start.39
  395.0 6.4 copy-start.5
  687.6 9.6 copy-start.75
  709.5 7.0 copy-start.71
  735.0 107.7 %reduce-scatter.25.cloned.1.call-start = ((), (), s32[]{:S(2)}) async-start(), calls=%async_computation.28 | async-start | bytes 5242880 | tf_op jit(solution)/shard_map/reduce_scatter | solution.py:298
  735.1 10.5 copy-start.58
  735.1 10.5 copy-start.60
  738.7 6.9 copy-start.76
  749.6 5.8 copy-start.68
  799.7 89.9 %reduce-scatter.39.cloned.1.call-start = ((), (), s32[]{:S(2)}) async-start(), calls=%async_computation.35 | async-start | bytes 5242880 | tf_op jit(solution)/shard_map/reduce_scatter | solution.py:318
  808.1 115.5 %reduce-scatter.31.cloned.1.call-start = ((), (), s32[]{:S(2)}) async-start(), calls=%async_computation.31 | async-start | bytes 2621440 | tf_op jit(solution)/shard_map/reduce_scatter | solution.py:312
  811.7 145.8 %reduce-scatter.35.cloned.1.call-start = ((), (), s32[]{:S(2)}) async-start(), calls=%async_computation.33 | async-start | bytes 2621440 | tf_op jit(solution)/shard_map/reduce_scatter | solution.py:315
  815.1 176.4 %reduce-scatter.43.cloned.1.call-start = ((), (), s32[]{:S(2)}) async-start(), calls=%async_computation.37 | async-start | bytes 2621440 | tf_op jit(solution)/shard_map/reduce_scatter | solution.py:321
  818.4 247.3 %reduce-scatter.47.cloned.1.call-start = ((), (), s32[]{:S(2)}) async-start(), calls=%async_computation.39 | async-start | bytes 10485760 | tf_op jit(solution)/shard_map/reduce_scatter | solution.py:324
  825.8 314.3 %reduce-scatter.51.cloned.1.call-start = ((), (), s32[]{:S(2)}) async-start(), calls=%async_computation.41 | async-start | bytes 10485760 | tf_op jit(solution)/shard_map/reduce_scatter | solution.py:327
  834.1 8.6 copy-start.46
  834.1 8.6 copy-start.48
  834.1 8.6 copy-start.53
  834.1 8.6 copy-start.55
  834.2 366.8 %reduce-scatter.27.cloned.1.call-start = ((), (), s32[]{:S(2)}) async-start(), calls=%async_computation.29 | async-start | bytes 7864320 | tf_op jit(solution)/shard_map/reduce_scatter | solution.py:309
  848.9 375.3 %reduce-scatter.57.cloned.1.call-start = ((), (), s32[]{:S(2)}) async-start(), calls=%async_computation.45 | async-start | bytes 327680
  851.6 6.6 copy-start.64
  859.7 387.0 %reduce-scatter.59.cloned.1.call-start = ((), (), s32[]{:S(2)}) async-start(), calls=%async_computation.46 | async-start | bytes 327680
  860.7 458.1 %reduce-scatter.41.cloned.1.call-start = ((), (), s32[]{:S(2)}) async-start(), calls=%async_computation.36 | async-start | bytes 2359296 | tf_op jit(solution)/shard_map/reduce_scatter | solution.py:341
  892.5 493.0 %reduce-scatter.33.cloned.1.call-start = ((), (), s32[]{:S(2)}) async-start(), calls=%async_computation.32 | async-start | bytes 1179648 | tf_op jit(solution)/shard_map/reduce_scatter | solution.py:339
  925.7 526.3 %reduce-scatter.37.cloned.1.call-start = ((), (), s32[]{:S(2)}) async-start(), calls=%async_computation.34 | async-start | bytes 1179648 | tf_op jit(solution)/shard_map/reduce_scatter | solution.py:340
  959.6 559.0 %reduce-scatter.45.cloned.1.call-start = ((), (), s32[]{:S(2)}) async-start(), calls=%async_computation.38 | async-start | bytes 1179648 | tf_op jit(solution)/shard_map/reduce_scatter | solution.py:342
  993.6 616.0 %reduce-scatter.49.cloned.1.call-start = ((), (), s32[]{:S(2)}) async-start(), calls=%async_computation.40 | async-start | bytes 4718592 | tf_op jit(solution)/shard_map/reduce_scatter | solution.py:343
  1069.8 632.2 %reduce-scatter.53.cloned.1.call-start = ((), (), s32[]{:S(2)}) async-start(), calls=%async_computation.42 | async-start | bytes 4718592 | tf_op jit(solution)/shard_map/reduce_scatter | solution.py:344
  1144.1 636.2 %reduce-scatter.29.cloned.1.call-start = ((), (), s32[]{:S(2)}) async-start(), calls=%async_computation.30 | async-start | bytes 3538944 | tf_op jit(solution)/shard_map/reduce_scatter | solution.py:338
  1204.3 7.3 copy-start.4
  (44 other events, 117.3 us)
Sparse Core Ops, SparseCore 0:
  17.8 73.7 all-gather.20
  93.7 97.2 all-gather.12
  192.6 16.3 all-gather.24
  210.4 16.8 all-gather.28
  229.2 19.6 all-gather.32
  250.9 34.4 all-gather.14
  287.6 49.2 all-gather.16
  339.0 47.7 all-gather.18
  388.9 47.9 all-gather.22
  438.9 123.4 all-gather.26
  564.5 123.1 all-gather.30
  735.1 26.3 reduce-scatter.54
  799.8 42.8 reduce-scatter.24
  845.1 44.4 reduce-scatter.38
  892.2 31.3 reduce-scatter.30
  926.0 31.4 reduce-scatter.34
  960.0 31.4 reduce-scatter.42
  993.9 71.7 reduce-scatter.46
  1068.4 71.6 reduce-scatter.50
  1142.6 58.3 reduce-scatter.26
  1204.1 20.0 reduce-scatter.56
  1226.7 19.9 reduce-scatter.58
  1250.7 68.0 reduce-scatter.40
  1323.0 62.4 reduce-scatter.32
  1389.5 62.4 reduce-scatter.36
  1456.2 62.3 reduce-scatter.44
  1522.7 86.8 reduce-scatter.48
  1614.2 87.6 reduce-scatter.52
  1706.1 74.1 reduce-scatter.28
where the time goes:
time: 1790 us
  waiting for transfers between devices  1410 us (79%)
  matrix products  160 us (9%)
  local copies, waits for them, and re-layouts  80.3 us (4%)
  blocking collectives  73 us (4%)
  other arithmetic  49.4 us (3%)
    dot_general x73, matrix products, product(): return jnp.einsum(pattern, left, right, preferred_element_type=jnp.float32)  160 us
    all_gather x1, waiting for transfers between devices, local(): lax.all_gather(columns[5], 'rows', axis=0, tiled=True)  122 us
    all_gather x1, waiting for transfers between devices, local(): lax.all_gather(columns[6], 'rows', axis=0, tiled=True)  109 us
    reduce_scatter x1, waiting for transfers between devices, local(): lax.psum_scatter(parted[6], 'rows', scatter_dimension=0, tiled=True)  92.3 us
    reduce_scatter x1, waiting for transfers between devices, local(): lax.psum_scatter(parted[5], 'rows', scatter_dimension=0, tiled=True)  91 us
    all_gather x1, waiting for transfers between devices, local(): lax.all_gather(columns[0], 'rows', axis=0, tiled=True)  84.8 us
    reduce_scatter x1, waiting for transfers between devices, local(): lax.psum_scatter(parted[0], 'rows', scatter_dimension=0, tiled=True)  78.4 us
    reduce_scatter x1, waiting for transfers between devices, local(): lax.psum_scatter(grad_ffn_in.astype(jnp.bfloat16), 'text', scatter_dimens...  72 us
  transfers between devices with their start and end apart: 29, of which 27 were waited for; matrix products, arithmetic and copies ran while one was open for 13% of the time, Pallas kernels for 0%

commit v1 on v0

v1 whole, which is shorter than its diff:
```python
import math

import jax
import jax.numpy as jnp
from jax import lax
from jax.experimental import pallas as pl
from jax.experimental.pallas import tpu as pltpu
from jax.sharding import PartitionSpec as P

HEADS = 16
WAYS = 4
SLOTS = (0, 2, 1, 3)
LOW = jnp.bfloat16
WIDE = jnp.float32
NEVER = -1e30


def mm(left, right, left_dim=1, right_dim=0):
    return lax.dot_general(
        left, right, (((left_dim,), (right_dim,)), ((), ())), preferred_element_type=WIDE
    )


def swap(values, mask):
    return lax.ppermute(values, "text", [(i, i ^ mask) for i in range(WAYS)])


def gather_slots(block):
    pair = jnp.concatenate([block, swap(block, 2)], axis=0)
    return jnp.concatenate([pair, swap(pair, 1)], axis=0)


def scatter_slots(left, right, right_dim):
    half = left.shape[0] // 2
    block = half // 2
    away = mm(left[half:], right, 1, right_dim).astype(LOW)
    here = mm(left[:half], right, 1, right_dim)
    here = here + swap(away, 1).astype(WIDE)
    return here[:block] + swap(here[block:].astype(LOW), 2).astype(WIDE)


def norm_forward(values, gain, bias):
    average = jnp.mean(values, axis=-1, keepdims=True)
    centred = values - average
    spread = jnp.mean(centred * centred, axis=-1, keepdims=True)
    inverse = lax.rsqrt(spread + 1e-05)
    hat = centred * inverse
    return (hat * gain + bias).astype(LOW), hat, inverse


def norm_backward(grad, hat, inverse, gain):
    weighted = grad * gain
    first = jnp.mean(weighted, axis=-1, keepdims=True)
    second = jnp.mean(weighted * hat, axis=-1, keepdims=True)
    return (
        (weighted - first - hat * second) * inverse,
        jnp.sum(grad * hat, axis=0),
        jnp.sum(grad, axis=0),
    )


def slot_of(index, here):
    other = index ^ here
    return ((other & 1) << 1) | (other >> 1)


def half_lanes(values, head):
    lane = lax.broadcasted_iota(jnp.int32, values.shape, 1)
    keep = (lane < 64) if head == 0 else (lane >= 64)
    return jnp.where(keep, values, jnp.zeros_like(values))


def nt(left, right):
    return mm(left, right, 1, 1)


def rows_at(ref, slot, size, pair, offset):
    start = pl.multiple_of(slot * size, size)
    return ref[pl.ds(start, size), offset + pair * 128 : offset + (pair + 1) * 128]


def transposed(values):
    return values.astype(WIDE).T


def self_forward(here_ref, marks_ref, mixed_ref, out_ref, lse_ref):
    here = here_ref[0]
    size = mixed_ref.shape[0] // WAYS
    down = lax.broadcasted_iota(jnp.int32, (size, size), 0)
    across = lax.broadcasted_iota(jnp.int32, (size, size), 1)
    for pair in range(2):
        keys = [rows_at(mixed_ref, slot_of(j, here), size, pair, 256) for j in range(WAYS)]
        values_t = [
            transposed(rows_at(mixed_ref, slot_of(j, here), size, pair, 512)).astype(LOW)
            for j in range(WAYS)
        ]
        for i in range(WAYS):
            mine = slot_of(i, here)
            query = rows_at(mixed_ref, mine, size, pair, 0) * LOW(0.125)
            first = marks_ref[0:1, i * size : (i + 1) * size]
            outs = []
            for head in range(2):
                scores = []
                for j in range(i + 1):
                    s = nt(half_lanes(keys[j], head), query)
                    allowed = (down + j * size) >= first
                    if j == i:
                        allowed = allowed & (down <= across)
                    scores.append(jnp.where(allowed, s, NEVER))
                top = jnp.max(scores[0], axis=0, keepdims=True)
                for s in scores[1:]:
                    top = jnp.maximum(top, jnp.max(s, axis=0, keepdims=True))
                total = jnp.zeros_like(top)
                result = jnp.zeros((64, size), WIDE)
                for j, s in enumerate(scores):
                    probs = jnp.exp(s - top)
                    total = total + jnp.sum(probs, axis=0, keepdims=True)
                    part = values_t[j][head * 64 : (head + 1) * 64]
                    result = result + mm(part, probs.astype(LOW))
                outs.append(result / total)
                lse_ref[2 * pair + head : 2 * pair + head + 1, i * size : (i + 1) * size] = (
                    top + jnp.log(total)
                )
            start = pl.multiple_of(mine * size, size)
            out_ref[pl.ds(start, size), pair * 128 : (pair + 1) * 128] = (
                jnp.concatenate(outs, axis=0).T.astype(LOW)
            )


def self_backward(here_ref, marks_ref, mixed_ref, grad_ref, lse_ref, out_ref, dk_ref, dv_ref):
    here = here_ref[0]
    size = mixed_ref.shape[0] // WAYS
    down = lax.broadcasted_iota(jnp.int32, (size, size), 0)
    across = lax.broadcasted_iota(jnp.int32, (size, size), 1)
    for pair in range(2):
        keys = [rows_at(mixed_ref, slot_of(j, here), size, pair, 256) for j in range(WAYS)]
        values = [rows_at(mixed_ref, slot_of(j, here), size, pair, 512) for j in range(WAYS)]
        keys_t = [transposed(k).astype(LOW) for k in keys]
        for i in reversed(range(WAYS)):
            mine = slot_of(i, here)
            query = rows_at(mixed_ref, mine, size, pair, 0) * LOW(0.125)
            grad = rows_at(grad_ref, mine, size, pair, 0)
            first = marks_ref[0:1, i * size : (i + 1) * size]
            grads_q = []
            dk_parts = [None] * (i + 1)
            dv_parts = [None] * (i + 1)
            for head in range(2):
                mass = lse_ref[2 * pair + head : 2 * pair + head + 1, i * size : (i + 1) * size]
                grad_head = half_lanes(grad, head)
                query_head = half_lanes(query, head)
                probs, grad_probs = [], []
                delta = jnp.zeros((1, size), WIDE)
                for j in range(i + 1):
                    s = nt(half_lanes(keys[j], head), query)
                    allowed = (down + j * size) >= first
                    if j == i:
                        allowed = allowed & (down <= across)
                    p = jnp.exp(jnp.where(allowed, s, NEVER) - mass)
                    dp = nt(half_lanes(values[j], head), grad)
                    delta = delta + jnp.sum(p * dp, axis=0, keepdims=True)
                    probs.append(p)
                    grad_probs.append(dp)
                grad_q = jnp.zeros((64, size), WIDE)
                for j in range(i + 1):
                    ds = (probs[j] * (grad_probs[j] - delta)).astype(LOW)
                    dv = mm(probs[j].astype(LOW), grad_head)
                    dk = mm(ds, query_head)
                    dv_parts[j] = dv if head == 0 else dv_parts[j] + dv
                    dk_parts[j] = dk if head == 0 else dk_parts[j] + dk
                    grad_q = grad_q + mm(keys_t[j][head * 64 : (head + 1) * 64], ds)
                grads_q.append(grad_q)
            start = pl.multiple_of(mine * size, size)
            out_ref[pl.ds(start, size), pair * 128 : (pair + 1) * 128] = (
                (jnp.concatenate(grads_q, axis=0) * 0.125).T.astype(LOW)
            )
            for j in range(i + 1):
                rows = slice(j * size, (j + 1) * size)
                if i == WAYS - 1:
                    dk_ref[rows] = dk_parts[j]
                    dv_ref[rows] = dv_parts[j]
                else:
                    dk_ref[rows] = dk_ref[rows] + dk_parts[j]
                    dv_ref[rows] = dv_ref[rows] + dv_parts[j]
        for j in range(WAYS):
            rows = slice(j * size, (j + 1) * size)
            start = pl.multiple_of(slot_of(j, here) * size, size)
            out_ref[pl.ds(start, size), 256 + pair * 128 : 256 + (pair + 1) * 128] = dk_ref[
                rows
            ].astype(LOW)
            out_ref[pl.ds(start, size), 512 + pair * 128 : 512 + (pair + 1) * 128] = dv_ref[
                rows
            ].astype(LOW)


def token_places(here, count, width):
    row = lax.broadcasted_iota(jnp.int32, (count, width), 0)
    size = count // WAYS
    place = row
    for slot, mask in enumerate(SLOTS):
        inside = (row >= slot * size) & (row < (slot + 1) * size)
        place = jnp.where(inside, row - slot * size + (here ^ mask) * size, place)
    return place


def cross_forward(here_ref, marks_ref, query_ref, pairs_ref, out_ref, lse_ref):
    here = here_ref[0]
    size = query_ref.shape[0] // WAYS
    place = token_places(here, pairs_ref.shape[0], size)
    for pair in range(2):
        keys = pairs_ref[:, pair * 128 : (pair + 1) * 128]
        values_t = transposed(pairs_ref[:, 256 + pair * 128 : 256 + (pair + 1) * 128]).astype(LOW)
        for i in range(WAYS):
            mine = slot_of(i, here)
            query = rows_at(query_ref, mine, size, pair, 0) * LOW(0.125)
            low = marks_ref[1:2, i * size : (i + 1) * size]
            high = marks_ref[2:3, i * size : (i + 1) * size]
            allowed = (place >= low) & (place < high)
            outs = []
            for head in range(2):
                s = jnp.where(allowed, nt(half_lanes(keys, head), query), NEVER)
                top = jnp.max(s, axis=0, keepdims=True)
                probs = jnp.exp(s - top)
                total = jnp.sum(probs, axis=0, keepdims=True)
                result = mm(values_t[head * 64 : (head + 1) * 64], probs.astype(LOW))
                outs.append(result / total)
                lse_ref[2 * pair + head : 2 * pair + head + 1, i * size : (i + 1) * size] = (
                    top + jnp.log(total)
                )
            start = pl.multiple_of(mine * size, size)
            out_ref[pl.ds(start, size), pair * 128 : (pair + 1) * 128] = (
                jnp.concatenate(outs, axis=0).T.astype(LOW)
            )


def cross_backward(here_ref, marks_ref, query_ref, pairs_ref, grad_ref, lse_ref, dq_ref, dkv_ref):
    here = here_ref[0]
    size = query_ref.shape[0] // WAYS
    place = token_places(here, pairs_ref.shape[0], size)
    for pair in range(2):
        keys = pairs_ref[:, pair * 128 : (pair + 1) * 128]
        values = pairs_ref[:, 256 + pair * 128 : 256 + (pair + 1) * 128]
        keys_t = transposed(keys).astype(LOW)
        sum_k = jnp.zeros(keys.shape, WIDE)
        sum_v = jnp.zeros(keys.shape, WIDE)
        for i in range(WAYS):
            mine = slot_of(i, here)
            query = rows_at(query_ref, mine, size, pair, 0) * LOW(0.125)
            grad = rows_at(grad_ref, mine, size, pair, 0)
            low = marks_ref[1:2, i * size : (i + 1) * size]
            high = marks_ref[2:3, i * size : (i + 1) * size]
            allowed = (place >= low) & (place < high)
            grads_q = []
            for head in range(2):
                mass = lse_ref[2 * pair + head : 2 * pair + head + 1, i * size : (i + 1) * size]
                s = jnp.where(allowed, nt(half_lanes(keys, head), query), NEVER)
                p = jnp.exp(s - mass)
                dp = nt(half_lanes(values, head), grad)
                delta = jnp.sum(p * dp, axis=0, keepdims=True)
                ds = (p * (dp - delta)).astype(LOW)
                sum_v = sum_v + mm(p.astype(LOW), half_lanes(grad, head))
                sum_k = sum_k + mm(ds, half_lanes(query, head))
                grads_q.append(mm(keys_t[head * 64 : (head + 1) * 64], ds))
            start = pl.multiple_of(mine * size, size)
            dq_ref[pl.ds(start, size), pair * 128 : (pair + 1) * 128] = (
                (jnp.concatenate(grads_q, axis=0) * 0.125).T.astype(LOW)
            )
        dkv_ref[:, pair * 128 : (pair + 1) * 128] = sum_k.astype(LOW)
        dkv_ref[:, 256 + pair * 128 : 256 + (pair + 1) * 128] = sum_v.astype(LOW)


def call(body, outs, operands, scratch=(), flops=0, exps=0):
    specs = [pl.BlockSpec(memory_space=pltpu.SMEM)] + [
        pl.BlockSpec(memory_space=pltpu.VMEM) for _ in operands[1:]
    ]
    moved = sum(v.size * v.dtype.itemsize for v in operands)
    moved += sum(o.size * o.dtype.itemsize for o in outs)
    return pl.pallas_call(
        body,
        out_shape=outs,
        in_specs=specs,
        out_specs=[pl.BlockSpec(memory_space=pltpu.VMEM) for _ in outs],
        scratch_shapes=list(scratch),
        cost_estimate=pl.CostEstimate(flops=flops, bytes_accessed=moved, transcendentals=exps),
        compiler_params=pltpu.CompilerParams(vmem_limit_bytes=48 << 20),
    )(*operands)


def shaped(shape, dtype):
    return jax.ShapeDtypeStruct(shape, dtype)


def deal(matrix, groups):
    depth, width = matrix.shape
    piece = width // (groups * WAYS)
    return jnp.moveaxis(matrix.reshape(depth, groups, WAYS, piece), 2, 0).reshape(
        WAYS, depth, groups * piece
    )


def undeal(dealt, groups):
    _, depth, width = dealt.shape
    return jnp.moveaxis(dealt.reshape(WAYS, depth, groups, width // groups), 0, 2).reshape(
        depth, WAYS * width
    )


def exchange(dealt):
    return lax.all_to_all(dealt, "text", 0, 0, tiled=True)


def side_by_side(parts):
    return jnp.moveaxis(parts, 0, 1).reshape(parts.shape[1], -1)


def apart(columns):
    depth, width = columns.shape
    return jnp.moveaxis(columns.reshape(depth, WAYS, width // WAYS), 1, 0)


def gather_rows(block):
    return lax.all_gather(block, "rows", axis=0, tiled=True)


def sum_rows(whole):
    return lax.psum_scatter(whole, "rows", scatter_dimension=0, tiled=True)


def own_heads(matrix, here):
    rows = gather_rows(lax.all_gather(matrix, "text", axis=1, tiled=True))
    width = rows.shape[1]
    grouped = rows.reshape(HEADS // WAYS, WAYS, -1, width)
    return lax.dynamic_index_in_dim(grouped, here, 1, keepdims=False).reshape(-1, width)


def return_heads(grad, here):
    count, width = grad.shape
    spread = jnp.zeros((HEADS // WAYS, WAYS, count * WAYS // HEADS, width), grad.dtype)
    spread = lax.dynamic_update_index_in_dim(
        spread, grad.reshape(HEADS // WAYS, 1, -1, width), here, 1
    )
    columns = lax.psum_scatter(
        spread.reshape(count * WAYS, width), "text", scatter_dimension=1, tiled=True
    )
    return sum_rows(columns)


def local(
    frames,
    text_states,
    frame_segments,
    text_lengths,
    self_in,
    self_out,
    cross_query,
    cross_kv,
    cross_out,
    ffn_in,
    ffn_out,
    norm_gains,
    norm_biases,
    out_grad,
):
    here = lax.axis_index("text")
    here_low = here.astype(jnp.int32).reshape(1)
    row_count = lax.axis_size("rows")
    width = frames.shape[2]
    count = frames.shape[1] * WAYS
    inner = width // WAYS

    chunk = ffn_out.shape[0] // WAYS
    packed = jnp.concatenate(
        [deal(self_in, 3), deal(cross_query, 1), deal(cross_kv, 2)], axis=2
    )
    packed = exchange(packed)
    piece = inner // WAYS
    w_mixed = gather_rows(side_by_side(packed[:, :, : 3 * piece]))
    w_query = gather_rows(side_by_side(packed[:, :, 3 * piece : 4 * piece]))
    w_pairs = gather_rows(side_by_side(packed[:, :, 4 * piece :]))
    w_self = own_heads(self_out, here)
    w_cross = own_heads(cross_out, here)
    w_up = gather_rows(side_by_side(exchange(deal(ffn_in, row_count // WAYS))))
    w_down = gather_rows(
        side_by_side(exchange(ffn_out.reshape(WAYS, chunk, ffn_out.shape[1])))
    )

    norms = jnp.concatenate([norm_gains, norm_biases], axis=0)
    norms = lax.all_gather(norms, "text", axis=1, tiled=True).astype(WIDE)
    gains, biases = norms[:3], norms[3:]
    segments = frame_segments[0]
    clips = text_lengths.shape[1]
    ends = jnp.cumsum(text_lengths[0])
    clip = jnp.arange(clips, dtype=jnp.int32)
    begins = jnp.sum((segments[None, :] < clip[:, None]).astype(jnp.int32), axis=1)
    same = (segments[None, :] == clip[:, None]).astype(jnp.int32)
    marks = jnp.stack(
        [
            jnp.sum(same * begins[:, None], axis=0),
            jnp.sum(same * (ends - text_lengths[0])[:, None], axis=0),
            jnp.sum(same * ends[:, None], axis=0),
        ]
    )
    marks = jnp.concatenate([marks, jnp.zeros((5, count), jnp.int32)], axis=0)

    frames_wide = frames[0].astype(WIDE)
    one, hat_one, inverse_one = norm_forward(frames_wide, gains[0], biases[0])
    one_all = gather_slots(one)
    mixed = mm(one_all, w_mixed).astype(LOW)
    self_flops = count * count * inner * 2 * 5 // 8
    self_att, self_lse = call(
        self_forward,
        [shaped((count, inner), LOW), shaped((4, count), WIDE)],
        (here_low, marks, mixed),
        flops=2 * self_flops,
        exps=count * count * 5 // 2,
    )
    hidden = frames_wide + scatter_slots(self_att, w_self, 0)
    two, hat_two, inverse_two = norm_forward(hidden, gains[1], biases[1])
    two_all = gather_slots(two)
    query = mm(two_all, w_query).astype(LOW)
    text_all = gather_slots(text_states[0])
    text_count = text_all.shape[0]
    text_pairs = mm(text_all, w_pairs).astype(LOW)
    cross_flops = count * text_count * inner * 2
    cross_att, cross_lse = call(
        cross_forward,
        [shaped((count, inner), LOW), shaped((4, count), WIDE)],
        (here_low, marks, query, text_pairs),
        flops=2 * cross_flops,
        exps=count * text_count * 4,
    )
    hidden_two = hidden + scatter_slots(cross_att, w_cross, 0)
    three, hat_three, inverse_three = norm_forward(hidden_two, gains[2], biases[2])
    three_all = gather_slots(three)
    up = mm(three_all, w_up)
    phi = 0.5 * (1.0 + lax.erf(up * math.sqrt(0.5)))
    activ = (up * phi).astype(LOW)
    output = (hidden_two + scatter_slots(activ, w_down, 0)).astype(LOW)

    grad_all = gather_slots(out_grad[0])
    g_down = mm(activ, grad_all, 0, 0).astype(LOW)
    slope = phi + up * (jnp.exp(-0.5 * up * up) * (1.0 / math.sqrt(2.0 * math.pi)))
    grad_up = (mm(grad_all, w_down, 1, 1) * slope).astype(LOW)
    g_up = mm(three_all, grad_up, 0, 0).astype(LOW)
    part, gain_three, bias_three = norm_backward(
        scatter_slots(grad_up, w_up, 1), hat_three, inverse_three, gains[2]
    )
    grad_two = out_grad[0].astype(WIDE) + part
    branch_two = gather_slots(grad_two.astype(LOW))
    grad_cross = mm(branch_two, w_cross, 1, 1).astype(LOW)
    g_cross = mm(cross_att, branch_two, 0, 0).astype(LOW)
    grad_query, grad_pairs = call(
        cross_backward,
        [shaped((count, inner), LOW), shaped((text_count, 2 * inner), LOW)],
        (here_low, marks, query, text_pairs, grad_cross, cross_lse),
        flops=5 * cross_flops,
        exps=count * text_count * 4,
    )
    g_query = mm(two_all, grad_query, 0, 0).astype(LOW)
    g_pairs = mm(text_all, grad_pairs, 0, 0).astype(LOW)
    text_grad = scatter_slots(grad_pairs, w_pairs, 1)
    part, gain_two, bias_two = norm_backward(
        scatter_slots(grad_query, w_query, 1), hat_two, inverse_two, gains[1]
    )
    grad_hidden = grad_two + part
    branch = gather_slots(grad_hidden.astype(LOW))
    grad_self = mm(branch, w_self, 1, 1).astype(LOW)
    g_self = mm(self_att, branch, 0, 0).astype(LOW)
    (grad_mixed,) = call(
        self_backward,
        [shaped((count, 3 * inner), LOW)],
        (here_low, marks, mixed, grad_self, self_lse),
        scratch=[pltpu.VMEM((count, 128), WIDE), pltpu.VMEM((count, 128), WIDE)],
        flops=5 * self_flops,
        exps=count * count * 5 // 2,
    )
    g_mixed = mm(one_all, grad_mixed, 0, 0).astype(LOW)
    part, gain_one, bias_one = norm_backward(
        scatter_slots(grad_mixed, w_mixed, 1), hat_one, inverse_one, gains[0]
    )
    frame_grad = grad_hidden + part

    norm_sums = jnp.stack([gain_one, gain_two, gain_three, bias_one, bias_two, bias_three])
    norm_sums = lax.psum(norm_sums, ("rows", "text"))
    norm_sums = lax.dynamic_slice_in_dim(norm_sums, here * inner, inner, 1)

    d_down = exchange(apart(sum_rows(g_down))).reshape(ffn_out.shape).astype(WIDE)
    d_up = undeal(exchange(apart(sum_rows(g_up))), row_count // WAYS).astype(WIDE)
    d_cross = return_heads(g_cross, here).astype(WIDE)
    d_self = return_heads(g_self, here).astype(WIDE)
    d_query = undeal(exchange(apart(sum_rows(g_query))), 1).astype(WIDE)
    d_pairs = undeal(exchange(apart(sum_rows(g_pairs))), 2).astype(WIDE)
    d_mixed = undeal(exchange(apart(sum_rows(g_mixed))), 3).astype(WIDE)
    return (
        output[None],
        frame_grad[None],
        text_grad[None],
        d_mixed,
        d_self,
        d_query,
        d_pairs,
        d_cross,
        d_up,
        d_down,
        norm_sums[:3],
        norm_sums[3:],
    )


def solution(mesh):
    in_specs = (
        P("rows", "text", None),
        P("rows", "text", None),
        P("rows", None),
        P("rows", None),
        P("rows", "text"),
        P("rows", "text"),
        P("rows", "text"),
        P("rows", "text"),
        P("rows", "text"),
        P("rows", "text"),
        P("rows", "text"),
        P(None, "text"),
        P(None, "text"),
        P("rows", "text", None),
    )
    out_specs = (
        P("rows", "text", None),
        P("rows", "text", None),
        P("rows", "text", None),
        P("rows", "text"),
        P("rows", "text"),
        P("rows", "text"),
        P("rows", "text"),
        P("rows", "text"),
        P("rows", "text"),
        P("rows", "text"),
        P(None, "text"),
        P(None, "text"),
    )
    return jax.shard_map(local, mesh=mesh, in_specs=in_specs, out_specs=out_specs, check_vma=False)
```

time: 1790 us -> 935 us (0.52)
  waiting for transfers between devices: 1410 us -> 586 us
  matrix products: 160 us -> 63.8 us
  blocking collectives: 73 us -> 129 us
  local copies, waits for them, and re-layouts: 80.3 us -> 38.4 us
  starting transfers between devices: 1.83 us -> 39.5 us
  Pallas kernels: 0 us -> 29.4 us
  other arithmetic: 49.4 us -> 23 us
    reduce_scatter x15 -> x9, waiting for transfers between devices: 839 us -> 361 us  [the longest x7 309 us: sum_rows(): return lax.psum_scatter(whole, 'rows', scatter_dimension=0, tiled=True)]
    all_gather x11 -> x6, waiting for transfers between devices: 534 us -> 104 us  [gather_rows(): return lax.all_gather(block, 'rows', axis=0, tiled=True)]
    ppermute x0 -> x28, waiting for transfers between devices: none -> 119 us  [swap(): return lax.ppermute(values, 'text', [(i, i ^ mask) for i in range(WAYS)])]
    dot_general x73 -> x28, matrix products: 160 us -> 63.8 us  [mm(): lax.dot_general(left, right, (((left_dim,), (right_dim,)), ((), ())), pre...]
    all_to_all x0 -> x3, blocking collectives: none -> 41.5 us  [exchange(): return lax.all_to_all(dealt, 'text', 0, 0, tiled=True)]
    unnamed x32 -> x15, waiting for transfers between devices: 32.8 us -> 0.25 us
    pallas_call x0 -> x4, Pallas kernels: none -> 29.4 us  [call(): pl.pallas_call(body, out_shape=outs, in_specs=specs, out_specs=[pl.BlockS...]
    ppermute x0 -> x28, starting transfers between devices: none -> 21.2 us  [swap(): return lax.ppermute(values, 'text', [(i, i ^ mask) for i in range(WAYS)])]
  transfers between devices with their start and end apart: 29 -> 48, of which waited for: 27 -> 29; matrix products, arithmetic and copies ran while one was open for 13% -> 10% of each run, Pallas kernels for 0% -> 2%
where the time goes in v1:
time: 935 us; the launch traced here: 925 us
  waiting for transfers between devices  586 us (63%)
  blocking collectives  129 us (14%)
  matrix products  63.8 us (7%)
  starting transfers between devices  39.5 us (4%)
  local copies, waits for them, and re-layouts  38.4 us (4%)
  Pallas kernels  29.4 us (3%)
  other arithmetic  23 us (2%)
  between operations  15.3 us (2%)
    reduce_scatter x7, waiting for transfers between devices, sum_rows(): return lax.psum_scatter(whole, 'rows', scatter_dimension=0, tiled=True)  309 us
    ppermute x28, waiting for transfers between devices, swap(): return lax.ppermute(values, 'text', [(i, i ^ mask) for i in range(WAYS)])  119 us
    all_gather x6, waiting for transfers between devices, gather_rows(): return lax.all_gather(block, 'rows', axis=0, tiled=True)  104 us
    dot_general x28, matrix products, mm(): lax.dot_general(left, right, (((left_dim,), (right_dim,)), ((), ())), pre...  63.8 us
    reduce_scatter x2, waiting for transfers between devices, return_heads(): lax.psum_scatter(spread.reshape(count * WAYS, width), 'text', scatter_dim...  52 us
    all_to_all x3, blocking collectives, exchange(): return lax.all_to_all(dealt, 'text', 0, 0, tiled=True)  41.5 us
    psum x1, blocking collectives, local(): norm_sums = lax.psum(norm_sums, ('rows', 'text'))  40.4 us
    all_gather x1, blocking collectives, gather_rows(): return lax.all_gather(block, 'rows', axis=0, tiled=True)  29.5 us
  transfers between devices with their start and end apart: 48, of which 29 were waited for; matrix products, arithmetic and copies ran while one was open for 10% of the time, Pallas kernels for 2%

profile of v1, /device:TPU:0, one launch (start us, length us, event | category | flops | bytes accessed | tf_op | source)
XLA Modules:
  0.0 924.6 jit_solution(12082576736013837687)
XLA Ops:
  10.5 11.5 %all_to_all.40 = bf16[4,128,384]{1,2,0:T(8,128)(2,1)S(1)} all-to-all(bf16[4,128,384]{1,2,0:T(8,128)(2,1)S(1)} %pad_maximum_fusion.25), channel_id=1, replica_groups=mesh['rows'=8,'text'=4] {'text'}, dimensions={0} | all-to-all | bytes 786432 | tf_op jit(solution)/shard_map/all_to_all | solution.py:308
  22.7 6.3 all_gather.32
  29.1 5.2 all_gather.30
  36.4 13.6 %collective-permute-done = bf16[256,1024]{1,0:T(8,128)(2,1)S(1)} collective-permute-done((bf16[256,1024]{1,0:T(8,128)(2,1)S(1)}, bf16[256,1024]{1,0:T(8,128)(2,1)S(1)}, u32[]{:S(2)}, u32[]{:S(2)}) %collective-permute-start) | collective-permute-done | bytes 524320 | tf_op jit(solution)/shard_map/ppermute | solution.py:25
  50.2 6.5 all_gather.36
  57.3 11.1 %all-gather.7.cloned.1.call-done = bf16[1024,768]{0,1:T(8,128)(2,1)} async-done(((bf16[128,768]{0,1:T(8,128)(2,1)}), bf16[1024,768]{0,1:T(8,128)(2,1)}) %all-gather.7.cloned.1.call-update) | async-done | bytes 1572880 | tf_op jit(solution)/shard_map/all_gather | solution.py:321
  68.4 3.6 convolution_convert_fusion.3.mixed_ref
  72.0 6.4 shard_map.229
  79.6 38.6 %all-gather.9.cloned.1.call-done = bf16[1024,1024]{1,0:T(8,128)(2,1)} async-done(((bf16[128,1024]{1,0:T(8,128)(2,1)}), bf16[1024,1024]{1,0:T(8,128)(2,1)}) %all-gather.9.cloned.1.call-update) | async-done | bytes 2097168 | tf_op jit(solution)/shard_map/all_gather | solution.py:321
  119.8 2.6 collective-permute-done.2
  124.6 12.5 %collective-permute-done.3 = bf16[256,1024]{1,0:T(8,128)(2,1)S(1)} collective-permute-done((bf16[256,1024]{1,0:T(8,128)(2,1)S(1)}, bf16[256,1024]{1,0:T(8,128)(2,1)S(1)}, u32[]{:S(2)}, u32[]{:S(2)}) %collective-permute-start.3) | collective-permute-done | bytes 524320 | tf_op jit(solution)/shard_map/ppermute | solution.py:25
  139.6 14.5 %all_to_all.41 = bf16[4,128,256]{1,2,0:T(8,128)(2,1)} all-to-all(bf16[4,128,256]{1,2,0:T(8,128)(2,1)S(1)} %bitcast.198), channel_id=1, replica_groups=mesh['rows'=8,'text'=4] {'text'}, dimensions={0} | all-to-all | bytes 524288 | tf_op jit(solution)/shard_map/all_to_all | solution.py:308
  156.2 2.1 pad_maximum_fusion.7
  158.3 3.0 collective-permute-done.6
  161.4 29.5 %all_gather.34 = bf16[1024,256]{0,1:T(8,128)(2,1)S(1)} all-gather(bf16[128,256]{0,1:T(8,128)(2,1)S(1)} %bitcast.214), channel_id=1, replica_groups=mesh['rows'=8,'text'=4] {'rows'}, dimensions={0}, use_global_device_ids=true | all-gather | bytes 589824 | tf_op jit(solution)/shard_map/all_gather | solution.py:321
  190.9 2.1 convolution_convert_fusion.18.pairs_ref
  193.1 20.5 %all-gather.13.cloned.1.call-done = bf16[1024,1024]{1,0:T(8,128)(2,1)} async-done(((bf16[128,1024]{1,0:T(8,128)(2,1)}), bf16[1024,1024]{1,0:T(8,128)(2,1)}) %all-gather.13.cloned.1.call-update) | async-done | bytes 2097168 | tf_op jit(solution)/shard_map/all_gather | solution.py:321
  214.7 2.4 convolution_convert_fusion.16.query_ref
  217.1 5.9 shard_map.230
  223.5 2.6 collective-permute-done.8
  230.4 15.5 %all_to_all.42 = bf16[4,128,256]{2,1,0:T(8,128)(2,1)S(1)} all-to-all(bf16[4,128,256]{2,1,0:T(8,128)(2,1)S(1)} %bitcast.215), channel_id=1, replica_groups=mesh['rows'=8,'text'=4] {'text'}, dimensions={0} | all-to-all | bytes 524288 | tf_op jit(solution)/shard_map/all_to_all | solution.py:308
  251.3 12.5 %collective-permute-done.10 = bf16[256,1024]{1,0:T(8,128)(2,1)S(1)} collective-permute-done((bf16[256,1024]{1,0:T(8,128)(2,1)S(1)}, bf16[256,1024]{1,0:T(8,128)(2,1)S(1)}, u32[]{:S(2)}, u32[]{:S(2)}) %collective-permute-start.10) | collective-permute-done | bytes 524320 | tf_op jit(solution)/shard_map/ppermute | solution.py:25
  265.0 9.0 collective-permute-done.14
  275.8 7.3 multiply_convert_fusion
  283.2 33.7 %all-gather.17.cloned.1.call-done = bf16[1024,1024]{0,1:T(8,128)(2,1)} async-done(((bf16[128,1024]{0,1:T(8,128)(2,1)}), bf16[1024,1024]{0,1:T(8,128)(2,1)}) %all-gather.17.cloned.1.call-update) | async-done | bytes 2097168 | tf_op jit(solution)/shard_map/all_gather | solution.py:321
  316.8 6.8 fusion.5
  333.6 10.6 %collective-permute-done.17 = bf16[256,1024]{1,0:T(8,128)(2,1)S(1)} collective-permute-done((bf16[256,1024]{1,0:T(8,128)(2,1)S(1)}, bf16[256,1024]{1,0:T(8,128)(2,1)S(1)}, u32[]{:S(2)}, u32[]{:S(2)}) %collective-permute-start.17) | collective-permute-done | bytes 524320 | tf_op jit(solution)/shard_map/ppermute | solution.py:25
  344.8 10.2 %collective-permute-done.13 = bf16[256,1024]{1,0:T(8,128)(2,1)S(1)} collective-permute-done((bf16[256,1024]{1,0:T(8,128)(2,1)S(1)}, bf16[256,1024]{1,0:T(8,128)(2,1)S(1)}, u32[]{:S(2)}, u32[]{:S(2)}) %collective-permute-start.13) | collective-permute-done | bytes 524320 | tf_op jit(solution)/shard_map/ppermute | solution.py:25
  358.1 12.1 %collective-permute-done.18 = bf16[256,1024]{1,0:T(8,128)(2,1)S(1)} collective-permute-done((bf16[256,1024]{1,0:T(8,128)(2,1)S(1)}, bf16[256,1024]{1,0:T(8,128)(2,1)S(1)}, u32[]{:S(2)}, u32[]{:S(2)}) %collective-permute-start.18) | collective-permute-done | bytes 524320 | tf_op jit(solution)/shard_map/ppermute | solution.py:25
  370.3 2.6 collective-permute-done.19
  374.7 6.9 shard_map.231
  381.6 3.0 convolution_convert_fusion.12
  384.7 5.7 convolution_convert_fusion.1
  391.6 5.6 convolution_convert_fusion
  398.4 2.0 convolution_convert_fusion.11
  403.9 2.5 collective-permute-done.20
  408.5 12.5 %collective-permute-done.21 = bf16[256,1024]{1,0:T(8,128)(2,1)S(1)} collective-permute-done((bf16[256,1024]{1,0:T(8,128)(2,1)S(1)}, bf16[256,1024]{1,0:T(8,128)(2,1)S(1)}, u32[]{:S(2)}, u32[]{:S(2)}) %collective-permute-start.21) | collective-permute-done | bytes 524320 | tf_op jit(solution)/shard_map/ppermute | solution.py:25
  424.5 2.7 convolution_convert_fusion.5
  427.3 8.9 collective-permute-done.22
  436.4 2.6 collective-permute-done.23
  442.9 2.1 convolution_convert_fusion.14.grad_ref
  445.1 10.2 %shard_map.232 = bf16[1024,768]{1,0:T(8,128)(2,1)S(1)} custom-call(s32[1]{0:T(128)} %bitcast.1.here_ref, s32[8,1024]{1,0:T(8,128)S(1)} %add_add_fusion.marks_ref, bf16[1024,768]{1,0:T(8,128)(2,1)S(1)} %copy-done.1, bf16[1024,256]{1,0:T(8,128)(2,1)S(1)} %convolution_convert_fusion.14.grad_ref, f32[4,1024]{1,0:T(4,128)S(1)} %get-tuple-element.22.lse_ref), custom_call_target="tpu_custom_call" | custom-call | flops 1677721600 | bytes 3719172 | tf_op jit(solution)/shard_map/pallas_call | solution.py:277
  455.3 4.5 convolution_convert_fusion.2
  460.4 3.4 convolution_convert_fusion.4
  468.6 3.3 all-to-all-start.4
  472.5 1.8 fusion.43
  474.3 41.3 %reduce-scatter.24.cloned.1.call-done = bf16[128,1024]{1,0:T(8,128)(2,1)} async-done(((bf16[1024,1024]{1,0:T(8,128)(2,1)}), bf16[128,1024]{1,0:T(8,128)(2,1)}) %reduce-scatter.24.cloned.1.call-update) | async-done | bytes 262160 | tf_op jit(solution)/shard_map/reduce_scatter | solution.py:325
  517.3 69.0 %reduce-scatter.26.cloned.1.call-done = bf16[128,1024]{1,0:T(8,128)(2,1)} async-done(((bf16[1024,1024]{1,0:T(8,128)(2,1)}), bf16[128,1024]{1,0:T(8,128)(2,1)}) %reduce-scatter.26.cloned.1.call-update) | async-done | bytes 262160 | tf_op jit(solution)/shard_map/reduce_scatter | solution.py:325
  588.0 31.3 %reduce-scatter.20.cloned.1.call-done = bf16[1024,256]{1,0:T(8,128)(2,1)} async-done(((bf16[1024,1024]{1,0:T(8,128)(2,1)}), bf16[1024,256]{1,0:T(8,128)(2,1)}) %reduce-scatter.20.cloned.1.call-update) | async-done | bytes 524304 | tf_op jit(solution)/shard_map/reduce_scatter | solution.py:341
  619.3 3.4 all-to-all-start.6
  622.7 2.7 convert_add_fusion
  626.8 2.0 collective-permute-start.25
  628.9 3.4 all-to-all-start.7
  633.1 53.1 %reduce-scatter.18.cloned.1.call-done = bf16[128,512]{1,0:T(8,128)(2,1)} async-done(((bf16[1024,512]{1,0:T(8,128)(2,1)}), bf16[128,512]{1,0:T(8,128)(2,1)}) %reduce-scatter.18.cloned.1.call-update) | async-done | bytes 131088 | tf_op jit(solution)/shard_map/reduce_scatter | solution.py:325
  687.9 3.3 all-to-all-start.5
  693.7 2.1 all-to-all-done.5
  696.7 1.9 fusion.21
  698.6 20.7 %reduce-scatter.12.cloned.1.call-done = bf16[1024,256]{1,0:T(8,128)(2,1)} async-done(((bf16[1024,1024]{1,0:T(8,128)(2,1)}), bf16[1024,256]{1,0:T(8,128)(2,1)}) %reduce-scatter.12.cloned.1.call-update) | async-done | bytes 524304 | tf_op jit(solution)/shard_map/reduce_scatter | solution.py:341
  719.3 68.3 %reduce-scatter.10.cloned.1.call-done = bf16[128,768]{1,0:T(8,128)(2,1)} async-done(((bf16[1024,768]{1,0:T(8,128)(2,1)}), bf16[128,768]{1,0:T(8,128)(2,1)}) %reduce-scatter.10.cloned.1.call-update) | async-done | bytes 196624 | tf_op jit(solution)/shard_map/reduce_scatter | solution.py:325
  789.3 3.4 all-to-all-start.3
  792.7 2.6 fusion.20
  795.4 40.4 %psum.7 = f32[6,1024]{1,0:T(8,128)S(1)} all-reduce(f32[6,1024]{1,0:T(8,128)S(1)} %stack.39), channel_id=1, replica_groups=mesh['rows'=8,'text'=4] {'rows','text'}, use_global_device_ids=true, to_apply=%region_32.33 | all-reduce | flops 6144 | bytes 49152 | tf_op jit(solution)/shard_map/psum | solution.py:483
  836.5 15.7 %reduce-scatter.22.cloned.1.call-done = bf16[128,256]{1,0:T(8,128)(2,1)} async-done(((bf16[1024,256]{1,0:T(8,128)(2,1)}), bf16[128,256]{1,0:T(8,128)(2,1)}) %reduce-scatter.22.cloned.1.call-update) | async-done | bytes 65552 | tf_op jit(solution)/shard_map/reduce_scatter | solution.py:325
  854.6 61.7 %reduce-scatter.14.cloned.1.call-done = bf16[128,256]{1,0:T(8,128)(2,1)} async-done(((bf16[1024,256]{1,0:T(8,128)(2,1)}), bf16[128,256]{1,0:T(8,128)(2,1)}) %reduce-scatter.14.cloned.1.call-update) | async-done | bytes 65552 | tf_op jit(solution)/shard_map/reduce_scatter | solution.py:325
  (286 shorter events, 84.5 us)
Async XLA Ops:
  7.2 21.9 %copy-start.46 = (bf16[3,256]{1,0:T(4,128)(2,1)S(1)}, bf16[3,256]{1,0:T(4,128)(2,1)}, u32[]{:S(2)}) copy-start(bf16[3,256]{1,0:T(4,128)(2,1)} %param.26) | copy-start | bytes 4612
  7.2 21.9 %copy-start.47 = (bf16[3,256]{1,0:T(4,128)(2,1)S(1)}, bf16[3,256]{1,0:T(4,128)(2,1)}, u32[]{:S(2)}) copy-start(bf16[3,256]{1,0:T(4,128)(2,1)} %param.25) | copy-start | bytes 4612
  7.2 27.1 %copy-start.6 = (bf16[1,256,1024]{2,1,0:T(8,128)(2,1)S(1)}, bf16[1,256,1024]{2,1,0:T(8,128)(2,1)}, u32[]{:S(2)}) copy-start(bf16[1,256,1024]{2,1,0:T(8,128)(2,1)} %param.14) | copy-start | bytes 1572868
  7.2 61.2 %all-gather.7.cloned.1.call-start = ((), (), s32[]{:S(2)}) async-start(), calls=%async_computation.17 | async-start | bytes 1769472 | tf_op jit(solution)/shard_map/all_gather | solution.py:321
  22.7 95.5 %all-gather.9.cloned.1.call-start = ((), (), s32[]{:S(2)}) async-start(), calls=%async_computation.18 | async-start | bytes 2359296 | tf_op jit(solution)/shard_map/all_gather | solution.py:321
  29.0 161.9 %all-gather.11.cloned.1.call-start = ((), (), s32[]{:S(2)}) async-start(), calls=%async_computation.19 | async-start | bytes 1179648 | tf_op jit(solution)/shard_map/all_gather | solution.py:321
  35.2 21.6 %copy-start.52 = (s32[1,4]{1,0:T(1,128)S(1)}, s32[1,4]{1,0:T(1,128)}, u32[]{:S(2)}) copy-start(s32[1,4]{1,0:T(1,128)} %param.17) | copy-start | bytes 52
  35.2 21.9 %copy-start.45 = (s32[1,1024]{1,0:T(1,128)S(1)}, s32[1,1024]{1,0:T(1,128)}, u32[]{:S(2)}) copy-start(s32[1,1024]{1,0:T(1,128)} %param.16) | copy-start | bytes 12292
  35.2 178.4 %all-gather.13.cloned.1.call-start = ((), (), s32[]{:S(2)}) async-start(), calls=%async_computation.20 | async-start | bytes 2359296 | tf_op jit(solution)/shard_map/all_gather | solution.py:321
  35.8 36.2 %copy-start.20 = (bf16[256,1024]{1,0:T(8,128)(2,1)}, bf16[256,1024]{1,0:T(8,128)(2,1)S(1)}, u32[]{:S(2)}) copy-start(bf16[256,1024]{1,0:T(8,128)(2,1)S(1)} %fusion.15) | copy-start | bytes 1572868
  35.9 14.2 %collective-permute-start = (bf16[256,1024]{1,0:T(8,128)(2,1)S(1)}, bf16[256,1024]{1,0:T(8,128)(2,1)S(1)}, u32[]{:S(2)}, u32[]{:S(2)}) collective-permute-start(bf16[256,1024]{1,0:T(8,128)(2,1)S(1)} %fusion.15), channel_id=1, source_target_pairs={{0,2},{1,3},{2,0},{3,1},{4,6},{5,7},{6,4},{7,5},{8,10},{9,11},{10,... | collective-permute-start | bytes 1572872 | tf_op jit(solution)/shard_map/ppermute | solution.py:25
  50.0 22.0 %copy-start.29 = (bf16[256,1024]{1,0:T(8,128)(2,1)}, bf16[256,1024]{1,0:T(8,128)(2,1)S(1)}, u32[]{:S(2)}) copy-start(bf16[256,1024]{1,0:T(8,128)(2,1)S(1)} %collective-permute-done) | copy-start | bytes 1572868
  50.1 7.2 collective-permute-start.1
  56.7 219.1 %all-gather.15.cloned.1.call-start = ((), (), s32[]{:S(2)}) async-start(), calls=%async_computation.21 | async-start | bytes 2359296 | tf_op jit(solution)/shard_map/all_gather | solution.py:321
  119.8 2.7 collective-permute-start.2
  123.0 14.0 %collective-permute-start.3 = (bf16[256,1024]{1,0:T(8,128)(2,1)S(1)}, bf16[256,1024]{1,0:T(8,128)(2,1)S(1)}, u32[]{:S(2)}, u32[]{:S(2)}) collective-permute-start(bf16[256,1024]{1,0:T(8,128)(2,1)S(1)} %slice.306), channel_id=1, source_target_pairs={{0,2},{1,3},{2,0},{3,1},{4,6},{5,7},{6,4},{7,5},{8,10},{9,11},{10,... | collective-permute-start | bytes 1572872 | tf_op jit(solution)/shard_map/ppermute | solution.py:25
  137.3 109.5 %copy-start.2 = (f32[256,1024]{1,0:T(8,128)}, f32[256,1024]{1,0:T(8,128)S(1)}, u32[]{:S(2)}) copy-start(f32[256,1024]{1,0:T(8,128)S(1)} %get-tuple-element.94) | copy-start | bytes 3145732
  137.3 17.3 %copy-start.39 = (bf16[1,96,1024]{2,1,0:T(8,128)(2,1)S(1)}, bf16[1,96,1024]{2,1,0:T(8,128)(2,1)}, u32[]{:S(2)}) copy-start(bf16[1,96,1024]{2,1,0:T(8,128)(2,1)} %param.15) | copy-start | bytes 589828
  137.9 23.5 %copy-start.22 = (bf16[256,1024]{1,0:T(8,128)(2,1)}, bf16[256,1024]{1,0:T(8,128)(2,1)S(1)}, u32[]{:S(2)}) copy-start(bf16[256,1024]{1,0:T(8,128)(2,1)S(1)} %add_convert_fusion.1) | copy-start | bytes 1572868
  137.9 18.3 %collective-permute-start.4 = (bf16[256,1024]{1,0:T(8,128)(2,1)S(1)}, bf16[256,1024]{1,0:T(8,128)(2,1)}, u32[]{:S(2)}, u32[]{:S(2)}) collective-permute-start(bf16[256,1024]{1,0:T(8,128)(2,1)S(1)} %add_convert_fusion.1), channel_id=1, source_target_pairs={{0,2},{1,3},{2,0},{3,1},{4,6},{5,7},{6,4},{7,5},{8,10},{9,11},{10,... | collective-permute-start | bytes 1572872 | tf_op jit(solution)/shard_map/ppermute | solution.py:25
  154.1 162.7 %all-gather.17.cloned.1.call-start = ((), (), s32[]{:S(2)}) async-start(), calls=%async_computation.22 | async-start | bytes 2359296 | tf_op jit(solution)/shard_map/all_gather | solution.py:321
  154.7 6.6 collective-permute-start.6
  158.3 56.4 %collective-permute-start.5 = (bf16[512,1024]{1,0:T(8,128)(2,1)}, bf16[512,1024]{1,0:T(8,128)(2,1)}, u32[]{:S(2)}, u32[]{:S(2)}) collective-permute-start(bf16[512,1024]{1,0:T(8,128)(2,1)} %pad_maximum_fusion.7), channel_id=1, source_target_pairs={{0,1},{1,0},{2,3},{3,2},{4,5},{5,4},{6,7},{7,6},{8,9},{9,8},{10,11... | collective-permute-start | bytes 3145736 | tf_op jit(solution)/shard_map/ppermute | solution.py:25
  161.3 31.8 %copy-start.41 = (bf16[96,1024]{1,0:T(8,128)(2,1)}, bf16[96,1024]{1,0:T(8,128)(2,1)S(1)}, u32[]{:S(2)}) copy-start(bf16[96,1024]{1,0:T(8,128)(2,1)S(1)} %collective-permute-done.6) | copy-start | bytes 589828
  161.3 29.6 %collective-permute-start.7 = (bf16[192,1024]{1,0:T(8,128)(2,1)S(1)}, bf16[192,1024]{1,0:T(8,128)(2,1)}, u32[]{:S(2)}, u32[]{:S(2)}) collective-permute-start(bf16[192,1024]{1,0:T(8,128)(2,1)S(1)} %pad_maximum_fusion.26), channel_id=1, source_target_pairs={{0,1},{1,0},{2,3},{3,2},{4,5},{5,4},{6,7},{7,6},{8,9},{9,8},{10,11... | collective-permute-start | bytes 1179656 | tf_op jit(solution)/shard_map/ppermute | solution.py:25
  190.9 23.8 %copy-start.9 = (bf16[1024,256]{0,1:T(8,128)(2,1)}, bf16[1024,256]{0,1:T(8,128)(2,1)S(1)}, u32[]{:S(2)}) copy-start(bf16[1024,256]{0,1:T(8,128)(2,1)S(1)} %all_gather.34) | copy-start | bytes 1572868
  223.5 2.7 collective-permute-start.8
  228.9 17.9 %collective-permute-start.9 = (bf16[256,1024]{1,0:T(8,128)(2,1)}, bf16[256,1024]{1,0:T(8,128)(2,1)}, u32[]{:S(2)}, u32[]{:S(2)}) collective-permute-start(bf16[256,1024]{1,0:T(8,128)(2,1)} %slice.305), channel_id=1, source_target_pairs={{0,2},{1,3},{2,0},{3,1},{4,6},{5,7},{6,4},{7,5},{8,10},{9,11},{10,... | collective-permute-start | bytes 1572872 | tf_op jit(solution)/shard_map/ppermute | solution.py:25
  246.7 220.3 %reduce-scatter.16.cloned.1.call-start = ((), (), s32[]{:S(2)}) async-start(), calls=%async_computation.26 | async-start | bytes 589824 | tf_op jit(solution)/shard_map/reduce_scatter | solution.py:325
  249.0 14.9 %collective-permute-start.10 = (bf16[256,1024]{1,0:T(8,128)(2,1)S(1)}, bf16[256,1024]{1,0:T(8,128)(2,1)S(1)}, u32[]{:S(2)}, u32[]{:S(2)}) collective-permute-start(bf16[256,1024]{1,0:T(8,128)(2,1)S(1)} %add_convert_fusion), channel_id=1, source_target_pairs={{0,2},{1,3},{2,0},{3,1},{4,6},{5,7},{6,4},{7,5},{8,10},{9,11},{10,... | collective-permute-start | bytes 1572872 | tf_op jit(solution)/shard_map/ppermute | solution.py:25
  250.5 23.5 %collective-permute-start.14 = (bf16[256,1024]{1,0:T(8,128)(2,1)S(1)}, bf16[256,1024]{1,0:T(8,128)(2,1)S(1)}, u32[]{:S(2)}, u32[]{:S(2)}) collective-permute-start(bf16[256,1024]{1,0:T(8,128)(2,1)S(1)} %bitcast.191), channel_id=1, source_target_pairs={{0,2},{1,3},{2,0},{3,1},{4,6},{5,7},{6,4},{7,5},{8,10},{9,11},{10,... | collective-permute-start | bytes 1572872 | tf_op jit(solution)/shard_map/ppermute | solution.py:25
  265.0 10.9 %collective-permute-start.11 = (bf16[512,1024]{1,0:T(8,128)(2,1)}, bf16[512,1024]{1,0:T(8,128)(2,1)}, u32[]{:S(2)}, u32[]{:S(2)}) collective-permute-start(bf16[512,1024]{1,0:T(8,128)(2,1)} %pad_maximum_fusion.8), channel_id=1, source_target_pairs={{0,1},{1,0},{2,3},{3,2},{4,5},{5,4},{6,7},{7,6},{8,9},{9,8},{10,11... | collective-permute-start | bytes 3145736 | tf_op jit(solution)/shard_map/ppermute | solution.py:25
  275.8 7.3 collective-permute-start.15
  324.9 3.1 collective-permute-start.16
  327.9 3.0 collective-permute-start.12
  329.4 14.8 %collective-permute-start.17 = (bf16[256,1024]{1,0:T(8,128)(2,1)S(1)}, bf16[256,1024]{1,0:T(8,128)(2,1)S(1)}, u32[]{:S(2)}, u32[]{:S(2)}) collective-permute-start(bf16[256,1024]{1,0:T(8,128)(2,1)S(1)} %slice.303), channel_id=1, source_target_pairs={{0,2},{1,3},{2,0},{3,1},{4,6},{5,7},{6,4},{7,5},{8,10},{9,11},{10,... | collective-permute-start | bytes 1572872 | tf_op jit(solution)/shard_map/ppermute | solution.py:25
  332.2 22.8 %copy-start.25 = (bf16[1,256,1024]{2,1,0:T(8,128)(2,1)S(1)}, bf16[1,256,1024]{2,1,0:T(8,128)(2,1)}, u32[]{:S(2)}) copy-start(bf16[1,256,1024]{2,1,0:T(8,128)(2,1)} %param.27) | copy-start | bytes 1572868
  332.3 22.7 %collective-permute-start.13 = (bf16[256,1024]{1,0:T(8,128)(2,1)S(1)}, bf16[256,1024]{1,0:T(8,128)(2,1)S(1)}, u32[]{:S(2)}, u32[]{:S(2)}) collective-permute-start(bf16[256,1024]{1,0:T(8,128)(2,1)S(1)} %slice.304), channel_id=1, source_target_pairs={{0,2},{1,3},{2,0},{3,1},{4,6},{5,7},{6,4},{7,5},{8,10},{9,11},{10,... | collective-permute-start | bytes 1572872 | tf_op jit(solution)/shard_map/ppermute | solution.py:25
  356.6 17.3 %copy-start.14 = (bf16[4,1,64,1024]{3,2,1,0:T(8,128)(2,1)S(1)}, bf16[4,1,64,1024]{3,2,1,0:T(8,128)(2,1)}, u32[]{:S(2)}) copy-start(bf16[4,1,64,1024]{3,2,1,0:T(8,128)(2,1)} %copy-done.13) | copy-start | bytes 1572868
  356.6 13.5 %collective-permute-start.18 = (bf16[256,1024]{1,0:T(8,128)(2,1)S(1)}, bf16[256,1024]{1,0:T(8,128)(2,1)S(1)}, u32[]{:S(2)}, u32[]{:S(2)}) collective-permute-start(bf16[256,1024]{1,0:T(8,128)(2,1)S(1)} %get-tuple-element.89), channel_id=1, source_target_pairs={{0,2},{1,3},{2,0},{3,1},{4,6},{5,7},{6,4},{7,5},{8,10},{9,11},{10,... | collective-permute-start | bytes 1572872 | tf_op jit(solution)/shard_map/ppermute | solution.py:25
  370.2 2.7 collective-permute-start.19
  384.6 130.9 %reduce-scatter.24.cloned.1.call-start = ((), (), s32[]{:S(2)}) async-start(), calls=%async_computation.30 | async-start | bytes 2359296 | tf_op jit(solution)/shard_map/reduce_scatter | solution.py:325
  390.4 195.9 %reduce-scatter.26.cloned.1.call-start = ((), (), s32[]{:S(2)}) async-start(), calls=%async_computation.31 | async-start | bytes 2359296 | tf_op jit(solution)/shard_map/reduce_scatter | solution.py:325
  397.2 222.1 %reduce-scatter.20.cloned.1.call-start = ((), (), s32[]{:S(2)}) async-start(), calls=%async_computation.28 | async-start | bytes 2621440 | tf_op jit(solution)/shard_map/reduce_scatter | solution.py:341
  402.9 283.4 %reduce-scatter.18.cloned.1.call-start = ((), (), s32[]{:S(2)}) async-start(), calls=%async_computation.27 | async-start | bytes 1179648 | tf_op jit(solution)/shard_map/reduce_scatter | solution.py:325
  403.7 17.3 %copy-start.3 = (f32[256,1024]{1,0:T(8,128)S(1)}, f32[256,1024]{1,0:T(8,128)}, u32[]{:S(2)}) copy-start(f32[256,1024]{1,0:T(8,128)} %copy-done.2) | copy-start | bytes 3145732
  403.7 2.7 collective-permute-start.20
  406.9 14.0 %collective-permute-start.21 = (bf16[256,1024]{1,0:T(8,128)(2,1)S(1)}, bf16[256,1024]{1,0:T(8,128)(2,1)S(1)}, u32[]{:S(2)}, u32[]{:S(2)}) collective-permute-start(bf16[256,1024]{1,0:T(8,128)(2,1)S(1)} %slice.302), channel_id=1, source_target_pairs={{0,2},{1,3},{2,0},{3,1},{4,6},{5,7},{6,4},{7,5},{8,10},{9,11},{10,... | collective-permute-start | bytes 1572872 | tf_op jit(solution)/shard_map/ppermute | solution.py:25
  423.1 13.1 %collective-permute-start.22 = (bf16[256,1024]{1,0:T(8,128)(2,1)S(1)}, bf16[256,1024]{1,0:T(8,128)(2,1)S(1)}, u32[]{:S(2)}, u32[]{:S(2)}) collective-permute-start(bf16[256,1024]{1,0:T(8,128)(2,1)S(1)} %get-tuple-element.87), channel_id=1, source_target_pairs={{0,2},{1,3},{2,0},{3,1},{4,6},{5,7},{6,4},{7,5},{8,10},{9,11},{10,... | collective-permute-start | bytes 1572872 | tf_op jit(solution)/shard_map/ppermute | solution.py:25
  427.3 292.0 %reduce-scatter.12.cloned.1.call-start = ((), (), s32[]{:S(2)}) async-start(), calls=%async_computation.24 | async-start | bytes 2621440 | tf_op jit(solution)/shard_map/reduce_scatter | solution.py:341
  436.3 2.7 collective-permute-start.23
  442.5 345.1 %reduce-scatter.10.cloned.1.call-start = ((), (), s32[]{:S(2)}) async-start(), calls=%async_computation.23 | async-start | bytes 1769472 | tf_op jit(solution)/shard_map/reduce_scatter | solution.py:325
  460.2 4.0 collective-permute-start.26
  463.8 158.9 %collective-permute-start.24 = (bf16[512,1024]{1,0:T(8,128)(2,1)}, bf16[512,1024]{1,0:T(8,128)(2,1)}, u32[]{:S(2)}, u32[]{:S(2)}) collective-permute-start(bf16[512,1024]{1,0:T(8,128)(2,1)} %convolution_convert_fusion.4), channel_id=1, source_target_pairs={{0,1},{1,0},{2,3},{3,2},{4,5},{5,4},{6,7},{7,6},{8,9},{9,8},{10,11... | collective-permute-start | bytes 3145736 | tf_op jit(solution)/shard_map/ppermute | solution.py:25
  465.5 7.0 collective-permute-start.27
  468.6 150.7 %all-to-all-start.4 = ((bf16[4,128,64]{1,2,0:T(8,128)(2,1)}), bf16[4,128,64]{1,2,0:T(8,128)(2,1)S(1)}, u32[]{:S(2)}, u32[]{:S(2)}) async-start(bf16[4,128,64]{1,2,0:T(8,128)(2,1)} %bitcast.56), calls=%async_computation.8 | async-start | bytes 131072 | tf_op jit(solution)/shard_map/all_to_all | solution.py:308
  471.9 380.3 %reduce-scatter.22.cloned.1.call-start = ((), (), s32[]{:S(2)}) async-start(), calls=%async_computation.29 | async-start | bytes 589824 | tf_op jit(solution)/shard_map/reduce_scatter | solution.py:325
  619.3 9.6 %all-to-all-start.6 = ((bf16[4,128,256]{2,1,0:T(8,128)(2,1)}), bf16[4,128,256]{2,1,0:T(8,128)(2,1)S(1)}, u32[]{:S(2)}, u32[]{:S(2)}) async-start(bf16[4,128,256]{2,1,0:T(8,128)(2,1)} %bitcast.183), calls=%async_computation.14 | async-start | bytes 524288 | tf_op jit(solution)/shard_map/all_to_all | solution.py:308
  626.8 69.9 %collective-permute-start.25 = (bf16[256,1024]{1,0:T(8,128)(2,1)S(1)}, bf16[256,1024]{1,0:T(8,128)(2,1)S(1)}, u32[]{:S(2)}, u32[]{:S(2)}) collective-permute-start(bf16[256,1024]{1,0:T(8,128)(2,1)S(1)} %slice.301), channel_id=1, source_target_pairs={{0,2},{1,3},{2,0},{3,1},{4,6},{5,7},{6,4},{7,5},{8,10},{9,11},{10,... | collective-permute-start | bytes 1572872 | tf_op jit(solution)/shard_map/ppermute | solution.py:25
  628.9 59.0 %all-to-all-start.7 = ((bf16[4,128,256]{2,1,0:T(8,128)(2,1)}), bf16[4,128,256]{2,1,0:T(8,128)(2,1)S(1)}, u32[]{:S(2)}, u32[]{:S(2)}) async-start(bf16[4,128,256]{2,1,0:T(8,128)(2,1)} %bitcast.181), calls=%async_computation.16 | async-start | bytes 524288 | tf_op jit(solution)/shard_map/all_to_all | solution.py:308
  687.9 7.9 all-to-all-start.5
  691.2 225.1 %reduce-scatter.14.cloned.1.call-start = ((), (), s32[]{:S(2)}) async-start(), calls=%async_computation.25 | async-start | bytes 589824 | tf_op jit(solution)/shard_map/reduce_scatter | solution.py:325
  695.9 96.8 %copy-start.16 = (f32[256,1024]{1,0:T(8,128)S(1)}, f32[256,1024]{1,0:T(8,128)}, u32[]{:S(2)}) copy-start(f32[256,1024]{1,0:T(8,128)} %get-tuple-element.88) | copy-start | bytes 3145732
  789.3 64.4 %all-to-all-start.3 = ((bf16[4,128,192]{1,2,0:T(8,128)(2,1)}), bf16[4,128,192]{1,2,0:T(8,128)(2,1)S(1)}, u32[]{:S(2)}, u32[]{:S(2)}) async-start(bf16[4,128,192]{1,2,0:T(8,128)(2,1)} %bitcast.48), calls=%async_computation.4 | async-start | bytes 393216 | tf_op jit(solution)/shard_map/all_to_all | solution.py:308
  (39 other events, 215.2 us)
Sparse Core Ops, SparseCore 0:
  22.8 45.5 all-gather.6
  70.6 47.6 all-gather.8
  120.8 38.0 all-gather.10
  160.9 52.6 all-gather.12
  215.5 49.5 all-gather.14
  267.5 49.2 all-gather.16
  384.8 60.1 reduce-scatter.15
  448.9 66.6 reduce-scatter.23
  519.5 66.7 reduce-scatter.25
  588.8 30.3 reduce-scatter.19
  622.7 63.4 reduce-scatter.17
  688.8 30.4 reduce-scatter.11
  722.7 64.8 reduce-scatter.9
  791.1 60.9 reduce-scatter.21
  855.3 60.9 reduce-scatter.13

commit v2 on v1

--- a/solution.py
+++ b/solution.py
@@ -304,8 +304,22 @@
     )
 
 
-def exchange(dealt):
-    return lax.all_to_all(dealt, "text", 0, 0, tiled=True)
+def pick(values, index, axis):
+    return lax.dynamic_index_in_dim(values, index, axis, keepdims=False)
+
+
+def ordered(mine, other, bit, axis=0):
+    return jnp.stack([jnp.where(bit == 0, mine, other), jnp.where(bit == 0, other, mine)], axis)
+
+
+def exchange(dealt, here):
+    core, far = here & 1, here >> 1
+    tail = dealt.shape[1:]
+    dealt = dealt.reshape((2, 2) + tail)
+    stage = ordered(pick(dealt, core, 1), swap(pick(dealt, 1 - core, 1), 1), core, 1)
+    return ordered(pick(stage, far, 0), swap(pick(stage, 1 - far, 0), 2), far).reshape(
+        (WAYS,) + tail
+    )
 
 
 def side_by_side(parts):
@@ -317,19 +331,92 @@
     return jnp.moveaxis(columns.reshape(depth, WAYS, width // WAYS), 1, 0)
 
 
+def row_swap(values, mask):
+    size = lax.axis_size("rows")
+    return lax.ppermute(values, "rows", [(i, i ^ mask) for i in range(size)])
+
+
 def gather_rows(block):
     return lax.all_gather(block, "rows", axis=0, tiled=True)
 
 
 def sum_rows(whole):
     return lax.psum_scatter(whole, "rows", scatter_dimension=0, tiled=True)
+
+
+def place_pieces(depth, splits, heads_width, row_ref, *refs):
+    row = row_ref[0]
+    pieces, other = refs[:4], refs[4]
+    outs, sem = refs[5:-1], refs[-1]
+    copies = []
+
+    def copy(source, target):
+        copies.append(pltpu.make_async_copy(source, target, sem.at[len(copies)]))
+        copies[-1].start()
+
+    for k in range(4):
+        for flip in range(2):
+            owner = (row ^ flip) ^ (2 * k)
+            start = pl.multiple_of(owner * depth, depth)
+            column = 0
+            for index, width in enumerate(splits):
+                if flip:
+                    source = other.at[k, :, column : column + width]
+                else:
+                    source = pieces[k].at[:, column : column + width]
+                copy(source, outs[index].at[pl.ds(start, depth)])
+                column += width
+        if heads_width:
+            half = depth // 2
+            start = pl.multiple_of(((row >> 1) ^ k) * half, half)
+            for index in range(2):
+                source = pieces[k].at[index * half : (index + 1) * half, column:]
+                copy(source, outs[len(splits) + index].at[pl.ds(start, half)])
+    for pending in copies:
+        pending.wait()
+
+
+def gather_grid(block, row, splits, heads_width=0):
+    depth = block.shape[0]
+    uniform = sum(splits)
+    pieces = [block] + [row_swap(block, 2 * k) for k in range(1, 4)]
+    other = row_swap(jnp.stack([p[:, :uniform] for p in pieces]), 1)
+    outs = [shaped((8 * depth, width), LOW) for width in splits]
+    if heads_width:
+        outs += [shaped((2 * depth, heads_width), LOW)] * 2
+    copies = 8 * len(splits) + (8 if heads_width else 0)
+    moved = 4 * 8 * depth * uniform + 16 * depth * heads_width
+    body = lambda *refs: place_pieces(depth, splits, heads_width, *refs)
+    return pl.pallas_call(
+        body,
+        out_shape=outs,
+        in_specs=[pl.BlockSpec(memory_space=pltpu.SMEM)] + [pl.BlockSpec(memory_space=pl.ANY)] * 5,
+        out_specs=[pl.BlockSpec(memory_space=pl.ANY) for _ in outs],
+        scratch_shapes=[pltpu.SemaphoreType.DMA((copies,))],
+        cost_estimate=pl.CostEstimate(flops=0, bytes_accessed=moved, transcendentals=0),
+    )(row.astype(jnp.int32).reshape(1), *pieces, other)
+
+
+def sum_grid(whole, row):
+    grouped = whole.reshape(4, 2, -1, whole.shape[1])
+    far, x = row >> 1, row & 1
+    column = pick(grouped, x, 1).astype(WIDE) + row_swap(pick(grouped, 1 - x, 1), 1).astype(WIDE)
+    return sum_column(column, far)
+
+
+def sum_column(column, far):
+    low = column.astype(LOW)
+    total = pick(column, far, 0)
+    for k in range(1, 4):
+        total = total + row_swap(pick(low, far ^ k, 0), 2 * k).astype(WIDE)
+    return total
 
 
 def own_heads(matrix, here):
     rows = gather_rows(lax.all_gather(matrix, "text", axis=1, tiled=True))
     width = rows.shape[1]
     grouped = rows.reshape(HEADS // WAYS, WAYS, -1, width)
-    return lax.dynamic_index_in_dim(grouped, here, 1, keepdims=False).reshape(-1, width)
+    return pick(grouped, here, 1).reshape(-1, width)
 
 
 def return_heads(grad, here):
@@ -342,6 +429,30 @@
         spread.reshape(count * WAYS, width), "text", scatter_dimension=1, tiled=True
     )
     return sum_rows(columns)
+
+
+def lift_heads(both, here, row):
+    core, far, x = here & 1, here >> 1, row & 1
+    grouped = both.reshape(2, 2, -1, both.shape[2])
+    stage = ordered(pick(grouped, core, 1), swap(pick(grouped, 1 - core, 1), 1), core)
+    stage = ordered(stage, swap(stage, 2), far)
+    sorted_lines = stage.reshape(WAYS, 2 * grouped.shape[2], -1)
+    lines = jnp.concatenate([sorted_lines[i] for i in range(WAYS)], axis=1)
+    return jnp.where(x == far, lines, row_swap(lines, 1))
+
+
+def lower_heads(grads, here, row):
+    core, far, x = here & 1, here >> 1, row & 1
+    width = grads[0].shape[1]
+    column = jnp.stack([g.reshape(4, -1, width) for g in grads], axis=1)
+    total = sum_column(column, row >> 1)
+    total = total + row_swap(total.astype(LOW), 1).astype(WIDE)
+    half = total.reshape(total.shape[:2] + (2, width // 2))
+    sent = swap(pick(half, 1 - far, 2).astype(LOW), 2).astype(WIDE)
+    lines = jnp.where(x == far, pick(half, far, 2), sent)
+    quarter = lines.reshape(lines.shape[:2] + (2, width // WAYS))
+    sent = swap(pick(quarter, 1 - core, 2).astype(LOW), 1).astype(WIDE)
+    return ordered(pick(quarter, core, 2), sent, core, 1).reshape(2, -1, width // WAYS)
 
 
 def local(
@@ -367,25 +478,36 @@
     count = frames.shape[1] * WAYS
     inner = width // WAYS
 
+    row = lax.axis_index("rows")
+    grid = row_count == 8
     chunk = ffn_out.shape[0] // WAYS
-    packed = jnp.concatenate(
-        [deal(self_in, 3), deal(cross_query, 1), deal(cross_kv, 2)], axis=2
-    )
-    packed = exchange(packed)
+    norms = jnp.concatenate([norm_gains, norm_biases], axis=0)
+    norms = ordered(norms, swap(norms, 2), here >> 1)
+    norms = ordered(norms, swap(norms, 1), here & 1, 1)
+    norms = jnp.moveaxis(norms, 2, 0).reshape(6, width).astype(WIDE)
+    gains, biases = norms[:3], norms[3:]
+    mixed_block = side_by_side(exchange(deal(self_in, 3), here))
+    dealt = jnp.concatenate([deal(cross_query, 1), deal(cross_kv, 2)], axis=2)
+    parts = exchange(dealt, here)
     piece = inner // WAYS
-    w_mixed = gather_rows(side_by_side(packed[:, :, : 3 * piece]))
-    w_query = gather_rows(side_by_side(packed[:, :, 3 * piece : 4 * piece]))
-    w_pairs = gather_rows(side_by_side(packed[:, :, 4 * piece :]))
-    w_self = own_heads(self_out, here)
-    w_cross = own_heads(cross_out, here)
-    w_up = gather_rows(side_by_side(exchange(deal(ffn_in, row_count // WAYS))))
+    query_block = side_by_side(parts[:, :, :piece])
+    pairs_block = side_by_side(parts[:, :, piece:])
+    if grid:
+        (w_mixed,) = gather_grid(mixed_block, row, (3 * inner,))
+        lines = lift_heads(jnp.stack([self_out, cross_out]), here, row)
+        block = jnp.concatenate([query_block, pairs_block, lines], axis=1)
+        w_query, w_pairs, w_self, w_cross = gather_grid(block, row, (inner, 2 * inner), width)
+    else:
+        w_mixed = gather_rows(mixed_block)
+        w_query = gather_rows(query_block)
+        w_pairs = gather_rows(pairs_block)
+        w_self = own_heads(self_out, here)
+        w_cross = own_heads(cross_out, here)
+    w_up = gather_rows(side_by_side(exchange(deal(ffn_in, row_count // WAYS), here)))
     w_down = gather_rows(
-        side_by_side(exchange(ffn_out.reshape(WAYS, chunk, ffn_out.shape[1])))
-    )
-
-    norms = jnp.concatenate([norm_gains, norm_biases], axis=0)
-    norms = lax.all_gather(norms, "text", axis=1, tiled=True).astype(WIDE)
-    gains, biases = norms[:3], norms[3:]
+        side_by_side(exchange(ffn_out.reshape(WAYS, chunk, ffn_out.shape[1]), here))
+    )
+
     segments = frame_segments[0]
     clips = text_lengths.shape[1]
     ends = jnp.cumsum(text_lengths[0])
@@ -480,16 +602,29 @@
     frame_grad = grad_hidden + part
 
     norm_sums = jnp.stack([gain_one, gain_two, gain_three, bias_one, bias_two, bias_three])
-    norm_sums = lax.psum(norm_sums, ("rows", "text"))
-    norm_sums = lax.dynamic_slice_in_dim(norm_sums, here * inner, inner, 1)
-
-    d_down = exchange(apart(sum_rows(g_down))).reshape(ffn_out.shape).astype(WIDE)
-    d_up = undeal(exchange(apart(sum_rows(g_up))), row_count // WAYS).astype(WIDE)
-    d_cross = return_heads(g_cross, here).astype(WIDE)
-    d_self = return_heads(g_self, here).astype(WIDE)
-    d_query = undeal(exchange(apart(sum_rows(g_query))), 1).astype(WIDE)
-    d_pairs = undeal(exchange(apart(sum_rows(g_pairs))), 2).astype(WIDE)
-    d_mixed = undeal(exchange(apart(sum_rows(g_mixed))), 3).astype(WIDE)
+    split = norm_sums.reshape(6, 2, 2, inner)
+    split = pick(split, here & 1, 2) + swap(pick(split, 1 - (here & 1), 2), 1)
+    norm_sums = pick(split, here >> 1, 1) + swap(pick(split, 1 - (here >> 1), 1), 2)
+    mask = 1
+    while mask < row_count:
+        norm_sums = norm_sums + row_swap(norm_sums, mask)
+        mask = 2 * mask
+
+    d_down = exchange(apart(sum_rows(g_down)), here).reshape(ffn_out.shape).astype(WIDE)
+    d_up = undeal(exchange(apart(sum_rows(g_up)), here), row_count // WAYS).astype(WIDE)
+    if grid:
+        d_self, d_cross = lower_heads([g_self, g_cross], here, row)
+        other = sum_grid(jnp.concatenate([g_query, g_pairs], axis=1), row).astype(LOW)
+        s_query, s_pairs = other[:, :inner], other[:, inner:]
+        s_mixed = sum_grid(g_mixed, row).astype(LOW)
+    else:
+        d_cross = return_heads(g_cross, here).astype(WIDE)
+        d_self = return_heads(g_self, here).astype(WIDE)
+        s_query, s_pairs, s_mixed = sum_rows(g_query), sum_rows(g_pairs), sum_rows(g_mixed)
+    parts = exchange(jnp.concatenate([apart(s_query), apart(s_pairs)], axis=2), here)
+    d_query = undeal(parts[:, :, :piece], 1).astype(WIDE)
+    d_pairs = undeal(parts[:, :, piece:], 2).astype(WIDE)
+    d_mixed = undeal(exchange(apart(s_mixed), here), 3).astype(WIDE)
     return (
         output[None],
         frame_grad[None],

time: 935 us -> 705 us (0.75)
  waiting for transfers between devices: 586 us -> 278 us
  Pallas kernels: 29.4 us -> 159 us
  blocking collectives: 129 us -> 0 us
  starting transfers between devices: 39.5 us -> 76.7 us
  local copies, waits for them, and re-layouts: 38.4 us -> 54.2 us
  other arithmetic: 23 us -> 38 us
    reduce_scatter x7 -> x2, waiting for transfers between devices: 309 us -> 0.01 us  [sum_rows(): return lax.psum_scatter(whole, 'rows', scatter_dimension=0, tiled=True)]
    pallas_call x0 -> x2, Pallas kernels: none -> 130 us  [gather_grid(): pl.pallas_call(body, out_shape=outs, in_specs=[pl.BlockSpec(memory_space=...]
    ppermute x0 -> x24, waiting for transfers between devices: none -> 110 us  [row_swap(): return lax.ppermute(values, 'rows', [(i, i ^ mask) for i in range(size)])]
    all_gather x6 -> x2, waiting for transfers between devices: 104 us -> 14.6 us  [gather_rows(): return lax.all_gather(block, 'rows', axis=0, tiled=True)]
    reduce_scatter x2 -> x0, waiting for transfers between devices: 52 us -> none  [return_heads(): lax.psum_scatter(spread.reshape(count * WAYS, width), 'text', scatter_dim...]
    all_gather x4 -> x0, blocking collectives: 47.4 us -> none  [the longest x1 29.5 us: gather_rows(): return lax.all_gather(block, 'rows', axis=0, tiled=True)]
    all_to_all x3 -> x0, blocking collectives: 41.5 us -> none  [exchange(): return lax.all_to_all(dealt, 'text', 0, 0, tiled=True)]
    psum x1 -> x0, blocking collectives: 40.4 us -> none  [local(): norm_sums = lax.psum(norm_sums, ('rows', 'text'))]
  transfers between devices with their start and end apart: 48 -> 80, of which waited for: 29 -> 39; matrix products, arithmetic and copies ran while one was open for 10% -> 20% of each run, Pallas kernels for 2% -> 11%
where the time goes in v2:
time: 705 us; the launch traced here: 694 us
  waiting for transfers between devices  278 us (39%)
  Pallas kernels  159 us (23%)
  starting transfers between devices  76.7 us (11%)
  matrix products  72 us (10%)
  local copies, waits for them, and re-layouts  54.2 us (8%)
  other arithmetic  38 us (5%)
  between operations  16 us (2%)
    ppermute x52, waiting for transfers between devices, swap(): return lax.ppermute(values, 'text', [(i, i ^ mask) for i in range(WAYS)])  153 us
    pallas_call x2, Pallas kernels, gather_grid(): pl.pallas_call(body, out_shape=outs, in_specs=[pl.BlockSpec(memory_space=...  130 us
    ppermute x24, waiting for transfers between devices, row_swap(): return lax.ppermute(values, 'rows', [(i, i ^ mask) for i in range(size)])  110 us
    dot_general x28, matrix products, mm(): lax.dot_general(left, right, (((left_dim,), (right_dim,)), ((), ())), pre...  72 us
    ppermute x24, starting transfers between devices, row_swap(): return lax.ppermute(values, 'rows', [(i, i ^ mask) for i in range(size)])  38.1 us
    ppermute x52, starting transfers between devices, swap(): return lax.ppermute(values, 'text', [(i, i ^ mask) for i in range(WAYS)])  37.8 us
    pallas_call x4, Pallas kernels, call(): pl.pallas_call(body, out_shape=outs, in_specs=specs, out_specs=[pl.BlockS...  29.6 us
    unnamed x179, local copies, waits for them, and re-layouts  22 us
  transfers between devices with their start and end apart: 80, of which 39 were waited for; matrix products, arithmetic and copies ran while one was open for 20% of the time, Pallas kernels for 11%

profile of v2, /device:TPU:0, one launch (start us, length us, event | category | flops | bytes accessed | tf_op | source)
XLA Modules:
  0.0 694.2 jit_solution(15536947186921518456)
XLA Ops:
  12.5 2.6 collective-permute-start
  23.4 13.1 %collective-permute-done.13 = bf16[2,2,64,256]{3,2,1,0:T(8,128)(2,1)S(1)} collective-permute-done((bf16[2,2,64,256]{3,2,1,0:T(8,128)(2,1)S(1)}, bf16[2,2,64,256]{3,2,1,0:T(8,128)(2,1)S(1)}, u32[]{:S(2)}, u32[]{:S(2)}) %collective-permute-start.13) | collective-permute-done | bytes 131104 | tf_op jit(solution)/shard_map/ppermute | solution.py:25
  36.6 2.1 collective-permute-start.14
  42.9 2.6 collective-permute-start.7
  45.9 3.9 collective-permute-start.17
  52.6 27.4 %collective-permute-done.7.refs_3_ = bf16[128,768]{1,0:T(8,128)(2,1)S(1)} collective-permute-done((bf16[128,768]{1,0:T(8,128)(2,1)}, bf16[128,768]{1,0:T(8,128)(2,1)S(1)}, u32[]{:S(2)}, u32[]{:S(2)}) %collective-permute-start.7) | collective-permute-done | bytes 196640 | tf_op jit(solution)/shard_map/ppermute | solution.py:336
  82.6 4.8 collective-permute-start.15
  88.7 13.3 %collective-permute-done.16.refs_3_ = bf16[128,1792]{1,0:T(8,128)(2,1)S(1)} collective-permute-done((bf16[128,1792]{1,0:T(8,128)(2,1)S(1)}, bf16[128,1792]{1,0:T(8,128)(2,1)S(1)}, u32[]{:S(2)}, u32[]{:S(2)}) %collective-permute-start.16) | collective-permute-done | bytes 458784 | tf_op jit(solution)/shard_map/ppermute | solution.py:336
  106.7 48.8 %shard_map.229 = bf16[1024,768]{1,0:T(8,128)(2,1)} custom-call(s32[1]{0:T(128)} %bitcast.14.refs_0_, bf16[128,768]{1,0:T(8,128)(2,1)} %copy.132.refs_1_, bf16[128,768]{1,0:T(8,128)(2,1)} %copy-done.39, bf16[128,768]{1,0:T(8,128)(2,1)} %copy-done.40, bf16[128,768]{1,0:T(8,128)(2,1)} %collective-permute-done.8.refs_4_, bf16[4,128,768]{2,1,0:T(8,128)(2,1)} %copy-done.38), custom_call_target="tpu_custom_call" | custom-call | bytes 3145728 | tf_op jit(solution)/shard_map/pallas_call | solution.py:390
  155.5 3.7 convolution_convert_fusion.3.mixed_ref
  159.2 6.4 shard_map.230
  165.7 80.7 %shard_map.231 = (bf16[1024,256]{1,0:T(8,128)(2,1)}, bf16[1024,512]{1,0:T(8,128)(2,1)}, bf16[256,1024]{1,0:T(8,128)(2,1)}, bf16[256,1024]{1,0:T(8,128)(2,1)}) custom-call(s32[1]{0:T(128)} %bitcast.14.refs_0_, bf16[128,1792]{1,0:T(8,128)(2,1)} %copy-done.30, bf16[128,1792]{1,0:T(8,128)(2,1)} %copy-done.37, bf16[128,1792]{1,0:T(8,128)(2,1)} %copy-done.36, ...), custom_call_target="tpu_custom_call" | custom-call | bytes 5242880 | tf_op jit(solution)/shard_map/pallas_call | solution.py:390
  255.0 12.6 %collective-permute-done.20 = bf16[256,1024]{1,0:T(8,128)(2,1)S(1)} collective-permute-done((bf16[256,1024]{1,0:T(8,128)(2,1)S(1)}, bf16[256,1024]{1,0:T(8,128)(2,1)S(1)}, u32[]{:S(2)}, u32[]{:S(2)}) %collective-permute-start.20) | collective-permute-done | bytes 524320 | tf_op jit(solution)/shard_map/ppermute | solution.py:25
  271.0 9.9 %collective-permute-done.21 = bf16[256,1024]{1,0:T(8,128)(2,1)} collective-permute-done((bf16[256,1024]{1,0:T(8,128)(2,1)S(1)}, bf16[256,1024]{1,0:T(8,128)(2,1)}, u32[]{:S(2)}, u32[]{:S(2)}) %collective-permute-start.21) | collective-permute-done | bytes 524320 | tf_op jit(solution)/shard_map/ppermute | solution.py:25
  283.8 5.7 collective-permute-done.23
  296.1 5.9 shard_map.232
  303.1 2.3 collective-permute-done.31
  313.1 10.5 %collective-permute-done.26 = bf16[256,1024]{1,0:T(8,128)(2,1)} collective-permute-done((bf16[256,1024]{1,0:T(8,128)(2,1)}, bf16[256,1024]{1,0:T(8,128)(2,1)}, u32[]{:S(2)}, u32[]{:S(2)}) %collective-permute-start.26) | collective-permute-done | bytes 524320 | tf_op jit(solution)/shard_map/ppermute | solution.py:25
  327.9 12.8 %collective-permute-done.27 = bf16[256,1024]{1,0:T(8,128)(2,1)S(1)} collective-permute-done((bf16[256,1024]{1,0:T(8,128)(2,1)S(1)}, bf16[256,1024]{1,0:T(8,128)(2,1)S(1)}, u32[]{:S(2)}, u32[]{:S(2)}) %collective-permute-start.27) | collective-permute-done | bytes 524320 | tf_op jit(solution)/shard_map/ppermute | solution.py:25
  341.9 8.0 %collective-permute-done.35 = bf16[256,1024]{1,0:T(8,128)(2,1)S(1)} collective-permute-done((bf16[256,1024]{1,0:T(8,128)(2,1)S(1)}, bf16[256,1024]{1,0:T(8,128)(2,1)S(1)}, u32[]{:S(2)}, u32[]{:S(2)}) %collective-permute-start.35) | collective-permute-done | bytes 524320 | tf_op jit(solution)/shard_map/ppermute | solution.py:25
  351.8 7.4 %multiply_convert_fusion = (bf16[1024,1024]{1,0:T(8,128)(2,1)}, f32[1024,1024]{1,0:T(8,128)}) fusion(bf16[1024,1024]{0,1:T(8,128)(2,1)} %all-gather.3.cloned.1.call-done, bf16[512,1024]{1,0:T(8,128)(2,1)} %collective-permute-done.28, bf16[256,1024]{1,0:T(8,128)(2,1)} %copy-done.46, bf16[256,1024]{1,0:T(8,128)(2,1)S(1)} %add_convert_fusion), kind=kOutput, calls=%fused_computation.7 | convolution fusion | flops 2159017984 | bytes 10485760 | tf_op jit(solution)/shard_map/dot_general | solution.py:19
  359.1 14.6 %all-gather.5.cloned.1.call-done = bf16[1024,1024]{0,1:T(8,128)(2,1)} async-done(((bf16[128,1024]{0,1:T(8,128)(2,1)}), bf16[1024,1024]{0,1:T(8,128)(2,1)}) %all-gather.5.cloned.1.call-update) | async-done | bytes 2097168 | tf_op jit(solution)/shard_map/all_gather | solution.py:340
  373.7 6.6 fusion.5
  380.4 2.2 convolution_convert_fusion.7
  382.6 4.9 convolution_convert_fusion.1
  387.8 3.3 convolution_convert_fusion.8
  391.8 2.8 convert_add_fusion.2
  398.3 11.3 %collective-permute-done.38 = bf16[256,1024]{1,0:T(8,128)(2,1)S(1)} collective-permute-done((bf16[256,1024]{1,0:T(8,128)(2,1)S(1)}, bf16[256,1024]{1,0:T(8,128)(2,1)S(1)}, u32[]{:S(2)}, u32[]{:S(2)}) %collective-permute-start.38) | collective-permute-done | bytes 524320 | tf_op jit(solution)/shard_map/ppermute | solution.py:25
  410.2 9.5 %collective-permute-done.34 = bf16[256,1024]{1,0:T(8,128)(2,1)S(1)} collective-permute-done((bf16[256,1024]{1,0:T(8,128)(2,1)S(1)}, bf16[256,1024]{1,0:T(8,128)(2,1)S(1)}, u32[]{:S(2)}, u32[]{:S(2)}) %collective-permute-start.34) | collective-permute-done | bytes 524320 | tf_op jit(solution)/shard_map/ppermute | solution.py:25
  422.8 11.3 %collective-permute-done.39 = bf16[256,1024]{1,0:T(8,128)(2,1)S(1)} collective-permute-done((bf16[256,1024]{1,0:T(8,128)(2,1)S(1)}, bf16[256,1024]{1,0:T(8,128)(2,1)S(1)}, u32[]{:S(2)}, u32[]{:S(2)}) %collective-permute-start.39) | collective-permute-done | bytes 524320 | tf_op jit(solution)/shard_map/ppermute | solution.py:25
  436.0 5.0 convolution_convert_fusion
  442.3 2.1 convolution_convert_fusion.15.grad_ref
  444.4 6.9 shard_map.233
  457.1 3.8 reshape.304
  460.9 6.9 constant_dynamic-slice_fusion.5
  467.8 4.7 copy.184
  475.8 3.9 copy.183
  479.7 2.3 convolution_convert_fusion.12
  485.2 14.3 %collective-permute-done.61 = bf16[4,128,768]{2,1,0:T(8,128)(2,1)} collective-permute-done((bf16[4,128,768]{2,1,0:T(8,128)(2,1)}, bf16[4,128,768]{2,1,0:T(8,128)(2,1)}, u32[]{:S(2)}, u32[]{:S(2)}) %collective-permute-start.61) | collective-permute-done | bytes 786464 | tf_op jit(solution)/shard_map/ppermute | solution.py:336
  502.6 2.9 collective-permute-start.62
  506.2 4.5 collective-permute-done.64
  510.7 16.5 %collective-permute-done.63 = bf16[128,768]{1,0:T(8,128)(2,1)S(1)} collective-permute-done((bf16[128,768]{1,0:T(8,128)(2,1)S(1)}, bf16[128,768]{1,0:T(8,128)(2,1)S(1)}, u32[]{:S(2)}, u32[]{:S(2)}) %collective-permute-start.63) | collective-permute-done | bytes 196640 | tf_op jit(solution)/shard_map/ppermute | solution.py:336
  537.7 10.6 %collective-permute-done.66 = bf16[2,128,192]{1,2,0:T(8,128)(2,1)S(1)} collective-permute-done((bf16[2,128,192]{1,2,0:T(8,128)(2,1)S(1)}, bf16[2,128,192]{1,2,0:T(8,128)(2,1)S(1)}, u32[]{:S(2)}, u32[]{:S(2)}) %collective-permute-start.66) | collective-permute-done | bytes 98336 | tf_op jit(solution)/shard_map/ppermute | solution.py:25
  551.8 2.7 fusion.143
  560.1 9.4 %collective-permute-done.43 = bf16[256,1024]{1,0:T(8,128)(2,1)S(1)} collective-permute-done((bf16[256,1024]{1,0:T(8,128)(2,1)}, bf16[256,1024]{1,0:T(8,128)(2,1)S(1)}, u32[]{:S(2)}, u32[]{:S(2)}) %collective-permute-start.43) | collective-permute-done | bytes 524320 | tf_op jit(solution)/shard_map/ppermute | solution.py:25
  569.5 2.3 pad_maximum_fusion.12
  575.1 2.7 collective-permute-done.70
  578.7 2.3 convolution_convert_fusion.13
  581.1 2.7 collective-permute-start.57
  585.6 2.1 convolution_convert_fusion.14.grad_ref
  587.7 10.4 %shard_map.234 = bf16[1024,768]{1,0:T(8,128)(2,1)S(1)} custom-call(s32[1]{0:T(128)} %bitcast.1.here_ref, s32[8,1024]{1,0:T(8,128)S(1)} %add_add_fusion.marks_ref, bf16[1024,768]{1,0:T(8,128)(2,1)S(1)} %copy-done.1, bf16[1024,256]{1,0:T(8,128)(2,1)S(1)} %convolution_convert_fusion.14.grad_ref, f32[4,1024]{1,0:T(4,128)S(1)} %get-tuple-element.30.lse_ref), custom_call_target="tpu_custom_call" | custom-call | flops 1677721600 | bytes 3719172 | tf_op jit(solution)/shard_map/pallas_call | solution.py:277
  598.1 7.1 %collective-permute-done.56 = bf16[2,64,1024]{2,1,0:T(8,128)(2,1)S(1)} collective-permute-done((bf16[2,64,1024]{2,1,0:T(8,128)(2,1)S(1)}, bf16[2,64,1024]{2,1,0:T(8,128)(2,1)S(1)}, u32[]{:S(2)}, u32[]{:S(2)}) %collective-permute-start.56) | collective-permute-done | bytes 262176 | tf_op jit(solution)/shard_map/ppermute | solution.py:336
  606.6 3.2 convolution_convert_fusion.2
  617.3 3.4 convolution_convert_fusion.4
  622.1 7.4 %collective-permute-done.49 = bf16[4,128,768]{2,1,0:T(8,128)(2,1)} collective-permute-done((bf16[4,128,768]{2,1,0:T(8,128)(2,1)}, bf16[4,128,768]{2,1,0:T(8,128)(2,1)}, u32[]{:S(2)}, u32[]{:S(2)}) %collective-permute-start.49) | collective-permute-done | bytes 786464 | tf_op jit(solution)/shard_map/ppermute | solution.py:336
  629.4 2.7 fusion.142
  636.0 3.0 collective-permute-start.50
  640.3 2.6 collective-permute-done.52
  642.9 6.7 collective-permute-done.51
  649.8 2.7 convert_add_fusion
  655.5 13.6 %collective-permute-done.54 = bf16[2,128,192]{1,2,0:T(8,128)(2,1)S(1)} collective-permute-done((bf16[2,128,192]{1,2,0:T(8,128)(2,1)S(1)}, bf16[2,128,192]{1,2,0:T(8,128)(2,1)S(1)}, u32[]{:S(2)}, u32[]{:S(2)}) %collective-permute-start.54) | collective-permute-done | bytes 98336 | tf_op jit(solution)/shard_map/ppermute | solution.py:25
  676.3 2.4 collective-permute-done.73
  678.7 3.6 collective-permute-done.74
  683.2 2.6 fusion.20
  (495 shorter events, 146.9 us)
Async XLA Ops:
  7.2 344.5 %all-gather.3.cloned.1.call-start = ((), (), s32[]{:S(2)}) async-start(), calls=%async_computation.2 | async-start | bytes 2359296 | tf_op jit(solution)/shard_map/all_gather | solution.py:340
  8.1 12.8 %collective-permute-start.12 = (bf16[2,64,256]{2,1,0:T(8,128)(2,1)S(1)}, bf16[2,64,256]{2,1,0:T(8,128)(2,1)S(1)}, u32[]{:S(2)}, u32[]{:S(2)}) collective-permute-start(bf16[2,64,256]{2,1,0:T(8,128)(2,1)S(1)} %fusion.119), channel_id=1, source_target_pairs={{0,1},{1,0},{2,3},{3,2},{4,5},{5,4},{6,7},{7,6},{8,9},{9,8},{10,11... | collective-permute-start | bytes 196616 | tf_op jit(solution)/shard_map/ppermute | solution.py:25
  10.7 10.5 %collective-permute-start.10 = (bf16[2,128,192]{1,2,0:T(8,128)(2,1)S(1)}, bf16[2,128,192]{1,2,0:T(8,128)(2,1)S(1)}, u32[]{:S(2)}, u32[]{:S(2)}) collective-permute-start(bf16[2,128,192]{1,2,0:T(8,128)(2,1)S(1)} %fusion.93), channel_id=1, source_target_pairs={{0,1},{1,0},{2,3},{3,2},{4,5},{5,4},{6,7},{7,6},{8,9},{9,8},{10,11... | collective-permute-start | bytes 294920 | tf_op jit(solution)/shard_map/ppermute | solution.py:25
  11.9 11.3 %collective-permute-start.4 = (bf16[2,128,192]{1,2,0:T(8,128)(2,1)S(1)}, bf16[2,128,192]{1,2,0:T(8,128)(2,1)S(1)}, u32[]{:S(2)}, u32[]{:S(2)}) collective-permute-start(bf16[2,128,192]{1,2,0:T(8,128)(2,1)S(1)} %dynamic-slice_bitcast_fusion.9), channel_id=1, source_target_pairs={{0,1},{1,0},{2,3},{3,2},{4,5},{5,4},{6,7},{7,6},{8,9},{9,8},{10,11... | collective-permute-start | bytes 294920 | tf_op jit(solution)/shard_map/ppermute | solution.py:25
  18.9 68.6 %collective-permute-start.2 = (bf16[256,1024]{1,0:T(8,128)(2,1)S(1)}, bf16[256,1024]{1,0:T(8,128)(2,1)}, u32[]{:S(2)}, u32[]{:S(2)}) collective-permute-start(bf16[256,1024]{1,0:T(8,128)(2,1)S(1)} %fusion.15), channel_id=1, source_target_pairs={{0,2},{1,3},{2,0},{3,1},{4,6},{5,7},{6,4},{7,5},{8,10},{9,11},{10,... | collective-permute-start | bytes 1572872 | tf_op jit(solution)/shard_map/ppermute | solution.py:25
  21.0 15.5 %collective-permute-start.13 = (bf16[2,2,64,256]{3,2,1,0:T(8,128)(2,1)S(1)}, bf16[2,2,64,256]{3,2,1,0:T(8,128)(2,1)S(1)}, u32[]{:S(2)}, u32[]{:S(2)}) collective-permute-start(bf16[2,2,64,256]{3,2,1,0:T(8,128)(2,1)S(1)} %pad_maximum_fusion.43), channel_id=1, source_target_pairs={{0,2},{1,3},{2,0},{3,1},{4,6},{5,7},{6,4},{7,5},{8,10},{9,11},{10,... | collective-permute-start | bytes 393224 | tf_op jit(solution)/shard_map/ppermute | solution.py:25
  21.2 17.5 %collective-permute-start.11 = (bf16[2,128,192]{1,2,0:T(8,128)(2,1)S(1)}, bf16[2,128,192]{1,2,0:T(8,128)(2,1)S(1)}, u32[]{:S(2)}, u32[]{:S(2)}) collective-permute-start(bf16[2,128,192]{1,2,0:T(8,128)(2,1)S(1)} %fusion.105), channel_id=1, source_target_pairs={{0,2},{1,3},{2,0},{3,1},{4,6},{5,7},{6,4},{7,5},{8,10},{9,11},{10,... | collective-permute-start | bytes 294920 | tf_op jit(solution)/shard_map/ppermute | solution.py:25
  23.3 16.9 %collective-permute-start.5 = (bf16[2,128,192]{1,2,0:T(8,128)(2,1)S(1)}, bf16[2,128,192]{1,2,0:T(8,128)(2,1)S(1)}, u32[]{:S(2)}, u32[]{:S(2)}) collective-permute-start(bf16[2,128,192]{1,2,0:T(8,128)(2,1)S(1)} %fusion.109), channel_id=1, source_target_pairs={{0,2},{1,3},{2,0},{3,1},{4,6},{5,7},{6,4},{7,5},{8,10},{9,11},{10,... | collective-permute-start | bytes 294920 | tf_op jit(solution)/shard_map/ppermute | solution.py:25
  36.6 9.1 %collective-permute-start.14 = (bf16[128,1024]{1,0:T(8,128)(2,1)S(1)}, bf16[128,1024]{1,0:T(8,128)(2,1)S(1)}, u32[]{:S(2)}, u32[]{:S(2)}) collective-permute-start(bf16[128,1024]{1,0:T(8,128)(2,1)S(1)} %pad_maximum_fusion.33), channel_id=1, source_target_pairs={{0,4},{4,0},{8,12},{12,8},{16,20},{20,16},{24,28},{28,24},{1,5},{5... | collective-permute-start | bytes 786440 | tf_op jit(solution)/shard_map/ppermute | solution.py:336
  41.1 9.7 %collective-permute-start.6 = (bf16[128,768]{1,0:T(8,128)(2,1)}, bf16[128,768]{1,0:T(8,128)(2,1)S(1)}, u32[]{:S(2)}, u32[]{:S(2)}) collective-permute-start(bf16[128,768]{1,0:T(8,128)(2,1)} %copy.132.refs_1_), channel_id=1, source_target_pairs={{0,8},{4,12},{8,0},{12,4},{16,24},{20,28},{24,16},{28,20},{1,9},{5... | collective-permute-start | bytes 589832 | tf_op jit(solution)/shard_map/ppermute | solution.py:336
  42.9 37.0 %collective-permute-start.7 = (bf16[128,768]{1,0:T(8,128)(2,1)}, bf16[128,768]{1,0:T(8,128)(2,1)S(1)}, u32[]{:S(2)}, u32[]{:S(2)}) collective-permute-start(bf16[128,768]{1,0:T(8,128)(2,1)} %copy.132.refs_1_), channel_id=1, source_target_pairs={{0,16},{4,20},{8,24},{12,28},{16,0},{20,4},{24,8},{28,12},{1,17},{... | collective-permute-start | bytes 589832 | tf_op jit(solution)/shard_map/ppermute | solution.py:336
  45.5 34.5 %collective-permute-start.8 = (bf16[128,768]{1,0:T(8,128)(2,1)}, bf16[128,768]{1,0:T(8,128)(2,1)}, u32[]{:S(2)}, u32[]{:S(2)}) collective-permute-start(bf16[128,768]{1,0:T(8,128)(2,1)} %copy.132.refs_1_), channel_id=1, source_target_pairs={{0,24},{4,28},{8,16},{12,20},{16,8},{20,12},{24,0},{28,4},{1,25},{... | collective-permute-start | bytes 589832 | tf_op jit(solution)/shard_map/ppermute | solution.py:336
  45.9 42.8 %collective-permute-start.17 = (bf16[128,1792]{1,0:T(8,128)(2,1)S(1)}, bf16[128,1792]{1,0:T(8,128)(2,1)S(1)}, u32[]{:S(2)}, u32[]{:S(2)}) collective-permute-start(bf16[128,1792]{1,0:T(8,128)(2,1)S(1)} %pad_maximum_fusion.28.refs_1_), channel_id=1, source_target_pairs={{0,24},{4,28},{8,16},{12,20},{16,8},{20,12},{24,0},{28,4},{1,25},{... | collective-permute-start | bytes 1376264 | tf_op jit(solution)/shard_map/ppermute | solution.py:336
  50.8 51.2 %collective-permute-start.16 = (bf16[128,1792]{1,0:T(8,128)(2,1)S(1)}, bf16[128,1792]{1,0:T(8,128)(2,1)S(1)}, u32[]{:S(2)}, u32[]{:S(2)}) collective-permute-start(bf16[128,1792]{1,0:T(8,128)(2,1)S(1)} %pad_maximum_fusion.28.refs_1_), channel_id=1, source_target_pairs={{0,16},{4,20},{8,24},{12,28},{16,0},{20,4},{24,8},{28,12},{1,17},{... | collective-permute-start | bytes 1376264 | tf_op jit(solution)/shard_map/ppermute | solution.py:336
  81.1 24.7 %collective-permute-start.9 = (bf16[4,128,768]{2,1,0:T(8,128)(2,1)S(1)}, bf16[4,128,768]{2,1,0:T(8,128)(2,1)S(1)}, u32[]{:S(2)}, u32[]{:S(2)}) collective-permute-start(bf16[4,128,768]{2,1,0:T(8,128)(2,1)S(1)} %pad_maximum_fusion.25), channel_id=1, source_target_pairs={{0,4},{4,0},{8,12},{12,8},{16,20},{20,16},{24,28},{28,24},{1,5},{5... | collective-permute-start | bytes 2359304 | tf_op jit(solution)/shard_map/ppermute | solution.py:336
  82.6 21.3 %collective-permute-start.15 = (bf16[128,1792]{1,0:T(8,128)(2,1)S(1)}, bf16[128,1792]{1,0:T(8,128)(2,1)S(1)}, u32[]{:S(2)}, u32[]{:S(2)}) collective-permute-start(bf16[128,1792]{1,0:T(8,128)(2,1)S(1)} %pad_maximum_fusion.28.refs_1_), channel_id=1, source_target_pairs={{0,8},{4,12},{8,0},{12,4},{16,24},{20,28},{24,16},{28,20},{1,9},{5... | collective-permute-start | bytes 1376264 | tf_op jit(solution)/shard_map/ppermute | solution.py:336
  88.6 66.9 %collective-permute-start.3 = (bf16[512,1024]{1,0:T(8,128)(2,1)S(1)}, bf16[512,1024]{1,0:T(8,128)(2,1)}, u32[]{:S(2)}, u32[]{:S(2)}) collective-permute-start(bf16[512,1024]{1,0:T(8,128)(2,1)S(1)} %pad_maximum_fusion.7), channel_id=1, source_target_pairs={{0,1},{1,0},{2,3},{3,2},{4,5},{5,4},{6,7},{7,6},{8,9},{9,8},{10,11... | collective-permute-start | bytes 3145736 | tf_op jit(solution)/shard_map/ppermute | solution.py:25
  105.0 60.7 %collective-permute-start.18 = (bf16[4,128,768]{2,1,0:T(8,128)(2,1)}, bf16[4,128,768]{2,1,0:T(8,128)(2,1)}, u32[]{:S(2)}, u32[]{:S(2)}) collective-permute-start(bf16[4,128,768]{2,1,0:T(8,128)(2,1)} %pad_maximum_fusion.26), channel_id=1, source_target_pairs={{0,4},{4,0},{8,12},{12,8},{16,20},{20,16},{24,28},{28,24},{1,5},{5... | collective-permute-start | bytes 2359304 | tf_op jit(solution)/shard_map/ppermute | solution.py:336
  252.8 14.8 %collective-permute-start.20 = (bf16[256,1024]{1,0:T(8,128)(2,1)S(1)}, bf16[256,1024]{1,0:T(8,128)(2,1)S(1)}, u32[]{:S(2)}, u32[]{:S(2)}) collective-permute-start(bf16[256,1024]{1,0:T(8,128)(2,1)S(1)} %slice.368), channel_id=1, source_target_pairs={{0,2},{1,3},{2,0},{3,1},{4,6},{5,7},{6,4},{7,5},{8,10},{9,11},{10,... | collective-permute-start | bytes 1572872 | tf_op jit(solution)/shard_map/ppermute | solution.py:25
  254.5 15.6 %collective-permute-start.30 = (bf16[2,128,256]{2,1,0:T(8,128)(2,1)S(1)}, bf16[2,128,256]{2,1,0:T(8,128)(2,1)S(1)}, u32[]{:S(2)}, u32[]{:S(2)}) collective-permute-start(bf16[2,128,256]{2,1,0:T(8,128)(2,1)S(1)} %fusion.81), channel_id=1, source_target_pairs={{0,2},{1,3},{2,0},{3,1},{4,6},{5,7},{6,4},{7,5},{8,10},{9,11},{10,... | collective-permute-start | bytes 393224 | tf_op jit(solution)/shard_map/ppermute | solution.py:25
  268.5 12.5 %collective-permute-start.21 = (bf16[256,1024]{1,0:T(8,128)(2,1)S(1)}, bf16[256,1024]{1,0:T(8,128)(2,1)}, u32[]{:S(2)}, u32[]{:S(2)}) collective-permute-start(bf16[256,1024]{1,0:T(8,128)(2,1)S(1)} %add_convert_fusion.1), channel_id=1, source_target_pairs={{0,2},{1,3},{2,0},{3,1},{4,6},{5,7},{6,4},{7,5},{8,10},{9,11},{10,... | collective-permute-start | bytes 1572872 | tf_op jit(solution)/shard_map/ppermute | solution.py:25
  271.0 102.7 %all-gather.5.cloned.1.call-start = ((), (), s32[]{:S(2)}) async-start(), calls=%async_computation.3 | async-start | bytes 2359296 | tf_op jit(solution)/shard_map/all_gather | solution.py:340
  282.1 11.2 %collective-permute-start.22 = (bf16[512,1024]{1,0:T(8,128)(2,1)S(1)}, bf16[512,1024]{1,0:T(8,128)(2,1)S(1)}, u32[]{:S(2)}, u32[]{:S(2)}) collective-permute-start(bf16[512,1024]{1,0:T(8,128)(2,1)S(1)} %pad_maximum_fusion.8), channel_id=1, source_target_pairs={{0,1},{1,0},{2,3},{3,2},{4,5},{5,4},{6,7},{7,6},{8,9},{9,8},{10,11... | collective-permute-start | bytes 3145736 | tf_op jit(solution)/shard_map/ppermute | solution.py:25
  282.2 7.3 %collective-permute-start.23 = (bf16[96,1024]{1,0:T(8,128)(2,1)S(1)}, bf16[96,1024]{1,0:T(8,128)(2,1)S(1)}, u32[]{:S(2)}, u32[]{:S(2)}) collective-permute-start(bf16[96,1024]{1,0:T(8,128)(2,1)S(1)} %bitcast.599), channel_id=1, source_target_pairs={{0,2},{1,3},{2,0},{3,1},{4,6},{5,7},{6,4},{7,5},{8,10},{9,11},{10,... | collective-permute-start | bytes 589832 | tf_op jit(solution)/shard_map/ppermute | solution.py:25
  309.6 14.0 %collective-permute-start.26 = (bf16[256,1024]{1,0:T(8,128)(2,1)}, bf16[256,1024]{1,0:T(8,128)(2,1)}, u32[]{:S(2)}, u32[]{:S(2)}) collective-permute-start(bf16[256,1024]{1,0:T(8,128)(2,1)} %slice.367), channel_id=1, source_target_pairs={{0,2},{1,3},{2,0},{3,1},{4,6},{5,7},{6,4},{7,5},{8,10},{9,11},{10,... | collective-permute-start | bytes 1572872 | tf_op jit(solution)/shard_map/ppermute | solution.py:25
  311.9 221.3 %reduce-scatter.3.cloned.1.call-start = ((), (), s32[]{:S(2)}) async-start(), calls=%async_computation.4 | async-start | bytes 2359296 | tf_op jit(solution)/shard_map/reduce_scatter | solution.py:344
  325.8 14.9 %collective-permute-start.27 = (bf16[256,1024]{1,0:T(8,128)(2,1)S(1)}, bf16[256,1024]{1,0:T(8,128)(2,1)S(1)}, u32[]{:S(2)}, u32[]{:S(2)}) collective-permute-start(bf16[256,1024]{1,0:T(8,128)(2,1)S(1)} %add_convert_fusion), channel_id=1, source_target_pairs={{0,2},{1,3},{2,0},{3,1},{4,6},{5,7},{6,4},{7,5},{8,10},{9,11},{10,... | collective-permute-start | bytes 1572872 | tf_op jit(solution)/shard_map/ppermute | solution.py:25
  326.7 23.2 %collective-permute-start.35 = (bf16[256,1024]{1,0:T(8,128)(2,1)S(1)}, bf16[256,1024]{1,0:T(8,128)(2,1)S(1)}, u32[]{:S(2)}, u32[]{:S(2)}) collective-permute-start(bf16[256,1024]{1,0:T(8,128)(2,1)S(1)} %bitcast.544), channel_id=1, source_target_pairs={{0,2},{1,3},{2,0},{3,1},{4,6},{5,7},{6,4},{7,5},{8,10},{9,11},{10,... | collective-permute-start | bytes 1572872 | tf_op jit(solution)/shard_map/ppermute | solution.py:25
  341.9 9.9 %collective-permute-start.28 = (bf16[512,1024]{1,0:T(8,128)(2,1)}, bf16[512,1024]{1,0:T(8,128)(2,1)}, u32[]{:S(2)}, u32[]{:S(2)}) collective-permute-start(bf16[512,1024]{1,0:T(8,128)(2,1)} %pad_maximum_fusion.9), channel_id=1, source_target_pairs={{0,1},{1,0},{2,3},{3,2},{4,5},{5,4},{6,7},{7,6},{8,9},{9,8},{10,11... | collective-permute-start | bytes 3145736 | tf_op jit(solution)/shard_map/ppermute | solution.py:25
  351.8 7.4 %collective-permute-start.36 = (bf16[512,1024]{1,0:T(8,128)(2,1)}, bf16[512,1024]{1,0:T(8,128)(2,1)}, u32[]{:S(2)}, u32[]{:S(2)}) collective-permute-start(bf16[512,1024]{1,0:T(8,128)(2,1)} %pad_maximum_fusion.10), channel_id=1, source_target_pairs={{0,1},{1,0},{2,3},{3,2},{4,5},{5,4},{6,7},{7,6},{8,9},{9,8},{10,11... | collective-permute-start | bytes 3145736 | tf_op jit(solution)/shard_map/ppermute | solution.py:25
  382.6 9.2 %collective-permute-start.37 = (bf16[512,1024]{1,0:T(8,128)(2,1)}, bf16[512,1024]{1,0:T(8,128)(2,1)}, u32[]{:S(2)}, u32[]{:S(2)}) collective-permute-start(bf16[512,1024]{1,0:T(8,128)(2,1)} %convolution_convert_fusion.7), channel_id=1, source_target_pairs={{0,1},{1,0},{2,3},{3,2},{4,5},{5,4},{6,7},{7,6},{8,9},{9,8},{10,11... | collective-permute-start | bytes 3145736 | tf_op jit(solution)/shard_map/ppermute | solution.py:25
  387.6 147.6 %reduce-scatter.5.cloned.1.call-start = ((), (), s32[]{:S(2)}) async-start(), calls=%async_computation.5 | async-start | bytes 2359296 | tf_op jit(solution)/shard_map/reduce_scatter | solution.py:344
  394.7 14.9 %collective-permute-start.38 = (bf16[256,1024]{1,0:T(8,128)(2,1)S(1)}, bf16[256,1024]{1,0:T(8,128)(2,1)S(1)}, u32[]{:S(2)}, u32[]{:S(2)}) collective-permute-start(bf16[256,1024]{1,0:T(8,128)(2,1)S(1)} %slice.365), channel_id=1, source_target_pairs={{0,2},{1,3},{2,0},{3,1},{4,6},{5,7},{6,4},{7,5},{8,10},{9,11},{10,... | collective-permute-start | bytes 1572872 | tf_op jit(solution)/shard_map/ppermute | solution.py:25
  397.6 22.1 %collective-permute-start.34 = (bf16[256,1024]{1,0:T(8,128)(2,1)S(1)}, bf16[256,1024]{1,0:T(8,128)(2,1)S(1)}, u32[]{:S(2)}, u32[]{:S(2)}) collective-permute-start(bf16[256,1024]{1,0:T(8,128)(2,1)S(1)} %slice.366), channel_id=1, source_target_pairs={{0,2},{1,3},{2,0},{3,1},{4,6},{5,7},{6,4},{7,5},{8,10},{9,11},{10,... | collective-permute-start | bytes 1572872 | tf_op jit(solution)/shard_map/ppermute | solution.py:25
  421.3 12.8 %collective-permute-start.39 = (bf16[256,1024]{1,0:T(8,128)(2,1)S(1)}, bf16[256,1024]{1,0:T(8,128)(2,1)S(1)}, u32[]{:S(2)}, u32[]{:S(2)}) collective-permute-start(bf16[256,1024]{1,0:T(8,128)(2,1)S(1)} %get-tuple-element.87), channel_id=1, source_target_pairs={{0,2},{1,3},{2,0},{3,1},{4,6},{5,7},{6,4},{7,5},{8,10},{9,11},{10,... | collective-permute-start | bytes 1572872 | tf_op jit(solution)/shard_map/ppermute | solution.py:25
  436.0 6.3 collective-permute-start.40
  452.6 29.4 %collective-permute-start.47 = (bf16[192,1024]{1,0:T(8,128)(2,1)}, bf16[192,1024]{1,0:T(8,128)(2,1)}, u32[]{:S(2)}, u32[]{:S(2)}) collective-permute-start(bf16[192,1024]{1,0:T(8,128)(2,1)} %convolution_convert_fusion.17), channel_id=1, source_target_pairs={{0,1},{1,0},{2,3},{3,2},{4,5},{5,4},{6,7},{7,6},{8,9},{9,8},{10,11... | collective-permute-start | bytes 1179656 | tf_op jit(solution)/shard_map/ppermute | solution.py:25
  472.5 27.0 %collective-permute-start.61 = (bf16[4,128,768]{2,1,0:T(8,128)(2,1)}, bf16[4,128,768]{2,1,0:T(8,128)(2,1)}, u32[]{:S(2)}, u32[]{:S(2)}) collective-permute-start(bf16[4,128,768]{2,1,0:T(8,128)(2,1)} %bitcast.579), channel_id=1, source_target_pairs={{0,4},{4,0},{8,12},{12,8},{16,20},{20,16},{24,28},{28,24},{1,5},{5... | collective-permute-start | bytes 2359304 | tf_op jit(solution)/shard_map/ppermute | solution.py:336
  475.5 52.2 %collective-permute-start.41 = (bf16[512,1024]{1,0:T(8,128)(2,1)}, bf16[512,1024]{1,0:T(8,128)(2,1)}, u32[]{:S(2)}, u32[]{:S(2)}) collective-permute-start(bf16[512,1024]{1,0:T(8,128)(2,1)} %convolution_convert_fusion.6), channel_id=1, source_target_pairs={{0,1},{1,0},{2,3},{3,2},{4,5},{5,4},{6,7},{7,6},{8,9},{9,8},{10,11... | collective-permute-start | bytes 3145736 | tf_op jit(solution)/shard_map/ppermute | solution.py:25
  483.6 21.9 %collective-permute-start.48 = (bf16[96,1024]{1,0:T(8,128)(2,1)S(1)}, bf16[96,1024]{1,0:T(8,128)(2,1)S(1)}, u32[]{:S(2)}, u32[]{:S(2)}) collective-permute-start(bf16[96,1024]{1,0:T(8,128)(2,1)S(1)} %slice.369), channel_id=1, source_target_pairs={{0,2},{1,3},{2,0},{3,1},{4,6},{5,7},{6,4},{7,5},{8,10},{9,11},{10,... | collective-permute-start | bytes 589832 | tf_op jit(solution)/shard_map/ppermute | solution.py:25
  501.0 9.7 %collective-permute-start.64 = (bf16[128,768]{1,0:T(8,128)(2,1)S(1)}, bf16[128,768]{1,0:T(8,128)(2,1)S(1)}, u32[]{:S(2)}, u32[]{:S(2)}) collective-permute-start(bf16[128,768]{1,0:T(8,128)(2,1)S(1)} %get-tuple-element.102), channel_id=1, source_target_pairs={{0,24},{4,28},{8,16},{12,20},{16,8},{20,12},{24,0},{28,4},{1,25},{... | collective-permute-start | bytes 589832 | tf_op jit(solution)/shard_map/ppermute | solution.py:336
  502.6 24.7 %collective-permute-start.63 = (bf16[128,768]{1,0:T(8,128)(2,1)S(1)}, bf16[128,768]{1,0:T(8,128)(2,1)S(1)}, u32[]{:S(2)}, u32[]{:S(2)}) collective-permute-start(bf16[128,768]{1,0:T(8,128)(2,1)S(1)} %get-tuple-element.103), channel_id=1, source_target_pairs={{0,16},{4,20},{8,24},{12,28},{16,0},{20,4},{24,8},{28,12},{1,17},{... | collective-permute-start | bytes 589832 | tf_op jit(solution)/shard_map/ppermute | solution.py:336
  502.6 24.7 %collective-permute-start.62 = (bf16[128,768]{1,0:T(8,128)(2,1)S(1)}, bf16[128,768]{1,0:T(8,128)(2,1)S(1)}, u32[]{:S(2)}, u32[]{:S(2)}) collective-permute-start(bf16[128,768]{1,0:T(8,128)(2,1)S(1)} %get-tuple-element.101), channel_id=1, source_target_pairs={{0,8},{4,12},{8,0},{12,4},{16,24},{20,28},{24,16},{28,20},{1,9},{5... | collective-permute-start | bytes 589832 | tf_op jit(solution)/shard_map/ppermute | solution.py:336
  527.7 8.7 %collective-permute-start.65 = (bf16[2,128,192]{1,2,0:T(8,128)(2,1)S(1)}, bf16[2,128,192]{1,2,0:T(8,128)(2,1)S(1)}, u32[]{:S(2)}, u32[]{:S(2)}) collective-permute-start(bf16[2,128,192]{1,2,0:T(8,128)(2,1)S(1)} %dynamic-slice_bitcast_fusion.7), channel_id=1, source_target_pairs={{0,1},{1,0},{2,3},{3,2},{4,5},{5,4},{6,7},{7,6},{8,9},{9,8},{10,11... | collective-permute-start | bytes 294920 | tf_op jit(solution)/shard_map/ppermute | solution.py:25
  531.7 18.4 %collective-permute-start.42 = (bf16[256,1024]{1,0:T(8,128)(2,1)}, bf16[256,1024]{1,0:T(8,128)(2,1)}, u32[]{:S(2)}, u32[]{:S(2)}) collective-permute-start(bf16[256,1024]{1,0:T(8,128)(2,1)} %slice.364), channel_id=1, source_target_pairs={{0,2},{1,3},{2,0},{3,1},{4,6},{5,7},{6,4},{7,5},{8,10},{9,11},{10,... | collective-permute-start | bytes 1572872 | tf_op jit(solution)/shard_map/ppermute | solution.py:25
  535.0 14.1 %collective-permute-start.67 = (bf16[2,128,256]{2,1,0:T(8,128)(2,1)}, bf16[2,128,256]{2,1,0:T(8,128)(2,1)}, u32[]{:S(2)}, u32[]{:S(2)}) collective-permute-start(bf16[2,128,256]{2,1,0:T(8,128)(2,1)} %dynamic-slice_bitcast_fusion.5), channel_id=1, source_target_pairs={{0,1},{1,0},{2,3},{3,2},{4,5},{5,4},{6,7},{7,6},{8,9},{9,8},{10,11... | collective-permute-start | bytes 393224 | tf_op jit(solution)/shard_map/ppermute | solution.py:25
  536.4 11.9 %collective-permute-start.66 = (bf16[2,128,192]{1,2,0:T(8,128)(2,1)S(1)}, bf16[2,128,192]{1,2,0:T(8,128)(2,1)S(1)}, u32[]{:S(2)}, u32[]{:S(2)}) collective-permute-start(bf16[2,128,192]{1,2,0:T(8,128)(2,1)S(1)} %fusion.97), channel_id=1, source_target_pairs={{0,2},{1,3},{2,0},{3,1},{4,6},{5,7},{6,4},{7,5},{8,10},{9,11},{10,... | collective-permute-start | bytes 294920 | tf_op jit(solution)/shard_map/ppermute | solution.py:25
  537.7 21.4 %collective-permute-start.69 = (bf16[2,128,256]{2,1,0:T(8,128)(2,1)}, bf16[2,128,256]{2,1,0:T(8,128)(2,1)}, u32[]{:S(2)}, u32[]{:S(2)}) collective-permute-start(bf16[2,128,256]{2,1,0:T(8,128)(2,1)} %dynamic-slice_bitcast_fusion.4), channel_id=1, source_target_pairs={{0,1},{1,0},{2,3},{3,2},{4,5},{5,4},{6,7},{7,6},{8,9},{9,8},{10,11... | collective-permute-start | bytes 393224 | tf_op jit(solution)/shard_map/ppermute | solution.py:25
  554.4 15.0 %collective-permute-start.43 = (bf16[256,1024]{1,0:T(8,128)(2,1)}, bf16[256,1024]{1,0:T(8,128)(2,1)S(1)}, u32[]{:S(2)}, u32[]{:S(2)}) collective-permute-start(bf16[256,1024]{1,0:T(8,128)(2,1)} %get-tuple-element.85), channel_id=1, source_target_pairs={{0,2},{1,3},{2,0},{3,1},{4,6},{5,7},{6,4},{7,5},{8,10},{9,11},{10,... | collective-permute-start | bytes 1572872 | tf_op jit(solution)/shard_map/ppermute | solution.py:25
  558.5 14.8 %collective-permute-start.68 = (bf16[2,128,256]{2,1,0:T(8,128)(2,1)S(1)}, bf16[2,128,256]{2,1,0:T(8,128)(2,1)S(1)}, u32[]{:S(2)}, u32[]{:S(2)}) collective-permute-start(bf16[2,128,256]{2,1,0:T(8,128)(2,1)S(1)} %fusion.73), channel_id=1, source_target_pairs={{0,2},{1,3},{2,0},{3,1},{4,6},{5,7},{6,4},{7,5},{8,10},{9,11},{10,... | collective-permute-start | bytes 393224 | tf_op jit(solution)/shard_map/ppermute | solution.py:25
  571.8 6.9 collective-permute-start.44
  571.8 6.0 collective-permute-start.70
  581.1 17.0 %collective-permute-start.57 = (bf16[2,64,1024]{2,1,0:T(8,128)(2,1)S(1)}, bf16[2,64,1024]{2,1,0:T(8,128)(2,1)S(1)}, u32[]{:S(2)}, u32[]{:S(2)}) collective-permute-start(bf16[2,64,1024]{2,1,0:T(8,128)(2,1)S(1)} %get-tuple-element.99), channel_id=1, source_target_pairs={{0,24},{4,28},{8,16},{12,20},{16,8},{20,12},{24,0},{28,4},{1,25},{... | collective-permute-start | bytes 786440 | tf_op jit(solution)/shard_map/ppermute | solution.py:336
  583.9 21.3 %collective-permute-start.56 = (bf16[2,64,1024]{2,1,0:T(8,128)(2,1)S(1)}, bf16[2,64,1024]{2,1,0:T(8,128)(2,1)S(1)}, u32[]{:S(2)}, u32[]{:S(2)}) collective-permute-start(bf16[2,64,1024]{2,1,0:T(8,128)(2,1)S(1)} %get-tuple-element.98), channel_id=1, source_target_pairs={{0,16},{4,20},{8,24},{12,28},{16,0},{20,4},{24,8},{28,12},{1,17},{... | collective-permute-start | bytes 786440 | tf_op jit(solution)/shard_map/ppermute | solution.py:336
  583.9 21.3 %collective-permute-start.55 = (bf16[2,64,1024]{2,1,0:T(8,128)(2,1)S(1)}, bf16[2,64,1024]{2,1,0:T(8,128)(2,1)S(1)}, u32[]{:S(2)}, u32[]{:S(2)}) collective-permute-start(bf16[2,64,1024]{2,1,0:T(8,128)(2,1)S(1)} %get-tuple-element.97), channel_id=1, source_target_pairs={{0,8},{4,12},{8,0},{12,4},{16,24},{20,28},{24,16},{28,20},{1,9},{5... | collective-permute-start | bytes 786440 | tf_op jit(solution)/shard_map/ppermute | solution.py:336
  605.4 7.3 %collective-permute-start.58 = (bf16[2,64,1024]{2,1,0:T(8,128)(2,1)S(1)}, bf16[2,64,1024]{2,1,0:T(8,128)(2,1)S(1)}, u32[]{:S(2)}, u32[]{:S(2)}) collective-permute-start(bf16[2,64,1024]{2,1,0:T(8,128)(2,1)S(1)} %fusion.138), channel_id=1, source_target_pairs={{0,4},{4,0},{8,12},{12,8},{16,20},{20,16},{24,28},{28,24},{1,5},{5... | collective-permute-start | bytes 786440 | tf_op jit(solution)/shard_map/ppermute | solution.py:336
  610.9 18.6 %collective-permute-start.49 = (bf16[4,128,768]{2,1,0:T(8,128)(2,1)}, bf16[4,128,768]{2,1,0:T(8,128)(2,1)}, u32[]{:S(2)}, u32[]{:S(2)}) collective-permute-start(bf16[4,128,768]{2,1,0:T(8,128)(2,1)} %dynamic-slice_bitcast_fusion), channel_id=1, source_target_pairs={{0,4},{4,0},{8,12},{12,8},{16,20},{20,16},{24,28},{28,24},{1,5},{5... | collective-permute-start | bytes 2359304 | tf_op jit(solution)/shard_map/ppermute | solution.py:336
  620.7 29.0 %collective-permute-start.45 = (bf16[512,1024]{1,0:T(8,128)(2,1)}, bf16[512,1024]{1,0:T(8,128)(2,1)}, u32[]{:S(2)}, u32[]{:S(2)}) collective-permute-start(bf16[512,1024]{1,0:T(8,128)(2,1)} %convolution_convert_fusion.4), channel_id=1, source_target_pairs={{0,1},{1,0},{2,3},{3,2},{4,5},{5,4},{6,7},{7,6},{8,9},{9,8},{10,11... | collective-permute-start | bytes 3145736 | tf_op jit(solution)/shard_map/ppermute | solution.py:25
  621.4 17.7 %collective-permute-start.60 = (bf16[2,64,256]{2,1,0:T(8,128)(2,1)S(1)}, bf16[2,64,256]{2,1,0:T(8,128)(2,1)S(1)}, u32[]{:S(2)}, u32[]{:S(2)}) collective-permute-start(bf16[2,64,256]{2,1,0:T(8,128)(2,1)S(1)} %bitcast.610), channel_id=1, source_target_pairs={{0,1},{1,0},{2,3},{3,2},{4,5},{5,4},{6,7},{7,6},{8,9},{9,8},{10,11... | collective-permute-start | bytes 196616 | tf_op jit(solution)/shard_map/ppermute | solution.py:25
  633.0 9.8 %collective-permute-start.52 = (bf16[128,768]{0,1:T(8,128)(2,1)}, bf16[128,768]{0,1:T(8,128)(2,1)S(1)}, u32[]{:S(2)}, u32[]{:S(2)}) collective-permute-start(bf16[128,768]{0,1:T(8,128)(2,1)} %bitcast.112), channel_id=1, source_target_pairs={{0,24},{4,28},{8,16},{12,20},{16,8},{20,12},{24,0},{28,4},{1,25},{... | collective-permute-start | bytes 589832 | tf_op jit(solution)/shard_map/ppermute | solution.py:336
  635.2 14.3 %collective-permute-start.51 = (bf16[128,768]{0,1:T(8,128)(2,1)}, bf16[128,768]{0,1:T(8,128)(2,1)S(1)}, u32[]{:S(2)}, u32[]{:S(2)}) collective-permute-start(bf16[128,768]{0,1:T(8,128)(2,1)} %bitcast.111), channel_id=1, source_target_pairs={{0,16},{4,20},{8,24},{12,28},{16,0},{20,4},{24,8},{28,12},{1,17},{... | collective-permute-start | bytes 589832 | tf_op jit(solution)/shard_map/ppermute | solution.py:336
  636.0 13.5 %collective-permute-start.50 = (bf16[128,768]{0,1:T(8,128)(2,1)}, bf16[128,768]{0,1:T(8,128)(2,1)S(1)}, u32[]{:S(2)}, u32[]{:S(2)}) collective-permute-start(bf16[128,768]{0,1:T(8,128)(2,1)} %bitcast.110), channel_id=1, source_target_pairs={{0,8},{4,12},{8,0},{12,4},{16,24},{20,28},{24,16},{28,20},{1,9},{5... | collective-permute-start | bytes 589832 | tf_op jit(solution)/shard_map/ppermute | solution.py:336
  652.6 16.5 %collective-permute-start.46 = (bf16[256,1024]{1,0:T(8,128)(2,1)S(1)}, bf16[256,1024]{1,0:T(8,128)(2,1)S(1)}, u32[]{:S(2)}, u32[]{:S(2)}) collective-permute-start(bf16[256,1024]{1,0:T(8,128)(2,1)S(1)} %slice.363), channel_id=1, source_target_pairs={{0,2},{1,3},{2,0},{3,1},{4,6},{5,7},{6,4},{7,5},{8,10},{9,11},{10,... | collective-permute-start | bytes 1572872 | tf_op jit(solution)/shard_map/ppermute | solution.py:25
  654.2 14.9 %collective-permute-start.54 = (bf16[2,128,192]{1,2,0:T(8,128)(2,1)S(1)}, bf16[2,128,192]{1,2,0:T(8,128)(2,1)S(1)}, u32[]{:S(2)}, u32[]{:S(2)}) collective-permute-start(bf16[2,128,192]{1,2,0:T(8,128)(2,1)S(1)} %fusion.101), channel_id=1, source_target_pairs={{0,2},{1,3},{2,0},{3,1},{4,6},{5,7},{6,4},{7,5},{8,10},{9,11},{10,... | collective-permute-start | bytes 294920 | tf_op jit(solution)/shard_map/ppermute | solution.py:25
  (92 other events, 1124.7 us)
Sparse Core Ops, SparseCore 0:
  271.1 51.7 all-gather.2
  325.5 48.1 all-gather.4
  387.7 66.1 reduce-scatter.2
  457.3 71.1 reduce-scatter.4

commit v3 on v1

--- a/solution.py
+++ b/solution.py
@@ -1,3 +1,4 @@
+import functools
 import math
 
 import jax
@@ -25,18 +26,70 @@
     return lax.ppermute(values, "text", [(i, i ^ mask) for i in range(WAYS)])
 
 
-def gather_slots(block):
-    pair = jnp.concatenate([block, swap(block, 2)], axis=0)
-    return jnp.concatenate([pair, swap(pair, 1)], axis=0)
-
-
-def scatter_slots(left, right, right_dim):
+def after(value, *events):
+    return lax.optimization_barrier((value,) + events)[0]
+
+
+def copy_all(pairs, sem):
+    copies = [pltpu.make_async_copy(*pair, sem.at[i]) for i, pair in enumerate(pairs)]
+    for copy in copies:
+        copy.start()
+    for copy in copies:
+        copy.wait()
+
+
+def join_rows(_, *refs):
+    *blocks, whole, sem = refs
+    size = whole.shape[0] // len(blocks)
+    copy_all(
+        [(block, whole.at[i * size : (i + 1) * size]) for i, block in enumerate(blocks)], sem
+    )
+
+
+def join(ids, *blocks):
+    rows = sum(b.shape[0] for b in blocks)
+    (whole,) = call(
+        join_rows,
+        [shaped((rows, blocks[0].shape[1]), LOW)],
+        (ids, *blocks),
+        own_copies=len(blocks),
+    )
+    return whole
+
+
+def sync(*values):
+    return lax.optimization_barrier(values)
+
+
+def gather_slots(block, ids, *beside):
+    near = swap(block, 1)
+    far, *beside = sync(swap(block, 2), *beside)
+    whole = join(ids, block, far, near, swap(far, 1))
+    return (whole, *beside) if beside else whole
+
+
+def scatter_slots(left, right, right_dim, gate=None, beside=()):
     half = left.shape[0] // 2
     block = half // 2
     away = mm(left[half:], right, 1, right_dim).astype(LOW)
-    here = mm(left[:half], right, 1, right_dim)
-    here = here + swap(away, 1).astype(WIDE)
-    return here[:block] + swap(here[block:].astype(LOW), 2).astype(WIDE)
+    near = swap(away, 1)
+    far = (mm(left[block:half], right, 1, right_dim) + near[block:].astype(WIDE)).astype(LOW)
+    if gate is not None:
+        far = after(far, gate)
+    far, *beside = sync(swap(far, 2), *beside)
+    here = mm(left[:block], right, 1, right_dim) + near[:block].astype(WIDE)
+    result = here + far.astype(WIDE)
+    return (result, *beside) if beside else result
+
+
+def gather_pair(block, ids):
+    return join(ids, block, swap(block, 1))
+
+
+def scatter_pair(left, right, right_dim):
+    half = left.shape[0] // 2
+    away = mm(left[half:], right, 1, right_dim).astype(LOW)
+    return mm(left[:half], right, 1, right_dim) + swap(away, 1).astype(WIDE)
 
 
 def norm_forward(values, gain, bias):
@@ -202,87 +255,162 @@
     return place
 
 
-def cross_forward(here_ref, marks_ref, query_ref, pairs_ref, out_ref, lse_ref):
+def text_allowed(here, marks_ref, block, size, count):
+    start = pl.multiple_of((here ^ block) * size, size)
+    low = marks_ref[1:2, pl.ds(start, size)]
+    high = marks_ref[2:3, pl.ds(start, size)]
+    places = [token_places(here, count, size), token_places(here ^ 2, count, size)]
+    return [(place >= low) & (place < high) for place in places]
+
+
+def cross_forward(here_ref, marks_ref, query_ref, own_ref, other_ref, out_ref, lse_ref):
     here = here_ref[0]
-    size = query_ref.shape[0] // WAYS
-    place = token_places(here, pairs_ref.shape[0], size)
-    for pair in range(2):
-        keys = pairs_ref[:, pair * 128 : (pair + 1) * 128]
-        values_t = transposed(pairs_ref[:, 256 + pair * 128 : 256 + (pair + 1) * 128]).astype(LOW)
-        for i in range(WAYS):
-            mine = slot_of(i, here)
-            query = rows_at(query_ref, mine, size, pair, 0) * LOW(0.125)
-            low = marks_ref[1:2, i * size : (i + 1) * size]
-            high = marks_ref[2:3, i * size : (i + 1) * size]
-            allowed = (place >= low) & (place < high)
+    size = query_ref.shape[0] // 2
+    allowed = [text_allowed(here, marks_ref, b, size, own_ref.shape[0]) for b in range(2)]
+    for pair in range(4):
+        ref = (own_ref, other_ref)[pair // 2]
+        column = (pair % 2) * 128
+        keys = ref[:, column : column + 128]
+        values_t = transposed(ref[:, 256 + column : 384 + column]).astype(LOW)
+        for block in range(2):
+            rows = slice(block * size, (block + 1) * size)
+            query = query_ref[rows, pair * 128 : (pair + 1) * 128] * LOW(0.125)
             outs = []
             for head in range(2):
-                s = jnp.where(allowed, nt(half_lanes(keys, head), query), NEVER)
+                s = nt(half_lanes(keys, head), query)
+                s = jnp.where(allowed[block][pair // 2], s, NEVER)
                 top = jnp.max(s, axis=0, keepdims=True)
                 probs = jnp.exp(s - top)
                 total = jnp.sum(probs, axis=0, keepdims=True)
                 result = mm(values_t[head * 64 : (head + 1) * 64], probs.astype(LOW))
                 outs.append(result / total)
-                lse_ref[2 * pair + head : 2 * pair + head + 1, i * size : (i + 1) * size] = (
-                    top + jnp.log(total)
-                )
-            start = pl.multiple_of(mine * size, size)
-            out_ref[pl.ds(start, size), pair * 128 : (pair + 1) * 128] = (
+                lse_ref[2 * pair + head : 2 * pair + head + 1, rows] = top + jnp.log(total)
+            out_ref[rows, pair * 128 : (pair + 1) * 128] = (
                 jnp.concatenate(outs, axis=0).T.astype(LOW)
             )
 
 
-def cross_backward(here_ref, marks_ref, query_ref, pairs_ref, grad_ref, lse_ref, dq_ref, dkv_ref):
+def cross_backward(
+    here_ref, marks_ref, query_ref, own_ref, other_ref, grad_ref, lse_ref, dq_ref, down_ref, dother_ref
+):
     here = here_ref[0]
-    size = query_ref.shape[0] // WAYS
-    place = token_places(here, pairs_ref.shape[0], size)
-    for pair in range(2):
-        keys = pairs_ref[:, pair * 128 : (pair + 1) * 128]
-        values = pairs_ref[:, 256 + pair * 128 : 256 + (pair + 1) * 128]
+    size = query_ref.shape[0] // 2
+    allowed = [text_allowed(here, marks_ref, b, size, own_ref.shape[0]) for b in range(2)]
+    for pair in range(4):
+        ref, out = ((own_ref, down_ref), (other_ref, dother_ref))[pair // 2]
+        column = (pair % 2) * 128
+        keys = ref[:, column : column + 128]
+        values = ref[:, 256 + column : 384 + column]
         keys_t = transposed(keys).astype(LOW)
         sum_k = jnp.zeros(keys.shape, WIDE)
         sum_v = jnp.zeros(keys.shape, WIDE)
-        for i in range(WAYS):
-            mine = slot_of(i, here)
-            query = rows_at(query_ref, mine, size, pair, 0) * LOW(0.125)
-            grad = rows_at(grad_ref, mine, size, pair, 0)
-            low = marks_ref[1:2, i * size : (i + 1) * size]
-            high = marks_ref[2:3, i * size : (i + 1) * size]
-            allowed = (place >= low) & (place < high)
+        for block in range(2):
+            rows = slice(block * size, (block + 1) * size)
+            query = query_ref[rows, pair * 128 : (pair + 1) * 128] * LOW(0.125)
+            grad = grad_ref[rows, pair * 128 : (pair + 1) * 128]
             grads_q = []
             for head in range(2):
-                mass = lse_ref[2 * pair + head : 2 * pair + head + 1, i * size : (i + 1) * size]
-                s = jnp.where(allowed, nt(half_lanes(keys, head), query), NEVER)
-                p = jnp.exp(s - mass)
+                mass = lse_ref[2 * pair + head : 2 * pair + head + 1, rows]
+                s = nt(half_lanes(keys, head), query)
+                p = jnp.exp(jnp.where(allowed[block][pair // 2], s, NEVER) - mass)
                 dp = nt(half_lanes(values, head), grad)
                 delta = jnp.sum(p * dp, axis=0, keepdims=True)
                 ds = (p * (dp - delta)).astype(LOW)
                 sum_v = sum_v + mm(p.astype(LOW), half_lanes(grad, head))
                 sum_k = sum_k + mm(ds, half_lanes(query, head))
                 grads_q.append(mm(keys_t[head * 64 : (head + 1) * 64], ds))
-            start = pl.multiple_of(mine * size, size)
-            dq_ref[pl.ds(start, size), pair * 128 : (pair + 1) * 128] = (
+            dq_ref[rows, pair * 128 : (pair + 1) * 128] = (
                 (jnp.concatenate(grads_q, axis=0) * 0.125).T.astype(LOW)
             )
-        dkv_ref[:, pair * 128 : (pair + 1) * 128] = sum_k.astype(LOW)
-        dkv_ref[:, 256 + pair * 128 : 256 + (pair + 1) * 128] = sum_v.astype(LOW)
-
-
-def call(body, outs, operands, scratch=(), flops=0, exps=0):
-    specs = [pl.BlockSpec(memory_space=pltpu.SMEM)] + [
-        pl.BlockSpec(memory_space=pltpu.VMEM) for _ in operands[1:]
+        out[:, column : column + 128] = sum_k.astype(LOW)
+        out[:, 256 + column : 384 + column] = sum_v.astype(LOW)
+
+
+def bring_in(body, number, ids_ref, *refs):
+    scratch, sem = refs[len(refs) - number - 1 : -1], refs[-1]
+    copies = [
+        pltpu.make_async_copy(refs[i], scratch[i], sem.at[i]) for i in range(number)
     ]
-    moved = sum(v.size * v.dtype.itemsize for v in operands)
-    moved += sum(o.size * o.dtype.itemsize for o in outs)
+    for copy in copies:
+        copy.start()
+    for copy in copies:
+        copy.wait()
+    body(ids_ref, *scratch, *refs[number : len(refs) - number - 1])
+
+
+def call(body, outs, operands, scratch=(), resident=False, own_copies=0):
+    vmem = pl.BlockSpec(memory_space=pltpu.VMEM)
+    spec = vmem if resident else pl.BlockSpec(memory_space=pl.ANY)
+    scratch = list(scratch)
+    if own_copies:
+        scratch.append(pltpu.SemaphoreType.DMA((own_copies,)))
+    elif not resident:
+        scratch = [pltpu.VMEM(v.shape, v.dtype) for v in operands[1:]]
+        scratch.append(pltpu.SemaphoreType.DMA((len(scratch),)))
+        body = functools.partial(bring_in, body, len(operands) - 1)
+    moved = sum(v.size * v.dtype.itemsize for v in (*operands, *outs))
     return pl.pallas_call(
         body,
         out_shape=outs,
-        in_specs=specs,
-        out_specs=[pl.BlockSpec(memory_space=pltpu.VMEM) for _ in outs],
-        scratch_shapes=list(scratch),
-        cost_estimate=pl.CostEstimate(flops=flops, bytes_accessed=moved, transcendentals=exps),
+        in_specs=[pl.BlockSpec(memory_space=pltpu.SMEM)] + [spec for v in operands[1:]],
+        out_specs=[vmem for v in outs],
+        scratch_shapes=scratch,
+        cost_estimate=pl.CostEstimate(flops=0, bytes_accessed=moved, transcendentals=0),
         compiler_params=pltpu.CompilerParams(vmem_limit_bytes=48 << 20),
     )(*operands)
+
+
+def weight_block(row_ref, left, right, last_ref, first_ref, kept_ref):
+    step = pl.program_id(0)
+    value = mm(left[...], right[...], 0, 0).astype(LOW)
+
+    @pl.when(step < 2)
+    def _():
+        last_ref[0] = value
+
+    @pl.when((step >= 2) & (step < 4))
+    def _():
+        first_ref[0] = value
+
+    @pl.when(step >= 4)
+    def _():
+        kept_ref[0] = value
+
+
+def weight_grad(row, left, right):
+    count, rows = left.shape
+    columns = right.shape[1]
+    tile = rows // 8
+
+    def owner(step, row_ref):
+        k = jnp.where(step < 4, step ^ 2, step - 4)
+        away = jnp.where(step < 4, 1, 0)
+        return row_ref[0] ^ (2 * k) ^ away
+
+    def parked(first, number):
+        return pl.BlockSpec(
+            (1, tile, columns), lambda s, r: (jnp.clip(s - first, 0, number - 1), 0, 0)
+        )
+
+    return pl.pallas_call(
+        weight_block,
+        grid_spec=pltpu.PrefetchScalarGridSpec(
+            num_scalar_prefetch=1,
+            grid=(8,),
+            in_specs=[
+                pl.BlockSpec((count, tile), lambda s, r: (0, owner(s, r))),
+                pl.BlockSpec((count, columns), lambda s, r: (0, 0)),
+            ],
+            out_specs=[parked(0, 2), parked(2, 2), parked(4, 4)],
+        ),
+        out_shape=[shaped((n, tile, columns), LOW) for n in (2, 2, 4)],
+        cost_estimate=pl.CostEstimate(
+            flops=2 * count * rows * columns,
+            bytes_accessed=2 * count * (rows + columns) + 2 * rows * columns,
+            transcendentals=0,
+        ),
+        compiler_params=pltpu.CompilerParams(vmem_limit_bytes=48 << 20),
+    )(row.astype(jnp.int32).reshape(1), left, right)
 
 
 def shaped(shape, dtype):
@@ -304,8 +432,23 @@
     )
 
 
-def exchange(dealt):
-    return lax.all_to_all(dealt, "text", 0, 0, tiled=True)
+def pick(values, index, axis):
+    return lax.dynamic_index_in_dim(values, index, axis, keepdims=False)
+
+
+def ordered(mine, other, bit, axis=0):
+    return jnp.stack([jnp.where(bit == 0, mine, other), jnp.where(bit == 0, other, mine)], axis)
+
+
+def exchange(dealt, here, *gates):
+    core, far = here & 1, here >> 1
+    tail = dealt.shape[1:]
+    dealt = dealt.reshape((2, 2) + tail)
+    stage = ordered(pick(dealt, core, 1), swap(pick(dealt, 1 - core, 1), 1), core, 1)
+    sent = pick(stage, 1 - far, 0)
+    if gates:
+        sent = after(sent, *gates)
+    return ordered(pick(stage, far, 0), swap(sent, 2), far).reshape((WAYS,) + tail)
 
 
 def side_by_side(parts):
@@ -317,19 +460,394 @@
     return jnp.moveaxis(columns.reshape(depth, WAYS, width // WAYS), 1, 0)
 
 
+def row_swap(values, mask):
+    size = lax.axis_size("rows")
+    return lax.ppermute(values, "rows", [(i, i ^ mask) for i in range(size)])
+
+
 def gather_rows(block):
     return lax.all_gather(block, "rows", axis=0, tiled=True)
 
 
 def sum_rows(whole):
     return lax.psum_scatter(whole, "rows", scatter_dimension=0, tiled=True)
+
+
+def place_pieces(depth, splits, ids_ref, *refs):
+    row, outs, sem = ids_ref[1], refs[7:-1], refs[-1]
+    pairs = []
+    for k in range(4):
+        for flip in range(2):
+            owner = (row ^ flip) ^ (2 * k)
+            start = pl.multiple_of(owner * depth, depth)
+            column = 0
+            for index, width in enumerate(splits):
+                columns = slice(column, column + width)
+                if not flip:
+                    piece = refs[k].at[:, columns]
+                elif k < 2:
+                    piece = refs[4 + k].at[:, columns]
+                else:
+                    piece = refs[6].at[k - 2, :, columns]
+                pairs.append((piece, outs[index].at[pl.ds(start, depth)]))
+                column += width
+    copy_all(pairs, sem)
+
+
+def place(ids, splits, pieces, others):
+    depth = pieces[0].shape[0]
+    return call(
+        functools.partial(place_pieces, depth, splits),
+        [shaped((8 * depth, width), LOW) for width in splits],
+        (ids, *pieces, *others),
+        own_copies=8 * len(splits),
+    )
+
+
+def place_line_pieces(ids_ref, *refs):
+    far = ids_ref[1] >> 1
+    height = refs[0].shape[0]
+    pairs = []
+    for k in range(4):
+        start = pl.multiple_of((far ^ k) * height, height)
+        pairs.append((refs[k], refs[4].at[pl.ds(start, height)]))
+    copy_all(pairs, refs[5])
+
+
+def place_line(ids, *pieces):
+    whole = shaped((4 * pieces[0].shape[0], pieces[0].shape[1]), LOW)
+    return call(place_line_pieces, [whole], (ids, *pieces), own_copies=4)[0]
+
+
+def three_ways(block):
+    return [row_swap(block, 2 * k) for k in range(1, 4)]
+
+
+def split_sums(row_ref, whole_ref, sent_ref, own_ref, *low_refs):
+    row = row_ref[1]
+    x, far = row & 1, row >> 1
+    depth = own_ref.shape[0]
+    for k in range(4):
+        owner = far ^ k
+        start = pl.multiple_of((owner * 2 + x) * depth, depth)
+        value = whole_ref[pl.ds(start, depth)].astype(WIDE) + sent_ref[owner].astype(WIDE)
+        if k == 0:
+            own_ref[...] = value
+        else:
+            low_refs[k - 1][...] = value.astype(LOW)
+
+
+def choose(bit, zero, one):
+    return jnp.where(bit == 0, zero, one)
+
+
+def put(ref, column, *values):
+    for value in values:
+        ref[:, column : column + value.shape[1]] = value.astype(ref.dtype)
+        column += value.shape[1]
+
+
+def total(refs):
+    value = refs[0][...]
+    for ref in refs[1:]:
+        value = value + ref[...].astype(WIDE)
+    return value
+
+
+def device_bits(ids_ref):
+    here, row = ids_ref[0], ids_ref[1]
+    return here & 1, here >> 1, row & 1, row >> 1
+
+
+def keep_and_send(kept, sent, column, bit, zero, one):
+    put(kept, column, choose(bit, zero, one))
+    put(sent, column, choose(bit, one, zero))
+    return column + zero.shape[1]
+
+
+def deal_first_core(ids, self_in, self_out, cross_out, kept, sent):
+    core, _, _, _ = device_bits(ids)
+    column = 0
+    for y in range(2):
+        for j in range(3):
+            first = (4 * j + 2 * y) * 64
+            zero, one = self_in[:, first : first + 64], self_in[:, first + 64 : first + 128]
+            column = keep_and_send(kept, sent, column, core, zero, one)
+    for index, ref in enumerate((self_out, cross_out)):
+        rows = slice(64 * index, 64 * (index + 1))
+        kept[rows, column:] = choose(core, ref[:64], ref[64:])
+        sent[rows, column:] = choose(core, ref[64:], ref[:64])
+
+
+def deal_first_far(ids, kept, came, far_kept, far_sent):
+    core, y, _, _ = device_bits(ids)
+    column = 0
+    sources = [choose(core, kept[...], came[...]), choose(core, came[...], kept[...])]
+    for source in sources:
+        column = keep_and_send(far_kept, far_sent, column, y, source[:, :192], source[:, 192:384])
+    for source in sources:
+        put(far_kept, column, source[:, 384:])
+        put(far_sent, column, source[:, 384:])
+        column += 256
+
+
+def deal_first_last(ids, kept, came, mixed, lines):
+    _, y, _, _ = device_bits(ids)
+    zero, one = choose(y, kept[...], came[...]), choose(y, came[...], kept[...])
+    put(mixed, 0, zero[:, :384], one[:, :384])
+    put(lines, 0, zero[:, 384:], one[:, 384:])
+
+
+def deal_rest_core(ids, query, pairs, up, down, kept, sent):
+    core, _, _, _ = device_bits(ids)
+    column = 0
+    for y in range(2):
+        for r in range(2):
+            first = (4 * r + 2 * y) * 128
+            zero, one = up[:, first : first + 128], up[:, first + 128 : first + 256]
+            column = keep_and_send(kept, sent, column, core, zero, one)
+    for y in range(2):
+        zero, one = [down[(2 * y + c) * 128 : (2 * y + c + 1) * 128] for c in range(2)]
+        column = keep_and_send(kept, sent, column, core, zero, one)
+    for y in range(2):
+        for j in range(2):
+            first = (4 * j + 2 * y) * 64
+            zero, one = pairs[:, first : first + 64], pairs[:, first + 64 : first + 128]
+            column = keep_and_send(kept, sent, column, core, zero, one)
+    for y in range(2):
+        zero, one = query[:, 128 * y : 128 * y + 64], query[:, 128 * y + 64 : 128 * y + 128]
+        column = keep_and_send(kept, sent, column, core, zero, one)
+
+
+def deal_rest_far(ids, kept, came, far_kept, far_sent):
+    core, y, _, _ = device_bits(ids)
+    sources = [choose(core, kept[...], came[...]), choose(core, came[...], kept[...])]
+    column = 0
+    for first, width in ((0, 256), (512, 256), (1024, 128)):
+        for source in sources:
+            zero = source[:, first : first + width]
+            one = source[:, first + width : first + 2 * width]
+            column = keep_and_send(far_kept, far_sent, column, y, zero, one)
+    for source in sources:
+        put(far_kept, column, source[:, 1280:])
+        put(far_sent, column, source[:, 1280:])
+        column += 128
+
+
+def deal_rest_last(ids, kept, came, attend, up, down):
+    _, y, _, _ = device_bits(ids)
+    sources = [choose(y, kept[...], came[...]), choose(y, came[...], kept[...])]
+    put(up, 0, *[s[:, :512] for s in sources])
+    put(down, 0, *[s[:, 512:1024] for s in sources])
+    put(attend, 512, *[s[:, 1024:1280] for s in sources])
+    for group in range(2):
+        for place, source in enumerate(sources):
+            for c in range(2):
+                first = 1280 + c * 128
+                zero = source[:, first + group * 64 : first + group * 64 + 64]
+                one = source[:, first + (1 - group) * 64 : first + (1 - group) * 64 + 64]
+                put(attend, group * 256 + (2 * place + c) * 64, choose(y, zero, one))
+
+
+def ffn_far(ids, *refs):
+    _, y, _, _ = device_bits(ids)
+    kept, sent = refs[8:]
+    for half in range(2):
+        value = total(refs[4 * half : 4 * half + 4])
+        put(kept, half * 512, choose(y, value[:, :512], value[:, 512:]))
+        put(sent, half * 512, choose(y, value[:, 512:], value[:, :512]))
+
+
+def ffn_core(ids, kept, came, core_kept, core_sent):
+    core, y, _, _ = device_bits(ids)
+    mine, other = kept[...], came[...].astype(WIDE)
+    column = 0
+    for source in (choose(y, mine, other), choose(y, other, mine)):
+        for half in range(2):
+            zero = source[:, half * 512 : half * 512 + 256]
+            one = source[:, half * 512 + 256 : half * 512 + 512]
+            put(core_kept, column, choose(core, zero, one))
+            put(core_sent, column, choose(core, one, zero))
+            column += 256
+
+
+def ffn_last(ids, kept, came, up, down):
+    core, _, _, _ = device_bits(ids)
+    mine, other = kept[...], came[...].astype(WIDE)
+    for c, source in enumerate((choose(core, mine, other), choose(core, other, mine))):
+        for y in range(2):
+            sender = 2 * y + c
+            for r in range(2):
+                first = 512 * y + 128 * r
+                put(up, (4 * r + sender) * 128, source[:, first : first + 128])
+            down[sender * 128 : (sender + 1) * 128] = source[:, 512 * y + 256 : 512 * y + 512]
+
+
+def mixed_far(ids, own, a, b, c, kept, sent):
+    _, y, _, _ = device_bits(ids)
+    value = total((own, a, b, c))
+    put(kept, 0, choose(y, value[:, :384], value[:, 384:]))
+    put(sent, 0, choose(y, value[:, 384:], value[:, :384]))
+
+
+def mixed_core(ids, kept, came, core_kept, core_sent):
+    core, y, _, _ = device_bits(ids)
+    mine, other = kept[...], came[...].astype(WIDE)
+    for index, source in enumerate((choose(y, mine, other), choose(y, other, mine))):
+        put(core_kept, 192 * index, choose(core, source[:, :192], source[:, 192:]))
+        put(core_sent, 192 * index, choose(core, source[:, 192:], source[:, :192]))
+
+
+def mixed_last(ids, kept, came, mixed):
+    core, _, _, _ = device_bits(ids)
+    mine, other = kept[...], came[...].astype(WIDE)
+    for c, source in enumerate((choose(core, mine, other), choose(core, other, mine))):
+        for y in range(2):
+            for j in range(3):
+                first = 192 * y + 64 * j
+                put(mixed, (4 * j + 2 * y + c) * 64, source[:, first : first + 64])
+
+
+def attend_x(ids, query, pairs, cross, sent):
+    _, y, x, _ = device_bits(ids)
+    for z in range(4):
+        start = pl.multiple_of((2 * z + 1 - x) * 128, 128)
+        line = pl.multiple_of(((y ^ x ^ 1) * 4 + z) * 64, 64)
+        sent[z, :128, :512] = query[pl.ds(start, 128)]
+        sent[z, :128, 512:] = pairs[pl.ds(start, 128)]
+        sent[z, 128:] = cross[pl.ds(line, 64)]
+
+
+def attend_z(ids, query, pairs, cross, self_out, came, own, a, b, c):
+    _, y, x, z = device_bits(ids)
+    for k, ref in enumerate((own, a, b, c)):
+        owner = z ^ k
+        start = pl.multiple_of((2 * owner + x) * 128, 128)
+        line = pl.multiple_of(((y ^ x) * 4 + owner) * 64, 64)
+        below = pl.multiple_of(owner * 64, 64)
+        moved = came[owner].astype(WIDE)
+        value = query[pl.ds(start, 128)].astype(WIDE) + moved[:128, :512]
+        ref[:128, :512] = value.astype(ref.dtype)
+        value = pairs[pl.ds(start, 128)].astype(WIDE) + moved[:128, 512:]
+        ref[:128, 512:] = value.astype(ref.dtype)
+        value = cross[pl.ds(line, 64)].astype(WIDE) + moved[128:]
+        ref[128:192] = value.astype(ref.dtype)
+        ref[192:] = self_out[pl.ds(below, 64)].astype(ref.dtype)
+
+
+def attend_total(ids, own, a, b, c, value, line):
+    value[...] = total((own, a, b, c))
+    line[...] = value[192:].astype(LOW)
+
+
+def attend_far(ids, value, line, kept, sent):
+    _, y, _, _ = device_bits(ids)
+    lines = jnp.concatenate([value[192:] + line[...].astype(WIDE), value[128:192]], axis=0)
+    put(kept, 0, choose(y, lines[:, :512], lines[:, 512:]))
+    put(sent, 0, choose(y, lines[:, 512:], lines[:, :512]))
+    mine, other = value[:128, :256], value[:128, 256:512]
+    for index, group in enumerate((choose(y, mine, other), choose(y, other, mine))):
+        put(kept, 512 + 128 * index, choose(y, group[:, :128], group[:, 128:]))
+        put(sent, 512 + 128 * index, choose(y, group[:, 128:], group[:, :128]))
+    pairs = value[:128, 512:]
+    put(kept, 768, choose(y, pairs[:, :256], pairs[:, 256:]))
+    put(sent, 768, choose(y, pairs[:, 256:], pairs[:, :256]))
+
+
+def attend_core(ids, kept, came, core_kept, core_sent):
+    core, y, x, _ = device_bits(ids)
+    mine, other = kept[...], came[...].astype(WIDE)
+    owner = jnp.where(x == y, mine[:64, :512], other[:64, :512])
+    lines = jnp.concatenate([owner, mine[64:, :512] + other[64:, :512]], axis=0)
+    put(core_kept, 0, choose(core, lines[:, :256], lines[:, 256:]))
+    put(core_sent, 0, choose(core, lines[:, 256:], lines[:, :256]))
+    query = mine[:, 512:768] + other[:, 512:768]
+    for group in range(2):
+        zero, one = [query[:, 128 * group + 64 * c : 128 * group + 64 * c + 64] for c in range(2)]
+        put(core_kept, 256 + 64 * group, choose(core, zero, one))
+        put(core_sent, 256 + 64 * group, choose(core, one, zero))
+    mine, other = mine[:, 768:], other[:, 768:]
+    for index, source in enumerate((choose(y, mine, other), choose(y, other, mine))):
+        put(core_kept, 384 + 128 * index, choose(core, source[:, :128], source[:, 128:]))
+        put(core_sent, 384 + 128 * index, choose(core, source[:, 128:], source[:, :128]))
+
+
+def attend_last(ids, kept, came, self_out, query, pairs, cross):
+    core, _, _, _ = device_bits(ids)
+    mine, other = kept[...], came[...].astype(WIDE)
+    for c, source in enumerate((choose(core, mine, other), choose(core, other, mine))):
+        self_out[64 * c : 64 * c + 64] = source[:64, :256]
+        cross[64 * c : 64 * c + 64] = source[64:, :256]
+        for y in range(2):
+            put(query, 64 * (2 * y + c), source[:, 256 + 64 * y : 320 + 64 * y])
+            for j in range(2):
+                first = 384 + 128 * y + 64 * j
+                put(pairs, 64 * (4 * j + 2 * y + c), source[:, first : first + 64])
+
+
+def along_z(values):
+    return [row_swap(v, 2 * (k + 1)) for k, v in enumerate(values)]
+
+
+def add_parts(first, ids, kept, came, *outs):
+    for index, out in enumerate(outs):
+        value = kept[first + index].astype(WIDE) + came[index].astype(WIDE)
+        out[...] = value.astype(out.dtype)
+
+
+def return_ffn(ids, up, down):
+    low = lambda *shape: shaped(shape, LOW)
+    wide = lambda *shape: shaped(shape, WIDE)
+    kept, sent = call(ffn_far, [wide(128, 1024), low(128, 1024)], (ids, *up, *down))
+    kept, sent = call(ffn_core, [wide(128, 1024), low(128, 1024)], (ids, kept, swap(sent, 2)))
+    return call(ffn_last, [wide(128, 1024), wide(512, 256)], (ids, kept, swap(sent, 1)))
+
+
+def send_last(ids, kept, came):
+    second, third = call(
+        lambda *refs: add_parts(2, *refs), [shaped((128, 1024), LOW)] * 2, (ids, kept, came)
+    )
+    return row_swap(second, 4), row_swap(third, 6)
+
+
+def send_first(ids, kept, came):
+    own, part = call(
+        lambda *refs: add_parts(0, *refs),
+        [shaped((128, 1024), WIDE), shaped((128, 1024), LOW)],
+        (ids, kept, came),
+    )
+    return own, row_swap(part, 2)
+
+
+def return_mixed(ids, own, parts):
+    low = lambda *shape: shaped(shape, LOW)
+    wide = lambda *shape: shaped(shape, WIDE)
+    kept, sent = call(mixed_far, [wide(128, 384), low(128, 384)], (ids, own, *parts))
+    kept, sent = call(mixed_core, [wide(128, 384), low(128, 384)], (ids, kept, swap(sent, 2)))
+    (mixed,) = call(mixed_last, [wide(128, 768)], (ids, kept, swap(sent, 1)))
+    return mixed
+
+
+def return_attend(ids, own, parts):
+    low = lambda *shape: shaped(shape, LOW)
+    wide = lambda *shape: shaped(shape, WIDE)
+    value, line = call(attend_total, [wide(256, 1024), low(64, 1024)], (ids, own, *parts))
+    kept, sent = call(
+        attend_far, [wide(128, 1024), low(128, 1024)], (ids, value, row_swap(line, 1))
+    )
+    kept, sent = call(attend_core, [wide(128, 640), low(128, 640)], (ids, kept, swap(sent, 2)))
+    return call(
+        attend_last,
+        [wide(128, 256), wide(128, 256), wide(128, 512), wide(128, 256)],
+        (ids, kept, swap(sent, 1)),
+    )
 
 
 def own_heads(matrix, here):
     rows = gather_rows(lax.all_gather(matrix, "text", axis=1, tiled=True))
     width = rows.shape[1]
     grouped = rows.reshape(HEADS // WAYS, WAYS, -1, width)
-    return lax.dynamic_index_in_dim(grouped, here, 1, keepdims=False).reshape(-1, width)
+    return pick(grouped, here, 1).reshape(-1, width)
 
 
 def return_heads(grad, here):
@@ -344,7 +862,257 @@
     return sum_rows(columns)
 
 
-def local(
+def mask_marks(segments, lengths):
+    clip = jnp.arange(lengths.shape[0], dtype=jnp.int32)
+    ends = jnp.sum(jnp.where(clip[None, :] <= clip[:, None], lengths[None, :], 0), axis=1)
+    begins = jnp.sum((segments[None, :] < clip[:, None]).astype(jnp.int32), axis=1)
+    same = (segments[None, :] == clip[:, None]).astype(jnp.int32)
+    rows = [begins, ends - lengths, ends] + [jnp.zeros_like(ends)] * 5
+    return jnp.stack([jnp.sum(same * values[:, None], axis=0) for values in rows])
+
+
+def gelu_parts(up):
+    phi = 0.5 * (1.0 + lax.erf(up * math.sqrt(0.5)))
+    slope = phi + up * (jnp.exp(-0.5 * up * up) * (1.0 / math.sqrt(2.0 * math.pi)))
+    return lax.optimization_barrier(((up * phi).astype(LOW), slope))
+
+
+def reduce_norms(sums, here):
+    split = sums.reshape(6, 2, 2, -1)
+    split = pick(split, here & 1, 2) + swap(pick(split, 1 - (here & 1), 2), 1)
+    sums = pick(split, here >> 1, 1) + swap(pick(split, 1 - (here >> 1), 1), 2)
+    mask = 1
+    while mask < lax.axis_size("rows"):
+        sums = sums + row_swap(sums, mask)
+        mask = 2 * mask
+    return sums
+
+
+def local_grid(
+    frames,
+    text_states,
+    frame_segments,
+    text_lengths,
+    self_in,
+    self_out,
+    cross_query,
+    cross_kv,
+    cross_out,
+    ffn_in,
+    ffn_out,
+    norm_gains,
+    norm_biases,
+    out_grad,
+):
+    here, row = lax.axis_index("text"), lax.axis_index("rows")
+    ids = jnp.stack([here, row]).astype(jnp.int32)
+    width = frames.shape[2]
+    count = frames.shape[1] * WAYS
+    inner = width // WAYS
+    low = lambda *shape: shaped(shape, LOW)
+    wide = lambda *shape: shaped(shape, WIDE)
+    frames_wide = frames[0].astype(WIDE)
+    marks = mask_marks(frame_segments[0], text_lengths[0])
+
+    kept, sent = call(deal_first_core, [low(128, 640)] * 2, (ids, self_in, self_out, cross_out))
+    norms = jnp.concatenate([norm_gains, norm_biases], axis=0)
+    norms_far = swap(norms, 2)
+    kept, sent = call(deal_first_far, [low(128, 896)] * 2, (ids, kept, swap(sent, 1)))
+    norms = ordered(norms, norms_far, here >> 1)
+    norms = ordered(norms, swap(norms, 1), here & 1, 1)
+    norms = jnp.moveaxis(norms, 2, 0).reshape(6, width).astype(WIDE)
+    gains, biases = norms[:3], norms[3:]
+    one, hat_one, inverse_one = norm_forward(frames_wide, gains[0], biases[0])
+    came = swap(sent, 2)
+    rest = sync(cross_query, cross_kv, ffn_in, ffn_out, sent)[:4]
+    rest_kept, rest_sent = call(deal_rest_core, [low(128, 1408)] * 2, (ids, *rest))
+    rest_kept, rest_sent = call(
+        deal_rest_far, [low(128, 1536)] * 2, (ids, rest_kept, swap(rest_sent, 1))
+    )
+    mixed, lines = call(deal_first_last, [low(128, 768), low(128, 1024)], (ids, kept, came))
+    mixed, lines, rest_sent, one = sync(mixed, lines, rest_sent, one)
+    mixed_z = three_ways(mixed)
+    mixed_x = row_swap(mixed, 1)
+    lines_x = row_swap(lines, 1)
+    rest_came = swap(rest_sent, 2)
+    one_far, one_near = swap(one, 2), swap(one, 1)
+    attend, up_block, down_block = call(
+        deal_rest_last, [low(128, 1024)] * 3, (ids, rest_kept, rest_came)
+    )
+    lines = jnp.where((row & 1) == (here >> 1), lines, lines_x)
+    *mixed_z, mixed_x, attend, lines, text, grad = sync(
+        *mixed_z, mixed_x, attend, lines, text_states[0], out_grad[0]
+    )
+    mixed_x1 = row_swap(mixed_z[0], 1)
+    mixed_x2 = row_swap(jnp.stack(mixed_z[1:]), 1)
+    self_line, cross_line = lines[:64], lines[64:]
+    self_z = three_ways(sync(self_line, mixed_x1)[0])
+    attend_z1 = row_swap(sync(attend, mixed_x1)[0], 2)
+    one_all = join(ids, one, one_far, one_near, swap(one_far, 1))
+    text_far, text_near = swap(text, 2), swap(text, 1)
+    mixed_x1, mixed_x2, one_all, text_far, attend_z1, *self_z = sync(
+        mixed_x1, mixed_x2, one_all, text_far, attend_z1, *self_z
+    )
+    (w_mixed,) = place(ids, (768,), [mixed, *mixed_z], [mixed_x, mixed_x1, mixed_x2])
+    attend, grad, cross_line = sync(attend, grad, cross_line, mixed_x2)[:3]
+    attend_z2, attend_z3 = row_swap(attend, 4), row_swap(attend, 6)
+    attend_x0, attend_x1 = row_swap(attend, 1), row_swap(attend_z1, 1)
+    grad_far, grad_near = swap(grad, 2), swap(grad, 1)
+    mixed_low = mm(one_all, w_mixed).astype(LOW)
+    w_self = place_line(ids, self_line, *self_z)
+    text_all = join(ids, text, text_far, text_near, swap(text_far, 1))
+    self_att, self_lse = call(
+        self_forward, [low(count, inner), wide(4, count)], (ids, marks, mixed_low), resident=True
+    )
+    self_att, w_self, text_all, attend_x1, grad_far, attend_z2, attend_z3, cross_line = sync(
+        self_att, w_self, text_all, attend_x1, grad_far, attend_z2, attend_z3, cross_line
+    )
+    attend_x2 = row_swap(jnp.stack([attend_z2, attend_z3]), 1)
+    cross_z = three_ways(cross_line)
+    received, attend_x2, *cross_z = scatter_slots(self_att, w_self, 0, None, (attend_x2, *cross_z))
+    hidden = frames_wide + received
+    w_query, w_pairs = place(
+        ids,
+        (512, 512),
+        [attend, attend_z1, attend_z2, attend_z3],
+        [attend_x0, attend_x1, attend_x2],
+    )
+    grad_all = join(ids, grad, grad_far, grad_near, swap(grad_far, 1))
+    (up_block,) = sync(up_block, attend_x2)[:1]
+    up_z = three_ways(up_block)
+    up_x = row_swap(up_block, 1)
+    two, hat_two, inverse_two = norm_forward(hidden, gains[1], biases[1])
+    two_pair = gather_pair(two, ids)
+    pair_count = two_pair.shape[0]
+    text_count = text_all.shape[0]
+    pairs_own = mm(text_all, w_pairs).astype(LOW)
+    pairs_other = swap(pairs_own, 2)
+    w_cross = place_line(ids, cross_line, *cross_z)
+    w_cross_far = swap(sync(w_cross, pairs_own)[0], 2)
+    query = mm(two_pair, w_query).astype(LOW)
+    cross_att, cross_lse = call(
+        cross_forward,
+        [low(pair_count, 2 * inner), wide(8, pair_count)],
+        (ids, marks, query, pairs_own, pairs_other),
+        resident=True,
+    )
+    cross_att, *up_z = sync(cross_att, *up_z)
+    (down_block,) = sync(down_block, up_z[2])[:1]
+    up_x1 = row_swap(up_z[0], 1)
+    up_x2 = row_swap(jnp.stack(up_z[1:]), 1)
+    down_z = three_ways(down_block)
+    down_x = row_swap(down_block, 1)
+    w_cross_both = join(ids, w_cross, w_cross_far)
+    hidden_two = hidden + scatter_pair(cross_att, w_cross_both, 0)
+    three, hat_three, inverse_three = norm_forward(hidden_two, gains[2], biases[2])
+    three_all, up_x1, up_x2 = gather_slots(three, ids, up_x1, up_x2)
+    (w_up,) = place(ids, (1024,), [up_block, *up_z], [up_x, up_x1, up_x2])
+    three_all, *down_z = sync(three_all, *down_z)
+    down_x1 = row_swap(down_z[0], 1)
+    down_x2 = row_swap(jnp.stack(down_z[1:]), 1)
+    activ, slope = gelu_parts(mm(three_all, w_up))
+    (w_down,) = place(ids, (1024,), [down_block, *down_z], [down_x, down_x1, down_x2])
+
+    last_down, first_down, kept_down = weight_grad(row, activ, grad_all)
+    last_down = row_swap(last_down, 1)
+    first_down = row_swap(first_down, 1)
+    grad_up = (mm(grad_all, w_down, 1, 1) * slope).astype(LOW)
+    last_up, first_up, kept_up = weight_grad(row, three_all, grad_up)
+    grad_three, last_down, last_up, first_up = scatter_slots(
+        grad_up, w_up, 1, None, (last_down, last_up, first_up)
+    )
+    last_up = row_swap(last_up, 1)
+    down_two, down_three = send_last(ids, kept_down, last_down)
+    output = (hidden_two + scatter_slots(activ, w_down, 0, grad_three)).astype(LOW)
+    part, gain_three, bias_three = norm_backward(grad_three, hat_three, inverse_three, gains[2])
+    grad_two = out_grad[0].astype(WIDE) + part
+    branch_two = gather_pair(grad_two.astype(LOW), ids)
+    grad_cross = mm(branch_two, w_cross_both, 1, 1).astype(LOW)
+    grad_cross, first_down, first_up, down_two, down_three = sync(
+        grad_cross, first_down, first_up, down_two, down_three
+    )
+    first_up = row_swap(first_up, 1)
+    down_own, down_one = send_first(ids, kept_down, first_down)
+    grad_query, pairs_mine, pairs_away = call(
+        cross_backward,
+        [low(pair_count, 2 * inner)] + [low(text_count, 2 * inner)] * 2,
+        (ids, marks, query, pairs_own, pairs_other, grad_cross, cross_lse),
+        resident=True,
+    )
+    grad_query, pairs_away, last_up = sync(grad_query, pairs_away, last_up)
+    pairs_came = swap(pairs_away, 2)
+    up_two, up_three = send_last(ids, kept_up, last_up)
+    g_cross = mm(cross_att, branch_two, 0, 0).astype(LOW)
+    g_query = mm(two_pair, grad_query, 0, 0).astype(LOW)
+    part, gain_two, bias_two = norm_backward(
+        scatter_pair(grad_query, w_query, 1), hat_two, inverse_two, gains[1]
+    )
+    grad_hidden = grad_two + part
+    grad_low, pairs_came, g_cross, g_query = sync(
+        grad_hidden.astype(LOW), pairs_came, g_cross, g_query
+    )
+    grad_pairs = (pairs_mine.astype(WIDE) + pairs_came.astype(WIDE)).astype(LOW)
+    g_pairs = mm(text_all, grad_pairs, 0, 0).astype(LOW)
+    (attend_sent,) = call(attend_x, [low(4, 192, 1024)], (ids, g_query, g_pairs, g_cross))
+    attend_came = row_swap(attend_sent, 1)
+    branch, first_up, up_two, up_three, down_one = gather_slots(
+        grad_low, ids, first_up, up_two, up_three, down_one
+    )
+    up_own, up_one = send_first(ids, kept_up, first_up)
+    text_grad = scatter_slots(grad_pairs, w_pairs, 1, branch)
+    grad_self = mm(branch, w_self, 1, 1).astype(LOW)
+    g_self = mm(self_att, branch, 0, 0).astype(LOW)
+    (grad_mixed,) = call(
+        self_backward,
+        [low(count, 3 * inner)],
+        (ids, marks, mixed_low, grad_self, self_lse),
+        scratch=[pltpu.VMEM((count, 128), WIDE), pltpu.VMEM((count, 128), WIDE)],
+        resident=True,
+    )
+    grad_mixed, up_one = sync(grad_mixed, up_one)
+    g_mixed = mm(one_all, grad_mixed, 0, 0).astype(LOW)
+    mixed_sent = pick(g_mixed.reshape(4, 2, 128, 768), 1 - (row & 1), 1)
+    mixed_sent, grad_mixed, attend_came = sync(mixed_sent, grad_mixed, attend_came)
+    mixed_came = row_swap(mixed_sent, 1)
+    attend_own, *attend_parts = call(
+        attend_z,
+        [wide(256, 1024)] + [low(256, 1024)] * 3,
+        (ids, g_query, g_pairs, g_cross, g_self, attend_came),
+    )
+    attend_parts = along_z(attend_parts)
+    grad_one, mixed_came = scatter_slots(grad_mixed, w_mixed, 1, None, (mixed_came,))
+    mixed_own, *mixed_parts = call(
+        split_sums, [wide(128, 768)] + [low(128, 768)] * 3, (ids, g_mixed, mixed_came)
+    )
+    attend_own, *attend_parts, _ = sync(attend_own, *attend_parts, mixed_own)
+    mixed_parts = along_z(mixed_parts)
+    part, gain_one, bias_one = norm_backward(grad_one, hat_one, inverse_one, gains[0])
+    frame_grad = grad_hidden + part
+    d_up, d_down = return_ffn(
+        ids, (up_own, up_one, up_two, up_three), (down_own, down_one, down_two, down_three)
+    )
+    norm_sums = reduce_norms(
+        jnp.stack([gain_one, gain_two, gain_three, bias_one, bias_two, bias_three]), here
+    )
+    d_self, d_query, d_pairs, d_cross = return_attend(ids, attend_own, attend_parts)
+    d_mixed = return_mixed(ids, mixed_own, mixed_parts)
+    return (
+        output[None],
+        frame_grad[None],
+        text_grad[None],
+        d_mixed,
+        d_self,
+        d_query,
+        d_pairs,
+        d_cross,
+        d_up,
+        d_down,
+        norm_sums[:3],
+        norm_sums[3:],
+    )
+
+
+def local_general(
     frames,
     text_states,
     frame_segments,
@@ -361,117 +1129,101 @@
     out_grad,
 ):
     here = lax.axis_index("text")
-    here_low = here.astype(jnp.int32).reshape(1)
+    row = lax.axis_index("rows")
+    ids = jnp.stack([here, row]).astype(jnp.int32)
     row_count = lax.axis_size("rows")
     width = frames.shape[2]
     count = frames.shape[1] * WAYS
     inner = width // WAYS
 
     chunk = ffn_out.shape[0] // WAYS
-    packed = jnp.concatenate(
-        [deal(self_in, 3), deal(cross_query, 1), deal(cross_kv, 2)], axis=2
-    )
-    packed = exchange(packed)
-    piece = inner // WAYS
-    w_mixed = gather_rows(side_by_side(packed[:, :, : 3 * piece]))
-    w_query = gather_rows(side_by_side(packed[:, :, 3 * piece : 4 * piece]))
-    w_pairs = gather_rows(side_by_side(packed[:, :, 4 * piece :]))
+    norms = jnp.concatenate([norm_gains, norm_biases], axis=0)
+    norms = ordered(norms, swap(norms, 2), here >> 1)
+    norms = ordered(norms, swap(norms, 1), here & 1, 1)
+    norms = jnp.moveaxis(norms, 2, 0).reshape(6, width).astype(WIDE)
+    gains, biases = norms[:3], norms[3:]
+    depth = ffn_in.shape[0]
+    gate = norms
+    w_mixed = gather_rows(side_by_side(exchange(deal(self_in, 3), here)))
+    w_query = gather_rows(side_by_side(exchange(deal(cross_query, 1), here)))
+    w_query = jnp.concatenate([w_query, swap(w_query, 2)], axis=1)
+    w_pairs = gather_rows(side_by_side(exchange(deal(cross_kv, 2), here)))
     w_self = own_heads(self_out, here)
     w_cross = own_heads(cross_out, here)
-    w_up = gather_rows(side_by_side(exchange(deal(ffn_in, row_count // WAYS))))
-    w_down = gather_rows(
-        side_by_side(exchange(ffn_out.reshape(WAYS, chunk, ffn_out.shape[1])))
-    )
-
-    norms = jnp.concatenate([norm_gains, norm_biases], axis=0)
-    norms = lax.all_gather(norms, "text", axis=1, tiled=True).astype(WIDE)
-    gains, biases = norms[:3], norms[3:]
-    segments = frame_segments[0]
-    clips = text_lengths.shape[1]
-    ends = jnp.cumsum(text_lengths[0])
-    clip = jnp.arange(clips, dtype=jnp.int32)
-    begins = jnp.sum((segments[None, :] < clip[:, None]).astype(jnp.int32), axis=1)
-    same = (segments[None, :] == clip[:, None]).astype(jnp.int32)
-    marks = jnp.stack(
-        [
-            jnp.sum(same * begins[:, None], axis=0),
-            jnp.sum(same * (ends - text_lengths[0])[:, None], axis=0),
-            jnp.sum(same * ends[:, None], axis=0),
-        ]
-    )
-    marks = jnp.concatenate([marks, jnp.zeros((5, count), jnp.int32)], axis=0)
+    w_up = gather_rows(side_by_side(exchange(deal(ffn_in, row_count // WAYS), here)))
+    w_down = ffn_out.reshape(WAYS, chunk, inner)
+    w_down = gather_rows(side_by_side(exchange(w_down, here)))
+
+    marks = mask_marks(frame_segments[0], text_lengths[0])
 
     frames_wide = frames[0].astype(WIDE)
     one, hat_one, inverse_one = norm_forward(frames_wide, gains[0], biases[0])
-    one_all = gather_slots(one)
+    one_all = gather_slots(after(one, gate), ids)
+    text_all = gather_slots(after(text_states[0], one_all), ids)
+    grad_all = gather_slots(after(out_grad[0], text_all), ids)
+    one_all = after(one_all, text_all, grad_all)
     mixed = mm(one_all, w_mixed).astype(LOW)
-    self_flops = count * count * inner * 2 * 5 // 8
     self_att, self_lse = call(
         self_forward,
         [shaped((count, inner), LOW), shaped((4, count), WIDE)],
-        (here_low, marks, mixed),
-        flops=2 * self_flops,
-        exps=count * count * 5 // 2,
+        (ids, marks, mixed),
+        resident=True,
     )
     hidden = frames_wide + scatter_slots(self_att, w_self, 0)
     two, hat_two, inverse_two = norm_forward(hidden, gains[1], biases[1])
-    two_all = gather_slots(two)
-    query = mm(two_all, w_query).astype(LOW)
-    text_all = gather_slots(text_states[0])
+    two_pair = gather_pair(two, ids)
+    pair_count = two_pair.shape[0]
     text_count = text_all.shape[0]
-    text_pairs = mm(text_all, w_pairs).astype(LOW)
-    cross_flops = count * text_count * inner * 2
+    pairs_own = mm(text_all, w_pairs).astype(LOW)
+    pairs_other = swap(pairs_own, 2)
+    w_cross_both = join(ids, w_cross, swap(after(w_cross, pairs_other), 2))
+    query = mm(two_pair, w_query).astype(LOW)
     cross_att, cross_lse = call(
         cross_forward,
-        [shaped((count, inner), LOW), shaped((4, count), WIDE)],
-        (here_low, marks, query, text_pairs),
-        flops=2 * cross_flops,
-        exps=count * text_count * 4,
-    )
-    hidden_two = hidden + scatter_slots(cross_att, w_cross, 0)
+        [shaped((pair_count, 2 * inner), LOW), shaped((8, pair_count), WIDE)],
+        (ids, marks, query, pairs_own, pairs_other),
+        resident=True,
+    )
+    hidden_two = hidden + scatter_pair(cross_att, w_cross_both, 0)
     three, hat_three, inverse_three = norm_forward(hidden_two, gains[2], biases[2])
-    three_all = gather_slots(three)
+    three_all = gather_slots(three, ids)
     up = mm(three_all, w_up)
-    phi = 0.5 * (1.0 + lax.erf(up * math.sqrt(0.5)))
-    activ = (up * phi).astype(LOW)
-    output = (hidden_two + scatter_slots(activ, w_down, 0)).astype(LOW)
-
-    grad_all = gather_slots(out_grad[0])
+    activ, slope = gelu_parts(up)
+
+    grad_up = (mm(grad_all, w_down, 1, 1) * slope).astype(LOW)
+    grad_three = scatter_slots(grad_up, w_up, 1)
+    g_up = mm(three_all, grad_up, 0, 0).astype(LOW)
     g_down = mm(activ, grad_all, 0, 0).astype(LOW)
-    slope = phi + up * (jnp.exp(-0.5 * up * up) * (1.0 / math.sqrt(2.0 * math.pi)))
-    grad_up = (mm(grad_all, w_down, 1, 1) * slope).astype(LOW)
-    g_up = mm(three_all, grad_up, 0, 0).astype(LOW)
-    part, gain_three, bias_three = norm_backward(
-        scatter_slots(grad_up, w_up, 1), hat_three, inverse_three, gains[2]
-    )
+    output = (hidden_two + scatter_slots(activ, w_down, 0, grad_three)).astype(LOW)
+    part, gain_three, bias_three = norm_backward(grad_three, hat_three, inverse_three, gains[2])
     grad_two = out_grad[0].astype(WIDE) + part
-    branch_two = gather_slots(grad_two.astype(LOW))
-    grad_cross = mm(branch_two, w_cross, 1, 1).astype(LOW)
+    branch_two = gather_pair(grad_two.astype(LOW), ids)
+    grad_cross = mm(branch_two, w_cross_both, 1, 1).astype(LOW)
     g_cross = mm(cross_att, branch_two, 0, 0).astype(LOW)
-    grad_query, grad_pairs = call(
+    grad_query, pairs_mine, pairs_away = call(
         cross_backward,
-        [shaped((count, inner), LOW), shaped((text_count, 2 * inner), LOW)],
-        (here_low, marks, query, text_pairs, grad_cross, cross_lse),
-        flops=5 * cross_flops,
-        exps=count * text_count * 4,
-    )
-    g_query = mm(two_all, grad_query, 0, 0).astype(LOW)
+        [shaped((pair_count, 2 * inner), LOW)] + [shaped((text_count, 2 * inner), LOW)] * 2,
+        (ids, marks, query, pairs_own, pairs_other, grad_cross, cross_lse),
+        resident=True,
+    )
+    part, gain_two, bias_two = norm_backward(
+        scatter_pair(grad_query, w_query, 1), hat_two, inverse_two, gains[1]
+    )
+    grad_pairs = (pairs_mine.astype(WIDE) + swap(pairs_away, 2).astype(WIDE)).astype(LOW)
+    g_query = mm(two_pair, grad_query, 0, 0).astype(LOW)
     g_pairs = mm(text_all, grad_pairs, 0, 0).astype(LOW)
-    text_grad = scatter_slots(grad_pairs, w_pairs, 1)
-    part, gain_two, bias_two = norm_backward(
-        scatter_slots(grad_query, w_query, 1), hat_two, inverse_two, gains[1]
-    )
     grad_hidden = grad_two + part
-    branch = gather_slots(grad_hidden.astype(LOW))
+    grad_low = grad_hidden.astype(LOW)
+    branch = gather_slots(grad_low, ids)
+    text_grad = scatter_slots(grad_pairs, w_pairs, 1, branch)
     grad_self = mm(branch, w_self, 1, 1).astype(LOW)
     g_self = mm(self_att, branch, 0, 0).astype(LOW)
     (grad_mixed,) = call(
         self_backward,
         [shaped((count, 3 * inner), LOW)],
-        (here_low, marks, mixed, grad_self, self_lse),
+        (ids, marks, mixed, grad_self, self_lse),
         scratch=[pltpu.VMEM((count, 128), WIDE), pltpu.VMEM((count, 128), WIDE)],
-        flops=5 * self_flops,
-        exps=count * count * 5 // 2,
+        resident=True,
     )
     g_mixed = mm(one_all, grad_mixed, 0, 0).astype(LOW)
     part, gain_one, bias_one = norm_backward(
@@ -479,17 +1231,20 @@
     )
     frame_grad = grad_hidden + part
 
-    norm_sums = jnp.stack([gain_one, gain_two, gain_three, bias_one, bias_two, bias_three])
-    norm_sums = lax.psum(norm_sums, ("rows", "text"))
-    norm_sums = lax.dynamic_slice_in_dim(norm_sums, here * inner, inner, 1)
-
-    d_down = exchange(apart(sum_rows(g_down))).reshape(ffn_out.shape).astype(WIDE)
-    d_up = undeal(exchange(apart(sum_rows(g_up))), row_count // WAYS).astype(WIDE)
+    norm_sums = reduce_norms(
+        jnp.stack([gain_one, gain_two, gain_three, bias_one, bias_two, bias_three]), here
+    )
+    parts = jnp.concatenate([apart(sum_rows(g_up)), apart(sum_rows(g_down))], axis=1)
+    parts = exchange(parts, here)
+    d_up = undeal(parts[:, :depth], row_count // WAYS).astype(WIDE)
+    d_down = parts[:, depth:].reshape(ffn_out.shape).astype(WIDE)
+    g_query = g_query[:, :inner] + swap(g_query[:, inner:], 2)
+    g_cross = g_cross[:inner] + swap(g_cross[inner:], 2)
     d_cross = return_heads(g_cross, here).astype(WIDE)
     d_self = return_heads(g_self, here).astype(WIDE)
-    d_query = undeal(exchange(apart(sum_rows(g_query))), 1).astype(WIDE)
-    d_pairs = undeal(exchange(apart(sum_rows(g_pairs))), 2).astype(WIDE)
-    d_mixed = undeal(exchange(apart(sum_rows(g_mixed))), 3).astype(WIDE)
+    d_query = undeal(exchange(apart(sum_rows(g_query)), here), 1).astype(WIDE)
+    d_pairs = undeal(exchange(apart(sum_rows(g_pairs)), here), 2).astype(WIDE)
+    d_mixed = undeal(exchange(apart(sum_rows(g_mixed)), here), 3).astype(WIDE)
     return (
         output[None],
         frame_grad[None],
@@ -537,4 +1292,5 @@
         P(None, "text"),
         P(None, "text"),
     )
+    local = local_grid if mesh.shape["rows"] == 8 else local_general
     return jax.shard_map(local, mesh=mesh, in_specs=in_specs, out_specs=out_specs, check_vma=False)

time: 935 us -> 503 us (0.54)
  waiting for transfers between devices: 586 us -> 173 us
  blocking collectives: 129 us -> 0 us
  starting transfers between devices: 39.5 us -> 122 us
  Pallas kernels: 29.4 us -> 93.5 us
  between operations: 15.3 us -> 3.04 us
  other arithmetic: 23 us -> 11.6 us
    reduce_scatter x9 -> x0, waiting for transfers between devices: 361 us -> none  [the longest x7 309 us: sum_rows(): return lax.psum_scatter(whole, 'rows', scatter_dimension=0, tiled=True)]
    ppermute x0 -> x53, waiting for transfers between devices: none -> 123 us  [row_swap(): return lax.ppermute(values, 'rows', [(i, i ^ mask) for i in range(size)])]
    all_gather x6 -> x0, waiting for transfers between devices: 104 us -> none  [gather_rows(): return lax.all_gather(block, 'rows', axis=0, tiled=True)]
    ppermute x0 -> x53, starting transfers between devices: none -> 95 us  [row_swap(): return lax.ppermute(values, 'rows', [(i, i ^ mask) for i in range(size)])]
    ppermute x28 -> x46, waiting for transfers between devices: 119 us -> 50.5 us  [swap(): return lax.ppermute(values, 'text', [(i, i ^ mask) for i in range(WAYS)])]
    pallas_call x4 -> x43, Pallas kernels: 29.4 us -> 93.5 us  [the longest x41 81.1 us: call(): pl.pallas_call(body, out_shape=outs, in_specs=[pl.BlockSpec(memory_space=...]
    all_gather x4 -> x0, blocking collectives: 47.4 us -> none  [the longest x1 29.5 us: gather_rows(): return lax.all_gather(block, 'rows', axis=0, tiled=True)]
    all_to_all x3 -> x0, blocking collectives: 41.5 us -> none  [exchange(): return lax.all_to_all(dealt, 'text', 0, 0, tiled=True)]
  transfers between devices with their start and end apart: 48 -> 99, of which waited for: 29 -> 33; matrix products, arithmetic and copies ran while one was open for 10% -> 12% of each run, Pallas kernels for 2% -> 17%
where the time goes in v3:
time: 503 us; the launch traced here: 493 us
  waiting for transfers between devices  173 us (34%)
  starting transfers between devices  122 us (24%)
  Pallas kernels  93.5 us (19%)
  matrix products  56.5 us (11%)
  local copies, waits for them, and re-layouts  33.8 us (7%)
  other arithmetic  11.6 us (2%)
    ppermute x53, waiting for transfers between devices, row_swap(): return lax.ppermute(values, 'rows', [(i, i ^ mask) for i in range(size)])  123 us
    ppermute x53, starting transfers between devices, row_swap(): return lax.ppermute(values, 'rows', [(i, i ^ mask) for i in range(size)])  95 us
    pallas_call x41, Pallas kernels, call(): pl.pallas_call(body, out_shape=outs, in_specs=[pl.BlockSpec(memory_space=...  81.1 us
    dot_general x31, matrix products, mm(): lax.dot_general(left, right, (((left_dim,), (right_dim,)), ((), ())), pre...  56.5 us
    ppermute x46, waiting for transfers between devices, swap(): return lax.ppermute(values, 'text', [(i, i ^ mask) for i in range(WAYS)])  50.5 us
    unnamed x242, local copies, waits for them, and re-layouts  31.3 us
    ppermute x46, starting transfers between devices, swap(): return lax.ppermute(values, 'text', [(i, i ^ mask) for i in range(WAYS)])  27 us
    pallas_call x2, Pallas kernels, weight_grad(): pl.pallas_call(weight_block, grid_spec=pltpu.PrefetchScalarGridSpec(num_s...  12.4 us
  transfers between devices with their start and end apart: 99, of which 33 were waited for; matrix products, arithmetic and copies ran while one was open for 12% of the time, Pallas kernels for 17%

profile of v3, /device:TPU:0, one launch (start us, length us, event | category | flops | bytes accessed | tf_op | source)
XLA Modules:
  0.0 493.4 jit_solution(9873093525773297055)
XLA Ops:
  6.1 2.5 collective-permute-start.3
  19.2 6.5 %collective-permute-done.1.refs_1_ = bf16[128,896]{1,0:T(8,128)(2,1)S(1)} collective-permute-done((bf16[128,896]{1,0:T(8,128)(2,1)S(1)}, bf16[128,896]{1,0:T(8,128)(2,1)S(1)}, u32[]{:S(2)}, u32[]{:S(2)}) %collective-permute-start.1) | collective-permute-done | bytes 229408 | tf_op jit(solution)/shard_map/ppermute | solution.py:26
  33.0 2.6 collective-permute-start.6
  35.6 5.1 %collective-permute-done.5.refs_1_ = bf16[128,768]{1,0:T(8,128)(2,1)S(1)} collective-permute-done((bf16[128,768]{1,0:T(8,128)(2,1)S(1)}, bf16[128,768]{1,0:T(8,128)(2,1)S(1)}, u32[]{:S(2)}, u32[]{:S(2)}) %collective-permute-start.5) | collective-permute-done | bytes 196640 | tf_op jit(solution)/shard_map/ppermute | solution.py:465
  40.7 2.9 collective-permute-start.7
  46.1 2.1 collective-permute-done.7.refs_3_
  52.4 3.2 collective-permute-done.11.refs_5_
  56.3 3.8 collective-permute-start.18
  64.8 2.5 collective-permute-start.17
  69.3 2.1 collective-permute-done.19.refs_2_
  77.2 2.2 collective-permute-start.26
  85.0 2.7 shard_map.236
  91.1 6.9 %shard_map.237 = (bf16[1024,256]{1,0:T(8,128)(2,1)S(1)}, f32[4,1024]{1,0:T(4,128)S(1)}) custom-call(s32[2]{0:T(128)S(1)} %pad_add_fusion.ids_ref._.here_ref, s32[8,1024]{1,0:T(8,128)S(1)} %stack.110.marks_ref, bf16[1024,768]{1,0:T(8,128)(2,1)S(1)} %convolution_convert_fusion.1.mixed_ref), custom_call_target="tpu_custom_call" | custom-call | bytes 2146312 | tf_op jit(solution)/shard_map/pallas_call | solution.py:352
  108.8 2.4 collective-permute-start.32
  111.2 2.7 collective-permute-done.30.refs_1_
  114.4 5.7 %collective-permute-done.31.refs_2_ = bf16[64,1024]{1,0:T(8,128)(2,1)S(1)} collective-permute-done((bf16[64,1024]{1,0:T(8,128)(2,1)S(1)}, bf16[64,1024]{1,0:T(8,128)(2,1)S(1)}, u32[]{:S(2)}, u32[]{:S(2)}) %collective-permute-start.31) | collective-permute-done | bytes 131104 | tf_op jit(solution)/shard_map/ppermute | solution.py:465
  129.4 2.4 collective-permute-start.38
  133.2 14.4 %collective-permute-done.35.other_ref = bf16[384,512]{1,0:T(8,128)(2,1)S(1)} collective-permute-done((bf16[384,512]{1,0:T(8,128)(2,1)S(1)}, bf16[384,512]{1,0:T(8,128)(2,1)S(1)}, u32[]{:S(2)}, u32[]{:S(2)}) %collective-permute-start.35) | collective-permute-done | bytes 393248 | tf_op jit(solution)/shard_map/ppermute | solution.py:26
  147.6 6.4 %shard_map.242 = (bf16[512,512]{1,0:T(8,128)(2,1)S(1)}, f32[8,512]{1,0:T(8,128)S(1)}) custom-call(s32[2]{0:T(128)S(1)} %pad_add_fusion.ids_ref._.here_ref, s32[8,1024]{1,0:T(8,128)S(1)} %stack.110.marks_ref, bf16[512,512]{1,0:T(8,128)(2,1)S(1)} %convolution_convert_fusion.14.query_ref, bf16[384,512]{1,0:T(8,128)(2,1)S(1)} %convolution_convert_fusion.16.own_ref, ...), custom_call_target="tpu_custom_call" | custom-call | bytes 1884168 | tf_op jit(solution)/shard_map/pallas_call | solution.py:352
  160.6 14.7 %collective-permute-done.42.refs_5_ = bf16[128,1024]{1,0:T(8,128)(2,1)S(1)} collective-permute-done((bf16[128,1024]{1,0:T(8,128)(2,1)S(1)}, bf16[128,1024]{1,0:T(8,128)(2,1)S(1)}, u32[]{:S(2)}, u32[]{:S(2)}) %collective-permute-start.42) | collective-permute-done | bytes 262176 | tf_op jit(solution)/shard_map/ppermute | solution.py:465
  177.1 2.3 collective-permute-start.46
  179.6 5.2 %collective-permute-done.49.refs_4_ = bf16[128,1024]{1,0:T(8,128)(2,1)S(1)} collective-permute-done((bf16[128,1024]{1,0:T(8,128)(2,1)S(1)}, bf16[128,1024]{1,0:T(8,128)(2,1)S(1)}, u32[]{:S(2)}, u32[]{:S(2)}) %collective-permute-start.49) | collective-permute-done | bytes 262176 | tf_op jit(solution)/shard_map/ppermute | solution.py:465
  191.3 9.0 %collective-permute-done.47.refs_2_ = bf16[128,1024]{1,0:T(8,128)(2,1)S(1)} collective-permute-done((bf16[128,1024]{1,0:T(8,128)(2,1)S(1)}, bf16[128,1024]{1,0:T(8,128)(2,1)S(1)}, u32[]{:S(2)}, u32[]{:S(2)}) %collective-permute-start.47) | collective-permute-done | bytes 262176 | tf_op jit(solution)/shard_map/ppermute | solution.py:465
  202.5 5.8 %fusion.3 = (f32[1024,1024]{1,0:T(8,128)}, bf16[1024,1024]{1,0:T(8,128)(2,1)}) fusion(bf16[1024,1024]{1,0:T(8,128)(2,1)S(1)} %shard_map.245.left, bf16[1024,1024]{1,0:T(8,128)(2,1)S(1)} %shard_map.246), kind=kOutput, calls=%fused_computation.4 | convolution fusion | flops 2157969408 | bytes 10485760 | tf_op jit(solution)/shard_map/dot_general | solution.py:20
  208.3 8.4 %collective-permute-done.51.refs_5_ = bf16[128,1024]{1,0:T(8,128)(2,1)S(1)} collective-permute-done((bf16[128,1024]{1,0:T(8,128)(2,1)S(1)}, bf16[128,1024]{1,0:T(8,128)(2,1)S(1)}, u32[]{:S(2)}, u32[]{:S(2)}) %collective-permute-start.51) | collective-permute-done | bytes 262176 | tf_op jit(solution)/shard_map/ppermute | solution.py:465
  218.5 4.6 multiply_convert_fusion.right
  223.1 2.3 convolution_convert_fusion.4
  225.6 6.2 %shard_map.249 = (bf16[2,128,1024]{2,1,0:T(8,128)(2,1)S(1)}, bf16[2,128,1024]{2,1,0:T(8,128)(2,1)S(1)}, bf16[4,128,1024]{2,1,0:T(8,128)(2,1)S(1)}) custom-call(s32[1]{0:T(128)} %bitcast.2.row_ref, bf16[1024,1024]{1,0:T(8,128)(2,1)S(1)} %copy-done.81, bf16[1024,1024]{1,0:T(8,128)(2,1)} %copy-done.17), custom_call_target="tpu_custom_call" | custom-call | flops 2147483648 | bytes 6291456 | tf_op jit(solution)/shard_map/pallas_call | solution.py:395
  233.3 2.7 fusion.15
  237.3 6.2 %shard_map.250 = (bf16[2,128,1024]{2,1,0:T(8,128)(2,1)S(1)}, bf16[2,128,1024]{2,1,0:T(8,128)(2,1)S(1)}, bf16[4,128,1024]{2,1,0:T(8,128)(2,1)S(1)}) custom-call(s32[1]{0:T(128)} %bitcast.2.row_ref, bf16[1024,1024]{1,0:T(8,128)(2,1)S(1)} %copy-done.19, bf16[1024,1024]{1,0:T(8,128)(2,1)} %copy-done.112), custom_call_target="tpu_custom_call" | custom-call | flops 2147483648 | bytes 6291456 | tf_op jit(solution)/shard_map/pallas_call | solution.py:395
  243.6 2.4 collective-permute-done.58.refs_1_
  246.0 4.2 collective-permute-done.57
  250.2 2.9 multiply_reduce_fusion
  253.2 2.6 fusion.56
  258.6 8.0 %collective-permute-start.62 = (bf16[128,1024]{1,0:T(8,128)(2,1)S(1)}, bf16[128,1024]{1,0:T(8,128)(2,1)S(1)}, u32[]{:S(2)}, u32[]{:S(2)}) collective-permute-start(bf16[128,1024]{1,0:T(8,128)(2,1)S(1)} %get-tuple-element.252), channel_id=1, source_target_pairs={{0,16},{4,20},{8,24},{12,28},{16,0},{20,4},{24,8},{28,12},{1,17},{... | collective-permute-start | bytes 786440 | tf_op jit(solution)/shard_map/ppermute | solution.py:465
  270.5 14.4 %collective-permute-done.62.refs_6_ = bf16[128,1024]{1,0:T(8,128)(2,1)S(1)} collective-permute-done((bf16[128,1024]{1,0:T(8,128)(2,1)S(1)}, bf16[128,1024]{1,0:T(8,128)(2,1)S(1)}, u32[]{:S(2)}, u32[]{:S(2)}) %collective-permute-start.62) | collective-permute-done | bytes 262176 | tf_op jit(solution)/shard_map/ppermute | solution.py:465
  285.0 7.3 %shard_map.253 = (bf16[512,512]{1,0:T(8,128)(2,1)S(1)}, bf16[384,512]{1,0:T(8,128)(2,1)S(1)}, bf16[384,512]{1,0:T(8,128)(2,1)S(1)}) custom-call(s32[2]{0:T(128)S(1)} %pad_add_fusion.ids_ref._.here_ref, s32[8,1024]{1,0:T(8,128)S(1)} %stack.110.marks_ref, bf16[512,512]{1,0:T(8,128)(2,1)S(1)} %convolution_convert_fusion.14.query_ref, ...), custom_call_target="tpu_custom_call" | custom-call | bytes 3194888 | tf_op jit(solution)/shard_map/pallas_call | solution.py:352
  295.0 5.5 %collective-permute-start.71 = (bf16[128,1024]{1,0:T(8,128)(2,1)S(1)}, bf16[128,1024]{1,0:T(8,128)(2,1)S(1)}, u32[]{:S(2)}, u32[]{:S(2)}) collective-permute-start(bf16[128,1024]{1,0:T(8,128)(2,1)S(1)} %get-tuple-element.268), channel_id=1, source_target_pairs={{0,8},{4,12},{8,0},{12,4},{16,24},{20,28},{24,16},{28,20},{1,9},{5... | collective-permute-start | bytes 786440 | tf_op jit(solution)/shard_map/ppermute | solution.py:465
  310.5 2.0 shard_map.259
  314.4 8.3 %collective-permute-done.69.refs_2_ = bf16[128,1024]{1,0:T(8,128)(2,1)S(1)} collective-permute-done((bf16[128,1024]{1,0:T(8,128)(2,1)S(1)}, bf16[128,1024]{1,0:T(8,128)(2,1)S(1)}, u32[]{:S(2)}, u32[]{:S(2)}) %collective-permute-start.69) | collective-permute-done | bytes 262176 | tf_op jit(solution)/shard_map/ppermute | solution.py:465
  325.4 2.6 convolution_convert_fusion.5
  329.9 4.4 collective-permute-start.74
  334.3 2.1 shard_map.256
  338.6 10.7 %shard_map.257 = bf16[1024,768]{1,0:T(8,128)(2,1)S(1)} custom-call(s32[2]{0:T(128)S(1)} %pad_add_fusion.ids_ref._.here_ref, s32[8,1024]{1,0:T(8,128)S(1)} %stack.110.marks_ref, bf16[1024,768]{1,0:T(8,128)(2,1)S(1)} %copy-done.5, bf16[1024,256]{1,0:T(8,128)(2,1)S(1)} %convolution_convert_fusion.12.grad_ref, f32[4,1024]{1,0:T(4,128)S(1)} %get-tuple-element.270.lse_ref), custom_call_target="tpu_custom_call" | custom-call | bytes 3719176 | tf_op jit(solution)/shard_map/pallas_call | solution.py:352
  349.4 2.2 convolution_convert_fusion.refs_0_
  352.7 2.0 convolution_convert_fusion.2
  354.7 2.9 fusion.14
  358.5 13.8 %collective-permute-done.59 = bf16[256,1024]{1,0:T(8,128)(2,1)} collective-permute-done((bf16[256,1024]{1,0:T(8,128)(2,1)}, bf16[256,1024]{1,0:T(8,128)(2,1)}, u32[]{:S(2)}, u32[]{:S(2)}) %collective-permute-start.59) | collective-permute-done | bytes 524320 | tf_op jit(solution)/shard_map/ppermute | solution.py:26
  372.2 2.2 convolution_convert_fusion.15
  375.4 3.0 fusion.12
  379.3 2.8 fusion.23
  382.1 2.1 fusion.26
  394.9 3.8 fusion.34
  400.9 4.7 collective-permute-done.80
  406.5 2.8 shard_map.264
  415.1 2.3 fusion.25
  419.1 2.0 shard_map.260
  421.1 13.1 %collective-permute-done.86.refs_1_ = bf16[256,1024]{1,0:T(8,128)(2,1)S(1)} collective-permute-done((bf16[256,1024]{1,0:T(8,128)(2,1)S(1)}, bf16[256,1024]{1,0:T(8,128)(2,1)S(1)}, u32[]{:S(2)}, u32[]{:S(2)}) %collective-permute-start.86) | collective-permute-done | bytes 524320 | tf_op jit(solution)/shard_map/ppermute | solution.py:465
  434.2 14.2 %collective-permute-done.87.refs_2_ = bf16[256,1024]{1,0:T(8,128)(2,1)S(1)} collective-permute-done((bf16[256,1024]{1,0:T(8,128)(2,1)S(1)}, bf16[256,1024]{1,0:T(8,128)(2,1)S(1)}, u32[]{:S(2)}, u32[]{:S(2)}) %collective-permute-start.87) | collective-permute-done | bytes 524320 | tf_op jit(solution)/shard_map/ppermute | solution.py:465
  450.7 11.1 %collective-permute-start.81 = (bf16[128,768]{1,0:T(8,128)(2,1)S(1)}, bf16[128,768]{1,0:T(8,128)(2,1)S(1)}, u32[]{:S(2)}, u32[]{:S(2)}) collective-permute-start(bf16[128,768]{1,0:T(8,128)(2,1)S(1)} %get-tuple-element.284), channel_id=1, source_target_pairs={{0,8},{4,12},{8,0},{12,4},{16,24},{20,28},{24,16},{28,20},{1,9},{5... | collective-permute-start | bytes 589832 | tf_op jit(solution)/shard_map/ppermute | solution.py:465
  465.1 2.6 collective-permute-done.96
  468.9 4.9 collective-permute-done.97
  473.8 2.9 collective-permute-start.98
  483.0 2.9 collective-permute-done.84.refs_1_
  (508 shorter events, 168.2 us)
Async XLA Ops:
  27.9 16.3 %collective-permute-start.9 = (bf16[128,1536]{1,0:T(8,128)(2,1)S(1)}, bf16[128,1536]{1,0:T(8,128)(2,1)S(1)}, u32[]{:S(2)}, u32[]{:S(2)}) collective-permute-start(bf16[128,1536]{1,0:T(8,128)(2,1)S(1)} %get-tuple-element.183), channel_id=1, source_target_pairs={{0,2},{1,3},{2,0},{3,1},{4,6},{5,7},{6,4},{7,5},{8,10},{9,11},{10,... | collective-permute-start | bytes 1179656 | tf_op jit(solution)/shard_map/ppermute | solution.py:26
  29.0 21.5 %collective-permute-start.13 = (bf16[256,1024]{1,0:T(8,128)(2,1)S(1)}, bf16[256,1024]{1,0:T(8,128)(2,1)S(1)}, u32[]{:S(2)}, u32[]{:S(2)}) collective-permute-start(bf16[256,1024]{1,0:T(8,128)(2,1)S(1)} %fusion.28.refs_0_), channel_id=1, source_target_pairs={{0,2},{1,3},{2,0},{3,1},{4,6},{5,7},{6,4},{7,5},{8,10},{9,11},{10,... | collective-permute-start | bytes 1572872 | tf_op jit(solution)/shard_map/ppermute | solution.py:26
  30.0 13.6 %collective-permute-start.10 = (bf16[128,1024]{1,0:T(8,128)(2,1)S(1)}, bf16[128,1024]{1,0:T(8,128)(2,1)}, u32[]{:S(2)}, u32[]{:S(2)}) collective-permute-start(bf16[128,1024]{1,0:T(8,128)(2,1)S(1)} %get-tuple-element.185), channel_id=1, source_target_pairs={{0,4},{4,0},{8,12},{12,8},{16,20},{20,16},{24,28},{28,24},{1,5},{5... | collective-permute-start | bytes 786440 | tf_op jit(solution)/shard_map/ppermute | solution.py:465
  33.0 13.1 %collective-permute-start.6 = (bf16[128,768]{1,0:T(8,128)(2,1)S(1)}, bf16[128,768]{1,0:T(8,128)(2,1)S(1)}, u32[]{:S(2)}, u32[]{:S(2)}) collective-permute-start(bf16[128,768]{1,0:T(8,128)(2,1)S(1)} %get-tuple-element.181.refs_0_), channel_id=1, source_target_pairs={{0,16},{4,20},{8,24},{12,28},{16,0},{20,4},{24,8},{28,12},{1,17},{... | collective-permute-start | bytes 589832 | tf_op jit(solution)/shard_map/ppermute | solution.py:465
  44.1 16.8 %collective-permute-start.14 = (bf16[256,1024]{1,0:T(8,128)(2,1)S(1)}, bf16[256,1024]{1,0:T(8,128)(2,1)S(1)}, u32[]{:S(2)}, u32[]{:S(2)}) collective-permute-start(bf16[256,1024]{1,0:T(8,128)(2,1)S(1)} %fusion.28.refs_0_), channel_id=1, source_target_pairs={{0,1},{1,0},{2,3},{3,2},{4,5},{5,4},{6,7},{7,6},{8,9},{9,8},{10,11... | collective-permute-start | bytes 1572872 | tf_op jit(solution)/shard_map/ppermute | solution.py:26
  50.5 16.8 %collective-permute-start.15 = (bf16[256,1024]{1,0:T(8,128)(2,1)S(1)}, bf16[256,1024]{1,0:T(8,128)(2,1)S(1)}, u32[]{:S(2)}, u32[]{:S(2)}) collective-permute-start(bf16[256,1024]{1,0:T(8,128)(2,1)S(1)} %collective-permute-done.13.refs_1_), channel_id=1, source_target_pairs={{0,1},{1,0},{2,3},{3,2},{4,5},{5,4},{6,7},{7,6},{8,9},{9,8},{10,11... | collective-permute-start | bytes 1572872 | tf_op jit(solution)/shard_map/ppermute | solution.py:26
  60.2 12.6 %collective-permute-start.12 = (bf16[2,128,768]{2,1,0:T(8,128)(2,1)S(1)}, bf16[2,128,768]{2,1,0:T(8,128)(2,1)S(1)}, u32[]{:S(2)}, u32[]{:S(2)}) collective-permute-start(bf16[2,128,768]{2,1,0:T(8,128)(2,1)S(1)} %pad_maximum_fusion.3), channel_id=1, source_target_pairs={{0,4},{4,0},{8,12},{12,8},{16,20},{20,16},{24,28},{28,24},{1,5},{5... | collective-permute-start | bytes 1179656 | tf_op jit(solution)/shard_map/ppermute | solution.py:465
  67.3 20.5 %collective-permute-start.21 = (bf16[96,1024]{1,0:T(8,128)(2,1)}, bf16[96,1024]{1,0:T(8,128)(2,1)}, u32[]{:S(2)}, u32[]{:S(2)}) collective-permute-start(bf16[96,1024]{1,0:T(8,128)(2,1)} %bitcast.13.refs_0_), channel_id=1, source_target_pairs={{0,1},{1,0},{2,3},{3,2},{4,5},{5,4},{6,7},{7,6},{8,9},{9,8},{10,11... | collective-permute-start | bytes 589832 | tf_op jit(solution)/shard_map/ppermute | solution.py:26
  75.0 27.4 %collective-permute-start.24 = (bf16[256,1024]{1,0:T(8,128)(2,1)}, bf16[256,1024]{1,0:T(8,128)(2,1)}, u32[]{:S(2)}, u32[]{:S(2)}) collective-permute-start(bf16[256,1024]{1,0:T(8,128)(2,1)} %bitcast.14.refs_0_), channel_id=1, source_target_pairs={{0,2},{1,3},{2,0},{3,1},{4,6},{5,7},{6,4},{7,5},{8,10},{9,11},{10,... | collective-permute-start | bytes 1572872 | tf_op jit(solution)/shard_map/ppermute | solution.py:26
  76.4 26.0 %collective-permute-start.25 = (bf16[128,1024]{1,0:T(8,128)(2,1)}, bf16[128,1024]{1,0:T(8,128)(2,1)S(1)}, u32[]{:S(2)}, u32[]{:S(2)}) collective-permute-start(bf16[128,1024]{1,0:T(8,128)(2,1)} %get-tuple-element.207.refs_0_), channel_id=1, source_target_pairs={{0,16},{4,20},{8,24},{12,28},{16,0},{20,4},{24,8},{28,12},{1,17},{... | collective-permute-start | bytes 786440 | tf_op jit(solution)/shard_map/ppermute | solution.py:465
  77.2 25.2 %collective-permute-start.26 = (bf16[128,1024]{1,0:T(8,128)(2,1)}, bf16[128,1024]{1,0:T(8,128)(2,1)S(1)}, u32[]{:S(2)}, u32[]{:S(2)}) collective-permute-start(bf16[128,1024]{1,0:T(8,128)(2,1)} %get-tuple-element.207.refs_0_), channel_id=1, source_target_pairs={{0,24},{4,28},{8,16},{12,20},{16,8},{20,12},{24,0},{28,4},{1,25},{... | collective-permute-start | bytes 786440 | tf_op jit(solution)/shard_map/ppermute | solution.py:465
  79.4 21.2 %collective-permute-start.22 = (bf16[96,1024]{1,0:T(8,128)(2,1)}, bf16[96,1024]{1,0:T(8,128)(2,1)S(1)}, u32[]{:S(2)}, u32[]{:S(2)}) collective-permute-start(bf16[96,1024]{1,0:T(8,128)(2,1)} %copy-done.71), channel_id=1, source_target_pairs={{0,1},{1,0},{2,3},{3,2},{4,5},{5,4},{6,7},{7,6},{8,9},{9,8},{10,11... | collective-permute-start | bytes 589832 | tf_op jit(solution)/shard_map/ppermute | solution.py:26
  87.8 14.6 %collective-permute-start.23 = (bf16[128,1024]{1,0:T(8,128)(2,1)S(1)}, bf16[128,1024]{1,0:T(8,128)(2,1)S(1)}, u32[]{:S(2)}, u32[]{:S(2)}) collective-permute-start(bf16[128,1024]{1,0:T(8,128)(2,1)S(1)} %copy-done.51), channel_id=1, source_target_pairs={{0,4},{4,0},{8,12},{12,8},{16,20},{20,16},{24,28},{28,24},{1,5},{5... | collective-permute-start | bytes 786440 | tf_op jit(solution)/shard_map/ppermute | solution.py:465
  103.2 16.8 %collective-permute-start.29 = (bf16[2,128,1024]{2,1,0:T(8,128)(2,1)S(1)}, bf16[2,128,1024]{2,1,0:T(8,128)(2,1)S(1)}, u32[]{:S(2)}, u32[]{:S(2)}) collective-permute-start(bf16[2,128,1024]{2,1,0:T(8,128)(2,1)S(1)} %pad_maximum_fusion), channel_id=1, source_target_pairs={{0,4},{4,0},{8,12},{12,8},{16,20},{20,16},{24,28},{28,24},{1,5},{5... | collective-permute-start | bytes 1572872 | tf_op jit(solution)/shard_map/ppermute | solution.py:465
  105.9 14.1 %collective-permute-start.28 = (bf16[256,1024]{1,0:T(8,128)(2,1)S(1)}, bf16[256,1024]{1,0:T(8,128)(2,1)S(1)}, u32[]{:S(2)}, u32[]{:S(2)}) collective-permute-start(bf16[256,1024]{1,0:T(8,128)(2,1)S(1)} %fusion.16), channel_id=1, source_target_pairs={{0,2},{1,3},{2,0},{3,1},{4,6},{5,7},{6,4},{7,5},{8,10},{9,11},{10,... | collective-permute-start | bytes 1572872 | tf_op jit(solution)/shard_map/ppermute | solution.py:26
  107.3 12.8 %collective-permute-start.31 = (bf16[64,1024]{1,0:T(8,128)(2,1)S(1)}, bf16[64,1024]{1,0:T(8,128)(2,1)S(1)}, u32[]{:S(2)}, u32[]{:S(2)}) collective-permute-start(bf16[64,1024]{1,0:T(8,128)(2,1)S(1)} %copy-done.40), channel_id=1, source_target_pairs={{0,16},{4,20},{8,24},{12,28},{16,0},{20,4},{24,8},{28,12},{1,17},{... | collective-permute-start | bytes 393224 | tf_op jit(solution)/shard_map/ppermute | solution.py:465
  125.3 28.7 %collective-permute-start.39 = (bf16[256,1024]{1,0:T(8,128)(2,1)S(1)}, bf16[256,1024]{1,0:T(8,128)(2,1)S(1)}, u32[]{:S(2)}, u32[]{:S(2)}) collective-permute-start(bf16[256,1024]{1,0:T(8,128)(2,1)S(1)} %shard_map.243.refs_0_), channel_id=1, source_target_pairs={{0,2},{1,3},{2,0},{3,1},{4,6},{5,7},{6,4},{7,5},{8,10},{9,11},{10,... | collective-permute-start | bytes 1572872 | tf_op jit(solution)/shard_map/ppermute | solution.py:26
  126.2 21.4 %collective-permute-start.35 = (bf16[384,512]{1,0:T(8,128)(2,1)S(1)}, bf16[384,512]{1,0:T(8,128)(2,1)S(1)}, u32[]{:S(2)}, u32[]{:S(2)}) collective-permute-start(bf16[384,512]{1,0:T(8,128)(2,1)S(1)} %convolution_convert_fusion.16.own_ref), channel_id=1, source_target_pairs={{0,2},{1,3},{2,0},{3,1},{4,6},{5,7},{6,4},{7,5},{8,10},{9,11},{10,... | collective-permute-start | bytes 1179656 | tf_op jit(solution)/shard_map/ppermute | solution.py:26
  127.4 26.6 %collective-permute-start.36 = (bf16[128,1024]{1,0:T(8,128)(2,1)S(1)}, bf16[128,1024]{1,0:T(8,128)(2,1)S(1)}, u32[]{:S(2)}, u32[]{:S(2)}) collective-permute-start(bf16[128,1024]{1,0:T(8,128)(2,1)S(1)} %copy-done.49), channel_id=1, source_target_pairs={{0,8},{4,12},{8,0},{12,4},{16,24},{20,28},{24,16},{28,20},{1,9},{5... | collective-permute-start | bytes 786440 | tf_op jit(solution)/shard_map/ppermute | solution.py:465
  129.1 24.9 %collective-permute-start.37 = (bf16[128,1024]{1,0:T(8,128)(2,1)S(1)}, bf16[128,1024]{1,0:T(8,128)(2,1)S(1)}, u32[]{:S(2)}, u32[]{:S(2)}) collective-permute-start(bf16[128,1024]{1,0:T(8,128)(2,1)S(1)} %copy-done.49), channel_id=1, source_target_pairs={{0,16},{4,20},{8,24},{12,28},{16,0},{20,4},{24,8},{28,12},{1,17},{... | collective-permute-start | bytes 786440 | tf_op jit(solution)/shard_map/ppermute | solution.py:465
  129.4 24.6 %collective-permute-start.38 = (bf16[128,1024]{1,0:T(8,128)(2,1)S(1)}, bf16[128,1024]{1,0:T(8,128)(2,1)S(1)}, u32[]{:S(2)}, u32[]{:S(2)}) collective-permute-start(bf16[128,1024]{1,0:T(8,128)(2,1)S(1)} %copy-done.49), channel_id=1, source_target_pairs={{0,24},{4,28},{8,16},{12,20},{16,8},{20,12},{24,0},{28,4},{1,25},{... | collective-permute-start | bytes 786440 | tf_op jit(solution)/shard_map/ppermute | solution.py:465
  155.3 20.7 %collective-permute-start.43 = (bf16[2,128,1024]{2,1,0:T(8,128)(2,1)S(1)}, bf16[2,128,1024]{2,1,0:T(8,128)(2,1)S(1)}, u32[]{:S(2)}, u32[]{:S(2)}) collective-permute-start(bf16[2,128,1024]{2,1,0:T(8,128)(2,1)S(1)} %pad_maximum_fusion.1), channel_id=1, source_target_pairs={{0,4},{4,0},{8,12},{12,8},{16,20},{20,16},{24,28},{28,24},{1,5},{5... | collective-permute-start | bytes 1572872 | tf_op jit(solution)/shard_map/ppermute | solution.py:465
  158.2 17.8 %collective-permute-start.41 = (bf16[256,1024]{1,0:T(8,128)(2,1)S(1)}, bf16[256,1024]{1,0:T(8,128)(2,1)S(1)}, u32[]{:S(2)}, u32[]{:S(2)}) collective-permute-start(bf16[256,1024]{1,0:T(8,128)(2,1)S(1)} %add_convert_fusion.refs_0_), channel_id=1, source_target_pairs={{0,2},{1,3},{2,0},{3,1},{4,6},{5,7},{6,4},{7,5},{8,10},{9,11},{10,... | collective-permute-start | bytes 1572872 | tf_op jit(solution)/shard_map/ppermute | solution.py:26
  159.6 15.7 %collective-permute-start.42 = (bf16[128,1024]{1,0:T(8,128)(2,1)S(1)}, bf16[128,1024]{1,0:T(8,128)(2,1)S(1)}, u32[]{:S(2)}, u32[]{:S(2)}) collective-permute-start(bf16[128,1024]{1,0:T(8,128)(2,1)S(1)} %collective-permute-done.36.refs_1_), channel_id=1, source_target_pairs={{0,4},{4,0},{8,12},{12,8},{16,20},{20,16},{24,28},{28,24},{1,5},{5... | collective-permute-start | bytes 786440 | tf_op jit(solution)/shard_map/ppermute | solution.py:465
  160.1 17.0 %collective-permute-start.54 = (bf16[256,1024]{1,0:T(8,128)(2,1)}, bf16[256,1024]{1,0:T(8,128)(2,1)S(1)}, u32[]{:S(2)}, u32[]{:S(2)}) collective-permute-start(bf16[256,1024]{1,0:T(8,128)(2,1)} %bitcast.14.refs_0_), channel_id=1, source_target_pairs={{0,1},{1,0},{2,3},{3,2},{4,5},{5,4},{6,7},{7,6},{8,9},{9,8},{10,11... | collective-permute-start | bytes 1572872 | tf_op jit(solution)/shard_map/ppermute | solution.py:26
  160.1 19.3 %collective-permute-start.55 = (bf16[256,1024]{1,0:T(8,128)(2,1)}, bf16[256,1024]{1,0:T(8,128)(2,1)S(1)}, u32[]{:S(2)}, u32[]{:S(2)}) collective-permute-start(bf16[256,1024]{1,0:T(8,128)(2,1)} %collective-permute-done.24.refs_1_), channel_id=1, source_target_pairs={{0,1},{1,0},{2,3},{3,2},{4,5},{5,4},{6,7},{7,6},{8,9},{9,8},{10,11... | collective-permute-start | bytes 1572872 | tf_op jit(solution)/shard_map/ppermute | solution.py:26
  176.0 13.8 %collective-permute-start.44 = (bf16[256,1024]{1,0:T(8,128)(2,1)S(1)}, bf16[256,1024]{1,0:T(8,128)(2,1)S(1)}, u32[]{:S(2)}, u32[]{:S(2)}) collective-permute-start(bf16[256,1024]{1,0:T(8,128)(2,1)S(1)} %add_convert_fusion.refs_0_), channel_id=1, source_target_pairs={{0,1},{1,0},{2,3},{3,2},{4,5},{5,4},{6,7},{7,6},{8,9},{9,8},{10,11... | collective-permute-start | bytes 1572872 | tf_op jit(solution)/shard_map/ppermute | solution.py:26
  176.0 14.5 %collective-permute-start.45 = (bf16[256,1024]{1,0:T(8,128)(2,1)S(1)}, bf16[256,1024]{1,0:T(8,128)(2,1)S(1)}, u32[]{:S(2)}, u32[]{:S(2)}) collective-permute-start(bf16[256,1024]{1,0:T(8,128)(2,1)S(1)} %collective-permute-done.41.refs_1_), channel_id=1, source_target_pairs={{0,1},{1,0},{2,3},{3,2},{4,5},{5,4},{6,7},{7,6},{8,9},{9,8},{10,11... | collective-permute-start | bytes 1572872 | tf_op jit(solution)/shard_map/ppermute | solution.py:26
  177.1 14.1 %collective-permute-start.46 = (bf16[128,1024]{1,0:T(8,128)(2,1)S(1)}, bf16[128,1024]{1,0:T(8,128)(2,1)S(1)}, u32[]{:S(2)}, u32[]{:S(2)}) collective-permute-start(bf16[128,1024]{1,0:T(8,128)(2,1)S(1)} %copy-done.46), channel_id=1, source_target_pairs={{0,8},{4,12},{8,0},{12,4},{16,24},{20,28},{24,16},{28,20},{1,9},{5... | collective-permute-start | bytes 786440 | tf_op jit(solution)/shard_map/ppermute | solution.py:465
  179.4 20.9 %collective-permute-start.47 = (bf16[128,1024]{1,0:T(8,128)(2,1)S(1)}, bf16[128,1024]{1,0:T(8,128)(2,1)S(1)}, u32[]{:S(2)}, u32[]{:S(2)}) collective-permute-start(bf16[128,1024]{1,0:T(8,128)(2,1)S(1)} %copy-done.46), channel_id=1, source_target_pairs={{0,16},{4,20},{8,24},{12,28},{16,0},{20,4},{24,8},{28,12},{1,17},{... | collective-permute-start | bytes 786440 | tf_op jit(solution)/shard_map/ppermute | solution.py:465
  185.5 14.8 %collective-permute-start.48 = (bf16[128,1024]{1,0:T(8,128)(2,1)S(1)}, bf16[128,1024]{1,0:T(8,128)(2,1)S(1)}, u32[]{:S(2)}, u32[]{:S(2)}) collective-permute-start(bf16[128,1024]{1,0:T(8,128)(2,1)S(1)} %copy-done.46), channel_id=1, source_target_pairs={{0,24},{4,28},{8,16},{12,20},{16,8},{20,12},{24,0},{28,4},{1,25},{... | collective-permute-start | bytes 786440 | tf_op jit(solution)/shard_map/ppermute | solution.py:465
  189.9 18.5 %collective-permute-start.50 = (bf16[128,1024]{1,0:T(8,128)(2,1)S(1)}, bf16[128,1024]{1,0:T(8,128)(2,1)S(1)}, u32[]{:S(2)}, u32[]{:S(2)}) collective-permute-start(bf16[128,1024]{1,0:T(8,128)(2,1)S(1)} %copy-done.46), channel_id=1, source_target_pairs={{0,4},{4,0},{8,12},{12,8},{16,20},{20,16},{24,28},{28,24},{1,5},{5... | collective-permute-start | bytes 786440 | tf_op jit(solution)/shard_map/ppermute | solution.py:465
  200.4 16.3 %collective-permute-start.52 = (bf16[2,128,1024]{2,1,0:T(8,128)(2,1)S(1)}, bf16[2,128,1024]{2,1,0:T(8,128)(2,1)S(1)}, u32[]{:S(2)}, u32[]{:S(2)}) collective-permute-start(bf16[2,128,1024]{2,1,0:T(8,128)(2,1)S(1)} %pad_maximum_fusion.2), channel_id=1, source_target_pairs={{0,4},{4,0},{8,12},{12,8},{16,20},{20,16},{24,28},{28,24},{1,5},{5... | collective-permute-start | bytes 1572872 | tf_op jit(solution)/shard_map/ppermute | solution.py:465
  201.9 14.8 %collective-permute-start.51 = (bf16[128,1024]{1,0:T(8,128)(2,1)S(1)}, bf16[128,1024]{1,0:T(8,128)(2,1)S(1)}, u32[]{:S(2)}, u32[]{:S(2)}) collective-permute-start(bf16[128,1024]{1,0:T(8,128)(2,1)S(1)} %collective-permute-done.46.refs_1_), channel_id=1, source_target_pairs={{0,4},{4,0},{8,12},{12,8},{16,20},{20,16},{24,28},{28,24},{1,5},{5... | collective-permute-start | bytes 786440 | tf_op jit(solution)/shard_map/ppermute | solution.py:465
  231.8 14.2 %collective-permute-start.58 = (bf16[2,128,1024]{2,1,0:T(8,128)(2,1)S(1)}, bf16[2,128,1024]{2,1,0:T(8,128)(2,1)S(1)}, u32[]{:S(2)}, u32[]{:S(2)}) collective-permute-start(bf16[2,128,1024]{2,1,0:T(8,128)(2,1)S(1)} %get-tuple-element.243), channel_id=1, source_target_pairs={{0,4},{4,0},{8,12},{12,8},{16,20},{20,16},{24,28},{28,24},{1,5},{5... | collective-permute-start | bytes 1572872 | tf_op jit(solution)/shard_map/ppermute | solution.py:465
  236.1 14.1 %collective-permute-start.57 = (bf16[256,1024]{1,0:T(8,128)(2,1)}, bf16[256,1024]{1,0:T(8,128)(2,1)}, u32[]{:S(2)}, u32[]{:S(2)}) collective-permute-start(bf16[256,1024]{1,0:T(8,128)(2,1)} %fusion.15), channel_id=1, source_target_pairs={{0,2},{1,3},{2,0},{3,1},{4,6},{5,7},{6,4},{7,5},{8,10},{9,11},{10,... | collective-permute-start | bytes 1572872 | tf_op jit(solution)/shard_map/ppermute | solution.py:26
  255.8 12.7 %collective-permute-start.60 = (bf16[256,1024]{1,0:T(8,128)(2,1)S(1)}, bf16[256,1024]{1,0:T(8,128)(2,1)S(1)}, u32[]{:S(2)}, u32[]{:S(2)}) collective-permute-start(bf16[256,1024]{1,0:T(8,128)(2,1)S(1)} %get-tuple-element.341.refs_0_), channel_id=1, source_target_pairs={{0,1},{1,0},{2,3},{3,2},{4,5},{5,4},{6,7},{7,6},{8,9},{9,8},{10,11... | collective-permute-start | bytes 1572872 | tf_op jit(solution)/shard_map/ppermute | solution.py:26
  255.8 14.7 %collective-permute-start.61 = (bf16[2,128,1024]{2,1,0:T(8,128)(2,1)S(1)}, bf16[2,128,1024]{2,1,0:T(8,128)(2,1)S(1)}, u32[]{:S(2)}, u32[]{:S(2)}) collective-permute-start(bf16[2,128,1024]{2,1,0:T(8,128)(2,1)S(1)} %copy-done.95), channel_id=1, source_target_pairs={{0,4},{4,0},{8,12},{12,8},{16,20},{20,16},{24,28},{28,24},{1,5},{5... | collective-permute-start | bytes 1572872 | tf_op jit(solution)/shard_map/ppermute | solution.py:465
  256.8 35.5 %collective-permute-start.64 = (bf16[2,128,1024]{2,1,0:T(8,128)(2,1)S(1)}, bf16[2,128,1024]{2,1,0:T(8,128)(2,1)S(1)}, u32[]{:S(2)}, u32[]{:S(2)}) collective-permute-start(bf16[2,128,1024]{2,1,0:T(8,128)(2,1)S(1)} %copy-done.93), channel_id=1, source_target_pairs={{0,4},{4,0},{8,12},{12,8},{16,20},{20,16},{24,28},{28,24},{1,5},{5... | collective-permute-start | bytes 1572872 | tf_op jit(solution)/shard_map/ppermute | solution.py:465
  258.6 26.3 %collective-permute-start.62 = (bf16[128,1024]{1,0:T(8,128)(2,1)S(1)}, bf16[128,1024]{1,0:T(8,128)(2,1)S(1)}, u32[]{:S(2)}, u32[]{:S(2)}) collective-permute-start(bf16[128,1024]{1,0:T(8,128)(2,1)S(1)} %get-tuple-element.252), channel_id=1, source_target_pairs={{0,16},{4,20},{8,24},{12,28},{16,0},{20,4},{24,8},{28,12},{1,17},{... | collective-permute-start | bytes 786440 | tf_op jit(solution)/shard_map/ppermute | solution.py:465
  266.6 18.4 %collective-permute-start.63 = (bf16[128,1024]{1,0:T(8,128)(2,1)S(1)}, bf16[128,1024]{1,0:T(8,128)(2,1)S(1)}, u32[]{:S(2)}, u32[]{:S(2)}) collective-permute-start(bf16[128,1024]{1,0:T(8,128)(2,1)S(1)} %get-tuple-element.253), channel_id=1, source_target_pairs={{0,24},{4,28},{8,16},{12,20},{16,8},{20,12},{24,0},{28,4},{1,25},{... | collective-permute-start | bytes 786440 | tf_op jit(solution)/shard_map/ppermute | solution.py:465
  292.9 16.0 %collective-permute-start.66 = (bf16[384,512]{1,0:T(8,128)(2,1)S(1)}, bf16[384,512]{1,0:T(8,128)(2,1)S(1)}, u32[]{:S(2)}, u32[]{:S(2)}) collective-permute-start(bf16[384,512]{1,0:T(8,128)(2,1)S(1)} %get-tuple-element.260), channel_id=1, source_target_pairs={{0,2},{1,3},{2,0},{3,1},{4,6},{5,7},{6,4},{7,5},{8,10},{9,11},{10,... | collective-permute-start | bytes 1179656 | tf_op jit(solution)/shard_map/ppermute | solution.py:26
  295.0 17.7 %collective-permute-start.71 = (bf16[128,1024]{1,0:T(8,128)(2,1)S(1)}, bf16[128,1024]{1,0:T(8,128)(2,1)S(1)}, u32[]{:S(2)}, u32[]{:S(2)}) collective-permute-start(bf16[128,1024]{1,0:T(8,128)(2,1)S(1)} %get-tuple-element.268), channel_id=1, source_target_pairs={{0,8},{4,12},{8,0},{12,4},{16,24},{20,28},{24,16},{28,20},{1,9},{5... | collective-permute-start | bytes 786440 | tf_op jit(solution)/shard_map/ppermute | solution.py:465
  301.3 21.4 %collective-permute-start.69 = (bf16[128,1024]{1,0:T(8,128)(2,1)S(1)}, bf16[128,1024]{1,0:T(8,128)(2,1)S(1)}, u32[]{:S(2)}, u32[]{:S(2)}) collective-permute-start(bf16[128,1024]{1,0:T(8,128)(2,1)S(1)} %get-tuple-element.265), channel_id=1, source_target_pairs={{0,16},{4,20},{8,24},{12,28},{16,0},{20,4},{24,8},{28,12},{1,17},{... | collective-permute-start | bytes 786440 | tf_op jit(solution)/shard_map/ppermute | solution.py:465
  301.8 21.6 %collective-permute-start.70 = (bf16[128,1024]{1,0:T(8,128)(2,1)S(1)}, bf16[128,1024]{1,0:T(8,128)(2,1)S(1)}, u32[]{:S(2)}, u32[]{:S(2)}) collective-permute-start(bf16[128,1024]{1,0:T(8,128)(2,1)S(1)} %get-tuple-element.266), channel_id=1, source_target_pairs={{0,24},{4,28},{8,16},{12,20},{16,8},{20,12},{24,0},{28,4},{1,25},{... | collective-permute-start | bytes 786440 | tf_op jit(solution)/shard_map/ppermute | solution.py:465
  305.3 18.8 %collective-permute-start.68 = (bf16[2,128,1024]{2,1,0:T(8,128)(2,1)S(1)}, bf16[2,128,1024]{2,1,0:T(8,128)(2,1)S(1)}, u32[]{:S(2)}, u32[]{:S(2)}) collective-permute-start(bf16[2,128,1024]{2,1,0:T(8,128)(2,1)S(1)} %get-tuple-element.262), channel_id=1, source_target_pairs={{0,4},{4,0},{8,12},{12,8},{16,20},{20,16},{24,28},{28,24},{1,5},{5... | collective-permute-start | bytes 1572872 | tf_op jit(solution)/shard_map/ppermute | solution.py:465
  308.8 16.1 %collective-permute-start.67 = (bf16[256,1024]{1,0:T(8,128)(2,1)}, bf16[256,1024]{1,0:T(8,128)(2,1)}, u32[]{:S(2)}, u32[]{:S(2)}) collective-permute-start(bf16[256,1024]{1,0:T(8,128)(2,1)} %get-tuple-element.261.refs_0_), channel_id=1, source_target_pairs={{0,2},{1,3},{2,0},{3,1},{4,6},{5,7},{6,4},{7,5},{8,10},{9,11},{10,... | collective-permute-start | bytes 1572872 | tf_op jit(solution)/shard_map/ppermute | solution.py:26
  313.3 39.3 %collective-permute-start.75 = (bf16[4,192,1024]{2,1,0:T(8,128)(2,1)}, bf16[4,192,1024]{2,1,0:T(8,128)(2,1)}, u32[]{:S(2)}, u32[]{:S(2)}) collective-permute-start(bf16[4,192,1024]{2,1,0:T(8,128)(2,1)} %shard_map.259), channel_id=1, source_target_pairs={{0,4},{4,0},{8,12},{12,8},{16,20},{20,16},{24,28},{28,24},{1,5},{5... | collective-permute-start | bytes 4718600 | tf_op jit(solution)/shard_map/ppermute | solution.py:465
  328.0 26.7 %collective-permute-start.53 = (bf16[512,1024]{1,0:T(8,128)(2,1)S(1)}, bf16[512,1024]{1,0:T(8,128)(2,1)S(1)}, u32[]{:S(2)}, u32[]{:S(2)}) collective-permute-start(bf16[512,1024]{1,0:T(8,128)(2,1)S(1)} %convolution_convert_fusion.5), channel_id=1, source_target_pairs={{0,1},{1,0},{2,3},{3,2},{4,5},{5,4},{6,7},{7,6},{8,9},{9,8},{10,11... | collective-permute-start | bytes 3145736 | tf_op jit(solution)/shard_map/ppermute | solution.py:26
  329.9 19.4 %collective-permute-start.74 = (bf16[128,1024]{1,0:T(8,128)(2,1)S(1)}, bf16[128,1024]{1,0:T(8,128)(2,1)S(1)}, u32[]{:S(2)}, u32[]{:S(2)}) collective-permute-start(bf16[128,1024]{1,0:T(8,128)(2,1)S(1)} %get-tuple-element.272), channel_id=1, source_target_pairs={{0,8},{4,12},{8,0},{12,4},{16,24},{20,28},{24,16},{28,20},{1,9},{5... | collective-permute-start | bytes 786440 | tf_op jit(solution)/shard_map/ppermute | solution.py:465
  354.7 20.7 %collective-permute-start.76 = (bf16[512,1024]{1,0:T(8,128)(2,1)}, bf16[512,1024]{1,0:T(8,128)(2,1)}, u32[]{:S(2)}, u32[]{:S(2)}) collective-permute-start(bf16[512,1024]{1,0:T(8,128)(2,1)} %convolution_convert_fusion.2), channel_id=1, source_target_pairs={{0,1},{1,0},{2,3},{3,2},{4,5},{5,4},{6,7},{7,6},{8,9},{9,8},{10,11... | collective-permute-start | bytes 3145736 | tf_op jit(solution)/shard_map/ppermute | solution.py:26
  357.6 14.6 %collective-permute-start.59 = (bf16[256,1024]{1,0:T(8,128)(2,1)}, bf16[256,1024]{1,0:T(8,128)(2,1)}, u32[]{:S(2)}, u32[]{:S(2)}) collective-permute-start(bf16[256,1024]{1,0:T(8,128)(2,1)} %fusion.14), channel_id=1, source_target_pairs={{0,2},{1,3},{2,0},{3,1},{4,6},{5,7},{6,4},{7,5},{8,10},{9,11},{10,... | collective-permute-start | bytes 1572872 | tf_op jit(solution)/shard_map/ppermute | solution.py:26
  374.4 20.5 %collective-permute-start.78 = (bf16[4,128,768]{2,1,0:T(8,128)(2,1)}, bf16[4,128,768]{2,1,0:T(8,128)(2,1)}, u32[]{:S(2)}, u32[]{:S(2)}) collective-permute-start(bf16[4,128,768]{2,1,0:T(8,128)(2,1)} %dynamic-slice_bitcast_fusion), channel_id=1, source_target_pairs={{0,4},{4,0},{8,12},{12,8},{16,20},{20,16},{24,28},{28,24},{1,5},{5... | collective-permute-start | bytes 2359304 | tf_op jit(solution)/shard_map/ppermute | solution.py:465
  378.5 16.5 %collective-permute-start.77 = (bf16[256,1024]{1,0:T(8,128)(2,1)}, bf16[256,1024]{1,0:T(8,128)(2,1)}, u32[]{:S(2)}, u32[]{:S(2)}) collective-permute-start(bf16[256,1024]{1,0:T(8,128)(2,1)} %fusion.12), channel_id=1, source_target_pairs={{0,2},{1,3},{2,0},{3,1},{4,6},{5,7},{6,4},{7,5},{8,10},{9,11},{10,... | collective-permute-start | bytes 1572872 | tf_op jit(solution)/shard_map/ppermute | solution.py:26
  392.8 12.8 %collective-permute-start.92 = (bf16[128,1024]{1,0:T(8,128)(2,1)}, bf16[128,1024]{1,0:T(8,128)(2,1)S(1)}, u32[]{:S(2)}, u32[]{:S(2)}) collective-permute-start(bf16[128,1024]{1,0:T(8,128)(2,1)} %get-tuple-element.319), channel_id=1, source_target_pairs={{0,2},{1,3},{2,0},{3,1},{4,6},{5,7},{6,4},{7,5},{8,10},{9,11},{10,... | collective-permute-start | bytes 786440 | tf_op jit(solution)/shard_map/ppermute | solution.py:26
  398.9 14.9 %collective-permute-start.94 = (f32[6,2,256]{2,1,0:T(2,128)S(1)}, f32[6,2,256]{2,1,0:T(2,128)S(1)}, u32[]{:S(2)}, u32[]{:S(2)}) collective-permute-start(f32[6,2,256]{2,1,0:T(2,128)S(1)} %bitcast.174), channel_id=1, source_target_pairs={{0,1},{1,0},{2,3},{3,2},{4,5},{5,4},{6,7},{7,6},{8,9},{9,8},{10,11... | collective-permute-start | bytes 36872 | tf_op jit(solution)/shard_map/ppermute | solution.py:26
  409.3 24.9 %collective-permute-start.86 = (bf16[256,1024]{1,0:T(8,128)(2,1)S(1)}, bf16[256,1024]{1,0:T(8,128)(2,1)S(1)}, u32[]{:S(2)}, u32[]{:S(2)}) collective-permute-start(bf16[256,1024]{1,0:T(8,128)(2,1)S(1)} %get-tuple-element.293), channel_id=1, source_target_pairs={{0,8},{4,12},{8,0},{12,4},{16,24},{20,28},{24,16},{28,20},{1,9},{5... | collective-permute-start | bytes 1572872 | tf_op jit(solution)/shard_map/ppermute | solution.py:465
  410.2 38.2 %collective-permute-start.87 = (bf16[256,1024]{1,0:T(8,128)(2,1)S(1)}, bf16[256,1024]{1,0:T(8,128)(2,1)S(1)}, u32[]{:S(2)}, u32[]{:S(2)}) collective-permute-start(bf16[256,1024]{1,0:T(8,128)(2,1)S(1)} %get-tuple-element.294), channel_id=1, source_target_pairs={{0,16},{4,20},{8,24},{12,28},{16,0},{20,4},{24,8},{28,12},{1,17},{... | collective-permute-start | bytes 1572872 | tf_op jit(solution)/shard_map/ppermute | solution.py:465
  411.8 36.5 %collective-permute-start.88 = (bf16[256,1024]{1,0:T(8,128)(2,1)S(1)}, bf16[256,1024]{1,0:T(8,128)(2,1)S(1)}, u32[]{:S(2)}, u32[]{:S(2)}) collective-permute-start(bf16[256,1024]{1,0:T(8,128)(2,1)S(1)} %get-tuple-element.295), channel_id=1, source_target_pairs={{0,24},{4,28},{8,16},{12,20},{16,8},{20,12},{24,0},{28,4},{1,25},{... | collective-permute-start | bytes 1572872 | tf_op jit(solution)/shard_map/ppermute | solution.py:465
  413.8 50.3 %collective-permute-start.95 = (f32[6,256]{1,0:T(8,128)S(1)}, f32[6,256]{1,0:T(8,128)S(1)}, u32[]{:S(2)}, u32[]{:S(2)}) collective-permute-start(f32[6,256]{1,0:T(8,128)S(1)} %bitcast.175), channel_id=1, source_target_pairs={{0,2},{1,3},{2,0},{3,1},{4,6},{5,7},{6,4},{7,5},{8,10},{9,11},{10,... | collective-permute-start | bytes 18440 | tf_op jit(solution)/shard_map/ppermute | solution.py:26
  449.6 27.1 %collective-permute-start.89 = (bf16[64,1024]{1,0:T(8,128)(2,1)S(1)}, bf16[64,1024]{1,0:T(8,128)(2,1)S(1)}, u32[]{:S(2)}, u32[]{:S(2)}) collective-permute-start(bf16[64,1024]{1,0:T(8,128)(2,1)S(1)} %get-tuple-element.301), channel_id=1, source_target_pairs={{0,4},{4,0},{8,12},{12,8},{16,20},{20,16},{24,28},{28,24},{1,5},{5... | collective-permute-start | bytes 393224 | tf_op jit(solution)/shard_map/ppermute | solution.py:465
  450.7 28.2 %collective-permute-start.81 = (bf16[128,768]{1,0:T(8,128)(2,1)S(1)}, bf16[128,768]{1,0:T(8,128)(2,1)S(1)}, u32[]{:S(2)}, u32[]{:S(2)}) collective-permute-start(bf16[128,768]{1,0:T(8,128)(2,1)S(1)} %get-tuple-element.284), channel_id=1, source_target_pairs={{0,8},{4,12},{8,0},{12,4},{16,24},{20,28},{24,16},{28,20},{1,9},{5... | collective-permute-start | bytes 589832 | tf_op jit(solution)/shard_map/ppermute | solution.py:465
  461.8 17.2 %collective-permute-start.82 = (bf16[128,768]{1,0:T(8,128)(2,1)S(1)}, bf16[128,768]{1,0:T(8,128)(2,1)S(1)}, u32[]{:S(2)}, u32[]{:S(2)}) collective-permute-start(bf16[128,768]{1,0:T(8,128)(2,1)S(1)} %get-tuple-element.285), channel_id=1, source_target_pairs={{0,16},{4,20},{8,24},{12,28},{16,0},{20,4},{24,8},{28,12},{1,17},{... | collective-permute-start | bytes 589832 | tf_op jit(solution)/shard_map/ppermute | solution.py:465
  462.2 16.8 %collective-permute-start.83 = (bf16[128,768]{1,0:T(8,128)(2,1)S(1)}, bf16[128,768]{1,0:T(8,128)(2,1)S(1)}, u32[]{:S(2)}, u32[]{:S(2)}) collective-permute-start(bf16[128,768]{1,0:T(8,128)(2,1)S(1)} %get-tuple-element.286), channel_id=1, source_target_pairs={{0,24},{4,28},{8,16},{12,20},{16,8},{20,12},{24,0},{28,4},{1,25},{... | collective-permute-start | bytes 589832 | tf_op jit(solution)/shard_map/ppermute | solution.py:465
  (148 other events, 1279.9 us)

commit v4 on v3

--- a/solution.py
+++ b/solution.py
@@ -340,7 +340,7 @@
 
 def call(body, outs, operands, scratch=(), resident=False, own_copies=0):
     vmem = pl.BlockSpec(memory_space=pltpu.VMEM)
-    spec = vmem if resident else pl.BlockSpec(memory_space=pl.ANY)
+    spec = vmem if resident else pl.BlockSpec(memory_space=pltpu.HBM)
     scratch = list(scratch)
     if own_copies:
         scratch.append(pltpu.SemaphoreType.DMA((own_copies,)))
@@ -360,57 +360,39 @@
     )(*operands)
 
 
-def weight_block(row_ref, left, right, last_ref, first_ref, kept_ref):
-    step = pl.program_id(0)
-    value = mm(left[...], right[...], 0, 0).astype(LOW)
-
-    @pl.when(step < 2)
+def weight_block(left_a, right_a, left_b, right_b, out_ref):
+    @pl.when(pl.program_id(0) == 0)
     def _():
-        last_ref[0] = value
-
-    @pl.when((step >= 2) & (step < 4))
+        out_ref[...] = mm(left_a[...], right_a[...], 0, 0).astype(LOW)
+
+    @pl.when(pl.program_id(0) == 1)
     def _():
-        first_ref[0] = value
-
-    @pl.when(step >= 4)
-    def _():
-        kept_ref[0] = value
-
-
-def weight_grad(row, left, right):
-    count, rows = left.shape
-    columns = right.shape[1]
-    tile = rows // 8
-
-    def owner(step, row_ref):
-        k = jnp.where(step < 4, step ^ 2, step - 4)
-        away = jnp.where(step < 4, 1, 0)
-        return row_ref[0] ^ (2 * k) ^ away
-
-    def parked(first, number):
-        return pl.BlockSpec(
-            (1, tile, columns), lambda s, r: (jnp.clip(s - first, 0, number - 1), 0, 0)
-        )
-
+        out_ref[...] = mm(left_b[...], right_b[...], 0, 0).astype(LOW)
+
+
+def weight_grads(left_a, right_a, left_b, right_b):
+    count, rows = left_a.shape
+    columns = right_a.shape[1]
+    tile = 256
+    last = rows // tile - 1
     return pl.pallas_call(
         weight_block,
-        grid_spec=pltpu.PrefetchScalarGridSpec(
-            num_scalar_prefetch=1,
-            grid=(8,),
-            in_specs=[
-                pl.BlockSpec((count, tile), lambda s, r: (0, owner(s, r))),
-                pl.BlockSpec((count, columns), lambda s, r: (0, 0)),
-            ],
-            out_specs=[parked(0, 2), parked(2, 2), parked(4, 4)],
-        ),
-        out_shape=[shaped((n, tile, columns), LOW) for n in (2, 2, 4)],
+        grid=(2, rows // tile),
+        out_shape=shaped((rows, 2 * columns), LOW),
+        in_specs=[
+            pl.BlockSpec((count, tile), lambda w, i: (0, jnp.where(w == 0, i, last))),
+            pl.BlockSpec((count, columns), lambda w, i: (0, 0)),
+            pl.BlockSpec((count, tile), lambda w, i: (0, jnp.where(w == 0, 0, i))),
+            pl.BlockSpec((count, columns), lambda w, i: (0, 0)),
+        ],
+        out_specs=pl.BlockSpec((tile, columns), lambda w, i: (i, w)),
         cost_estimate=pl.CostEstimate(
-            flops=2 * count * rows * columns,
-            bytes_accessed=2 * count * (rows + columns) + 2 * rows * columns,
+            flops=4 * count * rows * columns,
+            bytes_accessed=4 * count * (rows + columns) + 4 * rows * columns,
             transcendentals=0,
         ),
         compiler_params=pltpu.CompilerParams(vmem_limit_bytes=48 << 20),
-    )(row.astype(jnp.int32).reshape(1), left, right)
+    )(left_a, right_a, left_b, right_b)
 
 
 def shaped(shape, dtype):
@@ -506,17 +488,19 @@
 
 def place_line_pieces(ids_ref, *refs):
     far = ids_ref[1] >> 1
-    height = refs[0].shape[0]
+    height = refs[0].shape[0] // 2
     pairs = []
     for k in range(4):
         start = pl.multiple_of((far ^ k) * height, height)
-        pairs.append((refs[k], refs[4].at[pl.ds(start, height)]))
-    copy_all(pairs, refs[5])
-
-
-def place_line(ids, *pieces):
-    whole = shaped((4 * pieces[0].shape[0], pieces[0].shape[1]), LOW)
-    return call(place_line_pieces, [whole], (ids, *pieces), own_copies=4)[0]
+        for index in range(2):
+            piece = refs[k].at[index * height : (index + 1) * height]
+            pairs.append((piece, refs[4 + index].at[pl.ds(start, height)]))
+    copy_all(pairs, refs[6])
+
+
+def place_lines(ids, *pieces):
+    whole = shaped((2 * pieces[0].shape[0], pieces[0].shape[1]), LOW)
+    return call(place_line_pieces, [whole] * 2, (ids, *pieces), own_copies=8)
 
 
 def three_ways(block):
@@ -565,37 +549,50 @@
     return column + zero.shape[1]
 
 
-def deal_first_core(ids, self_in, self_out, cross_out, kept, sent):
+def deal_first_core(ids, self_in, self_out, cross_out, norms, kept, sent):
     core, _, _, _ = device_bits(ids)
-    column = 0
+    depth = self_in.shape[0]
     for y in range(2):
         for j in range(3):
-            first = (4 * j + 2 * y) * 64
+            first, column = (4 * j + 2 * y) * 64, (3 * y + j) * 64
             zero, one = self_in[:, first : first + 64], self_in[:, first + 64 : first + 128]
-            column = keep_and_send(kept, sent, column, core, zero, one)
+            kept[:depth, column : column + 64] = choose(core, zero, one)
+            sent[:depth, column : column + 64] = choose(core, one, zero)
     for index, ref in enumerate((self_out, cross_out)):
         rows = slice(64 * index, 64 * (index + 1))
-        kept[rows, column:] = choose(core, ref[:64], ref[64:])
-        sent[rows, column:] = choose(core, ref[64:], ref[:64])
+        kept[rows, 384:] = choose(core, ref[:64], ref[64:])
+        sent[rows, 384:] = choose(core, ref[64:], ref[:64])
+    for ref in (kept, sent):
+        ref[depth:] = jnp.zeros_like(ref[depth:])
+        ref[depth : depth + norms.shape[0], :256] = norms[...]
 
 
 def deal_first_far(ids, kept, came, far_kept, far_sent):
     core, y, _, _ = device_bits(ids)
+    depth = 128
     column = 0
     sources = [choose(core, kept[...], came[...]), choose(core, came[...], kept[...])]
     for source in sources:
-        column = keep_and_send(far_kept, far_sent, column, y, source[:, :192], source[:, 192:384])
-    for source in sources:
-        put(far_kept, column, source[:, 384:])
-        put(far_sent, column, source[:, 384:])
+        columns = slice(column, column + 192)
+        zero, one = source[:depth, :192], source[:depth, 192:384]
+        far_kept[:depth, columns] = choose(y, zero, one)
+        far_sent[:depth, columns] = choose(y, one, zero)
+        column += 192
+    for index, source in enumerate(sources):
+        for ref in (far_kept, far_sent):
+            ref[:depth, column : column + 256] = source[:depth, 384:]
+            ref[depth:, index * 256 : (index + 1) * 256] = source[depth:, :256]
         column += 256
-
-
-def deal_first_last(ids, kept, came, mixed, lines):
+    for ref in (far_kept, far_sent):
+        ref[depth:, 512:] = jnp.zeros_like(ref[depth:, 512:])
+
+
+def deal_first_last(ids, kept, came, mixed, lines, norms):
     _, y, _, _ = device_bits(ids)
     zero, one = choose(y, kept[...], came[...]), choose(y, came[...], kept[...])
-    put(mixed, 0, zero[:, :384], one[:, :384])
-    put(lines, 0, zero[:, 384:], one[:, 384:])
+    put(mixed, 0, zero[:128, :384], one[:128, :384])
+    put(lines, 0, zero[:128, 384:], one[:128, 384:])
+    put(norms, 0, zero[128:, :512], one[128:, :512])
 
 
 def deal_rest_core(ids, query, pairs, up, down, kept, sent):
@@ -634,11 +631,10 @@
         column += 128
 
 
-def deal_rest_last(ids, kept, came, attend, up, down):
+def deal_rest_last(ids, kept, came, attend, ffn):
     _, y, _, _ = device_bits(ids)
     sources = [choose(y, kept[...], came[...]), choose(y, came[...], kept[...])]
-    put(up, 0, *[s[:, :512] for s in sources])
-    put(down, 0, *[s[:, 512:1024] for s in sources])
+    put(ffn, 0, *[s[:, :512] for s in sources], *[s[:, 512:1024] for s in sources])
     put(attend, 512, *[s[:, 1024:1280] for s in sources])
     for group in range(2):
         for place, source in enumerate(sources):
@@ -649,18 +645,18 @@
                 put(attend, group * 256 + (2 * place + c) * 64, choose(y, zero, one))
 
 
-def ffn_far(ids, *refs):
+def ffn_far(ids, value, kept, sent):
     _, y, _, _ = device_bits(ids)
-    kept, sent = refs[8:]
     for half in range(2):
-        value = total(refs[4 * half : 4 * half + 4])
-        put(kept, half * 512, choose(y, value[:, :512], value[:, 512:]))
-        put(sent, half * 512, choose(y, value[:, 512:], value[:, :512]))
+        zero = value[:, half * 1024 : half * 1024 + 512]
+        one = value[:, half * 1024 + 512 : half * 1024 + 1024]
+        put(kept, half * 512, choose(y, zero, one))
+        put(sent, half * 512, choose(y, one, zero))
 
 
 def ffn_core(ids, kept, came, core_kept, core_sent):
     core, y, _, _ = device_bits(ids)
-    mine, other = kept[...], came[...].astype(WIDE)
+    mine, other = kept[...], came[...]
     column = 0
     for source in (choose(y, mine, other), choose(y, other, mine)):
         for half in range(2):
@@ -673,14 +669,15 @@
 
 def ffn_last(ids, kept, came, up, down):
     core, _, _, _ = device_bits(ids)
-    mine, other = kept[...], came[...].astype(WIDE)
+    mine, other = kept[...], came[...]
     for c, source in enumerate((choose(core, mine, other), choose(core, other, mine))):
         for y in range(2):
             sender = 2 * y + c
             for r in range(2):
                 first = 512 * y + 128 * r
                 put(up, (4 * r + sender) * 128, source[:, first : first + 128])
-            down[sender * 128 : (sender + 1) * 128] = source[:, 512 * y + 256 : 512 * y + 512]
+            rows = slice(sender * 128, (sender + 1) * 128)
+            down[rows] = source[:, 512 * y + 256 : 512 * y + 512].astype(WIDE)
 
 
 def mixed_far(ids, own, a, b, c, kept, sent):
@@ -708,48 +705,67 @@
                 put(mixed, (4 * j + 2 * y + c) * 64, source[:, first : first + 64])
 
 
-def attend_x(ids, query, pairs, cross, sent):
+def attend_x(ids, query, cross, sent):
     _, y, x, _ = device_bits(ids)
     for z in range(4):
         start = pl.multiple_of((2 * z + 1 - x) * 128, 128)
         line = pl.multiple_of(((y ^ x ^ 1) * 4 + z) * 64, 64)
-        sent[z, :128, :512] = query[pl.ds(start, 128)]
-        sent[z, :128, 512:] = pairs[pl.ds(start, 128)]
-        sent[z, 128:] = cross[pl.ds(line, 64)]
-
-
-def attend_z(ids, query, pairs, cross, self_out, came, own, a, b, c):
+        sent[z, :, :512] = query[pl.ds(start, 128)]
+        sent[z, :64, 512:] = cross[pl.ds(line, 64), :512]
+        sent[z, 64:, 512:] = cross[pl.ds(line, 64), 512:]
+
+
+def pairs_x(ids, pairs, sent):
+    _, _, x, _ = device_bits(ids)
+    for z in range(4):
+        sent[z] = pairs[pl.ds(pl.multiple_of((2 * z + 1 - x) * 128, 128), 128)]
+
+
+def attend_along_z(ids, query, cross, came, own, a, b, c):
     _, y, x, z = device_bits(ids)
     for k, ref in enumerate((own, a, b, c)):
         owner = z ^ k
         start = pl.multiple_of((2 * owner + x) * 128, 128)
         line = pl.multiple_of(((y ^ x) * 4 + owner) * 64, 64)
+        moved = came[owner].astype(WIDE)
+        value = query[pl.ds(start, 128)].astype(WIDE) + moved[:, :512]
+        ref[:, :512] = value.astype(ref.dtype)
+        value = cross[pl.ds(line, 64)].astype(WIDE)
+        ref[:64, 512:] = (value[:, :512] + moved[:64, 512:]).astype(ref.dtype)
+        ref[64:, 512:] = (value[:, 512:] + moved[64:, 512:]).astype(ref.dtype)
+
+
+def pairs_along_z(ids, pairs, self_out, came, own, a, b, c):
+    _, _, x, z = device_bits(ids)
+    for k, ref in enumerate((own, a, b, c)):
+        owner = z ^ k
+        start = pl.multiple_of((2 * owner + x) * 128, 128)
         below = pl.multiple_of(owner * 64, 64)
-        moved = came[owner].astype(WIDE)
-        value = query[pl.ds(start, 128)].astype(WIDE) + moved[:128, :512]
-        ref[:128, :512] = value.astype(ref.dtype)
-        value = pairs[pl.ds(start, 128)].astype(WIDE) + moved[:128, 512:]
-        ref[:128, 512:] = value.astype(ref.dtype)
-        value = cross[pl.ds(line, 64)].astype(WIDE) + moved[128:]
-        ref[128:192] = value.astype(ref.dtype)
-        ref[192:] = self_out[pl.ds(below, 64)].astype(ref.dtype)
-
-
-def attend_total(ids, own, a, b, c, value, line):
-    value[...] = total((own, a, b, c))
-    line[...] = value[192:].astype(LOW)
+        value = pairs[pl.ds(start, 128)].astype(WIDE) + came[owner].astype(WIDE)
+        ref[:, :512] = value.astype(ref.dtype)
+        ref[:64, 512:] = self_out[pl.ds(below, 64), :512].astype(ref.dtype)
+        ref[64:, 512:] = self_out[pl.ds(below, 64), 512:].astype(ref.dtype)
+
+
+def attend_total(ids, *refs):
+    value, line = refs[8:]
+    value[:, :1024] = total(refs[:4])
+    value[:, 1024:] = total(refs[4:8])
+    line[...] = value[:, 1536:].astype(LOW)
 
 
 def attend_far(ids, value, line, kept, sent):
     _, y, _, _ = device_bits(ids)
-    lines = jnp.concatenate([value[192:] + line[...].astype(WIDE), value[128:192]], axis=0)
-    put(kept, 0, choose(y, lines[:, :512], lines[:, 512:]))
-    put(sent, 0, choose(y, lines[:, 512:], lines[:, :512]))
-    mine, other = value[:128, :256], value[:128, 256:512]
+    own = value[:, 1536:] + line[...].astype(WIDE)
+    low_half = jnp.concatenate([own[:64], value[:64, 512:1024]], axis=0)
+    high_half = jnp.concatenate([own[64:], value[64:, 512:1024]], axis=0)
+    put(kept, 0, choose(y, low_half, high_half))
+    put(sent, 0, choose(y, high_half, low_half))
+    mine, other = value[:, :256], value[:, 256:512]
     for index, group in enumerate((choose(y, mine, other), choose(y, other, mine))):
         put(kept, 512 + 128 * index, choose(y, group[:, :128], group[:, 128:]))
         put(sent, 512 + 128 * index, choose(y, group[:, 128:], group[:, :128]))
-    pairs = value[:128, 512:]
+    pairs = value[:, 1024:1536]
     put(kept, 768, choose(y, pairs[:, :256], pairs[:, 256:]))
     put(sent, 768, choose(y, pairs[:, 256:], pairs[:, :256]))
 
@@ -789,34 +805,12 @@
     return [row_swap(v, 2 * (k + 1)) for k, v in enumerate(values)]
 
 
-def add_parts(first, ids, kept, came, *outs):
-    for index, out in enumerate(outs):
-        value = kept[first + index].astype(WIDE) + came[index].astype(WIDE)
-        out[...] = value.astype(out.dtype)
-
-
-def return_ffn(ids, up, down):
+def return_ffn(ids, sums):
     low = lambda *shape: shaped(shape, LOW)
     wide = lambda *shape: shaped(shape, WIDE)
-    kept, sent = call(ffn_far, [wide(128, 1024), low(128, 1024)], (ids, *up, *down))
-    kept, sent = call(ffn_core, [wide(128, 1024), low(128, 1024)], (ids, kept, swap(sent, 2)))
+    kept, sent = call(ffn_far, [low(128, 1024)] * 2, (ids, sums))
+    kept, sent = call(ffn_core, [low(128, 1024)] * 2, (ids, kept, swap(sent, 2)))
     return call(ffn_last, [wide(128, 1024), wide(512, 256)], (ids, kept, swap(sent, 1)))
-
-
-def send_last(ids, kept, came):
-    second, third = call(
-        lambda *refs: add_parts(2, *refs), [shaped((128, 1024), LOW)] * 2, (ids, kept, came)
-    )
-    return row_swap(second, 4), row_swap(third, 6)
-
-
-def send_first(ids, kept, came):
-    own, part = call(
-        lambda *refs: add_parts(0, *refs),
-        [shaped((128, 1024), WIDE), shaped((128, 1024), LOW)],
-        (ids, kept, came),
-    )
-    return own, row_swap(part, 2)
 
 
 def return_mixed(ids, own, parts):
@@ -828,10 +822,10 @@
     return mixed
 
 
-def return_attend(ids, own, parts):
+def return_attend(ids, *parts):
     low = lambda *shape: shaped(shape, LOW)
     wide = lambda *shape: shaped(shape, WIDE)
-    value, line = call(attend_total, [wide(256, 1024), low(64, 1024)], (ids, own, *parts))
+    value, line = call(attend_total, [wide(128, 2048), low(128, 512)], (ids, *parts))
     kept, sent = call(
         attend_far, [wide(128, 1024), low(128, 1024)], (ids, value, row_swap(line, 1))
     )
@@ -911,84 +905,76 @@
     inner = width // WAYS
     low = lambda *shape: shaped(shape, LOW)
     wide = lambda *shape: shaped(shape, WIDE)
-    frames_wide = frames[0].astype(WIDE)
     marks = mask_marks(frame_segments[0], text_lengths[0])
 
-    kept, sent = call(deal_first_core, [low(128, 640)] * 2, (ids, self_in, self_out, cross_out))
     norms = jnp.concatenate([norm_gains, norm_biases], axis=0)
-    norms_far = swap(norms, 2)
-    kept, sent = call(deal_first_far, [low(128, 896)] * 2, (ids, kept, swap(sent, 1)))
-    norms = ordered(norms, norms_far, here >> 1)
-    norms = ordered(norms, swap(norms, 1), here & 1, 1)
-    norms = jnp.moveaxis(norms, 2, 0).reshape(6, width).astype(WIDE)
-    gains, biases = norms[:3], norms[3:]
-    one, hat_one, inverse_one = norm_forward(frames_wide, gains[0], biases[0])
+    kept, sent = call(
+        deal_first_core, [low(144, 640)] * 2, (ids, self_in, self_out, cross_out, norms)
+    )
+    kept, sent = call(deal_first_far, [low(144, 896)] * 2, (ids, kept, swap(sent, 1)))
     came = swap(sent, 2)
+    (frames_low,) = sync(frames[0], sent)[:1]
+    frames_wide = frames_low.astype(WIDE)
     rest = sync(cross_query, cross_kv, ffn_in, ffn_out, sent)[:4]
     rest_kept, rest_sent = call(deal_rest_core, [low(128, 1408)] * 2, (ids, *rest))
     rest_kept, rest_sent = call(
         deal_rest_far, [low(128, 1536)] * 2, (ids, rest_kept, swap(rest_sent, 1))
     )
-    mixed, lines = call(deal_first_last, [low(128, 768), low(128, 1024)], (ids, kept, came))
+    mixed, lines, norms = call(
+        deal_first_last, [low(128, 768), low(128, 1024), wide(16, 1024)], (ids, kept, came)
+    )
+    gains, biases = norms[:3], norms[3:6]
+    one, hat_one, inverse_one = norm_forward(frames_wide, gains[0], biases[0])
     mixed, lines, rest_sent, one = sync(mixed, lines, rest_sent, one)
     mixed_z = three_ways(mixed)
     mixed_x = row_swap(mixed, 1)
     lines_x = row_swap(lines, 1)
     rest_came = swap(rest_sent, 2)
     one_far, one_near = swap(one, 2), swap(one, 1)
-    attend, up_block, down_block = call(
-        deal_rest_last, [low(128, 1024)] * 3, (ids, rest_kept, rest_came)
+    attend, ffn_block = call(
+        deal_rest_last, [low(128, 1024), low(128, 2048)], (ids, rest_kept, rest_came)
     )
     lines = jnp.where((row & 1) == (here >> 1), lines, lines_x)
-    *mixed_z, mixed_x, attend, lines, text, grad = sync(
-        *mixed_z, mixed_x, attend, lines, text_states[0], out_grad[0]
+    *mixed_z, mixed_x, attend, lines, one_far, text, grad = sync(
+        *mixed_z, mixed_x, attend, lines, one_far, text_states[0], out_grad[0]
     )
     mixed_x1 = row_swap(mixed_z[0], 1)
     mixed_x2 = row_swap(jnp.stack(mixed_z[1:]), 1)
-    self_line, cross_line = lines[:64], lines[64:]
-    self_z = three_ways(sync(self_line, mixed_x1)[0])
-    attend_z1 = row_swap(sync(attend, mixed_x1)[0], 2)
+    attend_z = three_ways(attend)
     one_all = join(ids, one, one_far, one_near, swap(one_far, 1))
     text_far, text_near = swap(text, 2), swap(text, 1)
-    mixed_x1, mixed_x2, one_all, text_far, attend_z1, *self_z = sync(
-        mixed_x1, mixed_x2, one_all, text_far, attend_z1, *self_z
-    )
+    mixed_x1, mixed_x2, one_all, text_far = sync(mixed_x1, mixed_x2, one_all, text_far)
     (w_mixed,) = place(ids, (768,), [mixed, *mixed_z], [mixed_x, mixed_x1, mixed_x2])
-    attend, grad, cross_line = sync(attend, grad, cross_line, mixed_x2)[:3]
-    attend_z2, attend_z3 = row_swap(attend, 4), row_swap(attend, 6)
-    attend_x0, attend_x1 = row_swap(attend, 1), row_swap(attend_z1, 1)
+    mixed_low = mm(one_all, w_mixed).astype(LOW)
+    mixed_low, *attend_z, grad, attend, lines, ffn_block = sync(
+        mixed_low, *attend_z, grad, attend, lines, ffn_block
+    )
+    w_ffn = gather_rows(ffn_block)
+    lines_z = three_ways(lines)
+    attend_x0, attend_x1 = row_swap(attend, 1), row_swap(attend_z[0], 1)
+    attend_x2 = row_swap(jnp.stack(attend_z[1:]), 1)
     grad_far, grad_near = swap(grad, 2), swap(grad, 1)
-    mixed_low = mm(one_all, w_mixed).astype(LOW)
-    w_self = place_line(ids, self_line, *self_z)
-    text_all = join(ids, text, text_far, text_near, swap(text_far, 1))
     self_att, self_lse = call(
         self_forward, [low(count, inner), wide(4, count)], (ids, marks, mixed_low), resident=True
     )
-    self_att, w_self, text_all, attend_x1, grad_far, attend_z2, attend_z3, cross_line = sync(
-        self_att, w_self, text_all, attend_x1, grad_far, attend_z2, attend_z3, cross_line
-    )
-    attend_x2 = row_swap(jnp.stack([attend_z2, attend_z3]), 1)
-    cross_z = three_ways(cross_line)
-    received, attend_x2, *cross_z = scatter_slots(self_att, w_self, 0, None, (attend_x2, *cross_z))
+    text_all = join(ids, text, text_far, text_near, swap(text_far, 1))
+    self_att, text_all, *lines_z, attend_x0, attend_x1, attend_x2, grad_far = sync(
+        self_att, text_all, *lines_z, attend_x0, attend_x1, attend_x2, grad_far
+    )
+    w_self, w_cross = place_lines(ids, lines, *lines_z)
+    w_query, w_pairs = place(
+        ids, (512, 512), [attend, *attend_z], [attend_x0, attend_x1, attend_x2]
+    )
+    received = scatter_slots(self_att, w_self, 0)
     hidden = frames_wide + received
-    w_query, w_pairs = place(
-        ids,
-        (512, 512),
-        [attend, attend_z1, attend_z2, attend_z3],
-        [attend_x0, attend_x1, attend_x2],
-    )
     grad_all = join(ids, grad, grad_far, grad_near, swap(grad_far, 1))
-    (up_block,) = sync(up_block, attend_x2)[:1]
-    up_z = three_ways(up_block)
-    up_x = row_swap(up_block, 1)
+    text_count = text_all.shape[0]
+    pairs_own = mm(text_all, w_pairs).astype(LOW)
+    pairs_other = swap(pairs_own, 2)
+    w_cross_far = swap(sync(w_cross, pairs_own)[0], 2)
     two, hat_two, inverse_two = norm_forward(hidden, gains[1], biases[1])
     two_pair = gather_pair(two, ids)
     pair_count = two_pair.shape[0]
-    text_count = text_all.shape[0]
-    pairs_own = mm(text_all, w_pairs).astype(LOW)
-    pairs_other = swap(pairs_own, 2)
-    w_cross = place_line(ids, cross_line, *cross_z)
-    w_cross_far = swap(sync(w_cross, pairs_own)[0], 2)
     query = mm(two_pair, w_query).astype(LOW)
     cross_att, cross_lse = call(
         cross_forward,
@@ -996,72 +982,46 @@
         (ids, marks, query, pairs_own, pairs_other),
         resident=True,
     )
-    cross_att, *up_z = sync(cross_att, *up_z)
-    (down_block,) = sync(down_block, up_z[2])[:1]
-    up_x1 = row_swap(up_z[0], 1)
-    up_x2 = row_swap(jnp.stack(up_z[1:]), 1)
-    down_z = three_ways(down_block)
-    down_x = row_swap(down_block, 1)
     w_cross_both = join(ids, w_cross, w_cross_far)
     hidden_two = hidden + scatter_pair(cross_att, w_cross_both, 0)
     three, hat_three, inverse_three = norm_forward(hidden_two, gains[2], biases[2])
-    three_all, up_x1, up_x2 = gather_slots(three, ids, up_x1, up_x2)
-    (w_up,) = place(ids, (1024,), [up_block, *up_z], [up_x, up_x1, up_x2])
-    three_all, *down_z = sync(three_all, *down_z)
-    down_x1 = row_swap(down_z[0], 1)
-    down_x2 = row_swap(jnp.stack(down_z[1:]), 1)
+    three_all = gather_slots(three, ids)
+    w_up, w_down = w_ffn[:, :width], w_ffn[:, width:]
     activ, slope = gelu_parts(mm(three_all, w_up))
-    (w_down,) = place(ids, (1024,), [down_block, *down_z], [down_x, down_x1, down_x2])
-
-    last_down, first_down, kept_down = weight_grad(row, activ, grad_all)
-    last_down = row_swap(last_down, 1)
-    first_down = row_swap(first_down, 1)
+
     grad_up = (mm(grad_all, w_down, 1, 1) * slope).astype(LOW)
-    last_up, first_up, kept_up = weight_grad(row, three_all, grad_up)
-    grad_three, last_down, last_up, first_up = scatter_slots(
-        grad_up, w_up, 1, None, (last_down, last_up, first_up)
-    )
-    last_up = row_swap(last_up, 1)
-    down_two, down_three = send_last(ids, kept_down, last_down)
-    output = (hidden_two + scatter_slots(activ, w_down, 0, grad_three)).astype(LOW)
+    grad_three = scatter_slots(grad_up, w_up, 1)
+    ffn_sums = sum_rows(weight_grads(three_all, grad_up, activ, grad_all))
+    output_part = scatter_slots(activ, w_down, 0, grad_three)
     part, gain_three, bias_three = norm_backward(grad_three, hat_three, inverse_three, gains[2])
     grad_two = out_grad[0].astype(WIDE) + part
     branch_two = gather_pair(grad_two.astype(LOW), ids)
     grad_cross = mm(branch_two, w_cross_both, 1, 1).astype(LOW)
-    grad_cross, first_down, first_up, down_two, down_three = sync(
-        grad_cross, first_down, first_up, down_two, down_three
-    )
-    first_up = row_swap(first_up, 1)
-    down_own, down_one = send_first(ids, kept_down, first_down)
     grad_query, pairs_mine, pairs_away = call(
         cross_backward,
         [low(pair_count, 2 * inner)] + [low(text_count, 2 * inner)] * 2,
         (ids, marks, query, pairs_own, pairs_other, grad_cross, cross_lse),
         resident=True,
     )
-    grad_query, pairs_away, last_up = sync(grad_query, pairs_away, last_up)
+    grad_query, pairs_away, output_part = sync(grad_query, pairs_away, output_part)
+    output = (hidden_two + output_part).astype(LOW)
     pairs_came = swap(pairs_away, 2)
-    up_two, up_three = send_last(ids, kept_up, last_up)
     g_cross = mm(cross_att, branch_two, 0, 0).astype(LOW)
     g_query = mm(two_pair, grad_query, 0, 0).astype(LOW)
+    (attend_sent,) = call(attend_x, [low(4, 128, 1024)], (ids, g_query, g_cross))
+    attend_came = row_swap(attend_sent, 1)
     part, gain_two, bias_two = norm_backward(
         scatter_pair(grad_query, w_query, 1), hat_two, inverse_two, gains[1]
     )
     grad_hidden = grad_two + part
-    grad_low, pairs_came, g_cross, g_query = sync(
-        grad_hidden.astype(LOW), pairs_came, g_cross, g_query
-    )
+    grad_low, pairs_came = sync(grad_hidden.astype(LOW), pairs_came)
     grad_pairs = (pairs_mine.astype(WIDE) + pairs_came.astype(WIDE)).astype(LOW)
     g_pairs = mm(text_all, grad_pairs, 0, 0).astype(LOW)
-    (attend_sent,) = call(attend_x, [low(4, 192, 1024)], (ids, g_query, g_pairs, g_cross))
-    attend_came = row_swap(attend_sent, 1)
-    branch, first_up, up_two, up_three, down_one = gather_slots(
-        grad_low, ids, first_up, up_two, up_three, down_one
-    )
-    up_own, up_one = send_first(ids, kept_up, first_up)
-    text_grad = scatter_slots(grad_pairs, w_pairs, 1, branch)
+    (pairs_sent,) = call(pairs_x, [low(4, 128, 512)], (ids, g_pairs))
+    pairs_came = row_swap(pairs_sent, 1)
+    branch = gather_slots(grad_low, ids)
+    text_part = scatter_slots(grad_pairs, w_pairs, 1, branch)
     grad_self = mm(branch, w_self, 1, 1).astype(LOW)
-    g_self = mm(self_att, branch, 0, 0).astype(LOW)
     (grad_mixed,) = call(
         self_backward,
         [low(count, 3 * inner)],
@@ -1069,32 +1029,37 @@
         scratch=[pltpu.VMEM((count, 128), WIDE), pltpu.VMEM((count, 128), WIDE)],
         resident=True,
     )
-    grad_mixed, up_one = sync(grad_mixed, up_one)
+    g_self = mm(self_att, branch, 0, 0).astype(LOW)
     g_mixed = mm(one_all, grad_mixed, 0, 0).astype(LOW)
     mixed_sent = pick(g_mixed.reshape(4, 2, 128, 768), 1 - (row & 1), 1)
-    mixed_sent, grad_mixed, attend_came = sync(mixed_sent, grad_mixed, attend_came)
+    grad_mixed, g_self, mixed_sent, attend_came, pairs_came, text_part = sync(
+        grad_mixed, g_self, mixed_sent, attend_came, pairs_came, text_part
+    )
+    text_grad = text_part
+    sums = [wide(128, 1024)] + [low(128, 1024)] * 3
+    attend_own, *attend_parts = call(attend_along_z, sums, (ids, g_query, g_cross, attend_came))
+    attend_parts = along_z(attend_parts)
     mixed_came = row_swap(mixed_sent, 1)
-    attend_own, *attend_parts = call(
-        attend_z,
-        [wide(256, 1024)] + [low(256, 1024)] * 3,
-        (ids, g_query, g_pairs, g_cross, g_self, attend_came),
-    )
-    attend_parts = along_z(attend_parts)
-    grad_one, mixed_came = scatter_slots(grad_mixed, w_mixed, 1, None, (mixed_came,))
+    pairs_own, *pairs_parts = call(pairs_along_z, sums, (ids, g_pairs, g_self, pairs_came))
+    pairs_parts = along_z(pairs_parts)
+    grad_one, mixed_came, *attend_parts = scatter_slots(
+        grad_mixed, w_mixed, 1, None, (mixed_came, *attend_parts)
+    )
     mixed_own, *mixed_parts = call(
         split_sums, [wide(128, 768)] + [low(128, 768)] * 3, (ids, g_mixed, mixed_came)
     )
-    attend_own, *attend_parts, _ = sync(attend_own, *attend_parts, mixed_own)
     mixed_parts = along_z(mixed_parts)
+    mixed_own, grad_one, *pairs_parts = sync(mixed_own, grad_one, *pairs_parts)
     part, gain_one, bias_one = norm_backward(grad_one, hat_one, inverse_one, gains[0])
     frame_grad = grad_hidden + part
-    d_up, d_down = return_ffn(
-        ids, (up_own, up_one, up_two, up_three), (down_own, down_one, down_two, down_three)
-    )
+    ffn_sums, *mixed_parts = sync(ffn_sums, *mixed_parts)
+    d_up, d_down = return_ffn(ids, ffn_sums)
     norm_sums = reduce_norms(
         jnp.stack([gain_one, gain_two, gain_three, bias_one, bias_two, bias_three]), here
     )
-    d_self, d_query, d_pairs, d_cross = return_attend(ids, attend_own, attend_parts)
+    d_self, d_query, d_pairs, d_cross = return_attend(
+        ids, attend_own, *attend_parts, pairs_own, *pairs_parts
+    )
     d_mixed = return_mixed(ids, mixed_own, mixed_parts)
     return (
         output[None],

time: 503 us -> 452 us (0.90)
  starting transfers between devices: 122 us -> 73.4 us
  waiting for transfers between devices: 173 us -> 191 us
  between operations: 3.04 us -> 16.5 us
  local copies, waits for them, and re-layouts: 33.8 us -> 20.9 us
  matrix products: 56.5 us -> 44.4 us
  Pallas kernels: 93.5 us -> 86.4 us
    ppermute x53 -> x32, starting transfers between devices: 95 us -> 47.9 us  [row_swap(): return lax.ppermute(values, 'rows', [(i, i ^ mask) for i in range(size)])]
    ppermute x46 -> x44, waiting for transfers between devices: 50.5 us -> 75.5 us  [swap(): return lax.ppermute(values, 'text', [(i, i ^ mask) for i in range(WAYS)])]
    unnamed x242 -> x225, local copies, waits for them, and re-layouts: 31.3 us -> 18.5 us
    dot_general x31, matrix products: 56.5 us -> 44.4 us  [mm(): lax.dot_general(left, right, (((left_dim,), (right_dim,)), ((), ())), pre...]
    ppermute x53 -> x32, waiting for transfers between devices: 123 us -> 115 us  [row_swap(): return lax.ppermute(values, 'rows', [(i, i ^ mask) for i in range(size)])]
    pallas_call x41 -> x36, Pallas kernels: 81.1 us -> 76.3 us  [call(): pl.pallas_call(body, out_shape=outs, in_specs=[pl.BlockSpec(memory_space=...]
    pallas_call x2 -> x1, Pallas kernels: 12.4 us -> 10.1 us  [weight_grads(): pl.pallas_call(weight_block, grid=(2, rows // tile), out_shape=shaped((ro...]
    ppermute x46 -> x44, starting transfers between devices: 27 us -> 25.2 us  [swap(): return lax.ppermute(values, 'text', [(i, i ^ mask) for i in range(WAYS)])]
  transfers between devices with their start and end apart: 99 -> 78, of which waited for: 33 -> 32; matrix products, arithmetic and copies ran while one was open for 12% -> 11% of each run, Pallas kernels for 17% -> 18%
where the time goes in v4:
time: 452 us; the launch traced here: 446 us
  waiting for transfers between devices  191 us (42%)
  Pallas kernels  86.4 us (19%)
  starting transfers between devices  73.4 us (16%)
  matrix products  44.4 us (10%)
  local copies, waits for them, and re-layouts  20.9 us (5%)
  between operations  16.5 us (4%)
  other arithmetic  14.2 us (3%)
    ppermute x32, waiting for transfers between devices, row_swap(): return lax.ppermute(values, 'rows', [(i, i ^ mask) for i in range(size)])  115 us
    pallas_call x36, Pallas kernels, call(): pl.pallas_call(body, out_shape=outs, in_specs=[pl.BlockSpec(memory_space=...  76.3 us
    ppermute x44, waiting for transfers between devices, swap(): return lax.ppermute(values, 'text', [(i, i ^ mask) for i in range(WAYS)])  75.5 us
    ppermute x32, starting transfers between devices, row_swap(): return lax.ppermute(values, 'rows', [(i, i ^ mask) for i in range(size)])  47.9 us
    dot_general x31, matrix products, mm(): lax.dot_general(left, right, (((left_dim,), (right_dim,)), ((), ())), pre...  44.4 us
    ppermute x44, starting transfers between devices, swap(): return lax.ppermute(values, 'text', [(i, i ^ mask) for i in range(WAYS)])  25.2 us
    unnamed x225, local copies, waits for them, and re-layouts  18.5 us
    pallas_call x1, Pallas kernels, weight_grads(): pl.pallas_call(weight_block, grid=(2, rows // tile), out_shape=shaped((ro...  10.1 us
  transfers between devices with their start and end apart: 78, of which 32 were waited for; matrix products, arithmetic and copies ran while one was open for 11% of the time, Pallas kernels for 18%

profile of v4, /device:TPU:0, one launch (start us, length us, event | category | flops | bytes accessed | tf_op | source)
XLA Modules:
  0.0 446.3 jit_solution(11016382616956064974)
XLA Ops:
  14.9 2.9 collective-permute-start.1
  27.8 1.7 shard_map.233
  33.6 3.6 collective-permute-start.5
  37.2 3.6 collective-permute-done.8
  40.8 2.6 collective-permute-start.4
  45.0 1.9 shard_map.234
  47.0 6.4 %collective-permute-done.4.refs_2_ = bf16[128,768]{1,0:T(8,128)(2,1)S(1)} collective-permute-done((bf16[128,768]{1,0:T(8,128)(2,1)S(1)}, bf16[128,768]{1,0:T(8,128)(2,1)S(1)}, u32[]{:S(2)}, u32[]{:S(2)}) %collective-permute-start.4) | collective-permute-done | bytes 196640 | tf_op jit(solution)/shard_map/ppermute | solution.py:447
  56.1 2.7 collective-permute-start.17
  59.6 9.7 %collective-permute-done.10.refs_5_ = bf16[128,768]{1,0:T(8,128)(2,1)S(1)} collective-permute-done((bf16[128,768]{1,0:T(8,128)(2,1)S(1)}, bf16[128,768]{1,0:T(8,128)(2,1)S(1)}, u32[]{:S(2)}, u32[]{:S(2)}) %collective-permute-start.10) | collective-permute-done | bytes 196640 | tf_op jit(solution)/shard_map/ppermute | solution.py:447
  72.6 2.7 shard_map.236
  75.3 1.8 convolution_convert_fusion.1.mixed_ref
  77.1 7.0 %collective-permute-done.16.refs_2_ = bf16[128,1024]{1,0:T(8,128)(2,1)S(1)} collective-permute-done((bf16[128,1024]{1,0:T(8,128)(2,1)}, bf16[128,1024]{1,0:T(8,128)(2,1)S(1)}, u32[]{:S(2)}, u32[]{:S(2)}) %collective-permute-start.16) | collective-permute-done | bytes 262176 | tf_op jit(solution)/shard_map/ppermute | solution.py:447
  90.0 2.2 collective-permute-start.22
  94.9 4.5 %collective-permute-done.24.refs_5_ = bf16[128,1024]{1,0:T(8,128)(2,1)S(1)} collective-permute-done((bf16[128,1024]{1,0:T(8,128)(2,1)}, bf16[128,1024]{1,0:T(8,128)(2,1)S(1)}, u32[]{:S(2)}, u32[]{:S(2)}) %collective-permute-start.24) | collective-permute-done | bytes 262176 | tf_op jit(solution)/shard_map/ppermute | solution.py:447
  101.3 6.9 %shard_map.237 = (bf16[1024,256]{1,0:T(8,128)(2,1)S(1)}, f32[4,1024]{1,0:T(4,128)S(1)}) custom-call(s32[2]{0:T(128)S(1)} %pad_add_fusion.ids_ref._.here_ref, s32[8,1024]{1,0:T(8,128)S(1)} %stack.74.marks_ref, bf16[1024,768]{1,0:T(8,128)(2,1)S(1)} %convolution_convert_fusion.1.mixed_ref), custom_call_target="tpu_custom_call" | custom-call | bytes 2146312 | tf_op jit(solution)/shard_map/pallas_call | solution.py:352
  109.2 1.7 shard_map.238
  110.9 14.1 %collective-permute-done.21.refs_2_ = bf16[128,1024]{1,0:T(8,128)(2,1)} collective-permute-done((bf16[128,1024]{1,0:T(8,128)(2,1)S(1)}, bf16[128,1024]{1,0:T(8,128)(2,1)}, u32[]{:S(2)}, u32[]{:S(2)}) %collective-permute-start.21) | collective-permute-done | bytes 262176 | tf_op jit(solution)/shard_map/ppermute | solution.py:447
  125.1 2.2 shard_map.239
  127.8 2.6 collective-permute-done.27
  130.8 1.7 collective-permute-start.28
  132.5 2.0 shard_map.241
  135.6 10.0 %collective-permute-done.28 = bf16[256,1024]{1,0:T(8,128)(2,1)S(1)} collective-permute-done((bf16[256,1024]{1,0:T(8,128)(2,1)S(1)}, bf16[256,1024]{1,0:T(8,128)(2,1)S(1)}, u32[]{:S(2)}, u32[]{:S(2)}) %collective-permute-start.28) | collective-permute-done | bytes 524320 | tf_op jit(solution)/shard_map/ppermute | solution.py:26
  146.8 1.7 collective-permute-start.30
  148.4 8.4 %collective-permute-done.31.refs_1_ = bf16[256,1024]{1,0:T(8,128)(2,1)S(1)} collective-permute-done((bf16[256,1024]{1,0:T(8,128)(2,1)S(1)}, bf16[256,1024]{1,0:T(8,128)(2,1)S(1)}, u32[]{:S(2)}, u32[]{:S(2)}) %collective-permute-start.31) | collective-permute-done | bytes 524320 | tf_op jit(solution)/shard_map/ppermute | solution.py:26
  159.1 5.3 %collective-permute-done.30.other_ref = bf16[384,512]{1,0:T(8,128)(2,1)S(1)} collective-permute-done((bf16[384,512]{1,0:T(8,128)(2,1)S(1)}, bf16[384,512]{1,0:T(8,128)(2,1)S(1)}, u32[]{:S(2)}, u32[]{:S(2)}) %collective-permute-start.30) | collective-permute-done | bytes 393248 | tf_op jit(solution)/shard_map/ppermute | solution.py:26
  164.5 6.4 %shard_map.242 = (bf16[512,512]{1,0:T(8,128)(2,1)S(1)}, f32[8,512]{1,0:T(8,128)S(1)}) custom-call(s32[2]{0:T(128)S(1)} %pad_add_fusion.ids_ref._.here_ref, s32[8,1024]{1,0:T(8,128)S(1)} %copy-done.27, bf16[512,512]{1,0:T(8,128)(2,1)S(1)} %convolution_convert_fusion.14.query_ref, bf16[384,512]{1,0:T(8,128)(2,1)S(1)} %convolution_convert_fusion.16.own_ref, ...), custom_call_target="tpu_custom_call" | custom-call | bytes 1884168 | tf_op jit(solution)/shard_map/pallas_call | solution.py:352
  171.4 1.9 collective-permute-done.32
  176.7 11.8 %collective-permute-done.35.refs_1_ = bf16[256,1024]{1,0:T(8,128)(2,1)S(1)} collective-permute-done((bf16[256,1024]{1,0:T(8,128)(2,1)S(1)}, bf16[256,1024]{1,0:T(8,128)(2,1)S(1)}, u32[]{:S(2)}, u32[]{:S(2)}) %collective-permute-start.35) | collective-permute-done | bytes 524320 | tf_op jit(solution)/shard_map/ppermute | solution.py:26
  192.7 6.2 %fusion.3 = (f32[1024,1024]{1,0:T(8,128)S(1)}, bf16[1024,1024]{1,0:T(8,128)(2,1)S(1)}) fusion(bf16[1024,1024]{1,0:T(8,128)(2,1)} %copy-done.13, bf16[1024,2048]{1,0:T(8,128)(2,1)} %all-gather.2.cloned.1.call-done), kind=kOutput, calls=%fused_computation.4 | convolution fusion | flops 2157969408 | bytes 10485760 | tf_op jit(solution)/shard_map/dot_general | solution.py:20
  199.0 2.4 multiply_convert_fusion.right_a
  203.2 2.3 collective-permute-done.38
  208.7 2.3 convolution_convert_fusion.4
  211.1 10.5 %collective-permute-done.39 = bf16[256,1024]{1,0:T(8,128)(2,1)} collective-permute-done((bf16[256,1024]{1,0:T(8,128)(2,1)}, bf16[256,1024]{1,0:T(8,128)(2,1)}, u32[]{:S(2)}, u32[]{:S(2)}) %collective-permute-start.39) | collective-permute-done | bytes 524320 | tf_op jit(solution)/shard_map/ppermute | solution.py:26
  221.6 4.1 multiply_reduce_fusion
  228.5 3.0 fusion.39
  233.1 10.1 %shard_map.255 = bf16[1024,2048]{1,0:T(8,128)(2,1)} custom-call(bf16[1024,1024]{1,0:T(8,128)(2,1)S(1)} %copy-done.14, bf16[1024,1024]{1,0:T(8,128)(2,1)S(1)} %copy-done.67, bf16[1024,1024]{1,0:T(8,128)(2,1)} %copy-done.108, bf16[1024,1024]{1,0:T(8,128)(2,1)} %copy-done.11), custom_call_target="tpu_custom_call" | custom-call | flops 4294967296 | bytes 12582912 | tf_op jit(solution)/shard_map/pallas_call | solution.py:378
  243.2 2.0 shard_map.246
  246.1 3.4 fusion.32
  249.5 7.3 %shard_map.247 = (bf16[512,512]{1,0:T(8,128)(2,1)S(1)}, bf16[384,512]{1,0:T(8,128)(2,1)S(1)}, bf16[384,512]{1,0:T(8,128)(2,1)S(1)}) custom-call(s32[2]{0:T(128)S(1)} %pad_add_fusion.ids_ref._.here_ref, s32[8,1024]{1,0:T(8,128)S(1)} %copy-done.28, bf16[512,512]{1,0:T(8,128)(2,1)S(1)} %convolution_convert_fusion.14.query_ref, ...), custom_call_target="tpu_custom_call" | custom-call | bytes 3194888 | tf_op jit(solution)/shard_map/pallas_call | solution.py:352
  263.3 7.3 %collective-permute-done.44 = bf16[384,512]{1,0:T(8,128)(2,1)S(1)} collective-permute-done((bf16[384,512]{1,0:T(8,128)(2,1)S(1)}, bf16[384,512]{1,0:T(8,128)(2,1)S(1)}, u32[]{:S(2)}, u32[]{:S(2)}) %collective-permute-start.44) | collective-permute-done | bytes 393248 | tf_op jit(solution)/shard_map/ppermute | solution.py:26
  274.7 9.5 %collective-permute-done.45.refs_1_ = bf16[256,1024]{1,0:T(8,128)(2,1)S(1)} collective-permute-done((bf16[256,1024]{1,0:T(8,128)(2,1)S(1)}, bf16[256,1024]{1,0:T(8,128)(2,1)S(1)}, u32[]{:S(2)}, u32[]{:S(2)}) %collective-permute-start.45) | collective-permute-done | bytes 524320 | tf_op jit(solution)/shard_map/ppermute | solution.py:26
  288.5 10.7 %shard_map.249 = bf16[1024,768]{1,0:T(8,128)(2,1)S(1)} custom-call(s32[2]{0:T(128)S(1)} %pad_add_fusion.ids_ref._.here_ref, s32[8,1024]{1,0:T(8,128)S(1)} %copy-done.28, bf16[1024,768]{1,0:T(8,128)(2,1)S(1)} %copy-done.1, bf16[1024,256]{1,0:T(8,128)(2,1)S(1)} %convolution_convert_fusion.12.grad_ref, f32[4,1024]{1,0:T(4,128)S(1)} %copy-done.61), custom_call_target="tpu_custom_call" | custom-call | bytes 3719176 | tf_op jit(solution)/shard_map/pallas_call | solution.py:352
  299.3 2.1 convolution_convert_fusion.refs_0_
  304.0 9.8 %collective-permute-done.49.refs_2_ = bf16[4,128,512]{2,1,0:T(8,128)(2,1)S(1)} collective-permute-done((bf16[4,128,512]{2,1,0:T(8,128)(2,1)}, bf16[4,128,512]{2,1,0:T(8,128)(2,1)S(1)}, u32[]{:S(2)}, u32[]{:S(2)}) %collective-permute-start.49) | collective-permute-done | bytes 524320 | tf_op jit(solution)/shard_map/ppermute | solution.py:447
  315.3 2.3 collective-permute-done.52
  321.5 1.7 shard_map.252
  324.9 3.6 collective-permute-start.57
  331.2 16.3 %collective-permute-done.55.refs_1_ = bf16[128,1024]{1,0:T(8,128)(2,1)S(1)} collective-permute-done((bf16[128,1024]{1,0:T(8,128)(2,1)}, bf16[128,1024]{1,0:T(8,128)(2,1)S(1)}, u32[]{:S(2)}, u32[]{:S(2)}) %collective-permute-start.55) | collective-permute-done | bytes 262176 | tf_op jit(solution)/shard_map/ppermute | solution.py:447
  348.9 1.8 collective-permute-start.59
  350.7 8.1 %collective-permute-done.57.refs_3_ = bf16[128,1024]{1,0:T(8,128)(2,1)} collective-permute-done((bf16[128,1024]{1,0:T(8,128)(2,1)}, bf16[128,1024]{1,0:T(8,128)(2,1)}, u32[]{:S(2)}, u32[]{:S(2)}) %collective-permute-start.57) | collective-permute-done | bytes 262176 | tf_op jit(solution)/shard_map/ppermute | solution.py:447
  359.0 2.6 shard_map.253
  361.7 1.8 fusion.4
  363.6 17.1 %collective-permute-done.59.refs_6_ = bf16[128,1024]{1,0:T(8,128)(2,1)S(1)} collective-permute-done((bf16[128,1024]{1,0:T(8,128)(2,1)S(1)}, bf16[128,1024]{1,0:T(8,128)(2,1)S(1)}, u32[]{:S(2)}, u32[]{:S(2)}) %collective-permute-start.59) | collective-permute-done | bytes 262176 | tf_op jit(solution)/shard_map/ppermute | solution.py:447
  383.9 2.5 fusion.64
  386.4 5.8 %collective-permute-start.61 = (bf16[128,768]{1,0:T(8,128)(2,1)}, bf16[128,768]{1,0:T(8,128)(2,1)S(1)}, u32[]{:S(2)}, u32[]{:S(2)}) collective-permute-start(bf16[128,768]{1,0:T(8,128)(2,1)} %get-tuple-element.227), channel_id=1, source_target_pairs={{0,8},{4,12},{8,0},{12,4},{16,24},{20,28},{24,16},{28,20},{1,9},{5... | collective-permute-start | bytes 589832 | tf_op jit(solution)/shard_map/ppermute | solution.py:447
  392.2 2.4 collective-permute-start.63
  396.0 4.3 collective-permute-done.61.refs_1_
  400.3 9.3 %collective-permute-done.62.refs_2_ = bf16[128,768]{1,0:T(8,128)(2,1)S(1)} collective-permute-done((bf16[128,768]{1,0:T(8,128)(2,1)}, bf16[128,768]{1,0:T(8,128)(2,1)S(1)}, u32[]{:S(2)}, u32[]{:S(2)}) %collective-permute-start.62) | collective-permute-done | bytes 196640 | tf_op jit(solution)/shard_map/ppermute | solution.py:447
  412.0 2.3 shard_map.259
  415.8 3.4 collective-permute-start.74
  420.9 2.0 collective-permute-start.75
  433.6 1.8 shard_map.262
  435.4 1.9 shard_map.258
  437.3 1.7 shard_map.265
  (440 shorter events, 114.2 us)
Async XLA Ops:
  7.2 185.5 %all-gather.2.cloned.1.call-start = ((), (), s32[]{:S(2)}) async-start(), calls=%async_computation.1 | async-start | bytes 4718592 | tf_op jit(solution)/shard_map/all_gather | solution.py:451
  14.9 10.6 %collective-permute-start.1 = (bf16[144,896]{1,0:T(8,128)(2,1)S(1)}, bf16[144,896]{1,0:T(8,128)(2,1)S(1)}, u32[]{:S(2)}, u32[]{:S(2)}) collective-permute-start(bf16[144,896]{1,0:T(8,128)(2,1)S(1)} %get-tuple-element.139), channel_id=1, source_target_pairs={{0,2},{1,3},{2,0},{3,1},{4,6},{5,7},{6,4},{7,5},{8,10},{9,11},{10,... | collective-permute-start | bytes 774152 | tf_op jit(solution)/shard_map/ppermute | solution.py:26
  29.5 13.9 %collective-permute-start.7 = (bf16[128,1536]{1,0:T(8,128)(2,1)}, bf16[128,1536]{1,0:T(8,128)(2,1)S(1)}, u32[]{:S(2)}, u32[]{:S(2)}) collective-permute-start(bf16[128,1536]{1,0:T(8,128)(2,1)} %get-tuple-element.154), channel_id=1, source_target_pairs={{0,2},{1,3},{2,0},{3,1},{4,6},{5,7},{6,4},{7,5},{8,10},{9,11},{10,... | collective-permute-start | bytes 1179656 | tf_op jit(solution)/shard_map/ppermute | solution.py:26
  30.2 23.3 %collective-permute-start.9 = (bf16[256,1024]{1,0:T(8,128)(2,1)S(1)}, bf16[256,1024]{1,0:T(8,128)(2,1)S(1)}, u32[]{:S(2)}, u32[]{:S(2)}) collective-permute-start(bf16[256,1024]{1,0:T(8,128)(2,1)S(1)} %fusion.53.refs_0_), channel_id=1, source_target_pairs={{0,2},{1,3},{2,0},{3,1},{4,6},{5,7},{6,4},{7,5},{8,10},{9,11},{10,... | collective-permute-start | bytes 1572872 | tf_op jit(solution)/shard_map/ppermute | solution.py:26
  31.6 9.2 %collective-permute-start.8 = (bf16[128,1024]{1,0:T(8,128)(2,1)S(1)}, bf16[128,1024]{1,0:T(8,128)(2,1)S(1)}, u32[]{:S(2)}, u32[]{:S(2)}) collective-permute-start(bf16[128,1024]{1,0:T(8,128)(2,1)S(1)} %get-tuple-element.156), channel_id=1, source_target_pairs={{0,4},{4,0},{8,12},{12,8},{16,20},{20,16},{24,28},{28,24},{1,5},{5... | collective-permute-start | bytes 786440 | tf_op jit(solution)/shard_map/ppermute | solution.py:447
  33.1 13.8 %collective-permute-start.6 = (bf16[128,768]{1,0:T(8,128)(2,1)S(1)}, bf16[128,768]{1,0:T(8,128)(2,1)S(1)}, u32[]{:S(2)}, u32[]{:S(2)}) collective-permute-start(bf16[128,768]{1,0:T(8,128)(2,1)S(1)} %get-tuple-element.152.refs_0_), channel_id=1, source_target_pairs={{0,4},{4,0},{8,12},{12,8},{16,20},{20,16},{24,28},{28,24},{1,5},{5... | collective-permute-start | bytes 589832 | tf_op jit(solution)/shard_map/ppermute | solution.py:447
  33.6 13.4 %collective-permute-start.5 = (bf16[128,768]{1,0:T(8,128)(2,1)S(1)}, bf16[128,768]{1,0:T(8,128)(2,1)S(1)}, u32[]{:S(2)}, u32[]{:S(2)}) collective-permute-start(bf16[128,768]{1,0:T(8,128)(2,1)S(1)} %get-tuple-element.152.refs_0_), channel_id=1, source_target_pairs={{0,24},{4,28},{8,16},{12,20},{16,8},{20,12},{24,0},{28,4},{1,25},{... | collective-permute-start | bytes 589832 | tf_op jit(solution)/shard_map/ppermute | solution.py:447
  40.8 12.7 %collective-permute-start.4 = (bf16[128,768]{1,0:T(8,128)(2,1)S(1)}, bf16[128,768]{1,0:T(8,128)(2,1)S(1)}, u32[]{:S(2)}, u32[]{:S(2)}) collective-permute-start(bf16[128,768]{1,0:T(8,128)(2,1)S(1)} %get-tuple-element.152.refs_0_), channel_id=1, source_target_pairs={{0,16},{4,20},{8,24},{12,28},{16,0},{20,4},{24,8},{28,12},{1,17},{... | collective-permute-start | bytes 589832 | tf_op jit(solution)/shard_map/ppermute | solution.py:447
  43.4 10.1 %collective-permute-start.3 = (bf16[128,768]{1,0:T(8,128)(2,1)S(1)}, bf16[128,768]{1,0:T(8,128)(2,1)S(1)}, u32[]{:S(2)}, u32[]{:S(2)}) collective-permute-start(bf16[128,768]{1,0:T(8,128)(2,1)S(1)} %get-tuple-element.152.refs_0_), channel_id=1, source_target_pairs={{0,8},{4,12},{8,0},{12,4},{16,24},{20,28},{24,16},{28,20},{1,9},{5... | collective-permute-start | bytes 589832 | tf_op jit(solution)/shard_map/ppermute | solution.py:447
  46.9 9.2 %collective-permute-start.12 = (bf16[256,1024]{1,0:T(8,128)(2,1)S(1)}, bf16[256,1024]{1,0:T(8,128)(2,1)S(1)}, u32[]{:S(2)}, u32[]{:S(2)}) collective-permute-start(bf16[256,1024]{1,0:T(8,128)(2,1)S(1)} %fusion.53.refs_0_), channel_id=1, source_target_pairs={{0,1},{1,0},{2,3},{3,2},{4,5},{5,4},{6,7},{7,6},{8,9},{9,8},{10,11... | collective-permute-start | bytes 1572872 | tf_op jit(solution)/shard_map/ppermute | solution.py:26
  53.5 19.0 %collective-permute-start.11 = (bf16[2,128,768]{2,1,0:T(8,128)(2,1)S(1)}, bf16[2,128,768]{2,1,0:T(8,128)(2,1)S(1)}, u32[]{:S(2)}, u32[]{:S(2)}) collective-permute-start(bf16[2,128,768]{2,1,0:T(8,128)(2,1)S(1)} %pad_maximum_fusion.1), channel_id=1, source_target_pairs={{0,4},{4,0},{8,12},{12,8},{16,20},{20,16},{24,28},{28,24},{1,5},{5... | collective-permute-start | bytes 1179656 | tf_op jit(solution)/shard_map/ppermute | solution.py:447
  55.1 14.2 %collective-permute-start.10 = (bf16[128,768]{1,0:T(8,128)(2,1)S(1)}, bf16[128,768]{1,0:T(8,128)(2,1)S(1)}, u32[]{:S(2)}, u32[]{:S(2)}) collective-permute-start(bf16[128,768]{1,0:T(8,128)(2,1)S(1)} %collective-permute-done.3.refs_1_), channel_id=1, source_target_pairs={{0,4},{4,0},{8,12},{12,8},{16,20},{20,16},{24,28},{28,24},{1,5},{5... | collective-permute-start | bytes 589832 | tf_op jit(solution)/shard_map/ppermute | solution.py:447
  55.6 15.4 %collective-permute-start.14 = (bf16[96,1024]{1,0:T(8,128)(2,1)}, bf16[96,1024]{1,0:T(8,128)(2,1)}, u32[]{:S(2)}, u32[]{:S(2)}) collective-permute-start(bf16[96,1024]{1,0:T(8,128)(2,1)} %bitcast.10.refs_0_), channel_id=1, source_target_pairs={{0,2},{1,3},{2,0},{3,1},{4,6},{5,7},{6,4},{7,5},{8,10},{9,11},{10,... | collective-permute-start | bytes 589832 | tf_op jit(solution)/shard_map/ppermute | solution.py:26
  56.1 32.6 %collective-permute-start.18 = (bf16[96,1024]{1,0:T(8,128)(2,1)}, bf16[96,1024]{1,0:T(8,128)(2,1)}, u32[]{:S(2)}, u32[]{:S(2)}) collective-permute-start(bf16[96,1024]{1,0:T(8,128)(2,1)} %bitcast.10.refs_0_), channel_id=1, source_target_pairs={{0,1},{1,0},{2,3},{3,2},{4,5},{5,4},{6,7},{7,6},{8,9},{9,8},{10,11... | collective-permute-start | bytes 589832 | tf_op jit(solution)/shard_map/ppermute | solution.py:26
  56.1 21.0 %collective-permute-start.17 = (bf16[128,1024]{1,0:T(8,128)(2,1)}, bf16[128,1024]{1,0:T(8,128)(2,1)S(1)}, u32[]{:S(2)}, u32[]{:S(2)}) collective-permute-start(bf16[128,1024]{1,0:T(8,128)(2,1)} %get-tuple-element.175.refs_0_), channel_id=1, source_target_pairs={{0,24},{4,28},{8,16},{12,20},{16,8},{20,12},{24,0},{28,4},{1,25},{... | collective-permute-start | bytes 786440 | tf_op jit(solution)/shard_map/ppermute | solution.py:447
  69.3 14.8 %collective-permute-start.16 = (bf16[128,1024]{1,0:T(8,128)(2,1)}, bf16[128,1024]{1,0:T(8,128)(2,1)S(1)}, u32[]{:S(2)}, u32[]{:S(2)}) collective-permute-start(bf16[128,1024]{1,0:T(8,128)(2,1)} %get-tuple-element.175.refs_0_), channel_id=1, source_target_pairs={{0,16},{4,20},{8,24},{12,28},{16,0},{20,4},{24,8},{28,12},{1,17},{... | collective-permute-start | bytes 786440 | tf_op jit(solution)/shard_map/ppermute | solution.py:447
  71.0 13.4 %collective-permute-start.15 = (bf16[128,1024]{1,0:T(8,128)(2,1)}, bf16[128,1024]{1,0:T(8,128)(2,1)}, u32[]{:S(2)}, u32[]{:S(2)}) collective-permute-start(bf16[128,1024]{1,0:T(8,128)(2,1)} %get-tuple-element.175.refs_0_), channel_id=1, source_target_pairs={{0,8},{4,12},{8,0},{12,4},{16,24},{20,28},{24,16},{28,20},{1,9},{5... | collective-permute-start | bytes 786440 | tf_op jit(solution)/shard_map/ppermute | solution.py:447
  84.4 9.4 %collective-permute-start.23 = (bf16[128,1024]{1,0:T(8,128)(2,1)}, bf16[128,1024]{1,0:T(8,128)(2,1)S(1)}, u32[]{:S(2)}, u32[]{:S(2)}) collective-permute-start(bf16[128,1024]{1,0:T(8,128)(2,1)} %get-tuple-element.175.refs_0_), channel_id=1, source_target_pairs={{0,4},{4,0},{8,12},{12,8},{16,20},{20,16},{24,28},{28,24},{1,5},{5... | collective-permute-start | bytes 786440 | tf_op jit(solution)/shard_map/ppermute | solution.py:447
  85.9 13.6 %collective-permute-start.24 = (bf16[128,1024]{1,0:T(8,128)(2,1)}, bf16[128,1024]{1,0:T(8,128)(2,1)S(1)}, u32[]{:S(2)}, u32[]{:S(2)}) collective-permute-start(bf16[128,1024]{1,0:T(8,128)(2,1)} %collective-permute-done.15.refs_1_), channel_id=1, source_target_pairs={{0,4},{4,0},{8,12},{12,8},{16,20},{20,16},{24,28},{28,24},{1,5},{5... | collective-permute-start | bytes 786440 | tf_op jit(solution)/shard_map/ppermute | solution.py:447
  87.2 37.8 %collective-permute-start.25 = (bf16[2,128,1024]{2,1,0:T(8,128)(2,1)}, bf16[2,128,1024]{2,1,0:T(8,128)(2,1)}, u32[]{:S(2)}, u32[]{:S(2)}) collective-permute-start(bf16[2,128,1024]{2,1,0:T(8,128)(2,1)} %pad_maximum_fusion), channel_id=1, source_target_pairs={{0,4},{4,0},{8,12},{12,8},{16,20},{20,16},{24,28},{28,24},{1,5},{5... | collective-permute-start | bytes 1572872 | tf_op jit(solution)/shard_map/ppermute | solution.py:447
  88.7 36.3 %collective-permute-start.26 = (bf16[256,1024]{1,0:T(8,128)(2,1)S(1)}, bf16[256,1024]{1,0:T(8,128)(2,1)S(1)}, u32[]{:S(2)}, u32[]{:S(2)}) collective-permute-start(bf16[256,1024]{1,0:T(8,128)(2,1)S(1)} %bitcast.79), channel_id=1, source_target_pairs={{0,2},{1,3},{2,0},{3,1},{4,6},{5,7},{6,4},{7,5},{8,10},{9,11},{10,... | collective-permute-start | bytes 1572872 | tf_op jit(solution)/shard_map/ppermute | solution.py:26
  90.0 20.9 %collective-permute-start.22 = (bf16[128,1024]{1,0:T(8,128)(2,1)S(1)}, bf16[128,1024]{1,0:T(8,128)(2,1)}, u32[]{:S(2)}, u32[]{:S(2)}) collective-permute-start(bf16[128,1024]{1,0:T(8,128)(2,1)S(1)} %broadcast_select_fusion.refs_0_), channel_id=1, source_target_pairs={{0,24},{4,28},{8,16},{12,20},{16,8},{20,12},{24,0},{28,4},{1,25},{... | collective-permute-start | bytes 786440 | tf_op jit(solution)/shard_map/ppermute | solution.py:447
  94.5 30.5 %collective-permute-start.21 = (bf16[128,1024]{1,0:T(8,128)(2,1)S(1)}, bf16[128,1024]{1,0:T(8,128)(2,1)}, u32[]{:S(2)}, u32[]{:S(2)}) collective-permute-start(bf16[128,1024]{1,0:T(8,128)(2,1)S(1)} %broadcast_select_fusion.refs_0_), channel_id=1, source_target_pairs={{0,16},{4,20},{8,24},{12,28},{16,0},{20,4},{24,8},{28,12},{1,17},{... | collective-permute-start | bytes 786440 | tf_op jit(solution)/shard_map/ppermute | solution.py:447
  100.1 24.9 %collective-permute-start.20 = (bf16[128,1024]{1,0:T(8,128)(2,1)S(1)}, bf16[128,1024]{1,0:T(8,128)(2,1)}, u32[]{:S(2)}, u32[]{:S(2)}) collective-permute-start(bf16[128,1024]{1,0:T(8,128)(2,1)S(1)} %broadcast_select_fusion.refs_0_), channel_id=1, source_target_pairs={{0,8},{4,12},{8,0},{12,4},{16,24},{20,28},{24,16},{28,20},{1,9},{5... | collective-permute-start | bytes 786440 | tf_op jit(solution)/shard_map/ppermute | solution.py:447
  100.7 308.9 %reduce-scatter.2.cloned.1.call-start = ((), (), s32[]{:S(2)}) async-start(), calls=%async_computation.2 | async-start | bytes 4718592 | tf_op jit(solution)/shard_map/reduce_scatter | solution.py:455
  130.8 14.8 %collective-permute-start.28 = (bf16[256,1024]{1,0:T(8,128)(2,1)S(1)}, bf16[256,1024]{1,0:T(8,128)(2,1)S(1)}, u32[]{:S(2)}, u32[]{:S(2)}) collective-permute-start(bf16[256,1024]{1,0:T(8,128)(2,1)S(1)} %fusion.45), channel_id=1, source_target_pairs={{0,2},{1,3},{2,0},{3,1},{4,6},{5,7},{6,4},{7,5},{8,10},{9,11},{10,... | collective-permute-start | bytes 1572872 | tf_op jit(solution)/shard_map/ppermute | solution.py:26
  135.1 21.8 %collective-permute-start.31 = (bf16[256,1024]{1,0:T(8,128)(2,1)S(1)}, bf16[256,1024]{1,0:T(8,128)(2,1)S(1)}, u32[]{:S(2)}, u32[]{:S(2)}) collective-permute-start(bf16[256,1024]{1,0:T(8,128)(2,1)S(1)} %get-tuple-element.193.refs_0_), channel_id=1, source_target_pairs={{0,2},{1,3},{2,0},{3,1},{4,6},{5,7},{6,4},{7,5},{8,10},{9,11},{10,... | collective-permute-start | bytes 1572872 | tf_op jit(solution)/shard_map/ppermute | solution.py:26
  146.7 10.8 %collective-permute-start.29 = (bf16[256,1024]{1,0:T(8,128)(2,1)S(1)}, bf16[256,1024]{1,0:T(8,128)(2,1)S(1)}, u32[]{:S(2)}, u32[]{:S(2)}) collective-permute-start(bf16[256,1024]{1,0:T(8,128)(2,1)S(1)} %add_convert_fusion.2.refs_0_), channel_id=1, source_target_pairs={{0,1},{1,0},{2,3},{3,2},{4,5},{5,4},{6,7},{7,6},{8,9},{9,8},{10,11... | collective-permute-start | bytes 1572872 | tf_op jit(solution)/shard_map/ppermute | solution.py:26
  146.8 17.7 %collective-permute-start.30 = (bf16[384,512]{1,0:T(8,128)(2,1)S(1)}, bf16[384,512]{1,0:T(8,128)(2,1)S(1)}, u32[]{:S(2)}, u32[]{:S(2)}) collective-permute-start(bf16[384,512]{1,0:T(8,128)(2,1)S(1)} %convolution_convert_fusion.16.own_ref), channel_id=1, source_target_pairs={{0,2},{1,3},{2,0},{3,1},{4,6},{5,7},{6,4},{7,5},{8,10},{9,11},{10,... | collective-permute-start | bytes 1179656 | tf_op jit(solution)/shard_map/ppermute | solution.py:26
  174.5 14.0 %collective-permute-start.35 = (bf16[256,1024]{1,0:T(8,128)(2,1)S(1)}, bf16[256,1024]{1,0:T(8,128)(2,1)S(1)}, u32[]{:S(2)}, u32[]{:S(2)}) collective-permute-start(bf16[256,1024]{1,0:T(8,128)(2,1)S(1)} %add_convert_fusion.1.refs_0_), channel_id=1, source_target_pairs={{0,2},{1,3},{2,0},{3,1},{4,6},{5,7},{6,4},{7,5},{8,10},{9,11},{10,... | collective-permute-start | bytes 1572872 | tf_op jit(solution)/shard_map/ppermute | solution.py:26
  176.2 12.4 %collective-permute-start.33 = (bf16[256,1024]{1,0:T(8,128)(2,1)S(1)}, bf16[256,1024]{1,0:T(8,128)(2,1)S(1)}, u32[]{:S(2)}, u32[]{:S(2)}) collective-permute-start(bf16[256,1024]{1,0:T(8,128)(2,1)S(1)} %bitcast.80), channel_id=1, source_target_pairs={{0,1},{1,0},{2,3},{3,2},{4,5},{5,4},{6,7},{7,6},{8,9},{9,8},{10,11... | collective-permute-start | bytes 1572872 | tf_op jit(solution)/shard_map/ppermute | solution.py:26
  176.2 12.4 %collective-permute-start.34 = (bf16[256,1024]{1,0:T(8,128)(2,1)S(1)}, bf16[256,1024]{1,0:T(8,128)(2,1)S(1)}, u32[]{:S(2)}, u32[]{:S(2)}) collective-permute-start(bf16[256,1024]{1,0:T(8,128)(2,1)S(1)} %copy-done.32), channel_id=1, source_target_pairs={{0,1},{1,0},{2,3},{3,2},{4,5},{5,4},{6,7},{7,6},{8,9},{9,8},{10,11... | collective-permute-start | bytes 1572872 | tf_op jit(solution)/shard_map/ppermute | solution.py:26
  176.7 14.0 %collective-permute-start.36 = (bf16[256,1024]{1,0:T(8,128)(2,1)S(1)}, bf16[256,1024]{1,0:T(8,128)(2,1)S(1)}, u32[]{:S(2)}, u32[]{:S(2)}) collective-permute-start(bf16[256,1024]{1,0:T(8,128)(2,1)S(1)} %add_convert_fusion.1.refs_0_), channel_id=1, source_target_pairs={{0,1},{1,0},{2,3},{3,2},{4,5},{5,4},{6,7},{7,6},{8,9},{9,8},{10,11... | collective-permute-start | bytes 1572872 | tf_op jit(solution)/shard_map/ppermute | solution.py:26
  207.1 14.5 %collective-permute-start.39 = (bf16[256,1024]{1,0:T(8,128)(2,1)}, bf16[256,1024]{1,0:T(8,128)(2,1)}, u32[]{:S(2)}, u32[]{:S(2)}) collective-permute-start(bf16[256,1024]{1,0:T(8,128)(2,1)} %fusion.42), channel_id=1, source_target_pairs={{0,2},{1,3},{2,0},{3,1},{4,6},{5,7},{6,4},{7,5},{8,10},{9,11},{10,... | collective-permute-start | bytes 1572872 | tf_op jit(solution)/shard_map/ppermute | solution.py:26
  211.0 16.3 %collective-permute-start.41 = (bf16[512,1024]{1,0:T(8,128)(2,1)}, bf16[512,1024]{1,0:T(8,128)(2,1)}, u32[]{:S(2)}, u32[]{:S(2)}) collective-permute-start(bf16[512,1024]{1,0:T(8,128)(2,1)} %convolution_convert_fusion.4), channel_id=1, source_target_pairs={{0,1},{1,0},{2,3},{3,2},{4,5},{5,4},{6,7},{7,6},{8,9},{9,8},{10,11... | collective-permute-start | bytes 3145736 | tf_op jit(solution)/shard_map/ppermute | solution.py:26
  227.3 15.9 %collective-permute-start.40 = (bf16[256,1024]{1,0:T(8,128)(2,1)}, bf16[256,1024]{1,0:T(8,128)(2,1)}, u32[]{:S(2)}, u32[]{:S(2)}) collective-permute-start(bf16[256,1024]{1,0:T(8,128)(2,1)} %get-tuple-element.279.refs_0_), channel_id=1, source_target_pairs={{0,1},{1,0},{2,3},{3,2},{4,5},{5,4},{6,7},{7,6},{8,9},{9,8},{10,11... | collective-permute-start | bytes 1572872 | tf_op jit(solution)/shard_map/ppermute | solution.py:26
  231.5 14.6 %collective-permute-start.42 = (bf16[256,1024]{1,0:T(8,128)(2,1)}, bf16[256,1024]{1,0:T(8,128)(2,1)}, u32[]{:S(2)}, u32[]{:S(2)}) collective-permute-start(bf16[256,1024]{1,0:T(8,128)(2,1)} %fusion.39), channel_id=1, source_target_pairs={{0,2},{1,3},{2,0},{3,1},{4,6},{5,7},{6,4},{7,5},{8,10},{9,11},{10,... | collective-permute-start | bytes 1572872 | tf_op jit(solution)/shard_map/ppermute | solution.py:26
  259.0 11.6 %collective-permute-start.44 = (bf16[384,512]{1,0:T(8,128)(2,1)S(1)}, bf16[384,512]{1,0:T(8,128)(2,1)S(1)}, u32[]{:S(2)}, u32[]{:S(2)}) collective-permute-start(bf16[384,512]{1,0:T(8,128)(2,1)S(1)} %get-tuple-element.204), channel_id=1, source_target_pairs={{0,2},{1,3},{2,0},{3,1},{4,6},{5,7},{6,4},{7,5},{8,10},{9,11},{10,... | collective-permute-start | bytes 1179656 | tf_op jit(solution)/shard_map/ppermute | solution.py:26
  260.4 43.6 %collective-permute-start.48 = (bf16[4,128,1024]{2,1,0:T(8,128)(2,1)S(1)}, bf16[4,128,1024]{2,1,0:T(8,128)(2,1)S(1)}, u32[]{:S(2)}, u32[]{:S(2)}) collective-permute-start(bf16[4,128,1024]{2,1,0:T(8,128)(2,1)S(1)} %shard_map.250), channel_id=1, source_target_pairs={{0,4},{4,0},{8,12},{12,8},{16,20},{20,16},{24,28},{28,24},{1,5},{5... | collective-permute-start | bytes 3145736 | tf_op jit(solution)/shard_map/ppermute | solution.py:447
  270.6 13.6 %collective-permute-start.45 = (bf16[256,1024]{1,0:T(8,128)(2,1)S(1)}, bf16[256,1024]{1,0:T(8,128)(2,1)S(1)}, u32[]{:S(2)}, u32[]{:S(2)}) collective-permute-start(bf16[256,1024]{1,0:T(8,128)(2,1)S(1)} %get-tuple-element.205.refs_0_), channel_id=1, source_target_pairs={{0,2},{1,3},{2,0},{3,1},{4,6},{5,7},{6,4},{7,5},{8,10},{9,11},{10,... | collective-permute-start | bytes 1572872 | tf_op jit(solution)/shard_map/ppermute | solution.py:26
  271.7 12.9 %collective-permute-start.50 = (bf16[192,1024]{1,0:T(8,128)(2,1)S(1)}, bf16[192,1024]{1,0:T(8,128)(2,1)S(1)}, u32[]{:S(2)}, u32[]{:S(2)}) collective-permute-start(bf16[192,1024]{1,0:T(8,128)(2,1)S(1)} %convolution_convert_fusion.15), channel_id=1, source_target_pairs={{0,1},{1,0},{2,3},{3,2},{4,5},{5,4},{6,7},{7,6},{8,9},{9,8},{10,11... | collective-permute-start | bytes 1179656 | tf_op jit(solution)/shard_map/ppermute | solution.py:26
  272.6 13.2 %collective-permute-start.46 = (bf16[256,1024]{1,0:T(8,128)(2,1)S(1)}, bf16[256,1024]{1,0:T(8,128)(2,1)S(1)}, u32[]{:S(2)}, u32[]{:S(2)}) collective-permute-start(bf16[256,1024]{1,0:T(8,128)(2,1)S(1)} %get-tuple-element.205.refs_0_), channel_id=1, source_target_pairs={{0,1},{1,0},{2,3},{3,2},{4,5},{5,4},{6,7},{7,6},{8,9},{9,8},{10,11... | collective-permute-start | bytes 1572872 | tf_op jit(solution)/shard_map/ppermute | solution.py:26
  274.6 39.2 %collective-permute-start.49 = (bf16[4,128,512]{2,1,0:T(8,128)(2,1)}, bf16[4,128,512]{2,1,0:T(8,128)(2,1)S(1)}, u32[]{:S(2)}, u32[]{:S(2)}) collective-permute-start(bf16[4,128,512]{2,1,0:T(8,128)(2,1)} %shard_map.251), channel_id=1, source_target_pairs={{0,4},{4,0},{8,12},{12,8},{16,20},{20,16},{24,28},{28,24},{1,5},{5... | collective-permute-start | bytes 1572872 | tf_op jit(solution)/shard_map/ppermute | solution.py:447
  287.1 16.1 %collective-permute-start.51 = (bf16[96,1024]{1,0:T(8,128)(2,1)}, bf16[96,1024]{1,0:T(8,128)(2,1)S(1)}, u32[]{:S(2)}, u32[]{:S(2)}) collective-permute-start(bf16[96,1024]{1,0:T(8,128)(2,1)} %add_convert_fusion.4), channel_id=1, source_target_pairs={{0,2},{1,3},{2,0},{3,1},{4,6},{5,7},{6,4},{7,5},{8,10},{9,11},{10,... | collective-permute-start | bytes 589832 | tf_op jit(solution)/shard_map/ppermute | solution.py:26
  314.9 44.1 %collective-permute-start.54 = (bf16[4,128,768]{2,1,0:T(8,128)(2,1)}, bf16[4,128,768]{2,1,0:T(8,128)(2,1)}, u32[]{:S(2)}, u32[]{:S(2)}) collective-permute-start(bf16[4,128,768]{2,1,0:T(8,128)(2,1)} %dynamic-slice_bitcast_fusion), channel_id=1, source_target_pairs={{0,4},{4,0},{8,12},{12,8},{16,20},{20,16},{24,28},{28,24},{1,5},{5... | collective-permute-start | bytes 2359304 | tf_op jit(solution)/shard_map/ppermute | solution.py:447
  320.0 39.1 %collective-permute-start.53 = (bf16[256,1024]{1,0:T(8,128)(2,1)}, bf16[256,1024]{1,0:T(8,128)(2,1)}, u32[]{:S(2)}, u32[]{:S(2)}) collective-permute-start(bf16[256,1024]{1,0:T(8,128)(2,1)} %fusion.38), channel_id=1, source_target_pairs={{0,2},{1,3},{2,0},{3,1},{4,6},{5,7},{6,4},{7,5},{8,10},{9,11},{10,... | collective-permute-start | bytes 1572872 | tf_op jit(solution)/shard_map/ppermute | solution.py:26
  324.0 23.5 %collective-permute-start.55 = (bf16[128,1024]{1,0:T(8,128)(2,1)}, bf16[128,1024]{1,0:T(8,128)(2,1)S(1)}, u32[]{:S(2)}, u32[]{:S(2)}) collective-permute-start(bf16[128,1024]{1,0:T(8,128)(2,1)} %get-tuple-element.213), channel_id=1, source_target_pairs={{0,8},{4,12},{8,0},{12,4},{16,24},{20,28},{24,16},{28,20},{1,9},{5... | collective-permute-start | bytes 786440 | tf_op jit(solution)/shard_map/ppermute | solution.py:447
  324.0 24.9 %collective-permute-start.56 = (bf16[128,1024]{1,0:T(8,128)(2,1)}, bf16[128,1024]{1,0:T(8,128)(2,1)}, u32[]{:S(2)}, u32[]{:S(2)}) collective-permute-start(bf16[128,1024]{1,0:T(8,128)(2,1)} %get-tuple-element.214), channel_id=1, source_target_pairs={{0,16},{4,20},{8,24},{12,28},{16,0},{20,4},{24,8},{28,12},{1,17},{... | collective-permute-start | bytes 786440 | tf_op jit(solution)/shard_map/ppermute | solution.py:447
  324.9 33.9 %collective-permute-start.57 = (bf16[128,1024]{1,0:T(8,128)(2,1)}, bf16[128,1024]{1,0:T(8,128)(2,1)}, u32[]{:S(2)}, u32[]{:S(2)}) collective-permute-start(bf16[128,1024]{1,0:T(8,128)(2,1)} %get-tuple-element.215), channel_id=1, source_target_pairs={{0,24},{4,28},{8,16},{12,20},{16,8},{20,12},{24,0},{28,4},{1,25},{... | collective-permute-start | bytes 786440 | tf_op jit(solution)/shard_map/ppermute | solution.py:447
  347.5 16.1 %collective-permute-start.58 = (bf16[128,1024]{1,0:T(8,128)(2,1)S(1)}, bf16[128,1024]{1,0:T(8,128)(2,1)S(1)}, u32[]{:S(2)}, u32[]{:S(2)}) collective-permute-start(bf16[128,1024]{1,0:T(8,128)(2,1)S(1)} %get-tuple-element.221), channel_id=1, source_target_pairs={{0,8},{4,12},{8,0},{12,4},{16,24},{20,28},{24,16},{28,20},{1,9},{5... | collective-permute-start | bytes 786440 | tf_op jit(solution)/shard_map/ppermute | solution.py:447
  348.9 31.8 %collective-permute-start.59 = (bf16[128,1024]{1,0:T(8,128)(2,1)S(1)}, bf16[128,1024]{1,0:T(8,128)(2,1)S(1)}, u32[]{:S(2)}, u32[]{:S(2)}) collective-permute-start(bf16[128,1024]{1,0:T(8,128)(2,1)S(1)} %get-tuple-element.222), channel_id=1, source_target_pairs={{0,16},{4,20},{8,24},{12,28},{16,0},{20,4},{24,8},{28,12},{1,17},{... | collective-permute-start | bytes 786440 | tf_op jit(solution)/shard_map/ppermute | solution.py:447
  358.8 22.0 %collective-permute-start.60 = (bf16[128,1024]{1,0:T(8,128)(2,1)S(1)}, bf16[128,1024]{1,0:T(8,128)(2,1)S(1)}, u32[]{:S(2)}, u32[]{:S(2)}) collective-permute-start(bf16[128,1024]{1,0:T(8,128)(2,1)S(1)} %get-tuple-element.223), channel_id=1, source_target_pairs={{0,24},{4,28},{8,16},{12,20},{16,8},{20,12},{24,0},{28,4},{1,25},{... | collective-permute-start | bytes 786440 | tf_op jit(solution)/shard_map/ppermute | solution.py:447
  382.8 11.8 %collective-permute-start.72 = (f32[6,256]{1,0:T(8,128)S(1)}, f32[6,256]{1,0:T(8,128)S(1)}, u32[]{:S(2)}, u32[]{:S(2)}) collective-permute-start(f32[6,256]{1,0:T(8,128)S(1)} %bitcast.111), channel_id=1, source_target_pairs={{0,2},{1,3},{2,0},{3,1},{4,6},{5,7},{6,4},{7,5},{8,10},{9,11},{10,... | collective-permute-start | bytes 18440 | tf_op jit(solution)/shard_map/ppermute | solution.py:26
  386.4 13.9 %collective-permute-start.61 = (bf16[128,768]{1,0:T(8,128)(2,1)}, bf16[128,768]{1,0:T(8,128)(2,1)S(1)}, u32[]{:S(2)}, u32[]{:S(2)}) collective-permute-start(bf16[128,768]{1,0:T(8,128)(2,1)} %get-tuple-element.227), channel_id=1, source_target_pairs={{0,8},{4,12},{8,0},{12,4},{16,24},{20,28},{24,16},{28,20},{1,9},{5... | collective-permute-start | bytes 589832 | tf_op jit(solution)/shard_map/ppermute | solution.py:447
  392.2 17.4 %collective-permute-start.62 = (bf16[128,768]{1,0:T(8,128)(2,1)}, bf16[128,768]{1,0:T(8,128)(2,1)S(1)}, u32[]{:S(2)}, u32[]{:S(2)}) collective-permute-start(bf16[128,768]{1,0:T(8,128)(2,1)} %get-tuple-element.228), channel_id=1, source_target_pairs={{0,16},{4,20},{8,24},{12,28},{16,0},{20,4},{24,8},{28,12},{1,17},{... | collective-permute-start | bytes 589832 | tf_op jit(solution)/shard_map/ppermute | solution.py:447
  392.2 17.4 %collective-permute-start.63 = (bf16[128,768]{1,0:T(8,128)(2,1)S(1)}, bf16[128,768]{1,0:T(8,128)(2,1)S(1)}, u32[]{:S(2)}, u32[]{:S(2)}) collective-permute-start(bf16[128,768]{1,0:T(8,128)(2,1)S(1)} %copy-done.65), channel_id=1, source_target_pairs={{0,24},{4,28},{8,16},{12,20},{16,8},{20,12},{24,0},{28,4},{1,25},{... | collective-permute-start | bytes 589832 | tf_op jit(solution)/shard_map/ppermute | solution.py:447
  394.6 21.3 %collective-permute-start.73 = (f32[6,256]{1,0:T(8,128)S(1)}, f32[6,256]{1,0:T(8,128)S(1)}, u32[]{:S(2)}, u32[]{:S(2)}) collective-permute-start(f32[6,256]{1,0:T(8,128)S(1)} %bitcast_add_fusion.1), channel_id=1, source_target_pairs={{0,4},{4,0},{8,12},{12,8},{16,20},{20,16},{24,28},{28,24},{1,5},{5... | collective-permute-start | bytes 18440 | tf_op jit(solution)/shard_map/ppermute | solution.py:447
  411.3 16.2 %collective-permute-start.69 = (bf16[128,1024]{1,0:T(8,128)(2,1)S(1)}, bf16[128,1024]{1,0:T(8,128)(2,1)S(1)}, u32[]{:S(2)}, u32[]{:S(2)}) collective-permute-start(bf16[128,1024]{1,0:T(8,128)(2,1)S(1)} %get-tuple-element.257), channel_id=1, source_target_pairs={{0,2},{1,3},{2,0},{3,1},{4,6},{5,7},{6,4},{7,5},{8,10},{9,11},{10,... | collective-permute-start | bytes 786440 | tf_op jit(solution)/shard_map/ppermute | solution.py:26
  414.3 8.5 %collective-permute-start.66 = (bf16[128,512]{1,0:T(8,128)(2,1)S(1)}, bf16[128,512]{1,0:T(8,128)(2,1)S(1)}, u32[]{:S(2)}, u32[]{:S(2)}) collective-permute-start(bf16[128,512]{1,0:T(8,128)(2,1)S(1)} %get-tuple-element.246), channel_id=1, source_target_pairs={{0,4},{4,0},{8,12},{12,8},{16,20},{20,16},{24,28},{28,24},{1,5},{5... | collective-permute-start | bytes 393224 | tf_op jit(solution)/shard_map/ppermute | solution.py:447
  415.8 5.0 %collective-permute-start.74 = (f32[6,256]{1,0:T(8,128)S(1)}, f32[6,256]{1,0:T(8,128)S(1)}, u32[]{:S(2)}, u32[]{:S(2)}) collective-permute-start(f32[6,256]{1,0:T(8,128)S(1)} %add.220), channel_id=1, source_target_pairs={{0,8},{4,12},{8,0},{12,4},{16,24},{20,28},{24,16},{28,20},{1,9},{5... | collective-permute-start | bytes 18440 | tf_op jit(solution)/shard_map/ppermute | solution.py:447
  420.9 8.9 %collective-permute-start.75 = (f32[6,256]{1,0:T(8,128)S(1)}, f32[6,256]{1,0:T(8,128)S(1)}, u32[]{:S(2)}, u32[]{:S(2)}) collective-permute-start(f32[6,256]{1,0:T(8,128)S(1)} %add.221), channel_id=1, source_target_pairs={{0,16},{4,20},{8,24},{12,28},{16,0},{20,4},{24,8},{28,12},{1,17},{... | collective-permute-start | bytes 18440 | tf_op jit(solution)/shard_map/ppermute | solution.py:447
  423.8 6.5 %collective-permute-start.67 = (bf16[128,1024]{1,0:T(8,128)(2,1)S(1)}, bf16[128,1024]{1,0:T(8,128)(2,1)S(1)}, u32[]{:S(2)}, u32[]{:S(2)}) collective-permute-start(bf16[128,1024]{1,0:T(8,128)(2,1)S(1)} %get-tuple-element.248), channel_id=1, source_target_pairs={{0,2},{1,3},{2,0},{3,1},{4,6},{5,7},{6,4},{7,5},{8,10},{9,11},{10,... | collective-permute-start | bytes 786440 | tf_op jit(solution)/shard_map/ppermute | solution.py:26
  427.0 4.7 %collective-permute-start.64 = (bf16[128,384]{1,0:T(8,128)(2,1)S(1)}, bf16[128,384]{1,0:T(8,128)(2,1)S(1)}, u32[]{:S(2)}, u32[]{:S(2)}) collective-permute-start(bf16[128,384]{1,0:T(8,128)(2,1)S(1)} %get-tuple-element.234), channel_id=1, source_target_pairs={{0,2},{1,3},{2,0},{3,1},{4,6},{5,7},{6,4},{7,5},{8,10},{9,11},{10,... | collective-permute-start | bytes 294920 | tf_op jit(solution)/shard_map/ppermute | solution.py:26
  428.3 9.0 %collective-permute-start.70 = (bf16[128,1024]{1,0:T(8,128)(2,1)S(1)}, bf16[128,1024]{1,0:T(8,128)(2,1)S(1)}, u32[]{:S(2)}, u32[]{:S(2)}) collective-permute-start(bf16[128,1024]{1,0:T(8,128)(2,1)S(1)} %get-tuple-element.259), channel_id=1, source_target_pairs={{0,1},{1,0},{2,3},{3,2},{4,5},{5,4},{6,7},{7,6},{8,9},{9,8},{10,11... | collective-permute-start | bytes 786440 | tf_op jit(solution)/shard_map/ppermute | solution.py:26
  (123 other events, 1084.8 us)
Sparse Core Ops, SparseCore 0:
  100.8 74.5 all-gather.1
  243.3 118.3 reduce-scatter.1

commit v5 on v4

--- a/solution.py
+++ b/solution.py
@@ -488,19 +488,17 @@
 
 def place_line_pieces(ids_ref, *refs):
     far = ids_ref[1] >> 1
-    height = refs[0].shape[0] // 2
+    height = refs[0].shape[0]
     pairs = []
     for k in range(4):
         start = pl.multiple_of((far ^ k) * height, height)
-        for index in range(2):
-            piece = refs[k].at[index * height : (index + 1) * height]
-            pairs.append((piece, refs[4 + index].at[pl.ds(start, height)]))
-    copy_all(pairs, refs[6])
-
-
-def place_lines(ids, *pieces):
-    whole = shaped((2 * pieces[0].shape[0], pieces[0].shape[1]), LOW)
-    return call(place_line_pieces, [whole] * 2, (ids, *pieces), own_copies=8)
+        pairs.append((refs[k], refs[4].at[pl.ds(start, height)]))
+    copy_all(pairs, refs[5])
+
+
+def place_line(ids, *pieces):
+    whole = shaped((4 * pieces[0].shape[0], pieces[0].shape[1]), LOW)
+    return call(place_line_pieces, [whole], (ids, *pieces), own_copies=4)[0]
 
 
 def three_ways(block):
@@ -871,15 +869,45 @@
     return lax.optimization_barrier(((up * phi).astype(LOW), slope))
 
 
-def reduce_norms(sums, here):
-    split = sums.reshape(6, 2, 2, -1)
-    split = pick(split, here & 1, 2) + swap(pick(split, 1 - (here & 1), 2), 1)
-    sums = pick(split, here >> 1, 1) + swap(pick(split, 1 - (here >> 1), 1), 2)
+def norms_core(ids, *refs):
+    core, _, _, _ = device_bits(ids)
+    kept, sent = refs[6:]
+    for ref in (kept, sent):
+        ref[...] = jnp.zeros_like(ref)
+    for index, row in enumerate(refs[:6]):
+        for y in range(2):
+            zero, one = [row[:, (2 * y + c) * 256 : (2 * y + c + 1) * 256] for c in range(2)]
+            columns = slice(256 * y, 256 * (y + 1))
+            kept[index : index + 1, columns] = choose(core, zero, one)
+            sent[index : index + 1, columns] = choose(core, one, zero)
+
+
+def norms_far(ids, kept, came, far_kept, far_sent):
+    _, y, _, _ = device_bits(ids)
+    value = kept[...] + came[...]
+    far_kept[...] = choose(y, value[:, :256], value[:, 256:])
+    far_sent[...] = choose(y, value[:, 256:], value[:, :256])
+
+
+def norms_over_text(ids, rows):
+    wide = lambda *shape: shaped(shape, WIDE)
+    kept, sent = call(norms_core, [wide(8, 512)] * 2, (ids, *[r[None] for r in rows]))
+    kept, sent = call(norms_far, [wide(8, 256)] * 2, (ids, kept, swap(sent, 1)))
+    return kept + swap(sent, 2)
+
+
+def over_rows(sums):
     mask = 1
     while mask < lax.axis_size("rows"):
         sums = sums + row_swap(sums, mask)
         mask = 2 * mask
     return sums
+
+
+def reduce_norms(rows, here):
+    split = jnp.stack(rows).reshape(6, 2, 2, -1)
+    split = pick(split, here & 1, 2) + swap(pick(split, 1 - (here & 1), 2), 1)
+    return over_rows(pick(split, here >> 1, 1) + swap(pick(split, 1 - (here >> 1), 1), 2))
 
 
 def local_grid(
@@ -929,49 +957,54 @@
     mixed_z = three_ways(mixed)
     mixed_x = row_swap(mixed, 1)
     lines_x = row_swap(lines, 1)
+    mixed_x1 = row_swap(mixed_z[0], 1)
     rest_came = swap(rest_sent, 2)
     one_far, one_near = swap(one, 2), swap(one, 1)
     attend, ffn_block = call(
         deal_rest_last, [low(128, 1024), low(128, 2048)], (ids, rest_kept, rest_came)
     )
     lines = jnp.where((row & 1) == (here >> 1), lines, lines_x)
-    *mixed_z, mixed_x, attend, lines, one_far, text, grad = sync(
-        *mixed_z, mixed_x, attend, lines, one_far, text_states[0], out_grad[0]
-    )
-    mixed_x1 = row_swap(mixed_z[0], 1)
+    *mixed_z, mixed_x, mixed_x1, attend, lines, one_far, text, grad = sync(
+        *mixed_z, mixed_x, mixed_x1, attend, lines, one_far, text_states[0], out_grad[0]
+    )
     mixed_x2 = row_swap(jnp.stack(mixed_z[1:]), 1)
+    self_line, cross_line = lines[:64], lines[64:]
+    self_z = three_ways(self_line)
     attend_z = three_ways(attend)
     one_all = join(ids, one, one_far, one_near, swap(one_far, 1))
     text_far, text_near = swap(text, 2), swap(text, 1)
-    mixed_x1, mixed_x2, one_all, text_far = sync(mixed_x1, mixed_x2, one_all, text_far)
+    mixed_x2, one_all, text_far, *self_z, ffn_block = sync(
+        mixed_x2, one_all, text_far, *self_z, ffn_block
+    )
+    w_ffn = gather_rows(ffn_block)
     (w_mixed,) = place(ids, (768,), [mixed, *mixed_z], [mixed_x, mixed_x1, mixed_x2])
     mixed_low = mm(one_all, w_mixed).astype(LOW)
-    mixed_low, *attend_z, grad, attend, lines, ffn_block = sync(
-        mixed_low, *attend_z, grad, attend, lines, ffn_block
-    )
-    w_ffn = gather_rows(ffn_block)
-    lines_z = three_ways(lines)
+    w_self = place_line(ids, self_line, *self_z)
+    mixed_low, *attend_z, grad, attend, cross_line, w_self = sync(
+        mixed_low, *attend_z, grad, attend, cross_line, w_self
+    )
     attend_x0, attend_x1 = row_swap(attend, 1), row_swap(attend_z[0], 1)
     attend_x2 = row_swap(jnp.stack(attend_z[1:]), 1)
+    cross_z = three_ways(cross_line)
     grad_far, grad_near = swap(grad, 2), swap(grad, 1)
     self_att, self_lse = call(
         self_forward, [low(count, inner), wide(4, count)], (ids, marks, mixed_low), resident=True
     )
     text_all = join(ids, text, text_far, text_near, swap(text_far, 1))
-    self_att, text_all, *lines_z, attend_x0, attend_x1, attend_x2, grad_far = sync(
-        self_att, text_all, *lines_z, attend_x0, attend_x1, attend_x2, grad_far
-    )
-    w_self, w_cross = place_lines(ids, lines, *lines_z)
+    self_att, text_all, attend_x0, attend_x1, grad_far, *cross_z = sync(
+        self_att, text_all, attend_x0, attend_x1, grad_far, *cross_z
+    )
+    received, attend_x2 = scatter_slots(self_att, w_self, 0, None, (attend_x2,))
+    hidden = frames_wide + received
     w_query, w_pairs = place(
         ids, (512, 512), [attend, *attend_z], [attend_x0, attend_x1, attend_x2]
     )
-    received = scatter_slots(self_att, w_self, 0)
-    hidden = frames_wide + received
+    w_cross = place_line(ids, cross_line, *cross_z)
     grad_all = join(ids, grad, grad_far, grad_near, swap(grad_far, 1))
     text_count = text_all.shape[0]
     pairs_own = mm(text_all, w_pairs).astype(LOW)
     pairs_other = swap(pairs_own, 2)
-    w_cross_far = swap(sync(w_cross, pairs_own)[0], 2)
+    w_cross_far = swap(sync(w_cross, pairs_other)[0], 2)
     two, hat_two, inverse_two = norm_forward(hidden, gains[1], biases[1])
     two_pair = gather_pair(two, ids)
     pair_count = two_pair.shape[0]
@@ -1029,34 +1062,35 @@
         scratch=[pltpu.VMEM((count, 128), WIDE), pltpu.VMEM((count, 128), WIDE)],
         resident=True,
     )
-    g_self = mm(self_att, branch, 0, 0).astype(LOW)
-    g_mixed = mm(one_all, grad_mixed, 0, 0).astype(LOW)
-    mixed_sent = pick(g_mixed.reshape(4, 2, 128, 768), 1 - (row & 1), 1)
-    grad_mixed, g_self, mixed_sent, attend_came, pairs_came, text_part = sync(
-        grad_mixed, g_self, mixed_sent, attend_came, pairs_came, text_part
-    )
-    text_grad = text_part
+    grad_mixed, attend_came, branch = sync(grad_mixed, attend_came, branch)
     sums = [wide(128, 1024)] + [low(128, 1024)] * 3
     attend_own, *attend_parts = call(attend_along_z, sums, (ids, g_query, g_cross, attend_came))
     attend_parts = along_z(attend_parts)
-    mixed_came = row_swap(mixed_sent, 1)
+    g_mixed = mm(one_all, grad_mixed, 0, 0).astype(LOW)
+    mixed_came = row_swap(pick(g_mixed.reshape(4, 2, 128, 768), 1 - (row & 1), 1), 1)
+    g_self = mm(self_att, branch, 0, 0).astype(LOW)
+    grad_one, g_self, text_part, pairs_came, *attend_parts = scatter_slots(
+        grad_mixed, w_mixed, 1, None, (g_self, text_part, pairs_came, *attend_parts)
+    )
+    text_grad = text_part
     pairs_own, *pairs_parts = call(pairs_along_z, sums, (ids, g_pairs, g_self, pairs_came))
     pairs_parts = along_z(pairs_parts)
-    grad_one, mixed_came, *attend_parts = scatter_slots(
-        grad_mixed, w_mixed, 1, None, (mixed_came, *attend_parts)
-    )
+    grad_one, pairs_first = sync(grad_one, pairs_parts[0])
+    part, gain_one, bias_one = norm_backward(grad_one, hat_one, inverse_one, gains[0])
+    frame_grad = grad_hidden + part
+    norm_sums = norms_over_text(
+        ids, [gain_one, gain_two, gain_three, bias_one, bias_two, bias_three]
+    )
+    mixed_came, *pairs_parts = sync(mixed_came, pairs_first, *pairs_parts[1:])
     mixed_own, *mixed_parts = call(
         split_sums, [wide(128, 768)] + [low(128, 768)] * 3, (ids, g_mixed, mixed_came)
     )
     mixed_parts = along_z(mixed_parts)
-    mixed_own, grad_one, *pairs_parts = sync(mixed_own, grad_one, *pairs_parts)
-    part, gain_one, bias_one = norm_backward(grad_one, hat_one, inverse_one, gains[0])
-    frame_grad = grad_hidden + part
-    ffn_sums, *mixed_parts = sync(ffn_sums, *mixed_parts)
+    mixed_parts[0], norm_sums, ffn_sums, pairs_own = sync(
+        mixed_parts[0], norm_sums, ffn_sums, pairs_own
+    )
+    norm_sums = over_rows(norm_sums)
     d_up, d_down = return_ffn(ids, ffn_sums)
-    norm_sums = reduce_norms(
-        jnp.stack([gain_one, gain_two, gain_three, bias_one, bias_two, bias_three]), here
-    )
     d_self, d_query, d_pairs, d_cross = return_attend(
         ids, attend_own, *attend_parts, pairs_own, *pairs_parts
     )
@@ -1073,7 +1107,7 @@
         d_up,
         d_down,
         norm_sums[:3],
-        norm_sums[3:],
+        norm_sums[3:6],
     )
 
 
@@ -1197,7 +1231,7 @@
     frame_grad = grad_hidden + part
 
     norm_sums = reduce_norms(
-        jnp.stack([gain_one, gain_two, gain_three, bias_one, bias_two, bias_three]), here
+        [gain_one, gain_two, gain_three, bias_one, bias_two, bias_three], here
     )
     parts = jnp.concatenate([apart(sum_rows(g_up)), apart(sum_rows(g_down))], axis=1)
     parts = exchange(parts, here)

time: 452 us -> 425 us (0.940)
  waiting for transfers between devices: 191 us -> 156 us
  starting transfers between devices: 73.4 us -> 80.9 us
  local copies, waits for them, and re-layouts: 20.9 us -> 25.8 us
    ppermute x44, waiting for transfers between devices: 75.5 us -> 56.3 us  [swap(): return lax.ppermute(values, 'text', [(i, i ^ mask) for i in range(WAYS)])]
    ppermute x32 -> x35, waiting for transfers between devices: 115 us -> 99.6 us  [row_swap(): return lax.ppermute(values, 'rows', [(i, i ^ mask) for i in range(size)])]
    unnamed x225 -> x234, local copies, waits for them, and re-layouts: 18.5 us -> 24.4 us
    ppermute x32 -> x35, starting transfers between devices: 47.9 us -> 53.7 us  [row_swap(): return lax.ppermute(values, 'rows', [(i, i ^ mask) for i in range(size)])]
    pallas_call x36 -> x39, Pallas kernels: 76.3 us -> 77.1 us  [call(): pl.pallas_call(body, out_shape=outs, in_specs=[pl.BlockSpec(memory_space=...]
  transfers between devices with their start and end apart: 78 -> 81, of which waited for: 32 -> 30; matrix products, arithmetic and copies ran while one was open for 11% -> 10% of each run, Pallas kernels for 18% -> 19%
where the time goes in v5:
time: 425 us; the launch traced here: 418 us
  waiting for transfers between devices  156 us (37%)
  Pallas kernels  87 us (20%)
  starting transfers between devices  80.9 us (19%)
  matrix products  40.6 us (10%)
  local copies, waits for them, and re-layouts  25.8 us (6%)
  between operations  16.4 us (4%)
  other arithmetic  11.8 us (3%)
    ppermute x35, waiting for transfers between devices, row_swap(): return lax.ppermute(values, 'rows', [(i, i ^ mask) for i in range(size)])  99.6 us
    pallas_call x39, Pallas kernels, call(): pl.pallas_call(body, out_shape=outs, in_specs=[pl.BlockSpec(memory_space=...  77.1 us
    ppermute x44, waiting for transfers between devices, swap(): return lax.ppermute(values, 'text', [(i, i ^ mask) for i in range(WAYS)])  56.3 us
    ppermute x35, starting transfers between devices, row_swap(): return lax.ppermute(values, 'rows', [(i, i ^ mask) for i in range(size)])  53.7 us
    dot_general x31, matrix products, mm(): lax.dot_general(left, right, (((left_dim,), (right_dim,)), ((), ())), pre...  40.6 us
    ppermute x44, starting transfers between devices, swap(): return lax.ppermute(values, 'text', [(i, i ^ mask) for i in range(WAYS)])  26.9 us
    unnamed x234, local copies, waits for them, and re-layouts  24.4 us
    pallas_call x1, Pallas kernels, weight_grads(): pl.pallas_call(weight_block, grid=(2, rows // tile), out_shape=shaped((ro...  9.95 us
  transfers between devices with their start and end apart: 81, of which 30 were waited for; matrix products, arithmetic and copies ran while one was open for 10% of the time, Pallas kernels for 19%

profile of v5, /device:TPU:0, one launch (start us, length us, event | category | flops | bytes accessed | tf_op | source)
XLA Modules:
  0.0 418.5 jit_solution(11346607934925295606)
XLA Ops:
  14.9 2.9 collective-permute-start.1
  34.5 4.3 %collective-permute-done.3.refs_1_ = bf16[128,768]{1,0:T(8,128)(2,1)S(1)} collective-permute-done((bf16[128,768]{1,0:T(8,128)(2,1)S(1)}, bf16[128,768]{1,0:T(8,128)(2,1)S(1)}, u32[]{:S(2)}, u32[]{:S(2)}) %collective-permute-start.3) | collective-permute-done | bytes 196640 | tf_op jit(solution)/shard_map/ppermute | solution.py:447
  38.8 3.6 collective-permute-start.5
  44.3 1.9 shard_map.234
  46.3 2.2 collective-permute-done.5.refs_3_
  48.5 9.6 %collective-permute-done.4.refs_2_ = bf16[128,768]{1,0:T(8,128)(2,1)S(1)} collective-permute-done((bf16[128,768]{1,0:T(8,128)(2,1)S(1)}, bf16[128,768]{1,0:T(8,128)(2,1)S(1)}, u32[]{:S(2)}, u32[]{:S(2)}) %collective-permute-start.4) | collective-permute-done | bytes 196640 | tf_op jit(solution)/shard_map/ppermute | solution.py:447
  59.8 2.5 collective-permute-start.17
  62.4 1.9 collective-permute-start.15
  68.8 3.9 collective-permute-done.16.refs_2_
  73.4 2.4 collective-permute-start.20
  76.5 1.9 collective-permute-start.18
  81.2 2.7 shard_map.236
  84.0 1.8 convolution_convert_fusion.1.mixed_ref
  87.1 10.6 %collective-permute-done.19.refs_2_ = bf16[128,1024]{1,0:T(8,128)(2,1)S(1)} collective-permute-done((bf16[128,1024]{1,0:T(8,128)(2,1)}, bf16[128,1024]{1,0:T(8,128)(2,1)S(1)}, u32[]{:S(2)}, u32[]{:S(2)}) %collective-permute-start.19) | collective-permute-done | bytes 262176 | tf_op jit(solution)/shard_map/ppermute | solution.py:447
  103.3 4.0 collective-permute-done.28.refs_3_
  108.7 2.2 collective-permute-start.26
  111.4 6.9 %shard_map.238 = (bf16[1024,256]{1,0:T(8,128)(2,1)S(1)}, f32[4,1024]{1,0:T(4,128)S(1)}) custom-call(s32[2]{0:T(128)S(1)} %pad_add_fusion.ids_ref._.here_ref, s32[8,1024]{1,0:T(8,128)S(1)} %stack.53.marks_ref, bf16[1024,768]{1,0:T(8,128)(2,1)S(1)} %convolution_convert_fusion.1.mixed_ref), custom_call_target="tpu_custom_call" | custom-call | bytes 2146312 | tf_op jit(solution)/shard_map/pallas_call | solution.py:352
  119.3 2.0 shard_map.239
  125.4 12.4 %collective-permute-done.31.refs_6_ = bf16[2,128,1024]{2,1,0:T(8,128)(2,1)S(1)} collective-permute-done((bf16[2,128,1024]{2,1,0:T(8,128)(2,1)S(1)}, bf16[2,128,1024]{2,1,0:T(8,128)(2,1)S(1)}, u32[]{:S(2)}, u32[]{:S(2)}) %collective-permute-start.31) | collective-permute-done | bytes 524320 | tf_op jit(solution)/shard_map/ppermute | solution.py:447
  139.0 2.0 shard_map.241
  143.8 1.8 shard_map.243.refs_0_
  145.7 6.4 %collective-permute-done.33.other_ref = bf16[384,512]{1,0:T(8,128)(2,1)S(1)} collective-permute-done((bf16[384,512]{1,0:T(8,128)(2,1)S(1)}, bf16[384,512]{1,0:T(8,128)(2,1)S(1)}, u32[]{:S(2)}, u32[]{:S(2)}) %collective-permute-start.33) | collective-permute-done | bytes 393248 | tf_op jit(solution)/shard_map/ppermute | solution.py:26
  155.6 6.4 %shard_map.242 = (bf16[512,512]{1,0:T(8,128)(2,1)S(1)}, f32[8,512]{1,0:T(8,128)S(1)}) custom-call(s32[2]{0:T(128)S(1)} %pad_add_fusion.ids_ref._.here_ref, s32[8,1024]{1,0:T(8,128)S(1)} %copy-done.25, bf16[512,512]{1,0:T(8,128)(2,1)S(1)} %convolution_convert_fusion.14.query_ref, bf16[384,512]{1,0:T(8,128)(2,1)S(1)} %convolution_convert_fusion.16.own_ref, ...), custom_call_target="tpu_custom_call" | custom-call | bytes 1884168 | tf_op jit(solution)/shard_map/pallas_call | solution.py:352
  162.0 2.5 collective-permute-done.34.refs_1_
  165.7 1.9 collective-permute-done.35
  168.7 1.8 collective-permute-start.38
  171.1 11.7 %collective-permute-done.38.refs_1_ = bf16[256,1024]{1,0:T(8,128)(2,1)S(1)} collective-permute-done((bf16[256,1024]{1,0:T(8,128)(2,1)S(1)}, bf16[256,1024]{1,0:T(8,128)(2,1)S(1)}, u32[]{:S(2)}, u32[]{:S(2)}) %collective-permute-start.38) | collective-permute-done | bytes 524320 | tf_op jit(solution)/shard_map/ppermute | solution.py:26
  187.9 6.2 %fusion.3 = (f32[1024,1024]{1,0:T(8,128)S(1)}, bf16[1024,1024]{1,0:T(8,128)(2,1)S(1)}) fusion(bf16[1024,1024]{1,0:T(8,128)(2,1)} %copy-done.11, bf16[1024,2048]{1,0:T(8,128)(2,1)} %all-gather.2.cloned.1.call-done), kind=kOutput, calls=%fused_computation.4 | convolution fusion | flops 2157969408 | bytes 10485760 | tf_op jit(solution)/shard_map/dot_general | solution.py:20
  194.2 2.4 multiply_convert_fusion.right_a
  198.4 2.2 convolution_convert_fusion.4
  202.3 1.7 collective-permute-start.42
  204.0 9.9 %shard_map.258 = bf16[1024,2048]{1,0:T(8,128)(2,1)} custom-call(bf16[1024,1024]{1,0:T(8,128)(2,1)S(1)} %copy-done.12, bf16[1024,1024]{1,0:T(8,128)(2,1)S(1)} %multiply_convert_fusion.right_a, bf16[1024,1024]{1,0:T(8,128)(2,1)} %copy-done.116, bf16[1024,1024]{1,0:T(8,128)(2,1)} %copy-done.9), custom_call_target="tpu_custom_call" | custom-call | flops 4294967296 | bytes 12582912 | tf_op jit(solution)/shard_map/pallas_call | solution.py:378
  214.0 2.7 fusion.39
  216.9 3.1 multiply_reduce_fusion
  223.3 11.6 %collective-permute-done.45 = bf16[256,1024]{1,0:T(8,128)(2,1)S(1)} collective-permute-done((bf16[256,1024]{1,0:T(8,128)(2,1)S(1)}, bf16[256,1024]{1,0:T(8,128)(2,1)S(1)}, u32[]{:S(2)}, u32[]{:S(2)}) %collective-permute-start.45) | collective-permute-done | bytes 524320 | tf_op jit(solution)/shard_map/ppermute | solution.py:26
  235.7 7.3 %shard_map.248 = (bf16[512,512]{1,0:T(8,128)(2,1)S(1)}, bf16[384,512]{1,0:T(8,128)(2,1)S(1)}, bf16[384,512]{1,0:T(8,128)(2,1)S(1)}) custom-call(s32[2]{0:T(128)S(1)} %pad_add_fusion.ids_ref._.here_ref, s32[8,1024]{1,0:T(8,128)S(1)} %copy-done.26, bf16[512,512]{1,0:T(8,128)(2,1)S(1)} %convolution_convert_fusion.14.query_ref, ...), custom_call_target="tpu_custom_call" | custom-call | bytes 3194888 | tf_op jit(solution)/shard_map/pallas_call | solution.py:352
  243.1 3.1 fusion.32
  246.7 1.8 collective-permute-start.47
  251.5 6.8 %collective-permute-done.47 = bf16[384,512]{1,0:T(8,128)(2,1)S(1)} collective-permute-done((bf16[384,512]{1,0:T(8,128)(2,1)S(1)}, bf16[384,512]{1,0:T(8,128)(2,1)S(1)}, u32[]{:S(2)}, u32[]{:S(2)}) %collective-permute-start.47) | collective-permute-done | bytes 393248 | tf_op jit(solution)/shard_map/ppermute | solution.py:26
  258.3 1.7 collective-permute-start.48
  261.5 1.7 shard_map.251
  264.5 7.5 %collective-permute-done.48.refs_1_ = bf16[256,1024]{1,0:T(8,128)(2,1)} collective-permute-done((bf16[256,1024]{1,0:T(8,128)(2,1)S(1)}, bf16[256,1024]{1,0:T(8,128)(2,1)}, u32[]{:S(2)}, u32[]{:S(2)}) %collective-permute-start.48) | collective-permute-done | bytes 524320 | tf_op jit(solution)/shard_map/ppermute | solution.py:26
  274.2 2.2 shard_map.249
  277.8 10.7 %shard_map.250 = bf16[1024,768]{1,0:T(8,128)(2,1)S(1)} custom-call(s32[2]{0:T(128)S(1)} %pad_add_fusion.ids_ref._.here_ref, s32[8,1024]{1,0:T(8,128)S(1)} %copy-done.27, bf16[1024,768]{1,0:T(8,128)(2,1)S(1)} %copy-done.1, bf16[1024,256]{1,0:T(8,128)(2,1)S(1)} %convolution_convert_fusion.12.grad_ref, f32[4,1024]{1,0:T(4,128)S(1)} %copy-done.67), custom_call_target="tpu_custom_call" | custom-call | bytes 3719176 | tf_op jit(solution)/shard_map/pallas_call | solution.py:352
  288.6 9.9 %collective-permute-done.51.refs_2_ = bf16[4,128,1024]{2,1,0:T(8,128)(2,1)} collective-permute-done((bf16[4,128,1024]{2,1,0:T(8,128)(2,1)}, bf16[4,128,1024]{2,1,0:T(8,128)(2,1)}, u32[]{:S(2)}, u32[]{:S(2)}) %collective-permute-start.51) | collective-permute-done | bytes 1048608 | tf_op jit(solution)/shard_map/ppermute | solution.py:447
  298.5 2.0 convolution_convert_fusion.2
  302.2 2.2 collective-permute-start.56
  306.8 1.9 convolution_convert_fusion.refs_0_
  311.7 2.2 shard_map.253
  316.1 2.2 collective-permute-start.59
  319.5 7.1 %collective-permute-done.57.refs_1_ = bf16[128,1024]{1,0:T(8,128)(2,1)S(1)} collective-permute-done((bf16[128,1024]{1,0:T(8,128)(2,1)S(1)}, bf16[128,1024]{1,0:T(8,128)(2,1)S(1)}, u32[]{:S(2)}, u32[]{:S(2)}) %collective-permute-start.57) | collective-permute-done | bytes 262176 | tf_op jit(solution)/shard_map/ppermute | solution.py:447
  326.6 9.8 %collective-permute-done.58.refs_2_ = bf16[128,1024]{1,0:T(8,128)(2,1)S(1)} collective-permute-done((bf16[128,1024]{1,0:T(8,128)(2,1)S(1)}, bf16[128,1024]{1,0:T(8,128)(2,1)S(1)}, u32[]{:S(2)}, u32[]{:S(2)}) %collective-permute-start.58) | collective-permute-done | bytes 262176 | tf_op jit(solution)/shard_map/ppermute | solution.py:447
  337.3 4.7 %collective-permute-start.60 = (bf16[128,1024]{1,0:T(8,128)(2,1)S(1)}, bf16[128,1024]{1,0:T(8,128)(2,1)S(1)}, u32[]{:S(2)}, u32[]{:S(2)}) collective-permute-start(bf16[128,1024]{1,0:T(8,128)(2,1)S(1)} %get-tuple-element.229), channel_id=1, source_target_pairs={{0,8},{4,12},{8,0},{12,4},{16,24},{20,28},{24,16},{28,20},{1,9},{5... | collective-permute-start | bytes 786440 | tf_op jit(solution)/shard_map/ppermute | solution.py:447
  345.1 5.8 %collective-permute-done.60.refs_5_ = bf16[128,1024]{1,0:T(8,128)(2,1)S(1)} collective-permute-done((bf16[128,1024]{1,0:T(8,128)(2,1)S(1)}, bf16[128,1024]{1,0:T(8,128)(2,1)S(1)}, u32[]{:S(2)}, u32[]{:S(2)}) %collective-permute-start.60) | collective-permute-done | bytes 262176 | tf_op jit(solution)/shard_map/ppermute | solution.py:447
  352.2 11.2 %collective-permute-done.62.refs_6_ = bf16[128,1024]{1,0:T(8,128)(2,1)S(1)} collective-permute-done((bf16[128,1024]{1,0:T(8,128)(2,1)S(1)}, bf16[128,1024]{1,0:T(8,128)(2,1)S(1)}, u32[]{:S(2)}, u32[]{:S(2)}) %collective-permute-start.62) | collective-permute-done | bytes 262176 | tf_op jit(solution)/shard_map/ppermute | solution.py:447
  364.9 3.4 collective-permute-start.64
  370.8 1.9 collective-permute-done.66
  376.1 1.7 collective-permute-start.67
  377.8 1.9 collective-permute-start.68
  382.4 7.0 %collective-permute-done.67.refs_2_ = bf16[128,768]{1,0:T(8,128)(2,1)S(1)} collective-permute-done((bf16[128,768]{1,0:T(8,128)(2,1)}, bf16[128,768]{1,0:T(8,128)(2,1)S(1)}, u32[]{:S(2)}, u32[]{:S(2)}) %collective-permute-start.67) | collective-permute-done | bytes 196640 | tf_op jit(solution)/shard_map/ppermute | solution.py:447
  392.1 4.5 %collective-permute-start.78 = (f32[8,256]{1,0:T(8,128)S(1)}, f32[8,256]{1,0:T(8,128)S(1)}, u32[]{:S(2)}, u32[]{:S(2)}) collective-permute-start(f32[8,256]{1,0:T(8,128)S(1)} %add.197), channel_id=1, source_target_pairs={{0,16},{4,20},{8,24},{12,28},{16,0},{20,4},{24,8},{28,12},{1,17},{... | collective-permute-start | bytes 24584 | tf_op jit(solution)/shard_map/ppermute | solution.py:447
  402.0 2.3 collective-permute-done.72.refs_1_
  405.7 1.9 shard_map.261
  409.3 1.8 shard_map.265
  (449 shorter events, 119.7 us)
Async XLA Ops:
  7.2 180.7 %all-gather.2.cloned.1.call-start = ((), (), s32[]{:S(2)}) async-start(), calls=%async_computation.1 | async-start | bytes 4718592 | tf_op jit(solution)/shard_map/all_gather | solution.py:451
  14.9 10.6 %collective-permute-start.1 = (bf16[144,896]{1,0:T(8,128)(2,1)S(1)}, bf16[144,896]{1,0:T(8,128)(2,1)S(1)}, u32[]{:S(2)}, u32[]{:S(2)}) collective-permute-start(bf16[144,896]{1,0:T(8,128)(2,1)S(1)} %get-tuple-element.146), channel_id=1, source_target_pairs={{0,2},{1,3},{2,0},{3,1},{4,6},{5,7},{6,4},{7,5},{8,10},{9,11},{10,... | collective-permute-start | bytes 774152 | tf_op jit(solution)/shard_map/ppermute | solution.py:26
  28.8 14.0 %collective-permute-start.8 = (bf16[128,1536]{1,0:T(8,128)(2,1)S(1)}, bf16[128,1536]{1,0:T(8,128)(2,1)S(1)}, u32[]{:S(2)}, u32[]{:S(2)}) collective-permute-start(bf16[128,1536]{1,0:T(8,128)(2,1)S(1)} %get-tuple-element.161), channel_id=1, source_target_pairs={{0,2},{1,3},{2,0},{3,1},{4,6},{5,7},{6,4},{7,5},{8,10},{9,11},{10,... | collective-permute-start | bytes 1179656 | tf_op jit(solution)/shard_map/ppermute | solution.py:26
  29.4 29.4 %collective-permute-start.10 = (bf16[256,1024]{1,0:T(8,128)(2,1)S(1)}, bf16[256,1024]{1,0:T(8,128)(2,1)S(1)}, u32[]{:S(2)}, u32[]{:S(2)}) collective-permute-start(bf16[256,1024]{1,0:T(8,128)(2,1)S(1)} %fusion.53.refs_0_), channel_id=1, source_target_pairs={{0,2},{1,3},{2,0},{3,1},{4,6},{5,7},{6,4},{7,5},{8,10},{9,11},{10,... | collective-permute-start | bytes 1572872 | tf_op jit(solution)/shard_map/ppermute | solution.py:26
  30.9 11.5 %collective-permute-start.9 = (bf16[128,1024]{1,0:T(8,128)(2,1)S(1)}, bf16[128,1024]{1,0:T(8,128)(2,1)}, u32[]{:S(2)}, u32[]{:S(2)}) collective-permute-start(bf16[128,1024]{1,0:T(8,128)(2,1)S(1)} %get-tuple-element.163), channel_id=1, source_target_pairs={{0,4},{4,0},{8,12},{12,8},{16,20},{20,16},{24,28},{28,24},{1,5},{5... | collective-permute-start | bytes 786440 | tf_op jit(solution)/shard_map/ppermute | solution.py:447
  33.9 12.3 %collective-permute-start.6 = (bf16[128,768]{1,0:T(8,128)(2,1)S(1)}, bf16[128,768]{1,0:T(8,128)(2,1)S(1)}, u32[]{:S(2)}, u32[]{:S(2)}) collective-permute-start(bf16[128,768]{1,0:T(8,128)(2,1)S(1)} %get-tuple-element.159.refs_0_), channel_id=1, source_target_pairs={{0,4},{4,0},{8,12},{12,8},{16,20},{20,16},{24,28},{28,24},{1,5},{5... | collective-permute-start | bytes 589832 | tf_op jit(solution)/shard_map/ppermute | solution.py:447
  38.8 9.7 %collective-permute-start.5 = (bf16[128,768]{1,0:T(8,128)(2,1)S(1)}, bf16[128,768]{1,0:T(8,128)(2,1)S(1)}, u32[]{:S(2)}, u32[]{:S(2)}) collective-permute-start(bf16[128,768]{1,0:T(8,128)(2,1)S(1)} %get-tuple-element.159.refs_0_), channel_id=1, source_target_pairs={{0,24},{4,28},{8,16},{12,20},{16,8},{20,12},{24,0},{28,4},{1,25},{... | collective-permute-start | bytes 589832 | tf_op jit(solution)/shard_map/ppermute | solution.py:447
  42.4 15.7 %collective-permute-start.4 = (bf16[128,768]{1,0:T(8,128)(2,1)S(1)}, bf16[128,768]{1,0:T(8,128)(2,1)S(1)}, u32[]{:S(2)}, u32[]{:S(2)}) collective-permute-start(bf16[128,768]{1,0:T(8,128)(2,1)S(1)} %get-tuple-element.159.refs_0_), channel_id=1, source_target_pairs={{0,16},{4,20},{8,24},{12,28},{16,0},{20,4},{24,8},{28,12},{1,17},{... | collective-permute-start | bytes 589832 | tf_op jit(solution)/shard_map/ppermute | solution.py:447
  42.7 15.4 %collective-permute-start.7 = (bf16[128,768]{1,0:T(8,128)(2,1)S(1)}, bf16[128,768]{1,0:T(8,128)(2,1)S(1)}, u32[]{:S(2)}, u32[]{:S(2)}) collective-permute-start(bf16[128,768]{1,0:T(8,128)(2,1)S(1)} %collective-permute-done.3.refs_1_), channel_id=1, source_target_pairs={{0,4},{4,0},{8,12},{12,8},{16,20},{20,16},{24,28},{28,24},{1,5},{5... | collective-permute-start | bytes 589832 | tf_op jit(solution)/shard_map/ppermute | solution.py:447
  46.2 16.2 %collective-permute-start.12 = (bf16[256,1024]{1,0:T(8,128)(2,1)S(1)}, bf16[256,1024]{1,0:T(8,128)(2,1)S(1)}, u32[]{:S(2)}, u32[]{:S(2)}) collective-permute-start(bf16[256,1024]{1,0:T(8,128)(2,1)S(1)} %fusion.53.refs_0_), channel_id=1, source_target_pairs={{0,1},{1,0},{2,3},{3,2},{4,5},{5,4},{6,7},{7,6},{8,9},{9,8},{10,11... | collective-permute-start | bytes 1572872 | tf_op jit(solution)/shard_map/ppermute | solution.py:26
  58.8 19.6 %collective-permute-start.11 = (bf16[2,128,768]{2,1,0:T(8,128)(2,1)S(1)}, bf16[2,128,768]{2,1,0:T(8,128)(2,1)S(1)}, u32[]{:S(2)}, u32[]{:S(2)}) collective-permute-start(bf16[2,128,768]{2,1,0:T(8,128)(2,1)S(1)} %pad_maximum_fusion.1), channel_id=1, source_target_pairs={{0,4},{4,0},{8,12},{12,8},{16,20},{20,16},{24,28},{28,24},{1,5},{5... | collective-permute-start | bytes 1179656 | tf_op jit(solution)/shard_map/ppermute | solution.py:447
  59.4 17.1 %collective-permute-start.14 = (bf16[96,1024]{1,0:T(8,128)(2,1)}, bf16[96,1024]{1,0:T(8,128)(2,1)S(1)}, u32[]{:S(2)}, u32[]{:S(2)}) collective-permute-start(bf16[96,1024]{1,0:T(8,128)(2,1)} %bitcast.10.refs_0_), channel_id=1, source_target_pairs={{0,2},{1,3},{2,0},{3,1},{4,6},{5,7},{6,4},{7,5},{8,10},{9,11},{10,... | collective-permute-start | bytes 589832 | tf_op jit(solution)/shard_map/ppermute | solution.py:26
  59.8 8.3 %collective-permute-start.17 = (bf16[64,1024]{1,0:T(8,128)(2,1)S(1)}, bf16[64,1024]{1,0:T(8,128)(2,1)S(1)}, u32[]{:S(2)}, u32[]{:S(2)}) collective-permute-start(bf16[64,1024]{1,0:T(8,128)(2,1)S(1)} %get-tuple-element.298.refs_0_), channel_id=1, source_target_pairs={{0,24},{4,28},{8,16},{12,20},{16,8},{20,12},{24,0},{28,4},{1,25},{... | collective-permute-start | bytes 393224 | tf_op jit(solution)/shard_map/ppermute | solution.py:447
  62.4 10.3 %collective-permute-start.16 = (bf16[64,1024]{1,0:T(8,128)(2,1)S(1)}, bf16[64,1024]{1,0:T(8,128)(2,1)S(1)}, u32[]{:S(2)}, u32[]{:S(2)}) collective-permute-start(bf16[64,1024]{1,0:T(8,128)(2,1)S(1)} %get-tuple-element.298.refs_0_), channel_id=1, source_target_pairs={{0,16},{4,20},{8,24},{12,28},{16,0},{20,4},{24,8},{28,12},{1,17},{... | collective-permute-start | bytes 393224 | tf_op jit(solution)/shard_map/ppermute | solution.py:447
  62.4 13.4 %collective-permute-start.15 = (bf16[64,1024]{1,0:T(8,128)(2,1)S(1)}, bf16[64,1024]{1,0:T(8,128)(2,1)S(1)}, u32[]{:S(2)}, u32[]{:S(2)}) collective-permute-start(bf16[64,1024]{1,0:T(8,128)(2,1)S(1)} %get-tuple-element.298.refs_0_), channel_id=1, source_target_pairs={{0,8},{4,12},{8,0},{12,4},{16,24},{20,28},{24,16},{28,20},{1,9},{5... | collective-permute-start | bytes 393224 | tf_op jit(solution)/shard_map/ppermute | solution.py:447
  68.8 34.0 %collective-permute-start.21 = (bf16[96,1024]{1,0:T(8,128)(2,1)}, bf16[96,1024]{1,0:T(8,128)(2,1)}, u32[]{:S(2)}, u32[]{:S(2)}) collective-permute-start(bf16[96,1024]{1,0:T(8,128)(2,1)} %bitcast.10.refs_0_), channel_id=1, source_target_pairs={{0,1},{1,0},{2,3},{3,2},{4,5},{5,4},{6,7},{7,6},{8,9},{9,8},{10,11... | collective-permute-start | bytes 589832 | tf_op jit(solution)/shard_map/ppermute | solution.py:26
  73.4 13.8 %collective-permute-start.20 = (bf16[128,1024]{1,0:T(8,128)(2,1)}, bf16[128,1024]{1,0:T(8,128)(2,1)S(1)}, u32[]{:S(2)}, u32[]{:S(2)}) collective-permute-start(bf16[128,1024]{1,0:T(8,128)(2,1)} %get-tuple-element.184.refs_0_), channel_id=1, source_target_pairs={{0,24},{4,28},{8,16},{12,20},{16,8},{20,12},{24,0},{28,4},{1,25},{... | collective-permute-start | bytes 786440 | tf_op jit(solution)/shard_map/ppermute | solution.py:447
  76.5 21.3 %collective-permute-start.19 = (bf16[128,1024]{1,0:T(8,128)(2,1)}, bf16[128,1024]{1,0:T(8,128)(2,1)S(1)}, u32[]{:S(2)}, u32[]{:S(2)}) collective-permute-start(bf16[128,1024]{1,0:T(8,128)(2,1)} %get-tuple-element.184.refs_0_), channel_id=1, source_target_pairs={{0,16},{4,20},{8,24},{12,28},{16,0},{20,4},{24,8},{28,12},{1,17},{... | collective-permute-start | bytes 786440 | tf_op jit(solution)/shard_map/ppermute | solution.py:447
  76.5 21.2 %collective-permute-start.18 = (bf16[128,1024]{1,0:T(8,128)(2,1)}, bf16[128,1024]{1,0:T(8,128)(2,1)}, u32[]{:S(2)}, u32[]{:S(2)}) collective-permute-start(bf16[128,1024]{1,0:T(8,128)(2,1)} %get-tuple-element.184.refs_0_), channel_id=1, source_target_pairs={{0,8},{4,12},{8,0},{12,4},{16,24},{20,28},{24,16},{28,20},{1,9},{5... | collective-permute-start | bytes 786440 | tf_op jit(solution)/shard_map/ppermute | solution.py:447
  97.7 23.7 %collective-permute-start.25 = (bf16[256,1024]{1,0:T(8,128)(2,1)S(1)}, bf16[256,1024]{1,0:T(8,128)(2,1)}, u32[]{:S(2)}, u32[]{:S(2)}) collective-permute-start(bf16[256,1024]{1,0:T(8,128)(2,1)S(1)} %bitcast.75), channel_id=1, source_target_pairs={{0,2},{1,3},{2,0},{3,1},{4,6},{5,7},{6,4},{7,5},{8,10},{9,11},{10,... | collective-permute-start | bytes 1572872 | tf_op jit(solution)/shard_map/ppermute | solution.py:26
  99.5 8.5 %collective-permute-start.22 = (bf16[96,1024]{1,0:T(8,128)(2,1)S(1)}, bf16[96,1024]{1,0:T(8,128)(2,1)S(1)}, u32[]{:S(2)}, u32[]{:S(2)}) collective-permute-start(bf16[96,1024]{1,0:T(8,128)(2,1)S(1)} %copy-done.42), channel_id=1, source_target_pairs={{0,1},{1,0},{2,3},{3,2},{4,5},{5,4},{6,7},{7,6},{8,9},{9,8},{10,11... | collective-permute-start | bytes 589832 | tf_op jit(solution)/shard_map/ppermute | solution.py:26
  101.3 20.1 %collective-permute-start.23 = (bf16[128,1024]{1,0:T(8,128)(2,1)}, bf16[128,1024]{1,0:T(8,128)(2,1)}, u32[]{:S(2)}, u32[]{:S(2)}) collective-permute-start(bf16[128,1024]{1,0:T(8,128)(2,1)} %get-tuple-element.184.refs_0_), channel_id=1, source_target_pairs={{0,4},{4,0},{8,12},{12,8},{16,20},{20,16},{24,28},{28,24},{1,5},{5... | collective-permute-start | bytes 786440 | tf_op jit(solution)/shard_map/ppermute | solution.py:447
  102.8 18.7 %collective-permute-start.24 = (bf16[128,1024]{1,0:T(8,128)(2,1)}, bf16[128,1024]{1,0:T(8,128)(2,1)}, u32[]{:S(2)}, u32[]{:S(2)}) collective-permute-start(bf16[128,1024]{1,0:T(8,128)(2,1)} %collective-permute-done.18.refs_1_), channel_id=1, source_target_pairs={{0,4},{4,0},{8,12},{12,8},{16,20},{20,16},{24,28},{28,24},{1,5},{5... | collective-permute-start | bytes 786440 | tf_op jit(solution)/shard_map/ppermute | solution.py:447
  108.0 13.4 %collective-permute-start.27 = (bf16[64,1024]{1,0:T(8,128)(2,1)S(1)}, bf16[64,1024]{1,0:T(8,128)(2,1)}, u32[]{:S(2)}, u32[]{:S(2)}) collective-permute-start(bf16[64,1024]{1,0:T(8,128)(2,1)S(1)} %get-tuple-element.187.refs_0_), channel_id=1, source_target_pairs={{0,16},{4,20},{8,24},{12,28},{16,0},{20,4},{24,8},{28,12},{1,17},{... | collective-permute-start | bytes 393224 | tf_op jit(solution)/shard_map/ppermute | solution.py:447
  108.7 12.7 %collective-permute-start.26 = (bf16[64,1024]{1,0:T(8,128)(2,1)S(1)}, bf16[64,1024]{1,0:T(8,128)(2,1)}, u32[]{:S(2)}, u32[]{:S(2)}) collective-permute-start(bf16[64,1024]{1,0:T(8,128)(2,1)S(1)} %get-tuple-element.187.refs_0_), channel_id=1, source_target_pairs={{0,8},{4,12},{8,0},{12,4},{16,24},{20,28},{24,16},{28,20},{1,9},{5... | collective-permute-start | bytes 393224 | tf_op jit(solution)/shard_map/ppermute | solution.py:447
  111.2 261.6 %reduce-scatter.2.cloned.1.call-start = ((), (), s32[]{:S(2)}) async-start(), calls=%async_computation.2 | async-start | bytes 4718592 | tf_op jit(solution)/shard_map/reduce_scatter | solution.py:455
  122.0 15.8 %collective-permute-start.31 = (bf16[2,128,1024]{2,1,0:T(8,128)(2,1)S(1)}, bf16[2,128,1024]{2,1,0:T(8,128)(2,1)S(1)}, u32[]{:S(2)}, u32[]{:S(2)}) collective-permute-start(bf16[2,128,1024]{2,1,0:T(8,128)(2,1)S(1)} %pad_maximum_fusion), channel_id=1, source_target_pairs={{0,4},{4,0},{8,12},{12,8},{16,20},{20,16},{24,28},{28,24},{1,5},{5... | collective-permute-start | bytes 1572872 | tf_op jit(solution)/shard_map/ppermute | solution.py:447
  124.9 14.0 %collective-permute-start.30 = (bf16[256,1024]{1,0:T(8,128)(2,1)S(1)}, bf16[256,1024]{1,0:T(8,128)(2,1)S(1)}, u32[]{:S(2)}, u32[]{:S(2)}) collective-permute-start(bf16[256,1024]{1,0:T(8,128)(2,1)S(1)} %fusion.45), channel_id=1, source_target_pairs={{0,2},{1,3},{2,0},{3,1},{4,6},{5,7},{6,4},{7,5},{8,10},{9,11},{10,... | collective-permute-start | bytes 1572872 | tf_op jit(solution)/shard_map/ppermute | solution.py:26
  141.6 10.5 %collective-permute-start.33 = (bf16[384,512]{1,0:T(8,128)(2,1)S(1)}, bf16[384,512]{1,0:T(8,128)(2,1)S(1)}, u32[]{:S(2)}, u32[]{:S(2)}) collective-permute-start(bf16[384,512]{1,0:T(8,128)(2,1)S(1)} %convolution_convert_fusion.16.own_ref), channel_id=1, source_target_pairs={{0,2},{1,3},{2,0},{3,1},{4,6},{5,7},{6,4},{7,5},{8,10},{9,11},{10,... | collective-permute-start | bytes 1179656 | tf_op jit(solution)/shard_map/ppermute | solution.py:26
  143.5 9.6 %collective-permute-start.32 = (bf16[256,1024]{1,0:T(8,128)(2,1)S(1)}, bf16[256,1024]{1,0:T(8,128)(2,1)S(1)}, u32[]{:S(2)}, u32[]{:S(2)}) collective-permute-start(bf16[256,1024]{1,0:T(8,128)(2,1)S(1)} %add_convert_fusion.2.refs_0_), channel_id=1, source_target_pairs={{0,1},{1,0},{2,3},{3,2},{4,5},{5,4},{6,7},{7,6},{8,9},{9,8},{10,11... | collective-permute-start | bytes 1572872 | tf_op jit(solution)/shard_map/ppermute | solution.py:26
  152.1 12.4 %collective-permute-start.34 = (bf16[256,1024]{1,0:T(8,128)(2,1)S(1)}, bf16[256,1024]{1,0:T(8,128)(2,1)S(1)}, u32[]{:S(2)}, u32[]{:S(2)}) collective-permute-start(bf16[256,1024]{1,0:T(8,128)(2,1)S(1)} %shard_map.243.refs_0_), channel_id=1, source_target_pairs={{0,2},{1,3},{2,0},{3,1},{4,6},{5,7},{6,4},{7,5},{8,10},{9,11},{10,... | collective-permute-start | bytes 1572872 | tf_op jit(solution)/shard_map/ppermute | solution.py:26
  168.7 14.0 %collective-permute-start.38 = (bf16[256,1024]{1,0:T(8,128)(2,1)S(1)}, bf16[256,1024]{1,0:T(8,128)(2,1)S(1)}, u32[]{:S(2)}, u32[]{:S(2)}) collective-permute-start(bf16[256,1024]{1,0:T(8,128)(2,1)S(1)} %add_convert_fusion.1.refs_0_), channel_id=1, source_target_pairs={{0,2},{1,3},{2,0},{3,1},{4,6},{5,7},{6,4},{7,5},{8,10},{9,11},{10,... | collective-permute-start | bytes 1572872 | tf_op jit(solution)/shard_map/ppermute | solution.py:26
  170.5 12.3 %collective-permute-start.36 = (bf16[256,1024]{1,0:T(8,128)(2,1)S(1)}, bf16[256,1024]{1,0:T(8,128)(2,1)S(1)}, u32[]{:S(2)}, u32[]{:S(2)}) collective-permute-start(bf16[256,1024]{1,0:T(8,128)(2,1)S(1)} %bitcast.76), channel_id=1, source_target_pairs={{0,1},{1,0},{2,3},{3,2},{4,5},{5,4},{6,7},{7,6},{8,9},{9,8},{10,11... | collective-permute-start | bytes 1572872 | tf_op jit(solution)/shard_map/ppermute | solution.py:26
  170.5 12.3 %collective-permute-start.37 = (bf16[256,1024]{1,0:T(8,128)(2,1)}, bf16[256,1024]{1,0:T(8,128)(2,1)S(1)}, u32[]{:S(2)}, u32[]{:S(2)}) collective-permute-start(bf16[256,1024]{1,0:T(8,128)(2,1)} %collective-permute-done.25.refs_1_), channel_id=1, source_target_pairs={{0,1},{1,0},{2,3},{3,2},{4,5},{5,4},{6,7},{7,6},{8,9},{9,8},{10,11... | collective-permute-start | bytes 1572872 | tf_op jit(solution)/shard_map/ppermute | solution.py:26
  171.0 14.8 %collective-permute-start.39 = (bf16[256,1024]{1,0:T(8,128)(2,1)S(1)}, bf16[256,1024]{1,0:T(8,128)(2,1)S(1)}, u32[]{:S(2)}, u32[]{:S(2)}) collective-permute-start(bf16[256,1024]{1,0:T(8,128)(2,1)S(1)} %add_convert_fusion.1.refs_0_), channel_id=1, source_target_pairs={{0,1},{1,0},{2,3},{3,2},{4,5},{5,4},{6,7},{7,6},{8,9},{9,8},{10,11... | collective-permute-start | bytes 1572872 | tf_op jit(solution)/shard_map/ppermute | solution.py:26
  200.7 13.3 %collective-permute-start.44 = (bf16[512,1024]{1,0:T(8,128)(2,1)}, bf16[512,1024]{1,0:T(8,128)(2,1)}, u32[]{:S(2)}, u32[]{:S(2)}) collective-permute-start(bf16[512,1024]{1,0:T(8,128)(2,1)} %convolution_convert_fusion.4), channel_id=1, source_target_pairs={{0,1},{1,0},{2,3},{3,2},{4,5},{5,4},{6,7},{7,6},{8,9},{9,8},{10,11... | collective-permute-start | bytes 3145736 | tf_op jit(solution)/shard_map/ppermute | solution.py:26
  202.3 14.6 %collective-permute-start.42 = (bf16[256,1024]{1,0:T(8,128)(2,1)}, bf16[256,1024]{1,0:T(8,128)(2,1)}, u32[]{:S(2)}, u32[]{:S(2)}) collective-permute-start(bf16[256,1024]{1,0:T(8,128)(2,1)} %fusion.42), channel_id=1, source_target_pairs={{0,2},{1,3},{2,0},{3,1},{4,6},{5,7},{6,4},{7,5},{8,10},{9,11},{10,... | collective-permute-start | bytes 1572872 | tf_op jit(solution)/shard_map/ppermute | solution.py:26
  220.6 14.3 %collective-permute-start.45 = (bf16[256,1024]{1,0:T(8,128)(2,1)S(1)}, bf16[256,1024]{1,0:T(8,128)(2,1)S(1)}, u32[]{:S(2)}, u32[]{:S(2)}) collective-permute-start(bf16[256,1024]{1,0:T(8,128)(2,1)S(1)} %fusion.39), channel_id=1, source_target_pairs={{0,2},{1,3},{2,0},{3,1},{4,6},{5,7},{6,4},{7,5},{8,10},{9,11},{10,... | collective-permute-start | bytes 1572872 | tf_op jit(solution)/shard_map/ppermute | solution.py:26
  246.7 11.5 %collective-permute-start.47 = (bf16[384,512]{1,0:T(8,128)(2,1)S(1)}, bf16[384,512]{1,0:T(8,128)(2,1)S(1)}, u32[]{:S(2)}, u32[]{:S(2)}) collective-permute-start(bf16[384,512]{1,0:T(8,128)(2,1)S(1)} %get-tuple-element.214), channel_id=1, source_target_pairs={{0,2},{1,3},{2,0},{3,1},{4,6},{5,7},{6,4},{7,5},{8,10},{9,11},{10,... | collective-permute-start | bytes 1179656 | tf_op jit(solution)/shard_map/ppermute | solution.py:26
  258.3 13.7 %collective-permute-start.48 = (bf16[256,1024]{1,0:T(8,128)(2,1)S(1)}, bf16[256,1024]{1,0:T(8,128)(2,1)}, u32[]{:S(2)}, u32[]{:S(2)}) collective-permute-start(bf16[256,1024]{1,0:T(8,128)(2,1)S(1)} %get-tuple-element.215.refs_0_), channel_id=1, source_target_pairs={{0,2},{1,3},{2,0},{3,1},{4,6},{5,7},{6,4},{7,5},{8,10},{9,11},{10,... | collective-permute-start | bytes 1572872 | tf_op jit(solution)/shard_map/ppermute | solution.py:26
  264.3 34.2 %collective-permute-start.51 = (bf16[4,128,1024]{2,1,0:T(8,128)(2,1)}, bf16[4,128,1024]{2,1,0:T(8,128)(2,1)}, u32[]{:S(2)}, u32[]{:S(2)}) collective-permute-start(bf16[4,128,1024]{2,1,0:T(8,128)(2,1)} %shard_map.251), channel_id=1, source_target_pairs={{0,4},{4,0},{8,12},{12,8},{16,20},{20,16},{24,28},{28,24},{1,5},{5... | collective-permute-start | bytes 3145736 | tf_op jit(solution)/shard_map/ppermute | solution.py:447
  264.5 9.7 %collective-permute-start.49 = (bf16[256,1024]{1,0:T(8,128)(2,1)S(1)}, bf16[256,1024]{1,0:T(8,128)(2,1)}, u32[]{:S(2)}, u32[]{:S(2)}) collective-permute-start(bf16[256,1024]{1,0:T(8,128)(2,1)S(1)} %get-tuple-element.215.refs_0_), channel_id=1, source_target_pairs={{0,1},{1,0},{2,3},{3,2},{4,5},{5,4},{6,7},{7,6},{8,9},{9,8},{10,11... | collective-permute-start | bytes 1572872 | tf_op jit(solution)/shard_map/ppermute | solution.py:26
  273.6 31.2 %collective-permute-start.54 = (bf16[192,1024]{1,0:T(8,128)(2,1)S(1)}, bf16[192,1024]{1,0:T(8,128)(2,1)S(1)}, u32[]{:S(2)}, u32[]{:S(2)}) collective-permute-start(bf16[192,1024]{1,0:T(8,128)(2,1)S(1)} %convolution_convert_fusion.15), channel_id=1, source_target_pairs={{0,1},{1,0},{2,3},{3,2},{4,5},{5,4},{6,7},{7,6},{8,9},{9,8},{10,11... | collective-permute-start | bytes 1179656 | tf_op jit(solution)/shard_map/ppermute | solution.py:26
  300.5 8.2 %collective-permute-start.52 = (bf16[512,1024]{1,0:T(8,128)(2,1)}, bf16[512,1024]{1,0:T(8,128)(2,1)S(1)}, u32[]{:S(2)}, u32[]{:S(2)}) collective-permute-start(bf16[512,1024]{1,0:T(8,128)(2,1)} %convolution_convert_fusion.2), channel_id=1, source_target_pairs={{0,1},{1,0},{2,3},{3,2},{4,5},{5,4},{6,7},{7,6},{8,9},{9,8},{10,11... | collective-permute-start | bytes 3145736 | tf_op jit(solution)/shard_map/ppermute | solution.py:26
  302.2 16.2 %collective-permute-start.56 = (bf16[4,128,512]{2,1,0:T(8,128)(2,1)S(1)}, bf16[4,128,512]{2,1,0:T(8,128)(2,1)S(1)}, u32[]{:S(2)}, u32[]{:S(2)}) collective-permute-start(bf16[4,128,512]{2,1,0:T(8,128)(2,1)S(1)} %shard_map.252), channel_id=1, source_target_pairs={{0,4},{4,0},{8,12},{12,8},{16,20},{20,16},{24,28},{28,24},{1,5},{5... | collective-permute-start | bytes 1572872 | tf_op jit(solution)/shard_map/ppermute | solution.py:447
  305.3 10.8 %collective-permute-start.55 = (bf16[96,1024]{1,0:T(8,128)(2,1)S(1)}, bf16[96,1024]{1,0:T(8,128)(2,1)S(1)}, u32[]{:S(2)}, u32[]{:S(2)}) collective-permute-start(bf16[96,1024]{1,0:T(8,128)(2,1)S(1)} %add_convert_fusion.4), channel_id=1, source_target_pairs={{0,2},{1,3},{2,0},{3,1},{4,6},{5,7},{6,4},{7,5},{8,10},{9,11},{10,... | collective-permute-start | bytes 589832 | tf_op jit(solution)/shard_map/ppermute | solution.py:26
  310.3 26.1 %collective-permute-start.53 = (bf16[256,1024]{1,0:T(8,128)(2,1)S(1)}, bf16[256,1024]{1,0:T(8,128)(2,1)S(1)}, u32[]{:S(2)}, u32[]{:S(2)}) collective-permute-start(bf16[256,1024]{1,0:T(8,128)(2,1)S(1)} %fusion.38), channel_id=1, source_target_pairs={{0,2},{1,3},{2,0},{3,1},{4,6},{5,7},{6,4},{7,5},{8,10},{9,11},{10,... | collective-permute-start | bytes 1572872 | tf_op jit(solution)/shard_map/ppermute | solution.py:26
  313.9 12.7 %collective-permute-start.57 = (bf16[128,1024]{1,0:T(8,128)(2,1)S(1)}, bf16[128,1024]{1,0:T(8,128)(2,1)S(1)}, u32[]{:S(2)}, u32[]{:S(2)}) collective-permute-start(bf16[128,1024]{1,0:T(8,128)(2,1)S(1)} %get-tuple-element.223), channel_id=1, source_target_pairs={{0,8},{4,12},{8,0},{12,4},{16,24},{20,28},{24,16},{28,20},{1,9},{5... | collective-permute-start | bytes 786440 | tf_op jit(solution)/shard_map/ppermute | solution.py:447
  315.0 21.4 %collective-permute-start.58 = (bf16[128,1024]{1,0:T(8,128)(2,1)S(1)}, bf16[128,1024]{1,0:T(8,128)(2,1)S(1)}, u32[]{:S(2)}, u32[]{:S(2)}) collective-permute-start(bf16[128,1024]{1,0:T(8,128)(2,1)S(1)} %get-tuple-element.224), channel_id=1, source_target_pairs={{0,16},{4,20},{8,24},{12,28},{16,0},{20,4},{24,8},{28,12},{1,17},{... | collective-permute-start | bytes 786440 | tf_op jit(solution)/shard_map/ppermute | solution.py:447
  316.1 20.3 %collective-permute-start.59 = (bf16[128,1024]{1,0:T(8,128)(2,1)S(1)}, bf16[128,1024]{1,0:T(8,128)(2,1)S(1)}, u32[]{:S(2)}, u32[]{:S(2)}) collective-permute-start(bf16[128,1024]{1,0:T(8,128)(2,1)S(1)} %get-tuple-element.225), channel_id=1, source_target_pairs={{0,24},{4,28},{8,16},{12,20},{16,8},{20,12},{24,0},{28,4},{1,25},{... | collective-permute-start | bytes 786440 | tf_op jit(solution)/shard_map/ppermute | solution.py:447
  318.4 33.8 %collective-permute-start.61 = (bf16[4,128,768]{2,1,0:T(8,128)(2,1)S(1)}, bf16[4,128,768]{2,1,0:T(8,128)(2,1)S(1)}, u32[]{:S(2)}, u32[]{:S(2)}) collective-permute-start(bf16[4,128,768]{2,1,0:T(8,128)(2,1)S(1)} %dynamic-slice_bitcast_fusion), channel_id=1, source_target_pairs={{0,4},{4,0},{8,12},{12,8},{16,20},{20,16},{24,28},{28,24},{1,5},{5... | collective-permute-start | bytes 2359304 | tf_op jit(solution)/shard_map/ppermute | solution.py:447
  337.3 13.5 %collective-permute-start.60 = (bf16[128,1024]{1,0:T(8,128)(2,1)S(1)}, bf16[128,1024]{1,0:T(8,128)(2,1)S(1)}, u32[]{:S(2)}, u32[]{:S(2)}) collective-permute-start(bf16[128,1024]{1,0:T(8,128)(2,1)S(1)} %get-tuple-element.229), channel_id=1, source_target_pairs={{0,8},{4,12},{8,0},{12,4},{16,24},{20,28},{24,16},{28,20},{1,9},{5... | collective-permute-start | bytes 786440 | tf_op jit(solution)/shard_map/ppermute | solution.py:447
  342.0 21.4 %collective-permute-start.62 = (bf16[128,1024]{1,0:T(8,128)(2,1)S(1)}, bf16[128,1024]{1,0:T(8,128)(2,1)S(1)}, u32[]{:S(2)}, u32[]{:S(2)}) collective-permute-start(bf16[128,1024]{1,0:T(8,128)(2,1)S(1)} %get-tuple-element.233), channel_id=1, source_target_pairs={{0,16},{4,20},{8,24},{12,28},{16,0},{20,4},{24,8},{28,12},{1,17},{... | collective-permute-start | bytes 786440 | tf_op jit(solution)/shard_map/ppermute | solution.py:447
  342.9 20.4 %collective-permute-start.63 = (bf16[128,1024]{1,0:T(8,128)(2,1)S(1)}, bf16[128,1024]{1,0:T(8,128)(2,1)S(1)}, u32[]{:S(2)}, u32[]{:S(2)}) collective-permute-start(bf16[128,1024]{1,0:T(8,128)(2,1)S(1)} %get-tuple-element.234), channel_id=1, source_target_pairs={{0,24},{4,28},{8,16},{12,20},{16,8},{20,12},{24,0},{28,4},{1,25},{... | collective-permute-start | bytes 786440 | tf_op jit(solution)/shard_map/ppermute | solution.py:447
  352.1 16.3 %collective-permute-start.65 = (f32[8,512]{1,0:T(8,128)S(1)}, f32[8,512]{1,0:T(8,128)S(1)}, u32[]{:S(2)}, u32[]{:S(2)}) collective-permute-start(f32[8,512]{1,0:T(8,128)S(1)} %get-tuple-element.239), channel_id=1, source_target_pairs={{0,1},{1,0},{2,3},{3,2},{4,5},{5,4},{6,7},{7,6},{8,9},{9,8},{10,11... | collective-permute-start | bytes 49160 | tf_op jit(solution)/shard_map/ppermute | solution.py:26
  372.7 9.6 %collective-permute-start.76 = (f32[8,256]{1,0:T(8,128)S(1)}, f32[8,256]{1,0:T(8,128)S(1)}, u32[]{:S(2)}, u32[]{:S(2)}) collective-permute-start(f32[8,256]{1,0:T(8,128)S(1)} %add.195), channel_id=1, source_target_pairs={{0,4},{4,0},{8,12},{12,8},{16,20},{20,16},{24,28},{28,24},{1,5},{5... | collective-permute-start | bytes 24584 | tf_op jit(solution)/shard_map/ppermute | solution.py:447
  375.1 22.9 %collective-permute-start.74 = (bf16[128,1024]{1,0:T(8,128)(2,1)S(1)}, bf16[128,1024]{1,0:T(8,128)(2,1)S(1)}, u32[]{:S(2)}, u32[]{:S(2)}) collective-permute-start(bf16[128,1024]{1,0:T(8,128)(2,1)S(1)} %get-tuple-element.270), channel_id=1, source_target_pairs={{0,2},{1,3},{2,0},{3,1},{4,6},{5,7},{6,4},{7,5},{8,10},{9,11},{10,... | collective-permute-start | bytes 786440 | tf_op jit(solution)/shard_map/ppermute | solution.py:26
  376.1 13.3 %collective-permute-start.67 = (bf16[128,768]{1,0:T(8,128)(2,1)}, bf16[128,768]{1,0:T(8,128)(2,1)S(1)}, u32[]{:S(2)}, u32[]{:S(2)}) collective-permute-start(bf16[128,768]{1,0:T(8,128)(2,1)} %copy-done.72), channel_id=1, source_target_pairs={{0,16},{4,20},{8,24},{12,28},{16,0},{20,4},{24,8},{28,12},{1,17},{... | collective-permute-start | bytes 589832 | tf_op jit(solution)/shard_map/ppermute | solution.py:447
  377.8 11.6 %collective-permute-start.68 = (bf16[128,768]{1,0:T(8,128)(2,1)}, bf16[128,768]{1,0:T(8,128)(2,1)S(1)}, u32[]{:S(2)}, u32[]{:S(2)}) collective-permute-start(bf16[128,768]{1,0:T(8,128)(2,1)} %copy-done.71), channel_id=1, source_target_pairs={{0,24},{4,28},{8,16},{12,20},{16,8},{20,12},{24,0},{28,4},{1,25},{... | collective-permute-start | bytes 589832 | tf_op jit(solution)/shard_map/ppermute | solution.py:447
  380.9 15.7 %collective-permute-start.71 = (bf16[128,512]{1,0:T(8,128)(2,1)S(1)}, bf16[128,512]{1,0:T(8,128)(2,1)S(1)}, u32[]{:S(2)}, u32[]{:S(2)}) collective-permute-start(bf16[128,512]{1,0:T(8,128)(2,1)S(1)} %get-tuple-element.259), channel_id=1, source_target_pairs={{0,4},{4,0},{8,12},{12,8},{16,20},{20,16},{24,28},{28,24},{1,5},{5... | collective-permute-start | bytes 393224 | tf_op jit(solution)/shard_map/ppermute | solution.py:447
  382.4 9.7 %collective-permute-start.77 = (f32[8,256]{1,0:T(8,128)S(1)}, f32[8,256]{1,0:T(8,128)S(1)}, u32[]{:S(2)}, u32[]{:S(2)}) collective-permute-start(f32[8,256]{1,0:T(8,128)S(1)} %add.196), channel_id=1, source_target_pairs={{0,8},{4,12},{8,0},{12,4},{16,24},{20,28},{24,16},{28,20},{1,9},{5... | collective-permute-start | bytes 24584 | tf_op jit(solution)/shard_map/ppermute | solution.py:447
  391.0 9.2 %collective-permute-start.69 = (bf16[128,384]{1,0:T(8,128)(2,1)S(1)}, bf16[128,384]{1,0:T(8,128)(2,1)S(1)}, u32[]{:S(2)}, u32[]{:S(2)}) collective-permute-start(bf16[128,384]{1,0:T(8,128)(2,1)S(1)} %get-tuple-element.247), channel_id=1, source_target_pairs={{0,2},{1,3},{2,0},{3,1},{4,6},{5,7},{6,4},{7,5},{8,10},{9,11},{10,... | collective-permute-start | bytes 294920 | tf_op jit(solution)/shard_map/ppermute | solution.py:26
  392.1 8.1 %collective-permute-start.78 = (f32[8,256]{1,0:T(8,128)S(1)}, f32[8,256]{1,0:T(8,128)S(1)}, u32[]{:S(2)}, u32[]{:S(2)}) collective-permute-start(f32[8,256]{1,0:T(8,128)S(1)} %add.197), channel_id=1, source_target_pairs={{0,16},{4,20},{8,24},{12,28},{16,0},{20,4},{24,8},{28,12},{1,17},{... | collective-permute-start | bytes 24584 | tf_op jit(solution)/shard_map/ppermute | solution.py:447
  398.7 8.9 %collective-permute-start.75 = (bf16[128,1024]{1,0:T(8,128)(2,1)S(1)}, bf16[128,1024]{1,0:T(8,128)(2,1)S(1)}, u32[]{:S(2)}, u32[]{:S(2)}) collective-permute-start(bf16[128,1024]{1,0:T(8,128)(2,1)S(1)} %get-tuple-element.272), channel_id=1, source_target_pairs={{0,1},{1,0},{2,3},{3,2},{4,5},{5,4},{6,7},{7,6},{8,9},{9,8},{10,11... | collective-permute-start | bytes 786440 | tf_op jit(solution)/shard_map/ppermute | solution.py:26
  (134 other events, 1186.7 us)
Sparse Core Ops, SparseCore 0:
  111.3 73.4 all-gather.1
  214.1 96.3 reduce-scatter.1

commit v6 on v5

--- a/solution.py
+++ b/solution.py
@@ -1023,8 +1023,9 @@
     activ, slope = gelu_parts(mm(three_all, w_up))
 
     grad_up = (mm(grad_all, w_down, 1, 1) * slope).astype(LOW)
-    grad_three = scatter_slots(grad_up, w_up, 1)
-    ffn_sums = sum_rows(weight_grads(three_all, grad_up, activ, grad_all))
+    g_ffn = weight_grads(three_all, grad_up, activ, grad_all)
+    grad_three, g_ffn = scatter_slots(grad_up, w_up, 1, None, (g_ffn,))
+    ffn_sums = sum_rows(g_ffn)
     output_part = scatter_slots(activ, w_down, 0, grad_three)
     part, gain_three, bias_three = norm_backward(grad_three, hat_three, inverse_three, gains[2])
     grad_two = out_grad[0].astype(WIDE) + part

time: 425 us -> 415 us (0.976)
  waiting for transfers between devices: 156 us -> 138 us
  starting transfers between devices: 80.9 us -> 89.2 us
  local copies, waits for them, and re-layouts: 25.8 us -> 20.2 us
    ppermute x35, waiting for transfers between devices: 99.6 us -> 82.3 us  [row_swap(): return lax.ppermute(values, 'rows', [(i, i ^ mask) for i in range(size)])]
    ppermute x35, starting transfers between devices: 53.7 us -> 62.4 us  [row_swap(): return lax.ppermute(values, 'rows', [(i, i ^ mask) for i in range(size)])]
    unnamed x234 -> x224, local copies, waits for them, and re-layouts: 24.4 us -> 18.8 us
  transfers between devices with their start and end apart: 81 -> 81, of which waited for: 30 -> 30; matrix products, arithmetic and copies ran while one was open for 10% -> 12% of each run, Pallas kernels for 19% -> 20%
where the time goes in v6:
time: 415 us; the launch traced here: 409 us
  waiting for transfers between devices  138 us (33%)
  starting transfers between devices  89.2 us (21%)
  Pallas kernels  88.2 us (21%)
  matrix products  44.6 us (11%)
  local copies, waits for them, and re-layouts  20.2 us (5%)
  between operations  16.4 us (4%)
  other arithmetic  12.4 us (3%)
    ppermute x35, waiting for transfers between devices, row_swap(): return lax.ppermute(values, 'rows', [(i, i ^ mask) for i in range(size)])  82.3 us
    pallas_call x39, Pallas kernels, call(): pl.pallas_call(body, out_shape=outs, in_specs=[pl.BlockSpec(memory_space=...  78.2 us
    ppermute x35, starting transfers between devices, row_swap(): return lax.ppermute(values, 'rows', [(i, i ^ mask) for i in range(size)])  62.4 us
    ppermute x44, waiting for transfers between devices, swap(): return lax.ppermute(values, 'text', [(i, i ^ mask) for i in range(WAYS)])  55.5 us
    dot_general x31, matrix products, mm(): lax.dot_general(left, right, (((left_dim,), (right_dim,)), ((), ())), pre...  44.6 us
    ppermute x44, starting transfers between devices, swap(): return lax.ppermute(values, 'text', [(i, i ^ mask) for i in range(WAYS)])  26.5 us
    unnamed x224, local copies, waits for them, and re-layouts  18.8 us
    pallas_call x1, Pallas kernels, weight_grads(): pl.pallas_call(weight_block, grid=(2, rows // tile), out_shape=shaped((ro...  9.96 us
  transfers between devices with their start and end apart: 81, of which 30 were waited for; matrix products, arithmetic and copies ran while one was open for 12% of the time, Pallas kernels for 20%

profile of v6, /device:TPU:0, one launch (start us, length us, event | category | flops | bytes accessed | tf_op | source)
XLA Modules:
  0.0 408.8 jit_solution(7197257532534345445)
XLA Ops:
  14.9 2.9 collective-permute-start.1
  33.9 2.6 collective-permute-start.4
  36.5 6.4 %collective-permute-done.3.refs_1_ = bf16[128,768]{1,0:T(8,128)(2,1)S(1)} collective-permute-done((bf16[128,768]{1,0:T(8,128)(2,1)S(1)}, bf16[128,768]{1,0:T(8,128)(2,1)S(1)}, u32[]{:S(2)}, u32[]{:S(2)}) %collective-permute-start.3) | collective-permute-done | bytes 196640 | tf_op jit(solution)/shard_map/ppermute | solution.py:447
  42.9 2.5 collective-permute-start.5
  47.4 1.9 shard_map.234
  50.5 2.4 collective-permute-done.6.refs_4_
  52.9 2.1 collective-permute-done.7.refs_5_
  58.0 2.8 collective-permute-start.17
  63.9 5.3 %collective-permute-done.16.refs_2_ = bf16[64,1024]{1,0:T(8,128)(2,1)S(1)} collective-permute-done((bf16[64,1024]{1,0:T(8,128)(2,1)S(1)}, bf16[64,1024]{1,0:T(8,128)(2,1)S(1)}, u32[]{:S(2)}, u32[]{:S(2)}) %collective-permute-start.16) | collective-permute-done | bytes 131104 | tf_op jit(solution)/shard_map/ppermute | solution.py:447
  70.6 2.3 collective-permute-start.19
  72.9 2.1 collective-permute-start.20
  75.9 2.7 shard_map.236
  78.7 1.8 convolution_convert_fusion.1.mixed_ref
  81.8 10.0 %collective-permute-done.19.refs_2_ = bf16[128,1024]{1,0:T(8,128)(2,1)S(1)} collective-permute-done((bf16[128,1024]{1,0:T(8,128)(2,1)}, bf16[128,1024]{1,0:T(8,128)(2,1)S(1)}, u32[]{:S(2)}, u32[]{:S(2)}) %collective-permute-start.19) | collective-permute-done | bytes 262176 | tf_op jit(solution)/shard_map/ppermute | solution.py:447
  95.7 3.7 collective-permute-start.26
  99.3 3.5 collective-permute-done.26.refs_1_
  103.5 2.7 collective-permute-start.27
  108.3 6.9 %shard_map.238 = (bf16[1024,256]{1,0:T(8,128)(2,1)S(1)}, f32[4,1024]{1,0:T(4,128)S(1)}) custom-call(s32[2]{0:T(128)S(1)} %pad_add_fusion.ids_ref._.here_ref, s32[8,1024]{1,0:T(8,128)S(1)} %stack.53.marks_ref, bf16[1024,768]{1,0:T(8,128)(2,1)S(1)} %convolution_convert_fusion.1.mixed_ref), custom_call_target="tpu_custom_call" | custom-call | bytes 2146312 | tf_op jit(solution)/shard_map/pallas_call | solution.py:352
  115.2 1.8 shard_map.239
  121.1 13.8 %collective-permute-done.31.refs_6_ = bf16[2,128,1024]{2,1,0:T(8,128)(2,1)S(1)} collective-permute-done((bf16[2,128,1024]{2,1,0:T(8,128)(2,1)S(1)}, bf16[2,128,1024]{2,1,0:T(8,128)(2,1)S(1)}, u32[]{:S(2)}, u32[]{:S(2)}) %collective-permute-start.31) | collective-permute-done | bytes 524320 | tf_op jit(solution)/shard_map/ppermute | solution.py:447
  134.9 2.0 shard_map.241
  140.8 1.9 shard_map.243.refs_0_
  142.7 5.9 %collective-permute-done.33.other_ref = bf16[384,512]{1,0:T(8,128)(2,1)S(1)} collective-permute-done((bf16[384,512]{1,0:T(8,128)(2,1)S(1)}, bf16[384,512]{1,0:T(8,128)(2,1)S(1)}, u32[]{:S(2)}, u32[]{:S(2)}) %collective-permute-start.33) | collective-permute-done | bytes 393248 | tf_op jit(solution)/shard_map/ppermute | solution.py:26
  152.4 6.4 %shard_map.242 = (bf16[512,512]{1,0:T(8,128)(2,1)S(1)}, f32[8,512]{1,0:T(8,128)S(1)}) custom-call(s32[2]{0:T(128)S(1)} %pad_add_fusion.ids_ref._.here_ref, s32[8,1024]{1,0:T(8,128)S(1)} %copy-done.25, bf16[512,512]{1,0:T(8,128)(2,1)S(1)} %convolution_convert_fusion.14.query_ref, bf16[384,512]{1,0:T(8,128)(2,1)S(1)} %convolution_convert_fusion.16.own_ref, ...), custom_call_target="tpu_custom_call" | custom-call | bytes 1884168 | tf_op jit(solution)/shard_map/pallas_call | solution.py:352
  158.9 2.9 collective-permute-done.34.refs_1_
  163.0 1.9 collective-permute-done.35
  168.1 12.0 %collective-permute-done.38.refs_1_ = bf16[256,1024]{1,0:T(8,128)(2,1)S(1)} collective-permute-done((bf16[256,1024]{1,0:T(8,128)(2,1)S(1)}, bf16[256,1024]{1,0:T(8,128)(2,1)S(1)}, u32[]{:S(2)}, u32[]{:S(2)}) %collective-permute-start.38) | collective-permute-done | bytes 524320 | tf_op jit(solution)/shard_map/ppermute | solution.py:26
  185.1 6.2 %fusion.3 = (f32[1024,1024]{1,0:T(8,128)S(1)}, bf16[1024,1024]{1,0:T(8,128)(2,1)S(1)}) fusion(bf16[1024,1024]{1,0:T(8,128)(2,1)} %copy-done.11, bf16[1024,2048]{1,0:T(8,128)(2,1)} %all-gather.2.cloned.1.call-done), kind=kOutput, calls=%fused_computation.4 | convolution fusion | flops 2157969408 | bytes 10485760 | tf_op jit(solution)/shard_map/dot_general | solution.py:20
  191.4 2.4 multiply_convert_fusion.right_a
  195.7 2.2 convolution_convert_fusion.4
  200.9 10.0 %shard_map.247 = bf16[1024,2048]{1,0:T(8,128)(2,1)} custom-call(bf16[1024,1024]{1,0:T(8,128)(2,1)S(1)} %copy-done.12, bf16[1024,1024]{1,0:T(8,128)(2,1)S(1)} %multiply_convert_fusion.right_a, bf16[1024,1024]{1,0:T(8,128)(2,1)} %copy-done.111, bf16[1024,1024]{1,0:T(8,128)(2,1)} %copy-done.9), custom_call_target="tpu_custom_call" | custom-call | flops 4294967296 | bytes 12582912 | tf_op jit(solution)/shard_map/pallas_call | solution.py:378
  210.9 3.3 fusion.39
  214.3 3.6 multiply_reduce_fusion
  221.3 11.7 %collective-permute-done.45 = bf16[256,1024]{1,0:T(8,128)(2,1)S(1)} collective-permute-done((bf16[256,1024]{1,0:T(8,128)(2,1)S(1)}, bf16[256,1024]{1,0:T(8,128)(2,1)S(1)}, u32[]{:S(2)}, u32[]{:S(2)}) %collective-permute-start.45) | collective-permute-done | bytes 524320 | tf_op jit(solution)/shard_map/ppermute | solution.py:26
  233.8 7.3 %shard_map.249 = (bf16[512,512]{1,0:T(8,128)(2,1)S(1)}, bf16[384,512]{1,0:T(8,128)(2,1)S(1)}, bf16[384,512]{1,0:T(8,128)(2,1)S(1)}) custom-call(s32[2]{0:T(128)S(1)} %pad_add_fusion.ids_ref._.here_ref, s32[8,1024]{1,0:T(8,128)S(1)} %copy-done.26, bf16[512,512]{1,0:T(8,128)(2,1)S(1)} %convolution_convert_fusion.14.query_ref, ...), custom_call_target="tpu_custom_call" | custom-call | bytes 3194888 | tf_op jit(solution)/shard_map/pallas_call | solution.py:352
  241.2 3.1 fusion.32
  249.6 6.8 %collective-permute-done.47 = bf16[384,512]{1,0:T(8,128)(2,1)S(1)} collective-permute-done((bf16[384,512]{1,0:T(8,128)(2,1)S(1)}, bf16[384,512]{1,0:T(8,128)(2,1)S(1)}, u32[]{:S(2)}, u32[]{:S(2)}) %collective-permute-start.47) | collective-permute-done | bytes 393248 | tf_op jit(solution)/shard_map/ppermute | solution.py:26
  259.1 1.8 shard_map.252
  262.5 7.6 %collective-permute-done.48.refs_1_ = bf16[256,1024]{1,0:T(8,128)(2,1)} collective-permute-done((bf16[256,1024]{1,0:T(8,128)(2,1)S(1)}, bf16[256,1024]{1,0:T(8,128)(2,1)}, u32[]{:S(2)}, u32[]{:S(2)}) %collective-permute-start.48) | collective-permute-done | bytes 524320 | tf_op jit(solution)/shard_map/ppermute | solution.py:26
  272.4 2.2 shard_map.250
  276.0 10.7 %shard_map.251 = bf16[1024,768]{1,0:T(8,128)(2,1)S(1)} custom-call(s32[2]{0:T(128)S(1)} %pad_add_fusion.ids_ref._.here_ref, s32[8,1024]{1,0:T(8,128)S(1)} %copy-done.27, bf16[1024,768]{1,0:T(8,128)(2,1)S(1)} %copy-done.1, bf16[1024,256]{1,0:T(8,128)(2,1)S(1)} %convolution_convert_fusion.12.grad_ref, f32[4,1024]{1,0:T(4,128)S(1)} %copy-done.62), custom_call_target="tpu_custom_call" | custom-call | bytes 3719176 | tf_op jit(solution)/shard_map/pallas_call | solution.py:352
  286.7 9.4 %collective-permute-done.51.refs_2_ = bf16[4,128,1024]{2,1,0:T(8,128)(2,1)} collective-permute-done((bf16[4,128,1024]{2,1,0:T(8,128)(2,1)}, bf16[4,128,1024]{2,1,0:T(8,128)(2,1)}, u32[]{:S(2)}, u32[]{:S(2)}) %collective-permute-start.51) | collective-permute-done | bytes 1048608 | tf_op jit(solution)/shard_map/ppermute | solution.py:447
  296.1 2.0 convolution_convert_fusion.2
  302.3 2.2 shard_map.254
  305.5 2.8 collective-permute-start.58
  308.5 1.9 convolution_convert_fusion.refs_0_
  310.4 1.7 fusion.38
  312.2 1.8 collective-permute-start.53
  319.6 7.0 %collective-permute-done.59.refs_3_ = bf16[128,1024]{1,0:T(8,128)(2,1)S(1)} collective-permute-done((bf16[128,1024]{1,0:T(8,128)(2,1)S(1)}, bf16[128,1024]{1,0:T(8,128)(2,1)S(1)}, u32[]{:S(2)}, u32[]{:S(2)}) %collective-permute-start.59) | collective-permute-done | bytes 262176 | tf_op jit(solution)/shard_map/ppermute | solution.py:447
  327.5 6.1 %collective-permute-start.60 = (bf16[128,1024]{1,0:T(8,128)(2,1)S(1)}, bf16[128,1024]{1,0:T(8,128)(2,1)S(1)}, u32[]{:S(2)}, u32[]{:S(2)}) collective-permute-start(bf16[128,1024]{1,0:T(8,128)(2,1)S(1)} %get-tuple-element.232), channel_id=1, source_target_pairs={{0,8},{4,12},{8,0},{12,4},{16,24},{20,28},{24,16},{28,20},{1,9},{5... | collective-permute-start | bytes 786440 | tf_op jit(solution)/shard_map/ppermute | solution.py:447
  334.2 1.8 collective-permute-start.63
  336.0 1.7 fusion.4
  337.7 6.5 %collective-permute-done.60.refs_5_ = bf16[128,1024]{1,0:T(8,128)(2,1)S(1)} collective-permute-done((bf16[128,1024]{1,0:T(8,128)(2,1)S(1)}, bf16[128,1024]{1,0:T(8,128)(2,1)S(1)}, u32[]{:S(2)}, u32[]{:S(2)}) %collective-permute-start.60) | collective-permute-done | bytes 262176 | tf_op jit(solution)/shard_map/ppermute | solution.py:447
  346.1 8.9 %collective-permute-done.62.refs_6_ = bf16[128,1024]{1,0:T(8,128)(2,1)S(1)} collective-permute-done((bf16[128,1024]{1,0:T(8,128)(2,1)S(1)}, bf16[128,1024]{1,0:T(8,128)(2,1)S(1)}, u32[]{:S(2)}, u32[]{:S(2)}) %collective-permute-start.62) | collective-permute-done | bytes 262176 | tf_op jit(solution)/shard_map/ppermute | solution.py:447
  356.5 5.0 %collective-permute-start.64 = (bf16[128,768]{1,0:T(8,128)(2,1)S(1)}, bf16[128,768]{1,0:T(8,128)(2,1)S(1)}, u32[]{:S(2)}, u32[]{:S(2)}) collective-permute-start(bf16[128,768]{1,0:T(8,128)(2,1)S(1)} %get-tuple-element.240), channel_id=1, source_target_pairs={{0,8},{4,12},{8,0},{12,4},{16,24},{20,28},{24,16},{28,20},{1,9},{5... | collective-permute-start | bytes 589832 | tf_op jit(solution)/shard_map/ppermute | solution.py:447
  364.0 2.4 collective-permute-start.68
  372.8 2.0 collective-permute-start.77
  374.8 4.3 %collective-permute-done.67.refs_2_ = bf16[128,768]{1,0:T(8,128)(2,1)S(1)} collective-permute-done((bf16[128,768]{1,0:T(8,128)(2,1)}, bf16[128,768]{1,0:T(8,128)(2,1)S(1)}, u32[]{:S(2)}, u32[]{:S(2)}) %collective-permute-start.67) | collective-permute-done | bytes 196640 | tf_op jit(solution)/shard_map/ppermute | solution.py:447
  379.1 2.3 shard_map.259
  382.1 4.0 collective-permute-start.78
  391.9 2.6 collective-permute-done.72.refs_1_
  396.1 1.9 shard_map.261
  397.9 1.7 shard_map.268
  399.6 1.8 shard_map.265
  (439 shorter events, 118.6 us)
Async XLA Ops:
  7.2 178.0 %all-gather.2.cloned.1.call-start = ((), (), s32[]{:S(2)}) async-start(), calls=%async_computation.1 | async-start | bytes 4718592 | tf_op jit(solution)/shard_map/all_gather | solution.py:451
  14.9 10.6 %collective-permute-start.1 = (bf16[144,896]{1,0:T(8,128)(2,1)S(1)}, bf16[144,896]{1,0:T(8,128)(2,1)S(1)}, u32[]{:S(2)}, u32[]{:S(2)}) collective-permute-start(bf16[144,896]{1,0:T(8,128)(2,1)S(1)} %get-tuple-element.148), channel_id=1, source_target_pairs={{0,2},{1,3},{2,0},{3,1},{4,6},{5,7},{6,4},{7,5},{8,10},{9,11},{10,... | collective-permute-start | bytes 774152 | tf_op jit(solution)/shard_map/ppermute | solution.py:26
  28.8 17.1 %collective-permute-start.8 = (bf16[128,1536]{1,0:T(8,128)(2,1)S(1)}, bf16[128,1536]{1,0:T(8,128)(2,1)S(1)}, u32[]{:S(2)}, u32[]{:S(2)}) collective-permute-start(bf16[128,1536]{1,0:T(8,128)(2,1)S(1)} %get-tuple-element.163), channel_id=1, source_target_pairs={{0,2},{1,3},{2,0},{3,1},{4,6},{5,7},{6,4},{7,5},{8,10},{9,11},{10,... | collective-permute-start | bytes 1179656 | tf_op jit(solution)/shard_map/ppermute | solution.py:26
  29.4 25.6 %collective-permute-start.10 = (bf16[256,1024]{1,0:T(8,128)(2,1)S(1)}, bf16[256,1024]{1,0:T(8,128)(2,1)S(1)}, u32[]{:S(2)}, u32[]{:S(2)}) collective-permute-start(bf16[256,1024]{1,0:T(8,128)(2,1)S(1)} %fusion.53.refs_0_), channel_id=1, source_target_pairs={{0,2},{1,3},{2,0},{3,1},{4,6},{5,7},{6,4},{7,5},{8,10},{9,11},{10,... | collective-permute-start | bytes 1572872 | tf_op jit(solution)/shard_map/ppermute | solution.py:26
  30.9 14.5 %collective-permute-start.9 = (bf16[128,1024]{1,0:T(8,128)(2,1)S(1)}, bf16[128,1024]{1,0:T(8,128)(2,1)S(1)}, u32[]{:S(2)}, u32[]{:S(2)}) collective-permute-start(bf16[128,1024]{1,0:T(8,128)(2,1)S(1)} %get-tuple-element.165), channel_id=1, source_target_pairs={{0,4},{4,0},{8,12},{12,8},{16,20},{20,16},{24,28},{28,24},{1,5},{5... | collective-permute-start | bytes 786440 | tf_op jit(solution)/shard_map/ppermute | solution.py:447
  32.3 10.5 %collective-permute-start.3 = (bf16[128,768]{1,0:T(8,128)(2,1)S(1)}, bf16[128,768]{1,0:T(8,128)(2,1)S(1)}, u32[]{:S(2)}, u32[]{:S(2)}) collective-permute-start(bf16[128,768]{1,0:T(8,128)(2,1)S(1)} %get-tuple-element.161.refs_0_), channel_id=1, source_target_pairs={{0,8},{4,12},{8,0},{12,4},{16,24},{20,28},{24,16},{28,20},{1,9},{5... | collective-permute-start | bytes 589832 | tf_op jit(solution)/shard_map/ppermute | solution.py:447
  33.9 15.5 %collective-permute-start.4 = (bf16[128,768]{1,0:T(8,128)(2,1)S(1)}, bf16[128,768]{1,0:T(8,128)(2,1)S(1)}, u32[]{:S(2)}, u32[]{:S(2)}) collective-permute-start(bf16[128,768]{1,0:T(8,128)(2,1)S(1)} %get-tuple-element.161.refs_0_), channel_id=1, source_target_pairs={{0,16},{4,20},{8,24},{12,28},{16,0},{20,4},{24,8},{28,12},{1,17},{... | collective-permute-start | bytes 589832 | tf_op jit(solution)/shard_map/ppermute | solution.py:447
  42.9 7.6 %collective-permute-start.5 = (bf16[128,768]{1,0:T(8,128)(2,1)S(1)}, bf16[128,768]{1,0:T(8,128)(2,1)S(1)}, u32[]{:S(2)}, u32[]{:S(2)}) collective-permute-start(bf16[128,768]{1,0:T(8,128)(2,1)S(1)} %get-tuple-element.161.refs_0_), channel_id=1, source_target_pairs={{0,24},{4,28},{8,16},{12,20},{16,8},{20,12},{24,0},{28,4},{1,25},{... | collective-permute-start | bytes 589832 | tf_op jit(solution)/shard_map/ppermute | solution.py:447
  45.4 7.5 %collective-permute-start.6 = (bf16[128,768]{1,0:T(8,128)(2,1)S(1)}, bf16[128,768]{1,0:T(8,128)(2,1)S(1)}, u32[]{:S(2)}, u32[]{:S(2)}) collective-permute-start(bf16[128,768]{1,0:T(8,128)(2,1)S(1)} %get-tuple-element.161.refs_0_), channel_id=1, source_target_pairs={{0,4},{4,0},{8,12},{12,8},{16,20},{20,16},{24,28},{28,24},{1,5},{5... | collective-permute-start | bytes 589832 | tf_op jit(solution)/shard_map/ppermute | solution.py:447
  45.9 9.1 %collective-permute-start.7 = (bf16[128,768]{1,0:T(8,128)(2,1)S(1)}, bf16[128,768]{1,0:T(8,128)(2,1)S(1)}, u32[]{:S(2)}, u32[]{:S(2)}) collective-permute-start(bf16[128,768]{1,0:T(8,128)(2,1)S(1)} %collective-permute-done.3.refs_1_), channel_id=1, source_target_pairs={{0,4},{4,0},{8,12},{12,8},{16,20},{20,16},{24,28},{28,24},{1,5},{5... | collective-permute-start | bytes 589832 | tf_op jit(solution)/shard_map/ppermute | solution.py:447
  55.1 19.9 %collective-permute-start.11 = (bf16[2,128,768]{2,1,0:T(8,128)(2,1)S(1)}, bf16[2,128,768]{2,1,0:T(8,128)(2,1)S(1)}, u32[]{:S(2)}, u32[]{:S(2)}) collective-permute-start(bf16[2,128,768]{2,1,0:T(8,128)(2,1)S(1)} %pad_maximum_fusion.1), channel_id=1, source_target_pairs={{0,4},{4,0},{8,12},{12,8},{16,20},{20,16},{24,28},{28,24},{1,5},{5... | collective-permute-start | bytes 1179656 | tf_op jit(solution)/shard_map/ppermute | solution.py:447
  55.7 17.2 %collective-permute-start.14 = (bf16[96,1024]{1,0:T(8,128)(2,1)}, bf16[96,1024]{1,0:T(8,128)(2,1)}, u32[]{:S(2)}, u32[]{:S(2)}) collective-permute-start(bf16[96,1024]{1,0:T(8,128)(2,1)} %bitcast.10.refs_0_), channel_id=1, source_target_pairs={{0,2},{1,3},{2,0},{3,1},{4,6},{5,7},{6,4},{7,5},{8,10},{9,11},{10,... | collective-permute-start | bytes 589832 | tf_op jit(solution)/shard_map/ppermute | solution.py:26
  56.3 13.0 %collective-permute-start.16 = (bf16[64,1024]{1,0:T(8,128)(2,1)S(1)}, bf16[64,1024]{1,0:T(8,128)(2,1)S(1)}, u32[]{:S(2)}, u32[]{:S(2)}) collective-permute-start(bf16[64,1024]{1,0:T(8,128)(2,1)S(1)} %get-tuple-element.302.refs_0_), channel_id=1, source_target_pairs={{0,16},{4,20},{8,24},{12,28},{16,0},{20,4},{24,8},{28,12},{1,17},{... | collective-permute-start | bytes 393224 | tf_op jit(solution)/shard_map/ppermute | solution.py:447
  58.0 11.9 %collective-permute-start.17 = (bf16[64,1024]{1,0:T(8,128)(2,1)S(1)}, bf16[64,1024]{1,0:T(8,128)(2,1)S(1)}, u32[]{:S(2)}, u32[]{:S(2)}) collective-permute-start(bf16[64,1024]{1,0:T(8,128)(2,1)S(1)} %get-tuple-element.302.refs_0_), channel_id=1, source_target_pairs={{0,24},{4,28},{8,16},{12,20},{16,8},{20,12},{24,0},{28,4},{1,25},{... | collective-permute-start | bytes 393224 | tf_op jit(solution)/shard_map/ppermute | solution.py:447
  63.9 31.7 %collective-permute-start.21 = (bf16[96,1024]{1,0:T(8,128)(2,1)}, bf16[96,1024]{1,0:T(8,128)(2,1)}, u32[]{:S(2)}, u32[]{:S(2)}) collective-permute-start(bf16[96,1024]{1,0:T(8,128)(2,1)} %bitcast.10.refs_0_), channel_id=1, source_target_pairs={{0,1},{1,0},{2,3},{3,2},{4,5},{5,4},{6,7},{7,6},{8,9},{9,8},{10,11... | collective-permute-start | bytes 589832 | tf_op jit(solution)/shard_map/ppermute | solution.py:26
  69.9 11.9 %collective-permute-start.18 = (bf16[128,1024]{1,0:T(8,128)(2,1)}, bf16[128,1024]{1,0:T(8,128)(2,1)}, u32[]{:S(2)}, u32[]{:S(2)}) collective-permute-start(bf16[128,1024]{1,0:T(8,128)(2,1)} %get-tuple-element.186.refs_0_), channel_id=1, source_target_pairs={{0,8},{4,12},{8,0},{12,4},{16,24},{20,28},{24,16},{28,20},{1,9},{5... | collective-permute-start | bytes 786440 | tf_op jit(solution)/shard_map/ppermute | solution.py:447
  70.6 21.3 %collective-permute-start.19 = (bf16[128,1024]{1,0:T(8,128)(2,1)}, bf16[128,1024]{1,0:T(8,128)(2,1)S(1)}, u32[]{:S(2)}, u32[]{:S(2)}) collective-permute-start(bf16[128,1024]{1,0:T(8,128)(2,1)} %get-tuple-element.186.refs_0_), channel_id=1, source_target_pairs={{0,16},{4,20},{8,24},{12,28},{16,0},{20,4},{24,8},{28,12},{1,17},{... | collective-permute-start | bytes 786440 | tf_op jit(solution)/shard_map/ppermute | solution.py:447
  72.9 18.9 %collective-permute-start.20 = (bf16[128,1024]{1,0:T(8,128)(2,1)}, bf16[128,1024]{1,0:T(8,128)(2,1)S(1)}, u32[]{:S(2)}, u32[]{:S(2)}) collective-permute-start(bf16[128,1024]{1,0:T(8,128)(2,1)} %get-tuple-element.186.refs_0_), channel_id=1, source_target_pairs={{0,24},{4,28},{8,16},{12,20},{16,8},{20,12},{24,0},{28,4},{1,25},{... | collective-permute-start | bytes 786440 | tf_op jit(solution)/shard_map/ppermute | solution.py:447
  91.8 25.2 %collective-permute-start.25 = (bf16[256,1024]{1,0:T(8,128)(2,1)S(1)}, bf16[256,1024]{1,0:T(8,128)(2,1)}, u32[]{:S(2)}, u32[]{:S(2)}) collective-permute-start(bf16[256,1024]{1,0:T(8,128)(2,1)S(1)} %bitcast.75), channel_id=1, source_target_pairs={{0,2},{1,3},{2,0},{3,1},{4,6},{5,7},{6,4},{7,5},{8,10},{9,11},{10,... | collective-permute-start | bytes 1572872 | tf_op jit(solution)/shard_map/ppermute | solution.py:26
  93.5 12.7 %collective-permute-start.22 = (bf16[96,1024]{1,0:T(8,128)(2,1)}, bf16[96,1024]{1,0:T(8,128)(2,1)S(1)}, u32[]{:S(2)}, u32[]{:S(2)}) collective-permute-start(bf16[96,1024]{1,0:T(8,128)(2,1)} %collective-permute-done.14.refs_1_), channel_id=1, source_target_pairs={{0,1},{1,0},{2,3},{3,2},{4,5},{5,4},{6,7},{7,6},{8,9},{9,8},{10,11... | collective-permute-start | bytes 589832 | tf_op jit(solution)/shard_map/ppermute | solution.py:26
  93.6 23.5 %collective-permute-start.23 = (bf16[128,1024]{1,0:T(8,128)(2,1)}, bf16[128,1024]{1,0:T(8,128)(2,1)}, u32[]{:S(2)}, u32[]{:S(2)}) collective-permute-start(bf16[128,1024]{1,0:T(8,128)(2,1)} %get-tuple-element.186.refs_0_), channel_id=1, source_target_pairs={{0,4},{4,0},{8,12},{12,8},{16,20},{20,16},{24,28},{28,24},{1,5},{5... | collective-permute-start | bytes 786440 | tf_op jit(solution)/shard_map/ppermute | solution.py:447
  95.1 22.0 %collective-permute-start.24 = (bf16[128,1024]{1,0:T(8,128)(2,1)}, bf16[128,1024]{1,0:T(8,128)(2,1)}, u32[]{:S(2)}, u32[]{:S(2)}) collective-permute-start(bf16[128,1024]{1,0:T(8,128)(2,1)} %collective-permute-done.18.refs_1_), channel_id=1, source_target_pairs={{0,4},{4,0},{8,12},{12,8},{16,20},{20,16},{24,28},{28,24},{1,5},{5... | collective-permute-start | bytes 786440 | tf_op jit(solution)/shard_map/ppermute | solution.py:447
  103.5 13.5 %collective-permute-start.27 = (bf16[64,1024]{1,0:T(8,128)(2,1)S(1)}, bf16[64,1024]{1,0:T(8,128)(2,1)}, u32[]{:S(2)}, u32[]{:S(2)}) collective-permute-start(bf16[64,1024]{1,0:T(8,128)(2,1)S(1)} %get-tuple-element.189.refs_0_), channel_id=1, source_target_pairs={{0,16},{4,20},{8,24},{12,28},{16,0},{20,4},{24,8},{28,12},{1,17},{... | collective-permute-start | bytes 393224 | tf_op jit(solution)/shard_map/ppermute | solution.py:447
  106.2 10.9 %collective-permute-start.28 = (bf16[64,1024]{1,0:T(8,128)(2,1)S(1)}, bf16[64,1024]{1,0:T(8,128)(2,1)}, u32[]{:S(2)}, u32[]{:S(2)}) collective-permute-start(bf16[64,1024]{1,0:T(8,128)(2,1)S(1)} %get-tuple-element.189.refs_0_), channel_id=1, source_target_pairs={{0,24},{4,28},{8,16},{12,20},{16,8},{20,12},{24,0},{28,4},{1,25},{... | collective-permute-start | bytes 393224 | tf_op jit(solution)/shard_map/ppermute | solution.py:447
  108.0 258.5 %reduce-scatter.2.cloned.1.call-start = ((), (), s32[]{:S(2)}) async-start(), calls=%async_computation.2 | async-start | bytes 4718592 | tf_op jit(solution)/shard_map/reduce_scatter | solution.py:455
  117.7 17.2 %collective-permute-start.31 = (bf16[2,128,1024]{2,1,0:T(8,128)(2,1)S(1)}, bf16[2,128,1024]{2,1,0:T(8,128)(2,1)S(1)}, u32[]{:S(2)}, u32[]{:S(2)}) collective-permute-start(bf16[2,128,1024]{2,1,0:T(8,128)(2,1)S(1)} %pad_maximum_fusion), channel_id=1, source_target_pairs={{0,4},{4,0},{8,12},{12,8},{16,20},{20,16},{24,28},{28,24},{1,5},{5... | collective-permute-start | bytes 1572872 | tf_op jit(solution)/shard_map/ppermute | solution.py:447
  120.6 14.3 %collective-permute-start.30 = (bf16[256,1024]{1,0:T(8,128)(2,1)S(1)}, bf16[256,1024]{1,0:T(8,128)(2,1)S(1)}, u32[]{:S(2)}, u32[]{:S(2)}) collective-permute-start(bf16[256,1024]{1,0:T(8,128)(2,1)S(1)} %fusion.45), channel_id=1, source_target_pairs={{0,2},{1,3},{2,0},{3,1},{4,6},{5,7},{6,4},{7,5},{8,10},{9,11},{10,... | collective-permute-start | bytes 1572872 | tf_op jit(solution)/shard_map/ppermute | solution.py:26
  137.5 11.1 %collective-permute-start.33 = (bf16[384,512]{1,0:T(8,128)(2,1)S(1)}, bf16[384,512]{1,0:T(8,128)(2,1)S(1)}, u32[]{:S(2)}, u32[]{:S(2)}) collective-permute-start(bf16[384,512]{1,0:T(8,128)(2,1)S(1)} %convolution_convert_fusion.16.own_ref), channel_id=1, source_target_pairs={{0,2},{1,3},{2,0},{3,1},{4,6},{5,7},{6,4},{7,5},{8,10},{9,11},{10,... | collective-permute-start | bytes 1179656 | tf_op jit(solution)/shard_map/ppermute | solution.py:26
  140.7 9.4 %collective-permute-start.32 = (bf16[256,1024]{1,0:T(8,128)(2,1)S(1)}, bf16[256,1024]{1,0:T(8,128)(2,1)S(1)}, u32[]{:S(2)}, u32[]{:S(2)}) collective-permute-start(bf16[256,1024]{1,0:T(8,128)(2,1)S(1)} %add_convert_fusion.2.refs_0_), channel_id=1, source_target_pairs={{0,1},{1,0},{2,3},{3,2},{4,5},{5,4},{6,7},{7,6},{8,9},{9,8},{10,11... | collective-permute-start | bytes 1572872 | tf_op jit(solution)/shard_map/ppermute | solution.py:26
  148.6 13.2 %collective-permute-start.34 = (bf16[256,1024]{1,0:T(8,128)(2,1)S(1)}, bf16[256,1024]{1,0:T(8,128)(2,1)S(1)}, u32[]{:S(2)}, u32[]{:S(2)}) collective-permute-start(bf16[256,1024]{1,0:T(8,128)(2,1)S(1)} %shard_map.243.refs_0_), channel_id=1, source_target_pairs={{0,2},{1,3},{2,0},{3,1},{4,6},{5,7},{6,4},{7,5},{8,10},{9,11},{10,... | collective-permute-start | bytes 1572872 | tf_op jit(solution)/shard_map/ppermute | solution.py:26
  166.0 14.0 %collective-permute-start.38 = (bf16[256,1024]{1,0:T(8,128)(2,1)S(1)}, bf16[256,1024]{1,0:T(8,128)(2,1)S(1)}, u32[]{:S(2)}, u32[]{:S(2)}) collective-permute-start(bf16[256,1024]{1,0:T(8,128)(2,1)S(1)} %add_convert_fusion.1.refs_0_), channel_id=1, source_target_pairs={{0,2},{1,3},{2,0},{3,1},{4,6},{5,7},{6,4},{7,5},{8,10},{9,11},{10,... | collective-permute-start | bytes 1572872 | tf_op jit(solution)/shard_map/ppermute | solution.py:26
  167.5 12.6 %collective-permute-start.36 = (bf16[256,1024]{1,0:T(8,128)(2,1)S(1)}, bf16[256,1024]{1,0:T(8,128)(2,1)S(1)}, u32[]{:S(2)}, u32[]{:S(2)}) collective-permute-start(bf16[256,1024]{1,0:T(8,128)(2,1)S(1)} %bitcast.76), channel_id=1, source_target_pairs={{0,1},{1,0},{2,3},{3,2},{4,5},{5,4},{6,7},{7,6},{8,9},{9,8},{10,11... | collective-permute-start | bytes 1572872 | tf_op jit(solution)/shard_map/ppermute | solution.py:26
  167.5 12.6 %collective-permute-start.37 = (bf16[256,1024]{1,0:T(8,128)(2,1)}, bf16[256,1024]{1,0:T(8,128)(2,1)S(1)}, u32[]{:S(2)}, u32[]{:S(2)}) collective-permute-start(bf16[256,1024]{1,0:T(8,128)(2,1)} %collective-permute-done.25.refs_1_), channel_id=1, source_target_pairs={{0,1},{1,0},{2,3},{3,2},{4,5},{5,4},{6,7},{7,6},{8,9},{9,8},{10,11... | collective-permute-start | bytes 1572872 | tf_op jit(solution)/shard_map/ppermute | solution.py:26
  168.0 15.1 %collective-permute-start.39 = (bf16[256,1024]{1,0:T(8,128)(2,1)S(1)}, bf16[256,1024]{1,0:T(8,128)(2,1)S(1)}, u32[]{:S(2)}, u32[]{:S(2)}) collective-permute-start(bf16[256,1024]{1,0:T(8,128)(2,1)S(1)} %add_convert_fusion.1.refs_0_), channel_id=1, source_target_pairs={{0,1},{1,0},{2,3},{3,2},{4,5},{5,4},{6,7},{7,6},{8,9},{9,8},{10,11... | collective-permute-start | bytes 1572872 | tf_op jit(solution)/shard_map/ppermute | solution.py:26
  197.9 13.0 %collective-permute-start.44 = (bf16[512,1024]{1,0:T(8,128)(2,1)}, bf16[512,1024]{1,0:T(8,128)(2,1)}, u32[]{:S(2)}, u32[]{:S(2)}) collective-permute-start(bf16[512,1024]{1,0:T(8,128)(2,1)} %convolution_convert_fusion.4), channel_id=1, source_target_pairs={{0,1},{1,0},{2,3},{3,2},{4,5},{5,4},{6,7},{7,6},{8,9},{9,8},{10,11... | collective-permute-start | bytes 3145736 | tf_op jit(solution)/shard_map/ppermute | solution.py:26
  199.5 14.7 %collective-permute-start.42 = (bf16[256,1024]{1,0:T(8,128)(2,1)}, bf16[256,1024]{1,0:T(8,128)(2,1)}, u32[]{:S(2)}, u32[]{:S(2)}) collective-permute-start(bf16[256,1024]{1,0:T(8,128)(2,1)} %fusion.42), channel_id=1, source_target_pairs={{0,2},{1,3},{2,0},{3,1},{4,6},{5,7},{6,4},{7,5},{8,10},{9,11},{10,... | collective-permute-start | bytes 1572872 | tf_op jit(solution)/shard_map/ppermute | solution.py:26
  219.0 14.0 %collective-permute-start.45 = (bf16[256,1024]{1,0:T(8,128)(2,1)S(1)}, bf16[256,1024]{1,0:T(8,128)(2,1)S(1)}, u32[]{:S(2)}, u32[]{:S(2)}) collective-permute-start(bf16[256,1024]{1,0:T(8,128)(2,1)S(1)} %copy-done.109), channel_id=1, source_target_pairs={{0,2},{1,3},{2,0},{3,1},{4,6},{5,7},{6,4},{7,5},{8,10},{9,11},{10,... | collective-permute-start | bytes 1572872 | tf_op jit(solution)/shard_map/ppermute | solution.py:26
  244.9 11.5 %collective-permute-start.47 = (bf16[384,512]{1,0:T(8,128)(2,1)S(1)}, bf16[384,512]{1,0:T(8,128)(2,1)S(1)}, u32[]{:S(2)}, u32[]{:S(2)}) collective-permute-start(bf16[384,512]{1,0:T(8,128)(2,1)S(1)} %get-tuple-element.217), channel_id=1, source_target_pairs={{0,2},{1,3},{2,0},{3,1},{4,6},{5,7},{6,4},{7,5},{8,10},{9,11},{10,... | collective-permute-start | bytes 1179656 | tf_op jit(solution)/shard_map/ppermute | solution.py:26
  256.4 13.7 %collective-permute-start.48 = (bf16[256,1024]{1,0:T(8,128)(2,1)S(1)}, bf16[256,1024]{1,0:T(8,128)(2,1)}, u32[]{:S(2)}, u32[]{:S(2)}) collective-permute-start(bf16[256,1024]{1,0:T(8,128)(2,1)S(1)} %get-tuple-element.218.refs_0_), channel_id=1, source_target_pairs={{0,2},{1,3},{2,0},{3,1},{4,6},{5,7},{6,4},{7,5},{8,10},{9,11},{10,... | collective-permute-start | bytes 1572872 | tf_op jit(solution)/shard_map/ppermute | solution.py:26
  261.9 34.1 %collective-permute-start.51 = (bf16[4,128,1024]{2,1,0:T(8,128)(2,1)}, bf16[4,128,1024]{2,1,0:T(8,128)(2,1)}, u32[]{:S(2)}, u32[]{:S(2)}) collective-permute-start(bf16[4,128,1024]{2,1,0:T(8,128)(2,1)} %shard_map.252), channel_id=1, source_target_pairs={{0,4},{4,0},{8,12},{12,8},{16,20},{20,16},{24,28},{28,24},{1,5},{5... | collective-permute-start | bytes 3145736 | tf_op jit(solution)/shard_map/ppermute | solution.py:447
  262.5 9.7 %collective-permute-start.49 = (bf16[256,1024]{1,0:T(8,128)(2,1)S(1)}, bf16[256,1024]{1,0:T(8,128)(2,1)}, u32[]{:S(2)}, u32[]{:S(2)}) collective-permute-start(bf16[256,1024]{1,0:T(8,128)(2,1)S(1)} %get-tuple-element.218.refs_0_), channel_id=1, source_target_pairs={{0,1},{1,0},{2,3},{3,2},{4,5},{5,4},{6,7},{7,6},{8,9},{9,8},{10,11... | collective-permute-start | bytes 1572872 | tf_op jit(solution)/shard_map/ppermute | solution.py:26
  271.7 29.5 %collective-permute-start.54 = (bf16[192,1024]{1,0:T(8,128)(2,1)S(1)}, bf16[192,1024]{1,0:T(8,128)(2,1)S(1)}, u32[]{:S(2)}, u32[]{:S(2)}) collective-permute-start(bf16[192,1024]{1,0:T(8,128)(2,1)S(1)} %convolution_convert_fusion.15), channel_id=1, source_target_pairs={{0,1},{1,0},{2,3},{3,2},{4,5},{5,4},{6,7},{7,6},{8,9},{9,8},{10,11... | collective-permute-start | bytes 1179656 | tf_op jit(solution)/shard_map/ppermute | solution.py:26
  298.1 12.4 %collective-permute-start.52 = (bf16[512,1024]{1,0:T(8,128)(2,1)}, bf16[512,1024]{1,0:T(8,128)(2,1)}, u32[]{:S(2)}, u32[]{:S(2)}) collective-permute-start(bf16[512,1024]{1,0:T(8,128)(2,1)} %convolution_convert_fusion.2), channel_id=1, source_target_pairs={{0,1},{1,0},{2,3},{3,2},{4,5},{5,4},{6,7},{7,6},{8,9},{9,8},{10,11... | collective-permute-start | bytes 3145736 | tf_op jit(solution)/shard_map/ppermute | solution.py:26
  299.7 16.6 %collective-permute-start.56 = (bf16[4,128,512]{2,1,0:T(8,128)(2,1)S(1)}, bf16[4,128,512]{2,1,0:T(8,128)(2,1)S(1)}, u32[]{:S(2)}, u32[]{:S(2)}) collective-permute-start(bf16[4,128,512]{2,1,0:T(8,128)(2,1)S(1)} %shard_map.253), channel_id=1, source_target_pairs={{0,4},{4,0},{8,12},{12,8},{16,20},{20,16},{24,28},{28,24},{1,5},{5... | collective-permute-start | bytes 1572872 | tf_op jit(solution)/shard_map/ppermute | solution.py:447
  304.5 15.0 %collective-permute-start.57 = (bf16[128,1024]{1,0:T(8,128)(2,1)S(1)}, bf16[128,1024]{1,0:T(8,128)(2,1)S(1)}, u32[]{:S(2)}, u32[]{:S(2)}) collective-permute-start(bf16[128,1024]{1,0:T(8,128)(2,1)S(1)} %get-tuple-element.226), channel_id=1, source_target_pairs={{0,8},{4,12},{8,0},{12,4},{16,24},{20,28},{24,16},{28,20},{1,9},{5... | collective-permute-start | bytes 786440 | tf_op jit(solution)/shard_map/ppermute | solution.py:447
  305.5 14.1 %collective-permute-start.58 = (bf16[128,1024]{1,0:T(8,128)(2,1)S(1)}, bf16[128,1024]{1,0:T(8,128)(2,1)S(1)}, u32[]{:S(2)}, u32[]{:S(2)}) collective-permute-start(bf16[128,1024]{1,0:T(8,128)(2,1)S(1)} %get-tuple-element.227), channel_id=1, source_target_pairs={{0,16},{4,20},{8,24},{12,28},{16,0},{20,4},{24,8},{28,12},{1,17},{... | collective-permute-start | bytes 786440 | tf_op jit(solution)/shard_map/ppermute | solution.py:447
  308.3 7.4 %collective-permute-start.55 = (bf16[96,1024]{1,0:T(8,128)(2,1)}, bf16[96,1024]{1,0:T(8,128)(2,1)S(1)}, u32[]{:S(2)}, u32[]{:S(2)}) collective-permute-start(bf16[96,1024]{1,0:T(8,128)(2,1)} %add_convert_fusion.4), channel_id=1, source_target_pairs={{0,2},{1,3},{2,0},{3,1},{4,6},{5,7},{6,4},{7,5},{8,10},{9,11},{10,... | collective-permute-start | bytes 589832 | tf_op jit(solution)/shard_map/ppermute | solution.py:26
  312.2 14.4 %collective-permute-start.53 = (bf16[256,1024]{1,0:T(8,128)(2,1)S(1)}, bf16[256,1024]{1,0:T(8,128)(2,1)S(1)}, u32[]{:S(2)}, u32[]{:S(2)}) collective-permute-start(bf16[256,1024]{1,0:T(8,128)(2,1)S(1)} %fusion.38), channel_id=1, source_target_pairs={{0,2},{1,3},{2,0},{3,1},{4,6},{5,7},{6,4},{7,5},{8,10},{9,11},{10,... | collective-permute-start | bytes 1572872 | tf_op jit(solution)/shard_map/ppermute | solution.py:26
  315.6 10.9 %collective-permute-start.59 = (bf16[128,1024]{1,0:T(8,128)(2,1)S(1)}, bf16[128,1024]{1,0:T(8,128)(2,1)S(1)}, u32[]{:S(2)}, u32[]{:S(2)}) collective-permute-start(bf16[128,1024]{1,0:T(8,128)(2,1)S(1)} %get-tuple-element.228), channel_id=1, source_target_pairs={{0,24},{4,28},{8,16},{12,20},{16,8},{20,12},{24,0},{28,4},{1,25},{... | collective-permute-start | bytes 786440 | tf_op jit(solution)/shard_map/ppermute | solution.py:447
  316.4 29.7 %collective-permute-start.61 = (bf16[4,128,768]{2,1,0:T(8,128)(2,1)S(1)}, bf16[4,128,768]{2,1,0:T(8,128)(2,1)S(1)}, u32[]{:S(2)}, u32[]{:S(2)}) collective-permute-start(bf16[4,128,768]{2,1,0:T(8,128)(2,1)S(1)} %dynamic-slice_bitcast_fusion), channel_id=1, source_target_pairs={{0,4},{4,0},{8,12},{12,8},{16,20},{20,16},{24,28},{28,24},{1,5},{5... | collective-permute-start | bytes 2359304 | tf_op jit(solution)/shard_map/ppermute | solution.py:447
  327.5 16.8 %collective-permute-start.60 = (bf16[128,1024]{1,0:T(8,128)(2,1)S(1)}, bf16[128,1024]{1,0:T(8,128)(2,1)S(1)}, u32[]{:S(2)}, u32[]{:S(2)}) collective-permute-start(bf16[128,1024]{1,0:T(8,128)(2,1)S(1)} %get-tuple-element.232), channel_id=1, source_target_pairs={{0,8},{4,12},{8,0},{12,4},{16,24},{20,28},{24,16},{28,20},{1,9},{5... | collective-permute-start | bytes 786440 | tf_op jit(solution)/shard_map/ppermute | solution.py:447
  333.6 21.3 %collective-permute-start.62 = (bf16[128,1024]{1,0:T(8,128)(2,1)S(1)}, bf16[128,1024]{1,0:T(8,128)(2,1)S(1)}, u32[]{:S(2)}, u32[]{:S(2)}) collective-permute-start(bf16[128,1024]{1,0:T(8,128)(2,1)S(1)} %get-tuple-element.236), channel_id=1, source_target_pairs={{0,16},{4,20},{8,24},{12,28},{16,0},{20,4},{24,8},{28,12},{1,17},{... | collective-permute-start | bytes 786440 | tf_op jit(solution)/shard_map/ppermute | solution.py:447
  334.2 20.8 %collective-permute-start.63 = (bf16[128,1024]{1,0:T(8,128)(2,1)S(1)}, bf16[128,1024]{1,0:T(8,128)(2,1)S(1)}, u32[]{:S(2)}, u32[]{:S(2)}) collective-permute-start(bf16[128,1024]{1,0:T(8,128)(2,1)S(1)} %get-tuple-element.237), channel_id=1, source_target_pairs={{0,24},{4,28},{8,16},{12,20},{16,8},{20,12},{24,0},{28,4},{1,25},{... | collective-permute-start | bytes 786440 | tf_op jit(solution)/shard_map/ppermute | solution.py:447
  346.0 15.5 %collective-permute-start.65 = (f32[8,512]{1,0:T(8,128)S(1)}, f32[8,512]{1,0:T(8,128)S(1)}, u32[]{:S(2)}, u32[]{:S(2)}) collective-permute-start(f32[8,512]{1,0:T(8,128)S(1)} %get-tuple-element.242), channel_id=1, source_target_pairs={{0,1},{1,0},{2,3},{3,2},{4,5},{5,4},{6,7},{7,6},{8,9},{9,8},{10,11... | collective-permute-start | bytes 49160 | tf_op jit(solution)/shard_map/ppermute | solution.py:26
  356.5 10.0 %collective-permute-start.64 = (bf16[128,768]{1,0:T(8,128)(2,1)S(1)}, bf16[128,768]{1,0:T(8,128)(2,1)S(1)}, u32[]{:S(2)}, u32[]{:S(2)}) collective-permute-start(bf16[128,768]{1,0:T(8,128)(2,1)S(1)} %get-tuple-element.240), channel_id=1, source_target_pairs={{0,8},{4,12},{8,0},{12,4},{16,24},{20,28},{24,16},{28,20},{1,9},{5... | collective-permute-start | bytes 589832 | tf_op jit(solution)/shard_map/ppermute | solution.py:447
  364.0 15.1 %collective-permute-start.67 = (bf16[128,768]{1,0:T(8,128)(2,1)}, bf16[128,768]{1,0:T(8,128)(2,1)S(1)}, u32[]{:S(2)}, u32[]{:S(2)}) collective-permute-start(bf16[128,768]{1,0:T(8,128)(2,1)} %get-tuple-element.248), channel_id=1, source_target_pairs={{0,16},{4,20},{8,24},{12,28},{16,0},{20,4},{24,8},{28,12},{1,17},{... | collective-permute-start | bytes 589832 | tf_op jit(solution)/shard_map/ppermute | solution.py:447
  364.0 15.1 %collective-permute-start.68 = (bf16[128,768]{1,0:T(8,128)(2,1)}, bf16[128,768]{1,0:T(8,128)(2,1)}, u32[]{:S(2)}, u32[]{:S(2)}) collective-permute-start(bf16[128,768]{1,0:T(8,128)(2,1)} %get-tuple-element.249), channel_id=1, source_target_pairs={{0,24},{4,28},{8,16},{12,20},{16,8},{20,12},{24,0},{28,4},{1,25},{... | collective-permute-start | bytes 589832 | tf_op jit(solution)/shard_map/ppermute | solution.py:447
  369.4 18.5 %collective-permute-start.74 = (bf16[128,1024]{1,0:T(8,128)(2,1)S(1)}, bf16[128,1024]{1,0:T(8,128)(2,1)S(1)}, u32[]{:S(2)}, u32[]{:S(2)}) collective-permute-start(bf16[128,1024]{1,0:T(8,128)(2,1)S(1)} %get-tuple-element.274), channel_id=1, source_target_pairs={{0,2},{1,3},{2,0},{3,1},{4,6},{5,7},{6,4},{7,5},{8,10},{9,11},{10,... | collective-permute-start | bytes 786440 | tf_op jit(solution)/shard_map/ppermute | solution.py:26
  371.8 14.3 %collective-permute-start.71 = (bf16[128,512]{1,0:T(8,128)(2,1)S(1)}, bf16[128,512]{1,0:T(8,128)(2,1)S(1)}, u32[]{:S(2)}, u32[]{:S(2)}) collective-permute-start(bf16[128,512]{1,0:T(8,128)(2,1)S(1)} %get-tuple-element.263), channel_id=1, source_target_pairs={{0,4},{4,0},{8,12},{12,8},{16,20},{20,16},{24,28},{28,24},{1,5},{5... | collective-permute-start | bytes 393224 | tf_op jit(solution)/shard_map/ppermute | solution.py:447
  372.8 9.3 %collective-permute-start.77 = (f32[8,256]{1,0:T(8,128)S(1)}, f32[8,256]{1,0:T(8,128)S(1)}, u32[]{:S(2)}, u32[]{:S(2)}) collective-permute-start(f32[8,256]{1,0:T(8,128)S(1)} %add.196), channel_id=1, source_target_pairs={{0,8},{4,12},{8,0},{12,4},{16,24},{20,28},{24,16},{28,20},{1,9},{5... | collective-permute-start | bytes 24584 | tf_op jit(solution)/shard_map/ppermute | solution.py:447
  381.4 8.7 %collective-permute-start.69 = (bf16[128,384]{1,0:T(8,128)(2,1)S(1)}, bf16[128,384]{1,0:T(8,128)(2,1)S(1)}, u32[]{:S(2)}, u32[]{:S(2)}) collective-permute-start(bf16[128,384]{1,0:T(8,128)(2,1)S(1)} %get-tuple-element.251), channel_id=1, source_target_pairs={{0,2},{1,3},{2,0},{3,1},{4,6},{5,7},{6,4},{7,5},{8,10},{9,11},{10,... | collective-permute-start | bytes 294920 | tf_op jit(solution)/shard_map/ppermute | solution.py:26
  382.1 8.1 %collective-permute-start.78 = (f32[8,256]{1,0:T(8,128)S(1)}, f32[8,256]{1,0:T(8,128)S(1)}, u32[]{:S(2)}, u32[]{:S(2)}) collective-permute-start(f32[8,256]{1,0:T(8,128)S(1)} %add.197), channel_id=1, source_target_pairs={{0,16},{4,20},{8,24},{12,28},{16,0},{20,4},{24,8},{28,12},{1,17},{... | collective-permute-start | bytes 24584 | tf_op jit(solution)/shard_map/ppermute | solution.py:447
  387.0 7.5 %collective-permute-start.72 = (bf16[128,1024]{1,0:T(8,128)(2,1)S(1)}, bf16[128,1024]{1,0:T(8,128)(2,1)S(1)}, u32[]{:S(2)}, u32[]{:S(2)}) collective-permute-start(bf16[128,1024]{1,0:T(8,128)(2,1)S(1)} %get-tuple-element.265), channel_id=1, source_target_pairs={{0,2},{1,3},{2,0},{3,1},{4,6},{5,7},{6,4},{7,5},{8,10},{9,11},{10,... | collective-permute-start | bytes 786440 | tf_op jit(solution)/shard_map/ppermute | solution.py:26
  388.7 9.3 %collective-permute-start.75 = (bf16[128,1024]{1,0:T(8,128)(2,1)S(1)}, bf16[128,1024]{1,0:T(8,128)(2,1)S(1)}, u32[]{:S(2)}, u32[]{:S(2)}) collective-permute-start(bf16[128,1024]{1,0:T(8,128)(2,1)S(1)} %get-tuple-element.276), channel_id=1, source_target_pairs={{0,1},{1,0},{2,3},{3,2},{4,5},{5,4},{6,7},{7,6},{8,9},{9,8},{10,11... | collective-permute-start | bytes 786440 | tf_op jit(solution)/shard_map/ppermute | solution.py:26
  (129 other events, 1182.7 us)
Sparse Core Ops, SparseCore 0:
  108.1 74.3 all-gather.1
  214.4 95.4 reduce-scatter.1

commit v7 on v6

--- a/solution.py
+++ b/solution.py
@@ -971,6 +971,7 @@
     self_line, cross_line = lines[:64], lines[64:]
     self_z = three_ways(self_line)
     attend_z = three_ways(attend)
+    attend_x0 = row_swap(attend, 1)
     one_all = join(ids, one, one_far, one_near, swap(one_far, 1))
     text_far, text_near = swap(text, 2), swap(text, 1)
     mixed_x2, one_all, text_far, *self_z, ffn_block = sync(
@@ -980,10 +981,10 @@
     (w_mixed,) = place(ids, (768,), [mixed, *mixed_z], [mixed_x, mixed_x1, mixed_x2])
     mixed_low = mm(one_all, w_mixed).astype(LOW)
     w_self = place_line(ids, self_line, *self_z)
-    mixed_low, *attend_z, grad, attend, cross_line, w_self = sync(
-        mixed_low, *attend_z, grad, attend, cross_line, w_self
-    )
-    attend_x0, attend_x1 = row_swap(attend, 1), row_swap(attend_z[0], 1)
+    mixed_low, *attend_z, grad, attend, cross_line, w_self, attend_x0 = sync(
+        mixed_low, *attend_z, grad, attend, cross_line, w_self, attend_x0
+    )
+    attend_x1 = row_swap(attend_z[0], 1)
     attend_x2 = row_swap(jnp.stack(attend_z[1:]), 1)
     cross_z = three_ways(cross_line)
     grad_far, grad_near = swap(grad, 2), swap(grad, 1)

time: 415 us -> 411 us (level)
  waiting for transfers between devices: 138 us -> 129 us
  local copies, waits for them, and re-layouts: 20.2 us -> 25.8 us
    ppermute x35, waiting for transfers between devices: 82.3 us -> 70.6 us  [row_swap(): return lax.ppermute(values, 'rows', [(i, i ^ mask) for i in range(size)])]
    unnamed x224 -> x232, local copies, waits for them, and re-layouts: 18.8 us -> 24.4 us
where the time goes in v7:
time: 411 us; the launch traced here: 405 us
  waiting for transfers between devices  129 us (31%)
  starting transfers between devices  88.6 us (22%)
  Pallas kernels  87.8 us (21%)
  matrix products  44.6 us (11%)
  local copies, waits for them, and re-layouts  25.8 us (6%)
  between operations  16.4 us (4%)
  other arithmetic  12.3 us (3%)
    pallas_call x39, Pallas kernels, call(): pl.pallas_call(body, out_shape=outs, in_specs=[pl.BlockSpec(memory_space=...  77.9 us
    ppermute x35, waiting for transfers between devices, row_swap(): return lax.ppermute(values, 'rows', [(i, i ^ mask) for i in range(size)])  70.6 us
    ppermute x35, starting transfers between devices, row_swap(): return lax.ppermute(values, 'rows', [(i, i ^ mask) for i in range(size)])  64.2 us
    ppermute x44, waiting for transfers between devices, swap(): return lax.ppermute(values, 'text', [(i, i ^ mask) for i in range(WAYS)])  58.7 us
    dot_general x31, matrix products, mm(): lax.dot_general(left, right, (((left_dim,), (right_dim,)), ((), ())), pre...  44.6 us
    unnamed x232, local copies, waits for them, and re-layouts  24.4 us
    ppermute x44, starting transfers between devices, swap(): return lax.ppermute(values, 'text', [(i, i ^ mask) for i in range(WAYS)])  24.1 us
    pallas_call x1, Pallas kernels, weight_grads(): pl.pallas_call(weight_block, grid=(2, rows // tile), out_shape=shaped((ro...  9.93 us
  transfers between devices with their start and end apart: 81, of which 30 were waited for; matrix products, arithmetic and copies ran while one was open for 12% of the time, Pallas kernels for 20%

profile of v7, /device:TPU:0, one launch (start us, length us, event | category | flops | bytes accessed | tf_op | source)
XLA Modules:
  0.0 405.0 jit_solution(12311211276326282873)
XLA Ops:
  14.9 2.9 collective-permute-start.1
  33.9 2.6 collective-permute-start.4
  36.5 6.4 %collective-permute-done.3.refs_1_ = bf16[128,768]{1,0:T(8,128)(2,1)S(1)} collective-permute-done((bf16[128,768]{1,0:T(8,128)(2,1)S(1)}, bf16[128,768]{1,0:T(8,128)(2,1)S(1)}, u32[]{:S(2)}, u32[]{:S(2)}) %collective-permute-start.3) | collective-permute-done | bytes 196640 | tf_op jit(solution)/shard_map/ppermute | solution.py:447
  42.9 2.5 collective-permute-start.5
  47.4 1.9 shard_map.234
  50.5 2.4 collective-permute-done.6.refs_4_
  52.9 2.1 collective-permute-done.7.refs_5_
  58.0 2.8 collective-permute-start.17
  63.9 5.3 %collective-permute-done.16.refs_2_ = bf16[64,1024]{1,0:T(8,128)(2,1)S(1)} collective-permute-done((bf16[64,1024]{1,0:T(8,128)(2,1)S(1)}, bf16[64,1024]{1,0:T(8,128)(2,1)S(1)}, u32[]{:S(2)}, u32[]{:S(2)}) %collective-permute-start.16) | collective-permute-done | bytes 131104 | tf_op jit(solution)/shard_map/ppermute | solution.py:447
  70.6 1.8 collective-permute-start.20
  78.8 2.7 shard_map.236
  81.6 1.8 convolution_convert_fusion.1.mixed_ref
  83.4 6.3 %collective-permute-done.19.refs_2_ = bf16[128,1024]{1,0:T(8,128)(2,1)S(1)} collective-permute-done((bf16[128,1024]{1,0:T(8,128)(2,1)}, bf16[128,1024]{1,0:T(8,128)(2,1)S(1)}, u32[]{:S(2)}, u32[]{:S(2)}) %collective-permute-start.19) | collective-permute-done | bytes 262176 | tf_op jit(solution)/shard_map/ppermute | solution.py:447
  93.5 4.4 %collective-permute-start.26 = (bf16[64,1024]{1,0:T(8,128)(2,1)S(1)}, bf16[64,1024]{1,0:T(8,128)(2,1)}, u32[]{:S(2)}, u32[]{:S(2)}) collective-permute-start(bf16[64,1024]{1,0:T(8,128)(2,1)S(1)} %get-tuple-element.190.refs_0_), channel_id=1, source_target_pairs={{0,8},{4,12},{8,0},{12,4},{16,24},{20,28},{24,16},{28,20},{1,9},{5... | collective-permute-start | bytes 393224 | tf_op jit(solution)/shard_map/ppermute | solution.py:447
  99.3 2.4 collective-permute-start.28
  102.2 6.9 %shard_map.238 = (bf16[1024,256]{1,0:T(8,128)(2,1)S(1)}, f32[4,1024]{1,0:T(4,128)S(1)}) custom-call(s32[2]{0:T(128)S(1)} %pad_add_fusion.ids_ref._.here_ref, s32[8,1024]{1,0:T(8,128)S(1)} %stack.53.marks_ref, bf16[1024,768]{1,0:T(8,128)(2,1)S(1)} %convolution_convert_fusion.1.mixed_ref), custom_call_target="tpu_custom_call" | custom-call | bytes 2146312 | tf_op jit(solution)/shard_map/pallas_call | solution.py:352
  116.8 10.9 %collective-permute-done.31.refs_6_ = bf16[2,128,1024]{2,1,0:T(8,128)(2,1)S(1)} collective-permute-done((bf16[2,128,1024]{2,1,0:T(8,128)(2,1)S(1)}, bf16[2,128,1024]{2,1,0:T(8,128)(2,1)S(1)}, u32[]{:S(2)}, u32[]{:S(2)}) %collective-permute-start.31) | collective-permute-done | bytes 524320 | tf_op jit(solution)/shard_map/ppermute | solution.py:447
  127.7 2.5 collective-permute-done.30
  130.3 2.0 shard_map.241
  135.2 1.8 shard_map.243.refs_0_
  137.0 6.4 %collective-permute-done.33.other_ref = bf16[384,512]{1,0:T(8,128)(2,1)S(1)} collective-permute-done((bf16[384,512]{1,0:T(8,128)(2,1)S(1)}, bf16[384,512]{1,0:T(8,128)(2,1)S(1)}, u32[]{:S(2)}, u32[]{:S(2)}) %collective-permute-start.33) | collective-permute-done | bytes 393248 | tf_op jit(solution)/shard_map/ppermute | solution.py:26
  146.3 6.4 %shard_map.242 = (bf16[512,512]{1,0:T(8,128)(2,1)S(1)}, f32[8,512]{1,0:T(8,128)S(1)}) custom-call(s32[2]{0:T(128)S(1)} %pad_add_fusion.ids_ref._.here_ref, s32[8,1024]{1,0:T(8,128)S(1)} %copy-done.25, bf16[512,512]{1,0:T(8,128)(2,1)S(1)} %convolution_convert_fusion.14.query_ref, bf16[384,512]{1,0:T(8,128)(2,1)S(1)} %convolution_convert_fusion.16.own_ref, ...), custom_call_target="tpu_custom_call" | custom-call | bytes 1884168 | tf_op jit(solution)/shard_map/pallas_call | solution.py:352
  152.7 3.0 collective-permute-done.34.refs_1_
  156.9 1.9 collective-permute-done.35
  161.5 12.5 %collective-permute-done.38.refs_1_ = bf16[256,1024]{1,0:T(8,128)(2,1)S(1)} collective-permute-done((bf16[256,1024]{1,0:T(8,128)(2,1)S(1)}, bf16[256,1024]{1,0:T(8,128)(2,1)S(1)}, u32[]{:S(2)}, u32[]{:S(2)}) %collective-permute-start.38) | collective-permute-done | bytes 524320 | tf_op jit(solution)/shard_map/ppermute | solution.py:26
  174.0 1.7 shard_map.245.right_b
  179.1 6.2 %fusion.3 = (f32[1024,1024]{1,0:T(8,128)S(1)}, bf16[1024,1024]{1,0:T(8,128)(2,1)S(1)}) fusion(bf16[1024,1024]{1,0:T(8,128)(2,1)} %copy-done.11, bf16[1024,2048]{1,0:T(8,128)(2,1)} %all-gather.2.cloned.1.call-done), kind=kOutput, calls=%fused_computation.4 | convolution fusion | flops 2157969408 | bytes 10485760 | tf_op jit(solution)/shard_map/dot_general | solution.py:20
  185.4 2.4 multiply_convert_fusion.right_a
  189.6 2.2 convolution_convert_fusion.4
  194.0 9.9 %shard_map.247 = bf16[1024,2048]{1,0:T(8,128)(2,1)} custom-call(bf16[1024,1024]{1,0:T(8,128)(2,1)S(1)} %copy-done.12, bf16[1024,1024]{1,0:T(8,128)(2,1)S(1)} %multiply_convert_fusion.right_a, bf16[1024,1024]{1,0:T(8,128)(2,1)} %copy-done.115, bf16[1024,1024]{1,0:T(8,128)(2,1)} %copy-done.9), custom_call_target="tpu_custom_call" | custom-call | flops 4294967296 | bytes 12582912 | tf_op jit(solution)/shard_map/pallas_call | solution.py:378
  203.9 3.3 fusion.39
  208.1 3.6 multiply_reduce_fusion
  215.1 11.6 %collective-permute-done.45 = bf16[256,1024]{1,0:T(8,128)(2,1)S(1)} collective-permute-done((bf16[256,1024]{1,0:T(8,128)(2,1)S(1)}, bf16[256,1024]{1,0:T(8,128)(2,1)S(1)}, u32[]{:S(2)}, u32[]{:S(2)}) %collective-permute-start.45) | collective-permute-done | bytes 524320 | tf_op jit(solution)/shard_map/ppermute | solution.py:26
  227.5 7.3 %shard_map.249 = (bf16[512,512]{1,0:T(8,128)(2,1)S(1)}, bf16[384,512]{1,0:T(8,128)(2,1)S(1)}, bf16[384,512]{1,0:T(8,128)(2,1)S(1)}) custom-call(s32[2]{0:T(128)S(1)} %pad_add_fusion.ids_ref._.here_ref, s32[8,1024]{1,0:T(8,128)S(1)} %copy-done.26, bf16[512,512]{1,0:T(8,128)(2,1)S(1)} %convolution_convert_fusion.14.query_ref, ...), custom_call_target="tpu_custom_call" | custom-call | bytes 3194888 | tf_op jit(solution)/shard_map/pallas_call | solution.py:352
  234.9 3.1 fusion.32
  243.3 6.8 %collective-permute-done.47 = bf16[384,512]{1,0:T(8,128)(2,1)S(1)} collective-permute-done((bf16[384,512]{1,0:T(8,128)(2,1)S(1)}, bf16[384,512]{1,0:T(8,128)(2,1)S(1)}, u32[]{:S(2)}, u32[]{:S(2)}) %collective-permute-start.47) | collective-permute-done | bytes 393248 | tf_op jit(solution)/shard_map/ppermute | solution.py:26
  252.5 1.7 shard_map.252
  256.3 7.5 %collective-permute-done.48.refs_1_ = bf16[256,1024]{1,0:T(8,128)(2,1)} collective-permute-done((bf16[256,1024]{1,0:T(8,128)(2,1)S(1)}, bf16[256,1024]{1,0:T(8,128)(2,1)}, u32[]{:S(2)}, u32[]{:S(2)}) %collective-permute-start.48) | collective-permute-done | bytes 524320 | tf_op jit(solution)/shard_map/ppermute | solution.py:26
  266.1 2.2 shard_map.250
  269.7 10.7 %shard_map.251 = bf16[1024,768]{1,0:T(8,128)(2,1)S(1)} custom-call(s32[2]{0:T(128)S(1)} %pad_add_fusion.ids_ref._.here_ref, s32[8,1024]{1,0:T(8,128)S(1)} %copy-done.27, bf16[1024,768]{1,0:T(8,128)(2,1)S(1)} %copy-done.1, bf16[1024,256]{1,0:T(8,128)(2,1)S(1)} %convolution_convert_fusion.12.grad_ref, f32[4,1024]{1,0:T(4,128)S(1)} %copy-done.66), custom_call_target="tpu_custom_call" | custom-call | bytes 3719176 | tf_op jit(solution)/shard_map/pallas_call | solution.py:352
  280.4 6.5 %collective-permute-done.51.refs_2_ = bf16[4,128,1024]{2,1,0:T(8,128)(2,1)} collective-permute-done((bf16[4,128,1024]{2,1,0:T(8,128)(2,1)}, bf16[4,128,1024]{2,1,0:T(8,128)(2,1)}, u32[]{:S(2)}, u32[]{:S(2)}) %collective-permute-start.51) | collective-permute-done | bytes 1048608 | tf_op jit(solution)/shard_map/ppermute | solution.py:447
  287.0 2.0 convolution_convert_fusion.2
  292.9 2.2 shard_map.254
  295.1 1.8 collective-permute-start.57
  296.9 5.6 %collective-permute-start.58 = (bf16[128,1024]{1,0:T(8,128)(2,1)S(1)}, bf16[128,1024]{1,0:T(8,128)(2,1)S(1)}, u32[]{:S(2)}, u32[]{:S(2)}) collective-permute-start(bf16[128,1024]{1,0:T(8,128)(2,1)S(1)} %get-tuple-element.229), channel_id=1, source_target_pairs={{0,16},{4,20},{8,24},{12,28},{16,0},{20,4},{24,8},{28,12},{1,17},{... | collective-permute-start | bytes 786440 | tf_op jit(solution)/shard_map/ppermute | solution.py:447
  303.4 1.9 convolution_convert_fusion.refs_0_
  305.3 1.7 fusion.38
  311.0 1.8 collective-permute-start.61
  313.6 2.6 collective-permute-done.57.refs_1_
  316.2 7.4 %collective-permute-done.59.refs_3_ = bf16[128,1024]{1,0:T(8,128)(2,1)S(1)} collective-permute-done((bf16[128,1024]{1,0:T(8,128)(2,1)S(1)}, bf16[128,1024]{1,0:T(8,128)(2,1)S(1)}, u32[]{:S(2)}, u32[]{:S(2)}) %collective-permute-start.59) | collective-permute-done | bytes 262176 | tf_op jit(solution)/shard_map/ppermute | solution.py:447
  324.5 6.0 %collective-permute-start.60 = (bf16[128,1024]{1,0:T(8,128)(2,1)S(1)}, bf16[128,1024]{1,0:T(8,128)(2,1)S(1)}, u32[]{:S(2)}, u32[]{:S(2)}) collective-permute-start(bf16[128,1024]{1,0:T(8,128)(2,1)S(1)} %get-tuple-element.234), channel_id=1, source_target_pairs={{0,8},{4,12},{8,0},{12,4},{16,24},{20,28},{24,16},{28,20},{1,9},{5... | collective-permute-start | bytes 786440 | tf_op jit(solution)/shard_map/ppermute | solution.py:447
  331.1 1.9 collective-permute-start.63
  333.0 1.7 fusion.4
  334.7 6.6 %collective-permute-done.60.refs_5_ = bf16[128,1024]{1,0:T(8,128)(2,1)S(1)} collective-permute-done((bf16[128,1024]{1,0:T(8,128)(2,1)S(1)}, bf16[128,1024]{1,0:T(8,128)(2,1)S(1)}, u32[]{:S(2)}, u32[]{:S(2)}) %collective-permute-start.60) | collective-permute-done | bytes 262176 | tf_op jit(solution)/shard_map/ppermute | solution.py:447
  343.1 8.7 %collective-permute-done.62.refs_6_ = bf16[128,1024]{1,0:T(8,128)(2,1)S(1)} collective-permute-done((bf16[128,1024]{1,0:T(8,128)(2,1)S(1)}, bf16[128,1024]{1,0:T(8,128)(2,1)S(1)}, u32[]{:S(2)}, u32[]{:S(2)}) %collective-permute-start.62) | collective-permute-done | bytes 262176 | tf_op jit(solution)/shard_map/ppermute | solution.py:447
  353.4 4.9 %collective-permute-start.64 = (bf16[128,768]{1,0:T(8,128)(2,1)S(1)}, bf16[128,768]{1,0:T(8,128)(2,1)S(1)}, u32[]{:S(2)}, u32[]{:S(2)}) collective-permute-start(bf16[128,768]{1,0:T(8,128)(2,1)S(1)} %get-tuple-element.242), channel_id=1, source_target_pairs={{0,8},{4,12},{8,0},{12,4},{16,24},{20,28},{24,16},{28,20},{1,9},{5... | collective-permute-start | bytes 589832 | tf_op jit(solution)/shard_map/ppermute | solution.py:447
  361.5 2.1 collective-permute-start.68
  370.0 2.5 collective-permute-start.77
  372.5 3.8 collective-permute-done.67.refs_2_
  376.3 2.3 shard_map.259
  380.2 3.2 collective-permute-start.78
  392.3 1.9 shard_map.261
  394.2 1.7 shard_map.268
  395.8 1.8 shard_map.265
  (447 shorter events, 123.0 us)
Async XLA Ops:
  7.2 171.9 %all-gather.2.cloned.1.call-start = ((), (), s32[]{:S(2)}) async-start(), calls=%async_computation.1 | async-start | bytes 4718592 | tf_op jit(solution)/shard_map/all_gather | solution.py:451
  14.9 10.6 %collective-permute-start.1 = (bf16[144,896]{1,0:T(8,128)(2,1)S(1)}, bf16[144,896]{1,0:T(8,128)(2,1)S(1)}, u32[]{:S(2)}, u32[]{:S(2)}) collective-permute-start(bf16[144,896]{1,0:T(8,128)(2,1)S(1)} %get-tuple-element.149), channel_id=1, source_target_pairs={{0,2},{1,3},{2,0},{3,1},{4,6},{5,7},{6,4},{7,5},{8,10},{9,11},{10,... | collective-permute-start | bytes 774152 | tf_op jit(solution)/shard_map/ppermute | solution.py:26
  28.8 17.1 %collective-permute-start.8 = (bf16[128,1536]{1,0:T(8,128)(2,1)S(1)}, bf16[128,1536]{1,0:T(8,128)(2,1)S(1)}, u32[]{:S(2)}, u32[]{:S(2)}) collective-permute-start(bf16[128,1536]{1,0:T(8,128)(2,1)S(1)} %get-tuple-element.164), channel_id=1, source_target_pairs={{0,2},{1,3},{2,0},{3,1},{4,6},{5,7},{6,4},{7,5},{8,10},{9,11},{10,... | collective-permute-start | bytes 1179656 | tf_op jit(solution)/shard_map/ppermute | solution.py:26
  29.4 25.6 %collective-permute-start.10 = (bf16[256,1024]{1,0:T(8,128)(2,1)S(1)}, bf16[256,1024]{1,0:T(8,128)(2,1)S(1)}, u32[]{:S(2)}, u32[]{:S(2)}) collective-permute-start(bf16[256,1024]{1,0:T(8,128)(2,1)S(1)} %fusion.53.refs_0_), channel_id=1, source_target_pairs={{0,2},{1,3},{2,0},{3,1},{4,6},{5,7},{6,4},{7,5},{8,10},{9,11},{10,... | collective-permute-start | bytes 1572872 | tf_op jit(solution)/shard_map/ppermute | solution.py:26
  30.9 14.5 %collective-permute-start.9 = (bf16[128,1024]{1,0:T(8,128)(2,1)S(1)}, bf16[128,1024]{1,0:T(8,128)(2,1)S(1)}, u32[]{:S(2)}, u32[]{:S(2)}) collective-permute-start(bf16[128,1024]{1,0:T(8,128)(2,1)S(1)} %get-tuple-element.166), channel_id=1, source_target_pairs={{0,4},{4,0},{8,12},{12,8},{16,20},{20,16},{24,28},{28,24},{1,5},{5... | collective-permute-start | bytes 786440 | tf_op jit(solution)/shard_map/ppermute | solution.py:447
  32.3 10.5 %collective-permute-start.3 = (bf16[128,768]{1,0:T(8,128)(2,1)S(1)}, bf16[128,768]{1,0:T(8,128)(2,1)S(1)}, u32[]{:S(2)}, u32[]{:S(2)}) collective-permute-start(bf16[128,768]{1,0:T(8,128)(2,1)S(1)} %get-tuple-element.162.refs_0_), channel_id=1, source_target_pairs={{0,8},{4,12},{8,0},{12,4},{16,24},{20,28},{24,16},{28,20},{1,9},{5... | collective-permute-start | bytes 589832 | tf_op jit(solution)/shard_map/ppermute | solution.py:447
  33.9 15.5 %collective-permute-start.4 = (bf16[128,768]{1,0:T(8,128)(2,1)S(1)}, bf16[128,768]{1,0:T(8,128)(2,1)S(1)}, u32[]{:S(2)}, u32[]{:S(2)}) collective-permute-start(bf16[128,768]{1,0:T(8,128)(2,1)S(1)} %get-tuple-element.162.refs_0_), channel_id=1, source_target_pairs={{0,16},{4,20},{8,24},{12,28},{16,0},{20,4},{24,8},{28,12},{1,17},{... | collective-permute-start | bytes 589832 | tf_op jit(solution)/shard_map/ppermute | solution.py:447
  42.9 7.6 %collective-permute-start.5 = (bf16[128,768]{1,0:T(8,128)(2,1)S(1)}, bf16[128,768]{1,0:T(8,128)(2,1)S(1)}, u32[]{:S(2)}, u32[]{:S(2)}) collective-permute-start(bf16[128,768]{1,0:T(8,128)(2,1)S(1)} %get-tuple-element.162.refs_0_), channel_id=1, source_target_pairs={{0,24},{4,28},{8,16},{12,20},{16,8},{20,12},{24,0},{28,4},{1,25},{... | collective-permute-start | bytes 589832 | tf_op jit(solution)/shard_map/ppermute | solution.py:447
  45.4 7.5 %collective-permute-start.6 = (bf16[128,768]{1,0:T(8,128)(2,1)S(1)}, bf16[128,768]{1,0:T(8,128)(2,1)S(1)}, u32[]{:S(2)}, u32[]{:S(2)}) collective-permute-start(bf16[128,768]{1,0:T(8,128)(2,1)S(1)} %get-tuple-element.162.refs_0_), channel_id=1, source_target_pairs={{0,4},{4,0},{8,12},{12,8},{16,20},{20,16},{24,28},{28,24},{1,5},{5... | collective-permute-start | bytes 589832 | tf_op jit(solution)/shard_map/ppermute | solution.py:447
  45.9 9.1 %collective-permute-start.7 = (bf16[128,768]{1,0:T(8,128)(2,1)S(1)}, bf16[128,768]{1,0:T(8,128)(2,1)S(1)}, u32[]{:S(2)}, u32[]{:S(2)}) collective-permute-start(bf16[128,768]{1,0:T(8,128)(2,1)S(1)} %collective-permute-done.3.refs_1_), channel_id=1, source_target_pairs={{0,4},{4,0},{8,12},{12,8},{16,20},{20,16},{24,28},{28,24},{1,5},{5... | collective-permute-start | bytes 589832 | tf_op jit(solution)/shard_map/ppermute | solution.py:447
  55.1 18.8 %collective-permute-start.11 = (bf16[2,128,768]{2,1,0:T(8,128)(2,1)S(1)}, bf16[2,128,768]{2,1,0:T(8,128)(2,1)S(1)}, u32[]{:S(2)}, u32[]{:S(2)}) collective-permute-start(bf16[2,128,768]{2,1,0:T(8,128)(2,1)S(1)} %pad_maximum_fusion.1), channel_id=1, source_target_pairs={{0,4},{4,0},{8,12},{12,8},{16,20},{20,16},{24,28},{28,24},{1,5},{5... | collective-permute-start | bytes 1179656 | tf_op jit(solution)/shard_map/ppermute | solution.py:447
  55.7 16.7 %collective-permute-start.14 = (bf16[96,1024]{1,0:T(8,128)(2,1)}, bf16[96,1024]{1,0:T(8,128)(2,1)S(1)}, u32[]{:S(2)}, u32[]{:S(2)}) collective-permute-start(bf16[96,1024]{1,0:T(8,128)(2,1)} %bitcast.10.refs_0_), channel_id=1, source_target_pairs={{0,2},{1,3},{2,0},{3,1},{4,6},{5,7},{6,4},{7,5},{8,10},{9,11},{10,... | collective-permute-start | bytes 589832 | tf_op jit(solution)/shard_map/ppermute | solution.py:26
  56.2 7.1 %collective-permute-start.15 = (bf16[64,1024]{1,0:T(8,128)(2,1)S(1)}, bf16[64,1024]{1,0:T(8,128)(2,1)S(1)}, u32[]{:S(2)}, u32[]{:S(2)}) collective-permute-start(bf16[64,1024]{1,0:T(8,128)(2,1)S(1)} %get-tuple-element.304.refs_0_), channel_id=1, source_target_pairs={{0,8},{4,12},{8,0},{12,4},{16,24},{20,28},{24,16},{28,20},{1,9},{5... | collective-permute-start | bytes 393224 | tf_op jit(solution)/shard_map/ppermute | solution.py:447
  56.3 13.0 %collective-permute-start.16 = (bf16[64,1024]{1,0:T(8,128)(2,1)S(1)}, bf16[64,1024]{1,0:T(8,128)(2,1)S(1)}, u32[]{:S(2)}, u32[]{:S(2)}) collective-permute-start(bf16[64,1024]{1,0:T(8,128)(2,1)S(1)} %get-tuple-element.304.refs_0_), channel_id=1, source_target_pairs={{0,16},{4,20},{8,24},{12,28},{16,0},{20,4},{24,8},{28,12},{1,17},{... | collective-permute-start | bytes 393224 | tf_op jit(solution)/shard_map/ppermute | solution.py:447
  58.0 11.9 %collective-permute-start.17 = (bf16[64,1024]{1,0:T(8,128)(2,1)S(1)}, bf16[64,1024]{1,0:T(8,128)(2,1)S(1)}, u32[]{:S(2)}, u32[]{:S(2)}) collective-permute-start(bf16[64,1024]{1,0:T(8,128)(2,1)S(1)} %get-tuple-element.304.refs_0_), channel_id=1, source_target_pairs={{0,24},{4,28},{8,16},{12,20},{16,8},{20,12},{24,0},{28,4},{1,25},{... | collective-permute-start | bytes 393224 | tf_op jit(solution)/shard_map/ppermute | solution.py:447
  63.9 19.5 %collective-permute-start.18 = (bf16[128,1024]{1,0:T(8,128)(2,1)}, bf16[128,1024]{1,0:T(8,128)(2,1)}, u32[]{:S(2)}, u32[]{:S(2)}) collective-permute-start(bf16[128,1024]{1,0:T(8,128)(2,1)} %get-tuple-element.196.refs_0_), channel_id=1, source_target_pairs={{0,8},{4,12},{8,0},{12,4},{16,24},{20,28},{24,16},{28,20},{1,9},{5... | collective-permute-start | bytes 786440 | tf_op jit(solution)/shard_map/ppermute | solution.py:447
  69.9 19.8 %collective-permute-start.19 = (bf16[128,1024]{1,0:T(8,128)(2,1)}, bf16[128,1024]{1,0:T(8,128)(2,1)S(1)}, u32[]{:S(2)}, u32[]{:S(2)}) collective-permute-start(bf16[128,1024]{1,0:T(8,128)(2,1)} %get-tuple-element.196.refs_0_), channel_id=1, source_target_pairs={{0,16},{4,20},{8,24},{12,28},{16,0},{20,4},{24,8},{28,12},{1,17},{... | collective-permute-start | bytes 786440 | tf_op jit(solution)/shard_map/ppermute | solution.py:447
  70.6 19.1 %collective-permute-start.20 = (bf16[128,1024]{1,0:T(8,128)(2,1)}, bf16[128,1024]{1,0:T(8,128)(2,1)S(1)}, u32[]{:S(2)}, u32[]{:S(2)}) collective-permute-start(bf16[128,1024]{1,0:T(8,128)(2,1)} %get-tuple-element.196.refs_0_), channel_id=1, source_target_pairs={{0,24},{4,28},{8,16},{12,20},{16,8},{20,12},{24,0},{28,4},{1,25},{... | collective-permute-start | bytes 786440 | tf_op jit(solution)/shard_map/ppermute | solution.py:447
  72.4 17.3 %collective-permute-start.21 = (bf16[128,1024]{1,0:T(8,128)(2,1)}, bf16[128,1024]{1,0:T(8,128)(2,1)}, u32[]{:S(2)}, u32[]{:S(2)}) collective-permute-start(bf16[128,1024]{1,0:T(8,128)(2,1)} %get-tuple-element.196.refs_0_), channel_id=1, source_target_pairs={{0,4},{4,0},{8,12},{12,8},{16,20},{20,16},{24,28},{28,24},{1,5},{5... | collective-permute-start | bytes 786440 | tf_op jit(solution)/shard_map/ppermute | solution.py:447
  89.7 23.0 %collective-permute-start.25 = (bf16[256,1024]{1,0:T(8,128)(2,1)S(1)}, bf16[256,1024]{1,0:T(8,128)(2,1)}, u32[]{:S(2)}, u32[]{:S(2)}) collective-permute-start(bf16[256,1024]{1,0:T(8,128)(2,1)S(1)} %bitcast.75), channel_id=1, source_target_pairs={{0,2},{1,3},{2,0},{3,1},{4,6},{5,7},{6,4},{7,5},{8,10},{9,11},{10,... | collective-permute-start | bytes 1572872 | tf_op jit(solution)/shard_map/ppermute | solution.py:26
  91.5 7.1 %collective-permute-start.23 = (bf16[96,1024]{1,0:T(8,128)(2,1)S(1)}, bf16[96,1024]{1,0:T(8,128)(2,1)S(1)}, u32[]{:S(2)}, u32[]{:S(2)}) collective-permute-start(bf16[96,1024]{1,0:T(8,128)(2,1)S(1)} %copy-done.42), channel_id=1, source_target_pairs={{0,1},{1,0},{2,3},{3,2},{4,5},{5,4},{6,7},{7,6},{8,9},{9,8},{10,11... | collective-permute-start | bytes 589832 | tf_op jit(solution)/shard_map/ppermute | solution.py:26
  92.0 20.7 %collective-permute-start.24 = (bf16[128,1024]{1,0:T(8,128)(2,1)}, bf16[128,1024]{1,0:T(8,128)(2,1)}, u32[]{:S(2)}, u32[]{:S(2)}) collective-permute-start(bf16[128,1024]{1,0:T(8,128)(2,1)} %collective-permute-done.18.refs_1_), channel_id=1, source_target_pairs={{0,4},{4,0},{8,12},{12,8},{16,20},{20,16},{24,28},{28,24},{1,5},{5... | collective-permute-start | bytes 786440 | tf_op jit(solution)/shard_map/ppermute | solution.py:447
  93.5 19.2 %collective-permute-start.26 = (bf16[64,1024]{1,0:T(8,128)(2,1)S(1)}, bf16[64,1024]{1,0:T(8,128)(2,1)}, u32[]{:S(2)}, u32[]{:S(2)}) collective-permute-start(bf16[64,1024]{1,0:T(8,128)(2,1)S(1)} %get-tuple-element.190.refs_0_), channel_id=1, source_target_pairs={{0,8},{4,12},{8,0},{12,4},{16,24},{20,28},{24,16},{28,20},{1,9},{5... | collective-permute-start | bytes 393224 | tf_op jit(solution)/shard_map/ppermute | solution.py:447
  98.6 14.1 %collective-permute-start.27 = (bf16[64,1024]{1,0:T(8,128)(2,1)S(1)}, bf16[64,1024]{1,0:T(8,128)(2,1)}, u32[]{:S(2)}, u32[]{:S(2)}) collective-permute-start(bf16[64,1024]{1,0:T(8,128)(2,1)S(1)} %get-tuple-element.190.refs_0_), channel_id=1, source_target_pairs={{0,16},{4,20},{8,24},{12,28},{16,0},{20,4},{24,8},{28,12},{1,17},{... | collective-permute-start | bytes 393224 | tf_op jit(solution)/shard_map/ppermute | solution.py:447
  99.3 13.4 %collective-permute-start.28 = (bf16[64,1024]{1,0:T(8,128)(2,1)S(1)}, bf16[64,1024]{1,0:T(8,128)(2,1)}, u32[]{:S(2)}, u32[]{:S(2)}) collective-permute-start(bf16[64,1024]{1,0:T(8,128)(2,1)S(1)} %get-tuple-element.190.refs_0_), channel_id=1, source_target_pairs={{0,24},{4,28},{8,16},{12,20},{16,8},{20,12},{24,0},{28,4},{1,25},{... | collective-permute-start | bytes 393224 | tf_op jit(solution)/shard_map/ppermute | solution.py:447
  102.0 261.7 %reduce-scatter.2.cloned.1.call-start = ((), (), s32[]{:S(2)}) async-start(), calls=%async_computation.2 | async-start | bytes 4718592 | tf_op jit(solution)/shard_map/reduce_scatter | solution.py:455
  113.3 14.4 %collective-permute-start.31 = (bf16[2,128,1024]{2,1,0:T(8,128)(2,1)S(1)}, bf16[2,128,1024]{2,1,0:T(8,128)(2,1)S(1)}, u32[]{:S(2)}, u32[]{:S(2)}) collective-permute-start(bf16[2,128,1024]{2,1,0:T(8,128)(2,1)S(1)} %pad_maximum_fusion), channel_id=1, source_target_pairs={{0,4},{4,0},{8,12},{12,8},{16,20},{20,16},{24,28},{28,24},{1,5},{5... | collective-permute-start | bytes 1572872 | tf_op jit(solution)/shard_map/ppermute | solution.py:447
  116.2 14.0 %collective-permute-start.30 = (bf16[256,1024]{1,0:T(8,128)(2,1)S(1)}, bf16[256,1024]{1,0:T(8,128)(2,1)S(1)}, u32[]{:S(2)}, u32[]{:S(2)}) collective-permute-start(bf16[256,1024]{1,0:T(8,128)(2,1)S(1)} %fusion.45), channel_id=1, source_target_pairs={{0,2},{1,3},{2,0},{3,1},{4,6},{5,7},{6,4},{7,5},{8,10},{9,11},{10,... | collective-permute-start | bytes 1572872 | tf_op jit(solution)/shard_map/ppermute | solution.py:26
  132.8 10.5 %collective-permute-start.33 = (bf16[384,512]{1,0:T(8,128)(2,1)S(1)}, bf16[384,512]{1,0:T(8,128)(2,1)S(1)}, u32[]{:S(2)}, u32[]{:S(2)}) collective-permute-start(bf16[384,512]{1,0:T(8,128)(2,1)S(1)} %convolution_convert_fusion.16.own_ref), channel_id=1, source_target_pairs={{0,2},{1,3},{2,0},{3,1},{4,6},{5,7},{6,4},{7,5},{8,10},{9,11},{10,... | collective-permute-start | bytes 1179656 | tf_op jit(solution)/shard_map/ppermute | solution.py:26
  135.1 8.8 %collective-permute-start.32 = (bf16[256,1024]{1,0:T(8,128)(2,1)S(1)}, bf16[256,1024]{1,0:T(8,128)(2,1)S(1)}, u32[]{:S(2)}, u32[]{:S(2)}) collective-permute-start(bf16[256,1024]{1,0:T(8,128)(2,1)S(1)} %add_convert_fusion.2.refs_0_), channel_id=1, source_target_pairs={{0,1},{1,0},{2,3},{3,2},{4,5},{5,4},{6,7},{7,6},{8,9},{9,8},{10,11... | collective-permute-start | bytes 1572872 | tf_op jit(solution)/shard_map/ppermute | solution.py:26
  143.3 12.4 %collective-permute-start.34 = (bf16[256,1024]{1,0:T(8,128)(2,1)S(1)}, bf16[256,1024]{1,0:T(8,128)(2,1)S(1)}, u32[]{:S(2)}, u32[]{:S(2)}) collective-permute-start(bf16[256,1024]{1,0:T(8,128)(2,1)S(1)} %shard_map.243.refs_0_), channel_id=1, source_target_pairs={{0,2},{1,3},{2,0},{3,1},{4,6},{5,7},{6,4},{7,5},{8,10},{9,11},{10,... | collective-permute-start | bytes 1572872 | tf_op jit(solution)/shard_map/ppermute | solution.py:26
  160.0 14.0 %collective-permute-start.38 = (bf16[256,1024]{1,0:T(8,128)(2,1)S(1)}, bf16[256,1024]{1,0:T(8,128)(2,1)S(1)}, u32[]{:S(2)}, u32[]{:S(2)}) collective-permute-start(bf16[256,1024]{1,0:T(8,128)(2,1)S(1)} %add_convert_fusion.1.refs_0_), channel_id=1, source_target_pairs={{0,2},{1,3},{2,0},{3,1},{4,6},{5,7},{6,4},{7,5},{8,10},{9,11},{10,... | collective-permute-start | bytes 1572872 | tf_op jit(solution)/shard_map/ppermute | solution.py:26
  160.8 13.2 %collective-permute-start.36 = (bf16[256,1024]{1,0:T(8,128)(2,1)S(1)}, bf16[256,1024]{1,0:T(8,128)(2,1)S(1)}, u32[]{:S(2)}, u32[]{:S(2)}) collective-permute-start(bf16[256,1024]{1,0:T(8,128)(2,1)S(1)} %bitcast.76), channel_id=1, source_target_pairs={{0,1},{1,0},{2,3},{3,2},{4,5},{5,4},{6,7},{7,6},{8,9},{9,8},{10,11... | collective-permute-start | bytes 1572872 | tf_op jit(solution)/shard_map/ppermute | solution.py:26
  161.0 13.1 %collective-permute-start.37 = (bf16[256,1024]{1,0:T(8,128)(2,1)}, bf16[256,1024]{1,0:T(8,128)(2,1)S(1)}, u32[]{:S(2)}, u32[]{:S(2)}) collective-permute-start(bf16[256,1024]{1,0:T(8,128)(2,1)} %collective-permute-done.25.refs_1_), channel_id=1, source_target_pairs={{0,1},{1,0},{2,3},{3,2},{4,5},{5,4},{6,7},{7,6},{8,9},{9,8},{10,11... | collective-permute-start | bytes 1572872 | tf_op jit(solution)/shard_map/ppermute | solution.py:26
  161.4 15.7 %collective-permute-start.39 = (bf16[256,1024]{1,0:T(8,128)(2,1)S(1)}, bf16[256,1024]{1,0:T(8,128)(2,1)S(1)}, u32[]{:S(2)}, u32[]{:S(2)}) collective-permute-start(bf16[256,1024]{1,0:T(8,128)(2,1)S(1)} %add_convert_fusion.1.refs_0_), channel_id=1, source_target_pairs={{0,1},{1,0},{2,3},{3,2},{4,5},{5,4},{6,7},{7,6},{8,9},{9,8},{10,11... | collective-permute-start | bytes 1572872 | tf_op jit(solution)/shard_map/ppermute | solution.py:26
  191.9 12.1 %collective-permute-start.44 = (bf16[512,1024]{1,0:T(8,128)(2,1)}, bf16[512,1024]{1,0:T(8,128)(2,1)}, u32[]{:S(2)}, u32[]{:S(2)}) collective-permute-start(bf16[512,1024]{1,0:T(8,128)(2,1)} %convolution_convert_fusion.4), channel_id=1, source_target_pairs={{0,1},{1,0},{2,3},{3,2},{4,5},{5,4},{6,7},{7,6},{8,9},{9,8},{10,11... | collective-permute-start | bytes 3145736 | tf_op jit(solution)/shard_map/ppermute | solution.py:26
  193.5 14.6 %collective-permute-start.42 = (bf16[256,1024]{1,0:T(8,128)(2,1)}, bf16[256,1024]{1,0:T(8,128)(2,1)}, u32[]{:S(2)}, u32[]{:S(2)}) collective-permute-start(bf16[256,1024]{1,0:T(8,128)(2,1)} %fusion.42), channel_id=1, source_target_pairs={{0,2},{1,3},{2,0},{3,1},{4,6},{5,7},{6,4},{7,5},{8,10},{9,11},{10,... | collective-permute-start | bytes 1572872 | tf_op jit(solution)/shard_map/ppermute | solution.py:26
  212.9 13.8 %collective-permute-start.45 = (bf16[256,1024]{1,0:T(8,128)(2,1)S(1)}, bf16[256,1024]{1,0:T(8,128)(2,1)S(1)}, u32[]{:S(2)}, u32[]{:S(2)}) collective-permute-start(bf16[256,1024]{1,0:T(8,128)(2,1)S(1)} %copy-done.113), channel_id=1, source_target_pairs={{0,2},{1,3},{2,0},{3,1},{4,6},{5,7},{6,4},{7,5},{8,10},{9,11},{10,... | collective-permute-start | bytes 1572872 | tf_op jit(solution)/shard_map/ppermute | solution.py:26
  238.6 11.5 %collective-permute-start.47 = (bf16[384,512]{1,0:T(8,128)(2,1)S(1)}, bf16[384,512]{1,0:T(8,128)(2,1)S(1)}, u32[]{:S(2)}, u32[]{:S(2)}) collective-permute-start(bf16[384,512]{1,0:T(8,128)(2,1)S(1)} %get-tuple-element.219), channel_id=1, source_target_pairs={{0,2},{1,3},{2,0},{3,1},{4,6},{5,7},{6,4},{7,5},{8,10},{9,11},{10,... | collective-permute-start | bytes 1179656 | tf_op jit(solution)/shard_map/ppermute | solution.py:26
  250.1 13.7 %collective-permute-start.48 = (bf16[256,1024]{1,0:T(8,128)(2,1)S(1)}, bf16[256,1024]{1,0:T(8,128)(2,1)}, u32[]{:S(2)}, u32[]{:S(2)}) collective-permute-start(bf16[256,1024]{1,0:T(8,128)(2,1)S(1)} %get-tuple-element.220.refs_0_), channel_id=1, source_target_pairs={{0,2},{1,3},{2,0},{3,1},{4,6},{5,7},{6,4},{7,5},{8,10},{9,11},{10,... | collective-permute-start | bytes 1572872 | tf_op jit(solution)/shard_map/ppermute | solution.py:26
  255.3 31.7 %collective-permute-start.51 = (bf16[4,128,1024]{2,1,0:T(8,128)(2,1)}, bf16[4,128,1024]{2,1,0:T(8,128)(2,1)}, u32[]{:S(2)}, u32[]{:S(2)}) collective-permute-start(bf16[4,128,1024]{2,1,0:T(8,128)(2,1)} %shard_map.252), channel_id=1, source_target_pairs={{0,4},{4,0},{8,12},{12,8},{16,20},{20,16},{24,28},{28,24},{1,5},{5... | collective-permute-start | bytes 3145736 | tf_op jit(solution)/shard_map/ppermute | solution.py:447
  256.3 9.7 %collective-permute-start.49 = (bf16[256,1024]{1,0:T(8,128)(2,1)S(1)}, bf16[256,1024]{1,0:T(8,128)(2,1)}, u32[]{:S(2)}, u32[]{:S(2)}) collective-permute-start(bf16[256,1024]{1,0:T(8,128)(2,1)S(1)} %get-tuple-element.220.refs_0_), channel_id=1, source_target_pairs={{0,1},{1,0},{2,3},{3,2},{4,5},{5,4},{6,7},{7,6},{8,9},{9,8},{10,11... | collective-permute-start | bytes 1572872 | tf_op jit(solution)/shard_map/ppermute | solution.py:26
  265.4 26.3 %collective-permute-start.54 = (bf16[192,1024]{1,0:T(8,128)(2,1)S(1)}, bf16[192,1024]{1,0:T(8,128)(2,1)S(1)}, u32[]{:S(2)}, u32[]{:S(2)}) collective-permute-start(bf16[192,1024]{1,0:T(8,128)(2,1)S(1)} %convolution_convert_fusion.15), channel_id=1, source_target_pairs={{0,1},{1,0},{2,3},{3,2},{4,5},{5,4},{6,7},{7,6},{8,9},{9,8},{10,11... | collective-permute-start | bytes 1179656 | tf_op jit(solution)/shard_map/ppermute | solution.py:26
  289.0 16.3 %collective-permute-start.52 = (bf16[512,1024]{1,0:T(8,128)(2,1)}, bf16[512,1024]{1,0:T(8,128)(2,1)}, u32[]{:S(2)}, u32[]{:S(2)}) collective-permute-start(bf16[512,1024]{1,0:T(8,128)(2,1)} %convolution_convert_fusion.2), channel_id=1, source_target_pairs={{0,1},{1,0},{2,3},{3,2},{4,5},{5,4},{6,7},{7,6},{8,9},{9,8},{10,11... | collective-permute-start | bytes 3145736 | tf_op jit(solution)/shard_map/ppermute | solution.py:26
  290.7 20.3 %collective-permute-start.56 = (bf16[4,128,512]{2,1,0:T(8,128)(2,1)S(1)}, bf16[4,128,512]{2,1,0:T(8,128)(2,1)S(1)}, u32[]{:S(2)}, u32[]{:S(2)}) collective-permute-start(bf16[4,128,512]{2,1,0:T(8,128)(2,1)S(1)} %shard_map.253), channel_id=1, source_target_pairs={{0,4},{4,0},{8,12},{12,8},{16,20},{20,16},{24,28},{28,24},{1,5},{5... | collective-permute-start | bytes 1572872 | tf_op jit(solution)/shard_map/ppermute | solution.py:447
  295.1 21.1 %collective-permute-start.57 = (bf16[128,1024]{1,0:T(8,128)(2,1)S(1)}, bf16[128,1024]{1,0:T(8,128)(2,1)S(1)}, u32[]{:S(2)}, u32[]{:S(2)}) collective-permute-start(bf16[128,1024]{1,0:T(8,128)(2,1)S(1)} %get-tuple-element.228), channel_id=1, source_target_pairs={{0,8},{4,12},{8,0},{12,4},{16,24},{20,28},{24,16},{28,20},{1,9},{5... | collective-permute-start | bytes 786440 | tf_op jit(solution)/shard_map/ppermute | solution.py:447
  296.9 19.3 %collective-permute-start.58 = (bf16[128,1024]{1,0:T(8,128)(2,1)S(1)}, bf16[128,1024]{1,0:T(8,128)(2,1)S(1)}, u32[]{:S(2)}, u32[]{:S(2)}) collective-permute-start(bf16[128,1024]{1,0:T(8,128)(2,1)S(1)} %get-tuple-element.229), channel_id=1, source_target_pairs={{0,16},{4,20},{8,24},{12,28},{16,0},{20,4},{24,8},{28,12},{1,17},{... | collective-permute-start | bytes 786440 | tf_op jit(solution)/shard_map/ppermute | solution.py:447
  302.5 7.0 %collective-permute-start.55 = (bf16[96,1024]{1,0:T(8,128)(2,1)}, bf16[96,1024]{1,0:T(8,128)(2,1)S(1)}, u32[]{:S(2)}, u32[]{:S(2)}) collective-permute-start(bf16[96,1024]{1,0:T(8,128)(2,1)} %add_convert_fusion.4), channel_id=1, source_target_pairs={{0,2},{1,3},{2,0},{3,1},{4,6},{5,7},{6,4},{7,5},{8,10},{9,11},{10,... | collective-permute-start | bytes 589832 | tf_op jit(solution)/shard_map/ppermute | solution.py:26
  307.0 16.6 %collective-permute-start.53 = (bf16[256,1024]{1,0:T(8,128)(2,1)S(1)}, bf16[256,1024]{1,0:T(8,128)(2,1)S(1)}, u32[]{:S(2)}, u32[]{:S(2)}) collective-permute-start(bf16[256,1024]{1,0:T(8,128)(2,1)S(1)} %fusion.38), channel_id=1, source_target_pairs={{0,2},{1,3},{2,0},{3,1},{4,6},{5,7},{6,4},{7,5},{8,10},{9,11},{10,... | collective-permute-start | bytes 1572872 | tf_op jit(solution)/shard_map/ppermute | solution.py:26
  309.5 14.1 %collective-permute-start.59 = (bf16[128,1024]{1,0:T(8,128)(2,1)S(1)}, bf16[128,1024]{1,0:T(8,128)(2,1)S(1)}, u32[]{:S(2)}, u32[]{:S(2)}) collective-permute-start(bf16[128,1024]{1,0:T(8,128)(2,1)S(1)} %get-tuple-element.230), channel_id=1, source_target_pairs={{0,24},{4,28},{8,16},{12,20},{16,8},{20,12},{24,0},{28,4},{1,25},{... | collective-permute-start | bytes 786440 | tf_op jit(solution)/shard_map/ppermute | solution.py:447
  311.0 32.1 %collective-permute-start.61 = (bf16[4,128,768]{2,1,0:T(8,128)(2,1)S(1)}, bf16[4,128,768]{2,1,0:T(8,128)(2,1)S(1)}, u32[]{:S(2)}, u32[]{:S(2)}) collective-permute-start(bf16[4,128,768]{2,1,0:T(8,128)(2,1)S(1)} %dynamic-slice_bitcast_fusion), channel_id=1, source_target_pairs={{0,4},{4,0},{8,12},{12,8},{16,20},{20,16},{24,28},{28,24},{1,5},{5... | collective-permute-start | bytes 2359304 | tf_op jit(solution)/shard_map/ppermute | solution.py:447
  324.5 16.7 %collective-permute-start.60 = (bf16[128,1024]{1,0:T(8,128)(2,1)S(1)}, bf16[128,1024]{1,0:T(8,128)(2,1)S(1)}, u32[]{:S(2)}, u32[]{:S(2)}) collective-permute-start(bf16[128,1024]{1,0:T(8,128)(2,1)S(1)} %get-tuple-element.234), channel_id=1, source_target_pairs={{0,8},{4,12},{8,0},{12,4},{16,24},{20,28},{24,16},{28,20},{1,9},{5... | collective-permute-start | bytes 786440 | tf_op jit(solution)/shard_map/ppermute | solution.py:447
  330.5 21.4 %collective-permute-start.62 = (bf16[128,1024]{1,0:T(8,128)(2,1)S(1)}, bf16[128,1024]{1,0:T(8,128)(2,1)S(1)}, u32[]{:S(2)}, u32[]{:S(2)}) collective-permute-start(bf16[128,1024]{1,0:T(8,128)(2,1)S(1)} %get-tuple-element.238), channel_id=1, source_target_pairs={{0,16},{4,20},{8,24},{12,28},{16,0},{20,4},{24,8},{28,12},{1,17},{... | collective-permute-start | bytes 786440 | tf_op jit(solution)/shard_map/ppermute | solution.py:447
  331.1 20.8 %collective-permute-start.63 = (bf16[128,1024]{1,0:T(8,128)(2,1)S(1)}, bf16[128,1024]{1,0:T(8,128)(2,1)S(1)}, u32[]{:S(2)}, u32[]{:S(2)}) collective-permute-start(bf16[128,1024]{1,0:T(8,128)(2,1)S(1)} %get-tuple-element.239), channel_id=1, source_target_pairs={{0,24},{4,28},{8,16},{12,20},{16,8},{20,12},{24,0},{28,4},{1,25},{... | collective-permute-start | bytes 786440 | tf_op jit(solution)/shard_map/ppermute | solution.py:447
  343.0 15.3 %collective-permute-start.65 = (f32[8,512]{1,0:T(8,128)S(1)}, f32[8,512]{1,0:T(8,128)S(1)}, u32[]{:S(2)}, u32[]{:S(2)}) collective-permute-start(f32[8,512]{1,0:T(8,128)S(1)} %get-tuple-element.244), channel_id=1, source_target_pairs={{0,1},{1,0},{2,3},{3,2},{4,5},{5,4},{6,7},{7,6},{8,9},{9,8},{10,11... | collective-permute-start | bytes 49160 | tf_op jit(solution)/shard_map/ppermute | solution.py:26
  353.4 10.2 %collective-permute-start.64 = (bf16[128,768]{1,0:T(8,128)(2,1)S(1)}, bf16[128,768]{1,0:T(8,128)(2,1)S(1)}, u32[]{:S(2)}, u32[]{:S(2)}) collective-permute-start(bf16[128,768]{1,0:T(8,128)(2,1)S(1)} %get-tuple-element.242), channel_id=1, source_target_pairs={{0,8},{4,12},{8,0},{12,4},{16,24},{20,28},{24,16},{28,20},{1,9},{5... | collective-permute-start | bytes 589832 | tf_op jit(solution)/shard_map/ppermute | solution.py:447
  361.2 15.1 %collective-permute-start.67 = (bf16[128,768]{1,0:T(8,128)(2,1)}, bf16[128,768]{1,0:T(8,128)(2,1)S(1)}, u32[]{:S(2)}, u32[]{:S(2)}) collective-permute-start(bf16[128,768]{1,0:T(8,128)(2,1)} %get-tuple-element.250), channel_id=1, source_target_pairs={{0,16},{4,20},{8,24},{12,28},{16,0},{20,4},{24,8},{28,12},{1,17},{... | collective-permute-start | bytes 589832 | tf_op jit(solution)/shard_map/ppermute | solution.py:447
  361.5 14.7 %collective-permute-start.68 = (bf16[128,768]{1,0:T(8,128)(2,1)}, bf16[128,768]{1,0:T(8,128)(2,1)}, u32[]{:S(2)}, u32[]{:S(2)}) collective-permute-start(bf16[128,768]{1,0:T(8,128)(2,1)} %get-tuple-element.251), channel_id=1, source_target_pairs={{0,24},{4,28},{8,16},{12,20},{16,8},{20,12},{24,0},{28,4},{1,25},{... | collective-permute-start | bytes 589832 | tf_op jit(solution)/shard_map/ppermute | solution.py:447
  367.0 18.9 %collective-permute-start.74 = (bf16[128,1024]{1,0:T(8,128)(2,1)S(1)}, bf16[128,1024]{1,0:T(8,128)(2,1)S(1)}, u32[]{:S(2)}, u32[]{:S(2)}) collective-permute-start(bf16[128,1024]{1,0:T(8,128)(2,1)S(1)} %get-tuple-element.276), channel_id=1, source_target_pairs={{0,2},{1,3},{2,0},{3,1},{4,6},{5,7},{6,4},{7,5},{8,10},{9,11},{10,... | collective-permute-start | bytes 786440 | tf_op jit(solution)/shard_map/ppermute | solution.py:26
  369.2 14.2 %collective-permute-start.71 = (bf16[128,512]{1,0:T(8,128)(2,1)S(1)}, bf16[128,512]{1,0:T(8,128)(2,1)S(1)}, u32[]{:S(2)}, u32[]{:S(2)}) collective-permute-start(bf16[128,512]{1,0:T(8,128)(2,1)S(1)} %get-tuple-element.265), channel_id=1, source_target_pairs={{0,4},{4,0},{8,12},{12,8},{16,20},{20,16},{24,28},{28,24},{1,5},{5... | collective-permute-start | bytes 393224 | tf_op jit(solution)/shard_map/ppermute | solution.py:447
  370.0 10.2 %collective-permute-start.77 = (f32[8,256]{1,0:T(8,128)S(1)}, f32[8,256]{1,0:T(8,128)S(1)}, u32[]{:S(2)}, u32[]{:S(2)}) collective-permute-start(f32[8,256]{1,0:T(8,128)S(1)} %add.196), channel_id=1, source_target_pairs={{0,8},{4,12},{8,0},{12,4},{16,24},{20,28},{24,16},{28,20},{1,9},{5... | collective-permute-start | bytes 24584 | tf_op jit(solution)/shard_map/ppermute | solution.py:447
  378.6 9.5 %collective-permute-start.69 = (bf16[128,384]{1,0:T(8,128)(2,1)S(1)}, bf16[128,384]{1,0:T(8,128)(2,1)S(1)}, u32[]{:S(2)}, u32[]{:S(2)}) collective-permute-start(bf16[128,384]{1,0:T(8,128)(2,1)S(1)} %get-tuple-element.253), channel_id=1, source_target_pairs={{0,2},{1,3},{2,0},{3,1},{4,6},{5,7},{6,4},{7,5},{8,10},{9,11},{10,... | collective-permute-start | bytes 294920 | tf_op jit(solution)/shard_map/ppermute | solution.py:26
  380.2 7.9 %collective-permute-start.78 = (f32[8,256]{1,0:T(8,128)S(1)}, f32[8,256]{1,0:T(8,128)S(1)}, u32[]{:S(2)}, u32[]{:S(2)}) collective-permute-start(f32[8,256]{1,0:T(8,128)S(1)} %add.197), channel_id=1, source_target_pairs={{0,16},{4,20},{8,24},{12,28},{16,0},{20,4},{24,8},{28,12},{1,17},{... | collective-permute-start | bytes 24584 | tf_op jit(solution)/shard_map/ppermute | solution.py:447
  386.6 7.6 %collective-permute-start.75 = (bf16[128,1024]{1,0:T(8,128)(2,1)S(1)}, bf16[128,1024]{1,0:T(8,128)(2,1)S(1)}, u32[]{:S(2)}, u32[]{:S(2)}) collective-permute-start(bf16[128,1024]{1,0:T(8,128)(2,1)S(1)} %get-tuple-element.278), channel_id=1, source_target_pairs={{0,1},{1,0},{2,3},{3,2},{4,5},{5,4},{6,7},{7,6},{8,9},{9,8},{10,11... | collective-permute-start | bytes 786440 | tf_op jit(solution)/shard_map/ppermute | solution.py:26
  (133 other events, 1159.8 us)
Sparse Core Ops, SparseCore 0:
  102.1 71.1 all-gather.1
  208.2 106.6 reduce-scatter.1
